TPU v7x, 128 devices: a whole 4x4x4 slice. The times are simulated.
128 devices in a mesh: row: 32 (over x, z, core), col: 4 (over y).
Axes of the slice: x: 4, y: 4, z: 4, core: 2. Of those that a mesh axis runs over, the one named last changes fastest.
Arguments:
- subspace: bfloat16 [256, 131072], P('col', 'row'), may hold values from -400 to 400
- onsite: float32 [131072], P('row'), may hold values from -1.5 to 1.5
- blocks: bfloat16 [20, 1024, 128, 128], P(None, 'row'), may hold values from -0.125 to 0.125
- cols: int32 [1024, 20], replicated, may hold values from 0 to 1023, as said below
Outputs:
- basis: float32 [256, 131072], P('col', 'row')
- factor: float32 [256, 256], replicated
Inputs may be any that keep to these rules, and one draw needn't show every extreme that they name: `cols`: the block rows are numbered by device: device r of row holds block rows r * 32 to (r + 1) * 32 - 1. A block row names block rows of its own device or of the devices r + 1, r - 1, r + 2 and r + 16 along row, counted round. The block rows of one device name between 1 and 4 distinct block rows of each of these four devices, and in every draw some device names exactly 4 on each of its four.
All inputs are finite; a program needn't handle non-finite values.
Results may differ from a plain program's by a relative error of at most 0.0044.
Values may be sent and summed in bfloat16 or wider, within the bound.
No kernel may reach another device: no remote copies, remote signals or barrier semaphores. Data moves between devices by JAX's collectives and lax.ppermute only.
A program may use at most 128 MiB of HBM per device.

v0:
```python
import math

import jax
import jax.numpy as jnp
from jax import lax
from jax.sharding import PartitionSpec as P

S = 256
HALO = 4
FILTER = 4


filter_scale = 0.4


def from_partner(value, axis, bit):
    return lax.ppermute(value, axis, [(i, i ^ 1 << bit) for i in range(lax.axis_size(axis))])


def pick_rows(columns, first_block, local_blocks):
    local_ids = first_block + jnp.arange(local_blocks, dtype=jnp.int32)
    hits = jnp.any(columns[..., :, None] == local_ids, axis=-2)
    ranks = jnp.cumsum(hits.astype(jnp.int32), axis=-1) - 1
    slots = jnp.arange(HALO, dtype=jnp.int32)
    select = hits[..., None, :] & (ranks[..., None, :] == slots[:, None])
    return select.astype(jnp.bfloat16)


def body(subspace, onsite, blocks, cols):
    row_count = lax.axis_size("row")
    row_index = lax.axis_index("row")
    part_width, local_rows = subspace.shape
    slot_count, local_blocks, block_size, _ = blocks.shape
    global_blocks = row_count * local_blocks
    first_block = row_index * local_blocks
    own_cols = lax.dynamic_slice_in_dim(cols, first_block, local_blocks, 0)
    every_block = jnp.arange(global_blocks, dtype=jnp.int32)
    matches = own_cols[:, :, None] == every_block
    needed = jnp.any(matches, axis=(0, 1)).astype(jnp.int32).reshape(row_count, local_blocks)
    rank_table = (jnp.cumsum(needed, axis=1) - 1).reshape(-1)
    slot_rank = jnp.sum(jnp.where(matches, rank_table, 0), axis=-1)
    owners = own_cols // local_blocks
    within = own_cols % local_blocks
    device_ids = jnp.arange(row_count, dtype=jnp.int32)
    select_all = pick_rows(
        cols.reshape(row_count, local_blocks * slot_count), first_block, local_blocks
    )
    bases = local_blocks + HALO * device_ids
    base_of = jnp.sum(jnp.where(owners[:, :, None] == device_ids, bases, 0), axis=-1)
    positions = jnp.where(owners == row_index, within, base_of + slot_rank)

    def coupled(lowered):
        shaped = lowered.reshape(part_width, local_blocks, block_size)
        outgoing = jnp.einsum(
            "dqj,cjb->cdqb", select_all, shaped, preferred_element_type=jnp.float32
        ).astype(jnp.bfloat16)
        incoming = lax.all_to_all(outgoing, "row", split_axis=1, concat_axis=1, tiled=True)
        extra = incoming.reshape(part_width, row_count * HALO, block_size)
        extended = jnp.concatenate([shaped, extra], axis=1)
        gathered = jnp.take(extended, positions, axis=1)
        product = jnp.einsum("clsa,slab->clb", gathered, blocks, preferred_element_type=jnp.float32)
        return product.reshape(part_width, local_rows) + onsite[None, :] * lowered.astype(
            jnp.float32
        )

    previous = subspace.astype(jnp.float32)
    current = filter_scale * coupled(subspace)
    for filter_step in range(FILTER - 1):
        lowered = current.astype(jnp.bfloat16)
        following = 2.0 * filter_scale * coupled(lowered) - previous
        previous, current = (current, following)
    final = current.astype(jnp.bfloat16)
    whole = lax.all_gather(final, "col", axis=0, tiled=True)
    gram_local = jnp.einsum("ar,br->ab", whole, whole, preferred_element_type=jnp.float32)
    upper = jnp.linalg.cholesky(gram_local).T
    for level_bit in range(row_count.bit_length() - 1):
        partner = from_partner(upper, "row", level_bit)
        combined = jnp.dot(upper.T, upper, precision=lax.Precision.HIGHEST) + jnp.dot(
            partner.T, partner, precision=lax.Precision.HIGHEST
        )
        upper = jnp.linalg.cholesky(combined).T
    lower = upper.T
    total_rows = row_count * local_rows
    inverse = lax.linalg.triangular_solve(
        lower, jnp.eye(S, dtype=jnp.float32), left_side=True, lower=True
    )
    own_part = lax.dynamic_slice_in_dim(inverse, lax.axis_index("col") * part_width, part_width, 0)
    basis = math.sqrt(total_rows) * jnp.dot(
        own_part, whole.astype(jnp.float32), precision=lax.Precision.HIGHEST
    )
    factor = lower.T / math.sqrt(total_rows)
    return (basis, factor)


def solution(mesh):
    in_specs = (P("col", "row"), P("row"), P(None, "row", None, None), P())
    out_specs = (P("col", "row"), P())
    return jax.shard_map(body, mesh=mesh, in_specs=in_specs, out_specs=out_specs, check_vma=False)
```

profile of v0, /device:TPU:0, one launch (start us, length us, event | category | flops | bytes accessed | tf_op | source)
XLA Modules:
  0.0 615.3 jit_solution(8231274170173515389)
XLA Ops:
  26.1 24.9 %all-to-all-done = bf16[64,32,4,128]{3,0,2,1:T(8,128)(2,1)S(1)} async-done(((bf16[64,32,4,128]{3,0,2,1:T(8,128)(2,1)}), bf16[64,32,4,128]{3,0,2,1:T(8,128)(2,1)S(1)}, u32[]{:S(2)}, u32[]{:S(2)}) %all-to-all-start) | async-done | bytes 2097184 | tf_op jit(solution)/shard_map/all_to_all | solution.py:57
  54.3 18.0 %gather_fusion = bf16[640,64,128]{2,1,0:T(8,128)(2,1)} fusion(bf16[64,160,128]{2,0,1:T(8,128)(2,1)S(1)} %pad_maximum_fusion, s32[1024]{0:T(1024)S(1)} %pad_clamp_fusion), kind=kCustom, calls=%fused_computation.clone | custom fusion | bytes 20974080 | tf_op jit(solution)/shard_map/jit(_take)/gather | solution.py:60
  72.3 12.4 %fusion.25 = f32[32,8,8,128]{3,2,1,0:T(8,128)S(1)} fusion(bf16[20,32,128,128]{3,2,1,0:T(8,128)(2,1)} %param.9, bf16[32,20,64,128]{3,2,1,0:T(8,128)(2,1)} %bitcast.270, pred[32,20]{1,0:T(8,128)(4,1)S(1)} %copy.168), kind=kOutput, calls=%fused_computation.43 | convolution fusion | flops 1347420160 | bytes 32506496 | tf_op jit(solution)/shard_map/clsa,slab->clb/dot_general | solution.py:61
  94.3 27.9 %all-to-all-done.1 = bf16[64,32,4,128]{3,2,0,1:T(4,128)(2,1)S(1)} async-done(((bf16[64,32,4,128]{3,2,0,1:T(4,128)(2,1)}), bf16[64,32,4,128]{3,2,0,1:T(4,128)(2,1)S(1)}, u32[]{:S(2)}, u32[]{:S(2)}) %all-to-all-start.1) | async-done | bytes 2097184 | tf_op jit(solution)/shard_map/all_to_all | solution.py:57
  123.5 18.0 %gather_fusion.1 = bf16[640,64,128]{2,1,0:T(8,128)(2,1)} fusion(bf16[64,160,128]{2,0,1:T(8,128)(2,1)S(1)} %pad_maximum_fusion.1, s32[1024]{0:T(1024)S(1)} %pad_clamp_fusion), kind=kCustom, calls=%fused_computation.1.clone | custom fusion | bytes 20974080 | tf_op jit(solution)/shard_map/jit(_take)/gather | solution.py:60
  141.5 12.4 %fusion.30 = f32[32,8,8,128]{3,2,1,0:T(8,128)S(1)} fusion(bf16[20,32,128,128]{3,2,1,0:T(8,128)(2,1)} %param.9, bf16[32,20,64,128]{3,2,1,0:T(8,128)(2,1)} %bitcast.271, pred[32,20]{1,0:T(8,128)(4,1)S(1)} %copy.168), kind=kOutput, calls=%fused_computation.44 | convolution fusion | flops 1347420160 | bytes 32506496 | tf_op jit(solution)/shard_map/clsa,slab->clb/dot_general | solution.py:61
  163.2 27.9 %all-to-all-done.2 = bf16[64,32,4,128]{3,2,0,1:T(4,128)(2,1)S(1)} async-done(((bf16[64,32,4,128]{3,2,0,1:T(4,128)(2,1)}), bf16[64,32,4,128]{3,2,0,1:T(4,128)(2,1)S(1)}, u32[]{:S(2)}, u32[]{:S(2)}) %all-to-all-start.2) | async-done | bytes 2097184 | tf_op jit(solution)/shard_map/all_to_all | solution.py:57
  192.4 18.0 %gather_fusion.2 = bf16[640,64,128]{2,1,0:T(8,128)(2,1)} fusion(bf16[64,160,128]{2,0,1:T(8,128)(2,1)S(1)} %pad_maximum_fusion.2, s32[1024]{0:T(1024)S(1)} %pad_clamp_fusion), kind=kCustom, calls=%fused_computation.2.clone | custom fusion | bytes 20974080 | tf_op jit(solution)/shard_map/jit(_take)/gather | solution.py:60
  210.5 12.4 %fusion.35 = f32[32,8,8,128]{3,2,1,0:T(8,128)S(1)} fusion(bf16[20,32,128,128]{3,2,1,0:T(8,128)(2,1)} %param.9, bf16[32,20,64,128]{3,2,1,0:T(8,128)(2,1)} %bitcast.272, pred[32,20]{1,0:T(8,128)(4,1)S(1)} %copy.168), kind=kOutput, calls=%fused_computation.45 | convolution fusion | flops 1347420160 | bytes 32506496 | tf_op jit(solution)/shard_map/clsa,slab->clb/dot_general | solution.py:61
  231.8 27.7 %all-to-all-done.3 = bf16[64,32,4,128]{3,2,0,1:T(4,128)(2,1)S(1)} async-done(((bf16[64,32,4,128]{3,2,0,1:T(4,128)(2,1)}), bf16[64,32,4,128]{3,2,0,1:T(4,128)(2,1)S(1)}, u32[]{:S(2)}, u32[]{:S(2)}) %all-to-all-start.3) | async-done | bytes 2097184 | tf_op jit(solution)/shard_map/all_to_all | solution.py:57
  260.7 18.0 %gather_fusion.3 = bf16[640,64,128]{2,1,0:T(8,128)(2,1)} fusion(bf16[64,160,128]{2,0,1:T(8,128)(2,1)S(1)} %pad_maximum_fusion.3, s32[1024]{0:T(1024)S(1)} %pad_clamp_fusion), kind=kCustom, calls=%fused_computation.3.clone | custom fusion | bytes 20974080 | tf_op jit(solution)/shard_map/jit(_take)/gather | solution.py:60
  278.8 12.9 %fusion.40 = f32[32,8,8,128]{3,2,1,0:T(8,128)S(1)} fusion(bf16[20,32,128,128]{3,2,1,0:T(8,128)(2,1)} %param.9, bf16[32,20,64,128]{3,2,1,0:T(8,128)(2,1)} %bitcast.269, pred[32,20]{1,0:T(8,128)(4,1)S(1)} %copy.168), kind=kOutput, calls=%fused_computation.46 | convolution fusion | flops 1347420160 | bytes 32506496 | tf_op jit(solution)/shard_map/clsa,slab->clb/dot_general | solution.py:61
  292.9 28.4 %all-gather.2.cloned.1.call-done = bf16[256,4096]{1,0:T(8,128)(2,1)} async-done(((bf16[64,4096]{1,0:T(8,128)(2,1)}), bf16[256,4096]{1,0:T(8,128)(2,1)}) %all-gather.2.cloned.1.call-update) | async-done | bytes 2097168 | tf_op jit(solution)/shard_map/all_gather | solution.py:73
  324.5 11.7 %cholesky.298 = f32[128,128]{1,0:T(8,128)S(1)} custom-call(f32[128,128]{1,0:T(8,128)S(1)} %cholesky.498), custom_call_target="Cholesky" | custom-call | tf_op jit(solution)/shard_map/jit(cholesky)/cholesky | solution.py:75
  336.3 9.8 %custom-call.17 = f32[1,128,128]{1,2,0:T(8,128)S(1)} custom-call(f32[1,128,128]{2,1,0:T(8,128)S(1)} %get-tuple-element.61), custom_call_target="InvertDiagBlocksLowerTriangular" | custom-call | tf_op jit(solution)/shard_map/jit(cholesky)/cholesky | solution.py:75
  346.6 11.7 %cholesky.315 = f32[128,128]{1,0:T(8,128)S(1)} custom-call(f32[128,128]{1,0:T(8,128)S(1)} %convolution_subtract_fusion.1), custom_call_target="Cholesky" | custom-call | tf_op jit(solution)/shard_map/jit(cholesky)/cholesky | solution.py:75
  362.7 11.7 %cholesky.332 = f32[128,128]{1,0:T(8,128)S(1)} custom-call(f32[128,128]{1,0:T(8,128)S(1)} %cholesky.501), custom_call_target="Cholesky" | custom-call | tf_op jit(solution)/shard_map/jit(cholesky)/cholesky | solution.py:81
  374.5 9.8 %custom-call.18 = f32[1,128,128]{1,2,0:T(8,128)S(1)} custom-call(f32[1,128,128]{2,1,0:T(8,128)S(1)} %get-tuple-element.57), custom_call_target="InvertDiagBlocksLowerTriangular" | custom-call | tf_op jit(solution)/shard_map/jit(cholesky)/cholesky | solution.py:81
  384.8 11.7 %cholesky.349 = f32[128,128]{1,0:T(8,128)S(1)} custom-call(f32[128,128]{1,0:T(8,128)S(1)} %slice_subtract_fusion.4), custom_call_target="Cholesky" | custom-call | tf_op jit(solution)/shard_map/jit(cholesky)/cholesky | solution.py:81
  408.4 11.7 %cholesky.366 = f32[128,128]{1,0:T(8,128)S(1)} custom-call(f32[128,128]{1,0:T(8,128)S(1)} %cholesky.504), custom_call_target="Cholesky" | custom-call | tf_op jit(solution)/shard_map/jit(cholesky)/cholesky | solution.py:81
  420.1 9.8 %custom-call.19 = f32[1,128,128]{1,2,0:T(8,128)S(1)} custom-call(f32[1,128,128]{2,1,0:T(8,128)S(1)} %get-tuple-element.53), custom_call_target="InvertDiagBlocksLowerTriangular" | custom-call | tf_op jit(solution)/shard_map/jit(cholesky)/cholesky | solution.py:81
  430.4 11.7 %cholesky.383 = f32[128,128]{1,0:T(8,128)S(1)} custom-call(f32[128,128]{1,0:T(8,128)S(1)} %slice_subtract_fusion.3), custom_call_target="Cholesky" | custom-call | tf_op jit(solution)/shard_map/jit(cholesky)/cholesky | solution.py:81
  454.9 11.7 %cholesky.400 = f32[128,128]{1,0:T(8,128)S(1)} custom-call(f32[128,128]{1,0:T(8,128)S(1)} %cholesky.507), custom_call_target="Cholesky" | custom-call | tf_op jit(solution)/shard_map/jit(cholesky)/cholesky | solution.py:81
  466.7 9.8 %custom-call.20 = f32[1,128,128]{1,2,0:T(8,128)S(1)} custom-call(f32[1,128,128]{2,1,0:T(8,128)S(1)} %get-tuple-element.49), custom_call_target="InvertDiagBlocksLowerTriangular" | custom-call | tf_op jit(solution)/shard_map/jit(cholesky)/cholesky | solution.py:81
  477.0 11.7 %cholesky.417 = f32[128,128]{1,0:T(8,128)S(1)} custom-call(f32[128,128]{1,0:T(8,128)S(1)} %slice_subtract_fusion.2), custom_call_target="Cholesky" | custom-call | tf_op jit(solution)/shard_map/jit(cholesky)/cholesky | solution.py:81
  498.8 11.7 %cholesky.434 = f32[128,128]{1,0:T(8,128)S(1)} custom-call(f32[128,128]{1,0:T(8,128)S(1)} %cholesky.510), custom_call_target="Cholesky" | custom-call | tf_op jit(solution)/shard_map/jit(cholesky)/cholesky | solution.py:81
  510.5 9.8 %custom-call.21 = f32[1,128,128]{1,2,0:T(8,128)S(1)} custom-call(f32[1,128,128]{2,1,0:T(8,128)S(1)} %get-tuple-element.45), custom_call_target="InvertDiagBlocksLowerTriangular" | custom-call | tf_op jit(solution)/shard_map/jit(cholesky)/cholesky | solution.py:81
  520.8 11.7 %cholesky.451 = f32[128,128]{1,0:T(8,128)S(1)} custom-call(f32[128,128]{1,0:T(8,128)S(1)} %slice_subtract_fusion.1), custom_call_target="Cholesky" | custom-call | tf_op jit(solution)/shard_map/jit(cholesky)/cholesky | solution.py:81
  544.0 11.7 %cholesky.468 = f32[128,128]{1,0:T(8,128)S(1)} custom-call(f32[128,128]{1,0:T(8,128)S(1)} %cholesky.513), custom_call_target="Cholesky" | custom-call | tf_op jit(solution)/shard_map/jit(cholesky)/cholesky | solution.py:81
  555.7 9.8 %custom-call.22 = f32[1,128,128]{1,2,0:T(8,128)S(1)} custom-call(f32[1,128,128]{2,1,0:T(8,128)S(1)} %get-tuple-element.41), custom_call_target="InvertDiagBlocksLowerTriangular" | custom-call | tf_op jit(solution)/shard_map/jit(cholesky)/cholesky | solution.py:81
  566.0 11.7 %cholesky.485 = f32[128,128]{1,0:T(8,128)S(1)} custom-call(f32[128,128]{1,0:T(8,128)S(1)} %slice_subtract_fusion), custom_call_target="Cholesky" | custom-call | tf_op jit(solution)/shard_map/jit(cholesky)/cholesky | solution.py:81
  584.6 19.7 %custom-call.11 = f32[2,128,128]{1,2,0:T(8,128)S(1)} custom-call(f32[2,128,128]{2,1,0:T(8,128)S(1)} %get-tuple-element.11), custom_call_target="InvertDiagBlocksLowerTriangular" | custom-call | tf_op jit(solution)/shard_map/triangular_solve | solution.py:84
  (193 shorter events, 118.2 us)
Async XLA Ops:
  11.4 13.8 %copy-start.1 = (bf16[64,4096]{1,0:T(8,128)(2,1)S(1)}, bf16[64,4096]{1,0:T(8,128)(2,1)}, u32[]{:S(2)}) copy-start(bf16[64,4096]{1,0:T(8,128)(2,1)} %param.7) | copy-start | bytes 1572868
  13.5 37.5 %all-to-all-start = ((bf16[64,32,4,128]{3,0,2,1:T(8,128)(2,1)}), bf16[64,32,4,128]{3,0,2,1:T(8,128)(2,1)S(1)}, u32[]{:S(2)}, u32[]{:S(2)}) async-start(bf16[64,32,4,128]{3,0,2,1:T(8,128)(2,1)} %copy.173), calls=%async_computation | async-start | bytes 4194304 | tf_op jit(solution)/shard_map/all_to_all | solution.py:57
  51.0 1.4 copy-start.7
  72.3 12.4 %copy-start.17 = (f32[4096]{0:T(1024)S(1)}, f32[4096]{0:T(1024)}, u32[]{:S(2)}) copy-start(f32[4096]{0:T(1024)} %param.8) | copy-start | bytes 49156
  84.7 1.0 copy-start.10
  84.9 8.4 %copy-start.2 = (bf16[64,4096]{1,0:T(8,128)(2,1)}, bf16[64,4096]{1,0:T(8,128)(2,1)S(1)}, u32[]{:S(2)}) copy-start(bf16[64,4096]{1,0:T(8,128)(2,1)S(1)} %fusion.54) | copy-start | bytes 1572868
  88.8 33.4 %all-to-all-start.1 = ((bf16[64,32,4,128]{3,2,0,1:T(4,128)(2,1)}), bf16[64,32,4,128]{3,2,0,1:T(4,128)(2,1)S(1)}, u32[]{:S(2)}, u32[]{:S(2)}) async-start(bf16[64,32,4,128]{3,2,0,1:T(4,128)(2,1)} %copy.178), calls=%async_computation.1 | async-start | bytes 4194304 | tf_op jit(solution)/shard_map/all_to_all | solution.py:57
  122.2 1.0 copy-start.14
  141.5 12.4 %copy-start.3 = (bf16[64,4096]{1,0:T(8,128)(2,1)S(1)}, bf16[64,4096]{1,0:T(8,128)(2,1)}, u32[]{:S(2)}) copy-start(bf16[64,4096]{1,0:T(8,128)(2,1)} %copy-done.2) | copy-start | bytes 1572868
  154.0 1.0 copy-start.12
  154.2 8.0 %copy-start.5 = (bf16[64,4096]{1,0:T(8,128)(2,1)}, bf16[64,4096]{1,0:T(8,128)(2,1)S(1)}, u32[]{:S(2)}) copy-start(bf16[64,4096]{1,0:T(8,128)(2,1)S(1)} %fusion.75) | copy-start | bytes 1572868
  158.1 33.1 %all-to-all-start.2 = ((bf16[64,32,4,128]{3,2,0,1:T(4,128)(2,1)}), bf16[64,32,4,128]{3,2,0,1:T(4,128)(2,1)S(1)}, u32[]{:S(2)}, u32[]{:S(2)}) async-start(bf16[64,32,4,128]{3,2,0,1:T(4,128)(2,1)} %copy.184), calls=%async_computation.2 | async-start | bytes 4194304 | tf_op jit(solution)/shard_map/all_to_all | solution.py:57
  191.1 1.0 copy-start.15
  210.4 12.5 %copy-start.6 = (bf16[64,4096]{1,0:T(8,128)(2,1)S(1)}, bf16[64,4096]{1,0:T(8,128)(2,1)}, u32[]{:S(2)}) copy-start(bf16[64,4096]{1,0:T(8,128)(2,1)} %copy-done.5) | copy-start | bytes 1572868
  210.5 12.5 %copy-start.11 = (f32[32,8,8,128]{3,2,1,0:T(8,128)S(1)}, f32[32,8,8,128]{3,2,1,0:T(8,128)}, u32[]{:S(2)}) copy-start(f32[32,8,8,128]{3,2,1,0:T(8,128)} %copy-done.10) | copy-start | bytes 3145732
  223.3 7.5 %copy-start.8 = (bf16[64,4096]{1,0:T(8,128)(2,1)}, bf16[64,4096]{1,0:T(8,128)(2,1)S(1)}, u32[]{:S(2)}) copy-start(bf16[64,4096]{1,0:T(8,128)(2,1)S(1)} %fusion.52) | copy-start | bytes 1572868
  226.5 32.9 %all-to-all-start.3 = ((bf16[64,32,4,128]{3,2,0,1:T(4,128)(2,1)}), bf16[64,32,4,128]{3,2,0,1:T(4,128)(2,1)S(1)}, u32[]{:S(2)}, u32[]{:S(2)}) async-start(bf16[64,32,4,128]{3,2,0,1:T(4,128)(2,1)} %copy.190), calls=%async_computation.3 | async-start | bytes 4194304 | tf_op jit(solution)/shard_map/all_to_all | solution.py:57
  230.6 90.8 %all-gather.2.cloned.1.call-start = ((), (), s32[]{:S(2)}) async-start(), calls=%async_computation.4 | async-start | bytes 2621440 | tf_op jit(solution)/shard_map/all_gather | solution.py:73
  259.5 1.0 copy-start.16
  278.8 12.9 %copy-start.4 = (bf16[64,4096]{1,0:T(8,128)(2,1)S(1)}, bf16[64,4096]{1,0:T(8,128)(2,1)}, u32[]{:S(2)}) copy-start(bf16[64,4096]{1,0:T(8,128)(2,1)} %copy-done.2) | copy-start | bytes 1572868
  278.8 12.9 %copy-start.9 = (bf16[64,4096]{1,0:T(8,128)(2,1)S(1)}, bf16[64,4096]{1,0:T(8,128)(2,1)}, u32[]{:S(2)}) copy-start(bf16[64,4096]{1,0:T(8,128)(2,1)} %copy-done.8) | copy-start | bytes 1572868
  278.8 12.9 %copy-start.13 = (f32[32,8,8,128]{3,2,1,0:T(8,128)S(1)}, f32[32,8,8,128]{3,2,1,0:T(8,128)}, u32[]{:S(2)}) copy-start(f32[32,8,8,128]{3,2,1,0:T(8,128)} %copy-done.12) | copy-start | bytes 3145732
  360.3 1.8 collective-permute-start
  399.1 8.6 %collective-permute-start.1 = (f32[256,256]{0,1:T(8,128)S(1)}, f32[256,256]{0,1:T(8,128)S(1)}, u32[]{:S(2)}, u32[]{:S(2)}) collective-permute-start(f32[256,256]{0,1:T(8,128)S(1)} %fusion.67), channel_id=1, source_target_pairs={{0,8},{4,12},{8,0},{12,4},{16,24},{20,28},{24,16},{28,20},{32,40},... | collective-permute-start | bytes 786440 | tf_op jit(solution)/shard_map/ppermute | solution.py:17
  444.8 9.5 %collective-permute-start.2 = (f32[256,256]{0,1:T(8,128)S(1)}, f32[256,256]{0,1:T(8,128)S(1)}, u32[]{:S(2)}, u32[]{:S(2)}) collective-permute-start(f32[256,256]{0,1:T(8,128)S(1)} %fusion.69), channel_id=1, source_target_pairs={{0,16},{4,20},{8,24},{12,28},{16,0},{20,4},{24,8},{28,12},{32,48},... | collective-permute-start | bytes 786440 | tf_op jit(solution)/shard_map/ppermute | solution.py:17
  491.3 6.8 %collective-permute-start.3 = (f32[256,256]{0,1:T(8,128)S(1)}, f32[256,256]{0,1:T(8,128)S(1)}, u32[]{:S(2)}, u32[]{:S(2)}) collective-permute-start(f32[256,256]{0,1:T(8,128)S(1)} %fusion.71), channel_id=1, source_target_pairs={{0,32},{4,36},{8,40},{12,44},{16,48},{20,52},{24,56},{28,60},{32,0... | collective-permute-start | bytes 786440 | tf_op jit(solution)/shard_map/ppermute | solution.py:17
  520.3 85.7 %copy-start = (bf16[256,4096]{1,0:T(8,128)(2,1)S(1)}, bf16[256,4096]{1,0:T(8,128)(2,1)}, u32[]{:S(2)}) copy-start(bf16[256,4096]{1,0:T(8,128)(2,1)} %all-gather.2.cloned.1.call-done) | copy-start | bytes 6291460
  535.2 8.2 %collective-permute-start.4 = (f32[256,256]{0,1:T(8,128)S(1)}, f32[256,256]{0,1:T(8,128)S(1)}, u32[]{:S(2)}, u32[]{:S(2)}) collective-permute-start(f32[256,256]{0,1:T(8,128)S(1)} %fusion.73), channel_id=1, source_target_pairs={{0,64},{4,68},{8,72},{12,76},{16,80},{20,84},{24,88},{28,92},{32,9... | collective-permute-start | bytes 786440 | tf_op jit(solution)/shard_map/ppermute | solution.py:17
Sparse Core Ops, SparseCore 0:
  293.1 28.2 all-gather.1
where the time goes:
time: 619 us; the launch traced here: 615 us
  other arithmetic  235 us (38%)
  waiting for transfers between devices  159 us (26%)
  local copies, waits for them, and re-layouts  100 us (16%)
  matrix products  65.8 us (11%)
  starting transfers between devices  32.3 us (5%)
  between operations  22.9 us (4%)
    another operation x35, other arithmetic, body(): upper = jnp.linalg.cholesky(combined).T  173 us
    all_to_all x4, waiting for transfers between devices, coupled(): lax.all_to_all(outgoing, 'row', split_axis=1, concat_axis=1, tiled=True)  108 us
    gather x4, local copies, waits for them, and re-layouts, coupled(): gathered = jnp.take(extended, positions, axis=1)  72.1 us
    dot_general x4, matrix products, coupled(): jnp.einsum('clsa,slab->clb', gathered, blocks, preferred_element_type=jnp...  50.1 us
    another operation x6, other arithmetic, body(): upper = jnp.linalg.cholesky(gram_local).T  34 us
    all_gather x1, waiting for transfers between devices, body(): whole = lax.all_gather(final, 'col', axis=0, tiled=True)  28.4 us
    ppermute x5, waiting for transfers between devices, from_partner(): lax.ppermute(value, axis, [(i, i ^ 1 << bit) for i in range(lax.axis_size...  22 us
    all_to_all x4, starting transfers between devices, coupled(): lax.all_to_all(outgoing, 'row', split_axis=1, concat_axis=1, tiled=True)  21.3 us
  transfers between devices with their start and end apart: 10, of which 10 were waited for; matrix products, arithmetic and copies ran while one was open for 1% of the time, Pallas kernels for 0%

commit v1 on v0

v1 whole, which is shorter than its diff:
```python
import functools
import math

import jax
import jax.numpy as jnp
from jax import lax
from jax.experimental import pallas as pl
from jax.experimental.pallas import tpu as pltpu
from jax.sharding import PartitionSpec as P

HALO = 4
FILTER = 4
ROWS = 2
CHUNK = 8
RING = 16

filter_scale = 0.4


def offsets(row_count):
    return (1, -1, 2, row_count // 2)


def ranks_of(hits):
    return jnp.cumsum(hits.astype(jnp.int32), axis=-1) - 1


def plan(cols, row_index, row_count, local_blocks):
    slot_count = cols.shape[1]
    slots = local_blocks * slot_count
    by_device = cols.reshape(row_count, slots)
    deltas = jnp.array(offsets(row_count), jnp.int32)
    local_ids = jnp.arange(local_blocks, dtype=jnp.int32)
    own = lax.dynamic_index_in_dim(by_device, row_index, 0, keepdims=False)
    askers = (row_index - deltas) % row_count
    asked = jnp.take(by_device, askers, axis=0) - row_index * local_blocks
    asked_hits = jnp.any(asked[:, :, None] == local_ids, axis=1)
    asked_ranks = ranks_of(asked_hits)
    wanted = jnp.arange(HALO, dtype=jnp.int32)
    pick = asked_hits[:, None, :] & (asked_ranks[:, None, :] == wanted[None, :, None])
    send = jnp.sum(jnp.where(pick, local_ids, 0), axis=-1).reshape(-1)
    sources = (row_index + deltas) % row_count
    named_ids = (sources[:, None] * local_blocks + local_ids).reshape(-1)
    matches = own[:, None] == named_ids
    named_hits = jnp.any(matches, axis=0).reshape(len(deltas), local_blocks)
    base = HALO * jnp.arange(len(deltas), dtype=jnp.int32)
    places = (ranks_of(named_hits) + base[:, None]).reshape(-1)
    slot_place = jnp.sum(jnp.where(matches, places, 0), axis=-1)
    within = own - row_index * local_blocks
    is_local = (within >= 0) & (within < local_blocks)
    position = jnp.where(is_local, within, local_blocks)
    order = ranks_of(~is_local)
    slot_ids = jnp.arange(slots, dtype=jnp.int32)
    hit = (~is_local)[:, None] & (order[:, None] == slot_ids)
    code = slot_ids * 32 + slot_place
    pad_code = HALO * len(deltas)
    listed = jnp.sum(jnp.where(hit, code[:, None] - pad_code, 0), axis=0) + pad_code
    count = (order[-1:] + 1).astype(jnp.int32)
    return position, jnp.concatenate([count, send, listed])


def local_kernel(scale, first, pos, *refs):
    if first:
        blocks, x, onsite, y, held = refs
    else:
        blocks, x, onsite, prev, y, held = refs
    step = pl.program_id(0)
    slot_count, rows, size, _ = blocks.shape
    local_blocks = held.shape[0] - 1

    @pl.when(step == 0)
    def _():
        for j in range(local_blocks):
            held[j] = x[:, j * size : (j + 1) * size]
        held[local_blocks] = jnp.zeros(held.shape[1:], held.dtype)

    for r in range(rows):
        row = step * rows + r
        taken = jnp.concatenate(
            [held[pos[row * slot_count + s]] for s in range(slot_count)], axis=1
        )
        product = jnp.dot(
            taken,
            blocks[:, r].reshape(slot_count * size, size),
            preferred_element_type=jnp.float32,
        )
        span = slice(r * size, (r + 1) * size)
        value = scale * (product + onsite[:, span] * held[row].astype(jnp.float32))
        y[:, span] = value if first else value - prev[:, span]


def local_part(scale, pos, blocks, x, onsite, prev):
    slot_count, local_blocks, size, _ = blocks.shape
    width = x.shape[0]
    first = prev is None
    wide = ROWS * size
    in_specs = [
        pl.BlockSpec((slot_count, ROWS, size, size), lambda g, p: (0, g, 0, 0)),
        pl.BlockSpec(x.shape, lambda g, p: (0, 0)),
        pl.BlockSpec((1, wide), lambda g, p: (0, g)),
    ]
    args = [blocks, x, onsite]
    if not first:
        in_specs.append(pl.BlockSpec((width, wide), lambda g, p: (0, g)))
        args.append(prev)
    return pl.pallas_call(
        functools.partial(local_kernel, scale, first),
        out_shape=jax.ShapeDtypeStruct(x.shape, jnp.float32),
        grid_spec=pltpu.PrefetchScalarGridSpec(
            num_scalar_prefetch=1,
            grid=(local_blocks // ROWS,),
            in_specs=in_specs,
            out_specs=pl.BlockSpec((width, wide), lambda g, p: (0, g)),
            scratch_shapes=[pltpu.VMEM((local_blocks + 1, width, size), jnp.bfloat16)],
        ),
        name="local_part",
    )(pos, *args)


def remote_kernel(scale, last, info, *refs):
    halos, rest = refs[:4], refs[4:]
    y_in, blocks, y, x, send, zero, held, sems = rest
    slot_count, local_blocks, size, _ = blocks.shape
    per = halos[0].shape[0]
    count = info[0]
    list_at = 1 + 4 * per
    chunks = (count + CHUNK - 1) // CHUNK

    def start(c):
        slot = lax.rem(c, RING)
        for k in range(CHUNK):
            entry = info[list_at + c * CHUNK + k] // 32
            row = entry // slot_count
            pltpu.make_async_copy(
                blocks.at[entry - row * slot_count, row],
                held.at[slot * CHUNK + k],
                sems.at[slot],
            ).start()

    @pl.loop(0, jnp.minimum(chunks, RING))
    def _(c):
        start(c)

    for q in range(4):
        zero[q * per : (q + 1) * per] = halos[q][...]
    zero[4 * per] = jnp.zeros(zero.shape[1:], zero.dtype)
    y[...] = y_in[...]

    @pl.loop(0, chunks)
    def _(c):
        slot = lax.rem(c, RING)
        part = held.at[pl.ds(slot * CHUNK, CHUNK)]
        pltpu.make_async_copy(part, part, sems.at[slot]).wait()
        for k in range(CHUNK):
            code = info[list_at + c * CHUNK + k]
            entry = code // 32
            place = lax.rem(code, 32)
            row = entry // slot_count
            product = jnp.dot(
                zero[place], held[slot * CHUNK + k], preferred_element_type=jnp.float32
            )
            span = pl.ds(pl.multiple_of(row * size, size), size)
            y[:, span] = y[:, span] + scale * product

        @pl.when(c + RING < chunks)
        def _():
            start(c + RING)

    x[...] = y[...].astype(jnp.bfloat16)
    if not last:
        for q in range(4):
            for k in range(per):
                j = info[1 + q * per + k]
                send[q, k] = x[:, pl.ds(pl.multiple_of(j * size, size), size)]
    else:
        own = info[list_at + slot_count * local_blocks]
        piece = x.shape[1] // 4
        for k in range(1, 4):
            at = lax.rem(own + k, 4) * piece
            send[k - 1] = x[:, pl.ds(pl.multiple_of(at, piece), piece)]


def remote_part(scale, last, info, halos, y, blocks):
    slot_count, local_blocks, size, _ = blocks.shape
    width, local_rows = y.shape
    per = halos[0].shape[0]
    vmem = pl.BlockSpec(memory_space=pltpu.VMEM)
    if last:
        send = (3, width, local_rows // 4)
    else:
        send = (4, per, width, size)
    return pl.pallas_call(
        functools.partial(remote_kernel, scale, last),
        out_shape=(
            jax.ShapeDtypeStruct(y.shape, jnp.float32),
            jax.ShapeDtypeStruct(y.shape, jnp.bfloat16),
            jax.ShapeDtypeStruct(send, jnp.bfloat16),
        ),
        in_specs=[pl.BlockSpec(memory_space=pltpu.SMEM)]
        + [vmem] * 5
        + [pl.BlockSpec(memory_space=pl.ANY)],
        out_specs=(vmem,) * 3,
        scratch_shapes=[
            pltpu.VMEM((4 * per + 1, width, size), jnp.bfloat16),
            pltpu.VMEM((RING * CHUNK, size, size), jnp.bfloat16),
            pltpu.SemaphoreType.DMA((RING,)),
        ],
        name="remote_part",
    )(info, *halos, y, blocks)


def shift(value, axis, by):
    n = lax.axis_size(axis)
    return lax.ppermute(value, axis, [(i, (i + by) % n) for i in range(n)])


def swap(value, axis, mask):
    n = lax.axis_size(axis)
    return lax.ppermute(value, axis, [(i, i ^ mask) for i in range(n)])


def xor_sum(value, axis, masks):
    terms = [value] + [swap(value, axis, m) for m in masks]
    while len(terms) > 1:
        terms = [terms[i] + terms[i + 1] for i in range(0, len(terms), 2)]
    return terms[0]


def body(subspace, onsite, blocks, cols):
    row_count = lax.axis_size("row")
    row_index = lax.axis_index("row")
    col_count = lax.axis_size("col")
    col_index = lax.axis_index("col")
    width, local_rows = subspace.shape
    slot_count, local_blocks, size, _ = blocks.shape
    total_cols = width * col_count
    pos, info = plan(cols, row_index, row_count, local_blocks)
    info = jnp.concatenate([info, col_index[None].astype(jnp.int32)])
    onsite = onsite[None, :]
    shaped = subspace.reshape(width, local_blocks, size)
    chosen = jnp.take(shaped, info[1 : 1 + 4 * HALO], axis=1)
    send = chosen.transpose(1, 0, 2).reshape(4, HALO, width, size)
    previous, x = None, subspace
    before = subspace.astype(jnp.float32)
    for step in range(FILTER):
        scale = filter_scale if step == 0 else 2.0 * filter_scale
        last = step == FILTER - 1
        halos = [shift(send[q], "row", -d) for q, d in enumerate(offsets(row_count))]
        partial = local_part(scale, pos, blocks, x, onsite, previous)
        y, x, send = remote_part(scale, last, info, halos, partial, blocks)
        previous, before = before, y
    final = x
    piece = local_rows // col_count
    mine = lax.dynamic_slice_in_dim(final, col_index * piece, piece, 1)
    got = [shift(send[k - 1], "col", k) for k in range(1, col_count)]
    others = [shift(final, "col", k) for k in range(1, col_count)]
    stack = jnp.concatenate([mine] + got, axis=0)
    gram = jnp.einsum("ar,br->ab", stack, stack, preferred_element_type=jnp.float32)
    gram = gram.reshape(col_count, width, col_count, width)
    order = (col_index - jnp.arange(col_count)) % col_count
    gram = jnp.take(jnp.take(gram, order, axis=0), order, axis=2)
    gram = gram.reshape(col_count, width, total_cols)

    def part(k):
        return lax.dynamic_index_in_dim(gram, (col_index + k) % col_count, 0, keepdims=False)

    strip = part(0)
    for k in range(1, col_count):
        strip = strip + shift(part(k), "col", k)
    low = row_count // 4
    strip = xor_sum(strip, "row", list(range(1, low)))
    strip = xor_sum(strip, "row", [low * m for m in (1, 2, 3)])
    strips = jnp.stack([strip] + [shift(strip, "col", k) for k in range(1, col_count)])
    gram = jnp.take(strips, order, axis=0).reshape(total_cols, total_cols)
    lower = jnp.linalg.cholesky(gram)
    total_rows = row_count * local_rows
    inverse = lax.linalg.triangular_solve(
        lower, jnp.eye(total_cols, dtype=jnp.float32), left_side=True, lower=True
    )
    own_part = lax.dynamic_slice_in_dim(inverse, col_index * width, width, 0)
    own_part = own_part.reshape(width, col_count, width)
    own_part = jnp.take(own_part, order, axis=1).reshape(width, total_cols)
    whole = jnp.concatenate([final] + others, axis=0)
    basis = math.sqrt(total_rows) * jnp.dot(
        own_part, whole.astype(jnp.float32), precision=lax.Precision.HIGHEST
    )
    factor = lower.T / math.sqrt(total_rows)
    return (basis, factor)


def solution(mesh):
    in_specs = (P("col", "row"), P("row"), P(None, "row", None, None), P())
    out_specs = (P("col", "row"), P())
    return jax.shard_map(body, mesh=mesh, in_specs=in_specs, out_specs=out_specs, check_vma=False)
```

time: 619 us -> 270 us (0.44)
  the two profiles are of different devices: /device:TPU:0 before, /device:TPU:30 now
where the time goes in v1:
time: 270 us; the launch traced here: 268 us
  Pallas kernels  86.5 us (32%)
  other arithmetic  60.7 us (22%)
  starting transfers between devices  57.1 us (21%)
  waiting for transfers between devices  32.5 us (12%)
  local copies, waits for them, and re-layouts  23.5 us (9%)
  matrix products  3.87 us (1%)
  between operations  3.33 us (1%)
    pallas_call x4, Pallas kernels, local_part(): pl.pallas_call(functools.partial(local_kernel, scale, first), out_shape=j...  67.1 us
    ppermute x28, starting transfers between devices, shift(): return lax.ppermute(value, axis, [(i, (i + by) % n) for i in range(n)])  40.7 us
    another operation x7, other arithmetic, body(): lower = jnp.linalg.cholesky(gram)  34.6 us
    ppermute x28, waiting for transfers between devices, shift(): return lax.ppermute(value, axis, [(i, (i + by) % n) for i in range(n)])  22.4 us
    another operation x3, other arithmetic, body(): lax.linalg.triangular_solve(lower, jnp.eye(total_cols, dtype=jnp.float32)...  19.7 us
    pallas_call x4, Pallas kernels, remote_part(): pl.pallas_call(functools.partial(remote_kernel, scale, last), out_shape=(...  19.4 us
    ppermute x10, starting transfers between devices, swap(): return lax.ppermute(value, axis, [(i, i ^ mask) for i in range(n)])  16.3 us
    ppermute x10, waiting for transfers between devices, swap(): return lax.ppermute(value, axis, [(i, i ^ mask) for i in range(n)])  10.1 us
  transfers between devices with their start and end apart: 38, of which 13 were waited for; matrix products, arithmetic and copies ran while one was open for 26% of the time, Pallas kernels for 25%

profile of v1, /device:TPU:30, one launch (start us, length us, event | category | flops | bytes accessed | tf_op | source)
XLA Modules:
  0.0 267.5 jit_solution(4681259319620528951)
XLA Ops:
  6.0 3.8 %collective-permute-start = (bf16[4,64,128]{2,1,0:T(8,128)(2,1)S(1)}, bf16[4,64,128]{2,1,0:T(8,128)(2,1)S(1)}, u32[]{:S(2)}, u32[]{:S(2)}) collective-permute-start(bf16[4,64,128]{2,1,0:T(8,128)(2,1)S(1)} %get-tuple-element.83), channel_id=1, source_target_pairs={{0,124},{4,0},{8,4},{12,8},{16,12},{20,16},{24,20},{28,24},{32,28}... | collective-permute-start | bytes 196616 | tf_op jit(solution)/shard_map/ppermute | solution.py:214
  16.0 16.7 %local_part.4.refs_4_ = f32[64,4096]{1,0:T(8,128)} custom-call(s32[640]{0:T(1024)} %subtract_select_fusion.pos, bf16[20,32,128,128]{3,2,1,0:T(8,128)(2,1)} %refs_5_.7, bf16[64,4096]{1,0:T(8,128)(2,1)} %refs_1_.1, f32[1,4096]{1,0:T(1,128)} %bitcast.98), custom_call_target="tpu_custom_call" | custom-call | tf_op jit(solution)/shard_map/local_part/pallas_call | solution.py:106
  34.7 4.8 %remote_part.4 = (f32[64,4096]{1,0:T(8,128)}, bf16[64,4096]{1,0:T(8,128)(2,1)}, bf16[4,4,64,128]{3,2,1,0:T(8,128)(2,1)}) custom-call(s32[658]{0:T(1024)} %pad_add_fusion.info, bf16[4,64,128]{2,1,0:T(8,128)(2,1)} %copy-done.1, bf16[4,64,128]{2,1,0:T(8,128)(2,1)} %copy-done.2, bf16[4,64,128]{2,1,0:T(8,128)(2,1)} %copy-done.3, bf16[4,64,128]{2,1,0:T(8,128)(2,1)} %copy-done.4, ...), custom_call_target="tpu_custom_call" | custom-call | tf_op jit(solution)/shard_map/remote_part/pallas_call | solution.py:192
  40.4 3.3 %collective-permute-start.4 = (bf16[4,64,128]{2,1,0:T(8,128)(2,1)S(1)}, bf16[4,64,128]{2,1,0:T(8,128)(2,1)S(1)}, u32[]{:S(2)}, u32[]{:S(2)}) collective-permute-start(bf16[4,64,128]{2,1,0:T(8,128)(2,1)S(1)} %get-tuple-element.79), channel_id=1, source_target_pairs={{0,124},{4,0},{8,4},{12,8},{16,12},{20,16},{24,20},{28,24},{32,28}... | collective-permute-start | bytes 196616 | tf_op jit(solution)/shard_map/ppermute | solution.py:214
  44.2 4.0 %collective-permute-start.7 = (bf16[4,64,128]{2,1,0:T(8,128)(2,1)S(1)}, bf16[4,64,128]{2,1,0:T(8,128)(2,1)S(1)}, u32[]{:S(2)}, u32[]{:S(2)}) collective-permute-start(bf16[4,64,128]{2,1,0:T(8,128)(2,1)S(1)} %get-tuple-element.76), channel_id=1, source_target_pairs={{0,64},{4,68},{8,72},{12,76},{16,80},{20,84},{24,88},{28,92},{32,9... | collective-permute-start | bytes 196616 | tf_op jit(solution)/shard_map/ppermute | solution.py:214
  49.2 16.8 %local_part.5.refs_4_ = f32[64,4096]{1,0:T(8,128)} custom-call(s32[640]{0:T(1024)} %subtract_select_fusion.pos, bf16[20,32,128,128]{3,2,1,0:T(8,128)(2,1)} %refs_5_.7, bf16[64,4096]{1,0:T(8,128)(2,1)} %get-tuple-element.13.refs_1_, f32[1,4096]{1,0:T(1,128)} %bitcast.99, f32[64,4096]{1,0:T(8,128)} %convert_element_type.26.refs_3_), custom_call_target="tpu_custom_call" | custom-call | tf_op jit(solution)/shard_map/local_part/pallas_call | solution.py:106
  67.3 4.8 %remote_part.5 = (f32[64,4096]{1,0:T(8,128)}, bf16[64,4096]{1,0:T(8,128)(2,1)}, bf16[4,4,64,128]{3,2,1,0:T(8,128)(2,1)}) custom-call(s32[658]{0:T(1024)} %pad_add_fusion.info, bf16[4,64,128]{2,1,0:T(8,128)(2,1)} %copy-done.7, bf16[4,64,128]{2,1,0:T(8,128)(2,1)} %copy-done.10, bf16[4,64,128]{2,1,0:T(8,128)(2,1)} %copy-done.12, ...), custom_call_target="tpu_custom_call" | custom-call | tf_op jit(solution)/shard_map/remote_part/pallas_call | solution.py:192
  75.3 2.2 collective-permute-start.8
  78.8 16.8 %local_part.6.refs_4_ = f32[64,4096]{1,0:T(8,128)} custom-call(s32[640]{0:T(1024)} %subtract_select_fusion.pos, bf16[20,32,128,128]{3,2,1,0:T(8,128)(2,1)} %refs_5_.7, bf16[64,4096]{1,0:T(8,128)(2,1)} %get-tuple-element.15.refs_1_, f32[1,4096]{1,0:T(1,128)} %bitcast.100, f32[64,4096]{1,0:T(8,128)} %get-tuple-element.16.refs_3_), custom_call_target="tpu_custom_call" | custom-call | tf_op jit(solution)/shard_map/local_part/pallas_call | solution.py:106
  96.9 4.8 %remote_part.6 = (f32[64,4096]{1,0:T(8,128)}, bf16[64,4096]{1,0:T(8,128)(2,1)}, bf16[4,4,64,128]{3,2,1,0:T(8,128)(2,1)}) custom-call(s32[658]{0:T(1024)} %pad_add_fusion.info, bf16[4,64,128]{2,1,0:T(8,128)(2,1)} %copy-done.13, bf16[4,64,128]{2,1,0:T(8,128)(2,1)} %copy-done.16, bf16[4,64,128]{2,1,0:T(8,128)(2,1)} %copy-done.8, ...), custom_call_target="tpu_custom_call" | custom-call | tf_op jit(solution)/shard_map/remote_part/pallas_call | solution.py:192
  102.7 5.5 %collective-permute-start.12 = (bf16[4,64,128]{2,1,0:T(8,128)(2,1)S(1)}, bf16[4,64,128]{2,1,0:T(8,128)(2,1)S(1)}, u32[]{:S(2)}, u32[]{:S(2)}) collective-permute-start(bf16[4,64,128]{2,1,0:T(8,128)(2,1)S(1)} %get-tuple-element.71), channel_id=1, source_target_pairs={{0,124},{4,0},{8,4},{12,8},{16,12},{20,16},{24,20},{28,24},{32,28}... | collective-permute-start | bytes 196616 | tf_op jit(solution)/shard_map/ppermute | solution.py:214
  108.1 2.0 collective-permute-start.14
  111.3 16.8 %local_part.7.refs_4_ = f32[64,4096]{1,0:T(8,128)} custom-call(s32[640]{0:T(1024)} %subtract_select_fusion.pos, bf16[20,32,128,128]{3,2,1,0:T(8,128)(2,1)} %refs_5_.7, bf16[64,4096]{1,0:T(8,128)(2,1)} %get-tuple-element.18.refs_1_, f32[1,4096]{1,0:T(1,128)} %bitcast.101, f32[64,4096]{1,0:T(8,128)} %get-tuple-element.19.refs_3_), custom_call_target="tpu_custom_call" | custom-call | tf_op jit(solution)/shard_map/local_part/pallas_call | solution.py:106
  129.4 5.0 %remote_part.7 = (f32[64,4096]{1,0:T(8,128)}, bf16[64,4096]{1,0:T(8,128)(2,1)}, bf16[3,64,1024]{2,1,0:T(8,128)(2,1)}) custom-call(s32[658]{0:T(1024)} %pad_add_fusion.info, bf16[4,64,128]{2,1,0:T(8,128)(2,1)} %copy-done.5, bf16[4,64,128]{2,1,0:T(8,128)(2,1)} %copy-done.6, bf16[4,64,128]{2,1,0:T(8,128)(2,1)} %copy-done.9, bf16[4,64,128]{2,1,0:T(8,128)(2,1)} %copy-done.14, ...), custom_call_target="tpu_custom_call" | custom-call | tf_op jit(solution)/shard_map/remote_part/pallas_call | solution.py:192
  135.8 2.6 collective-permute-start.17
  142.3 3.3 %collective-permute-done.18 = bf16[64,1024]{1,0:T(8,128)(2,1)S(1)} collective-permute-done((bf16[64,1024]{1,0:T(8,128)(2,1)S(1)}, bf16[64,1024]{1,0:T(8,128)(2,1)S(1)}, u32[]{:S(2)}, u32[]{:S(2)}) %collective-permute-start.18) | collective-permute-done | bytes 131104 | tf_op jit(solution)/shard_map/ppermute | solution.py:214
  150.4 2.3 collective-permute-done.19
  152.7 2.7 collective-permute-done.20
  158.9 6.0 %collective-permute-start.25 = (f32[64,256]{1,0:T(8,128)S(1)}, f32[64,256]{1,0:T(8,128)S(1)}, u32[]{:S(2)}, u32[]{:S(2)}) collective-permute-start(f32[64,256]{1,0:T(8,128)S(1)} %fusion.29), channel_id=1, source_target_pairs={{0,16},{4,20},{8,24},{12,28},{16,0},{20,4},{24,8},{28,12},{32,48},... | collective-permute-start | bytes 196616 | tf_op jit(solution)/shard_map/ppermute | solution.py:219
  165.0 3.5 %collective-permute-start.27 = (f32[64,256]{1,0:T(8,128)S(1)}, f32[64,256]{1,0:T(8,128)S(1)}, u32[]{:S(2)}, u32[]{:S(2)}) collective-permute-start(f32[64,256]{1,0:T(8,128)S(1)} %fusion.29), channel_id=1, source_target_pairs={{0,24},{4,28},{8,16},{12,20},{16,8},{20,12},{24,0},{28,4},{32,56},... | collective-permute-start | bytes 196616 | tf_op jit(solution)/shard_map/ppermute | solution.py:219
  168.5 2.2 collective-permute-done.25
  171.0 1.9 collective-permute-done.27
  175.6 2.4 collective-permute-start.30
  179.0 2.7 %collective-permute-done.30 = f32[64,256]{1,0:T(8,128)S(1)} collective-permute-done((f32[64,256]{1,0:T(8,128)S(1)}, f32[64,256]{1,0:T(8,128)S(1)}, u32[]{:S(2)}, u32[]{:S(2)}) %collective-permute-start.30) | collective-permute-done | bytes 65568 | tf_op jit(solution)/shard_map/ppermute | solution.py:219
  186.5 2.9 %collective-permute-start.35 = (bf16[64,4096]{1,0:T(8,128)(2,1)S(1)}, bf16[64,4096]{1,0:T(8,128)(2,1)S(1)}, u32[]{:S(2)}, u32[]{:S(2)}) collective-permute-start(bf16[64,4096]{1,0:T(8,128)(2,1)S(1)} %copy-done.17), channel_id=1, source_target_pairs={{0,1},{1,2},{2,3},{3,0},{4,5},{5,6},{6,7},{7,4},{8,9},{9,10},{10,1... | collective-permute-start | bytes 1572872 | tf_op jit(solution)/shard_map/ppermute | solution.py:214
  191.2 9.7 %collective-permute-done.34 = f32[64,256]{1,0:T(8,128)S(1)} collective-permute-done((f32[64,256]{1,0:T(8,128)S(1)}, f32[64,256]{1,0:T(8,128)S(1)}, u32[]{:S(2)}, u32[]{:S(2)}) %collective-permute-start.34) | collective-permute-done | bytes 65568 | tf_op jit(solution)/shard_map/ppermute | solution.py:214
  201.9 11.7 %cholesky.49 = f32[128,128]{1,0:T(8,128)S(1)} custom-call(f32[128,128]{1,0:T(8,128)S(1)} %cholesky.115), custom_call_target="Cholesky" | custom-call | tf_op jit(solution)/shard_map/jit(cholesky)/cholesky | solution.py:275
  213.6 9.8 %custom-call.14 = f32[1,128,128]{1,2,0:T(8,128)S(1)} custom-call(f32[1,128,128]{2,1,0:T(8,128)S(1)} %get-tuple-element.85), custom_call_target="InvertDiagBlocksLowerTriangular" | custom-call | tf_op jit(solution)/shard_map/jit(cholesky)/cholesky | solution.py:275
  223.9 11.7 %cholesky.103 = f32[128,128]{1,0:T(8,128)S(1)} custom-call(f32[128,128]{1,0:T(8,128)S(1)} %convolution_subtract_fusion.1), custom_call_target="Cholesky" | custom-call | tf_op jit(solution)/shard_map/jit(cholesky)/cholesky | solution.py:275
  239.4 4.3 %while.1 = (s32[]{:T(128)}, f32[256,256]{0,1:T(8,128)S(1)}, s32[2,2]{1,0:T(2,128)S(1)}, f32[2,128,128]{2,1,0:T(8,128)S(1)}, s32[]{:T(128)}) while((s32[]{:T(128)}, f32[256,256]{0,1:T(8,128)S(1)}, s32[2,2]{1,0:T(2,128)S(1)}, f32[2,128,128]{2,1,0:T(8,128)S(1)}, s32[]{:T(128)}) %tuple.48), condition=%wide.while_cond, body=%wide.while_body.sunk | while | flops 2 | bytes 393321 | solution.py:277
  243.7 19.7 %custom-call.15 = f32[2,128,128]{1,2,0:T(8,128)S(1)} custom-call(f32[2,128,128]{2,1,0:T(8,128)S(1)} %get-tuple-element.29), custom_call_target="InvertDiagBlocksLowerTriangular" | custom-call | tf_op jit(solution)/shard_map/triangular_solve | solution.py:277
  265.3 2.2 convolution_multiply_fusion
  (206 shorter events, 59.5 us)
Async XLA Ops:
  6.0 27.3 %collective-permute-start = (bf16[4,64,128]{2,1,0:T(8,128)(2,1)S(1)}, bf16[4,64,128]{2,1,0:T(8,128)(2,1)S(1)}, u32[]{:S(2)}, u32[]{:S(2)}) collective-permute-start(bf16[4,64,128]{2,1,0:T(8,128)(2,1)S(1)} %get-tuple-element.83), channel_id=1, source_target_pairs={{0,124},{4,0},{8,4},{12,8},{16,12},{20,16},{24,20},{28,24},{32,28}... | collective-permute-start | bytes 196616 | tf_op jit(solution)/shard_map/ppermute | solution.py:214
  9.9 23.5 %collective-permute-start.1 = (bf16[4,64,128]{2,1,0:T(8,128)(2,1)S(1)}, bf16[4,64,128]{2,1,0:T(8,128)(2,1)S(1)}, u32[]{:S(2)}, u32[]{:S(2)}) collective-permute-start(bf16[4,64,128]{2,1,0:T(8,128)(2,1)S(1)} %get-tuple-element.82), channel_id=1, source_target_pairs={{0,4},{4,8},{8,12},{12,16},{16,20},{20,24},{24,28},{28,32},{32,36}... | collective-permute-start | bytes 196616 | tf_op jit(solution)/shard_map/ppermute | solution.py:214
  9.9 23.5 %collective-permute-start.2 = (bf16[4,64,128]{2,1,0:T(8,128)(2,1)S(1)}, bf16[4,64,128]{2,1,0:T(8,128)(2,1)S(1)}, u32[]{:S(2)}, u32[]{:S(2)}) collective-permute-start(bf16[4,64,128]{2,1,0:T(8,128)(2,1)S(1)} %get-tuple-element.81), channel_id=1, source_target_pairs={{0,120},{4,124},{8,0},{12,4},{16,8},{20,12},{24,16},{28,20},{32,24... | collective-permute-start | bytes 196616 | tf_op jit(solution)/shard_map/ppermute | solution.py:214
  10.9 22.5 %collective-permute-start.3 = (bf16[4,64,128]{2,1,0:T(8,128)(2,1)S(1)}, bf16[4,64,128]{2,1,0:T(8,128)(2,1)S(1)}, u32[]{:S(2)}, u32[]{:S(2)}) collective-permute-start(bf16[4,64,128]{2,1,0:T(8,128)(2,1)S(1)} %get-tuple-element.80), channel_id=1, source_target_pairs={{0,64},{4,68},{8,72},{12,76},{16,80},{20,84},{24,88},{28,92},{32,9... | collective-permute-start | bytes 196616 | tf_op jit(solution)/shard_map/ppermute | solution.py:214
  40.4 25.6 %collective-permute-start.4 = (bf16[4,64,128]{2,1,0:T(8,128)(2,1)S(1)}, bf16[4,64,128]{2,1,0:T(8,128)(2,1)S(1)}, u32[]{:S(2)}, u32[]{:S(2)}) collective-permute-start(bf16[4,64,128]{2,1,0:T(8,128)(2,1)S(1)} %get-tuple-element.79), channel_id=1, source_target_pairs={{0,124},{4,0},{8,4},{12,8},{16,12},{20,16},{24,20},{28,24},{32,28}... | collective-permute-start | bytes 196616 | tf_op jit(solution)/shard_map/ppermute | solution.py:214
  43.7 22.3 %collective-permute-start.5 = (bf16[4,64,128]{2,1,0:T(8,128)(2,1)S(1)}, bf16[4,64,128]{2,1,0:T(8,128)(2,1)S(1)}, u32[]{:S(2)}, u32[]{:S(2)}) collective-permute-start(bf16[4,64,128]{2,1,0:T(8,128)(2,1)S(1)} %get-tuple-element.78), channel_id=1, source_target_pairs={{0,4},{4,8},{8,12},{12,16},{16,20},{20,24},{24,28},{28,32},{32,36}... | collective-permute-start | bytes 196616 | tf_op jit(solution)/shard_map/ppermute | solution.py:214
  44.2 21.9 %collective-permute-start.6 = (bf16[4,64,128]{2,1,0:T(8,128)(2,1)S(1)}, bf16[4,64,128]{2,1,0:T(8,128)(2,1)S(1)}, u32[]{:S(2)}, u32[]{:S(2)}) collective-permute-start(bf16[4,64,128]{2,1,0:T(8,128)(2,1)S(1)} %get-tuple-element.77), channel_id=1, source_target_pairs={{0,120},{4,124},{8,0},{12,4},{16,8},{20,12},{24,16},{28,20},{32,24... | collective-permute-start | bytes 196616 | tf_op jit(solution)/shard_map/ppermute | solution.py:214
  44.2 21.9 %collective-permute-start.7 = (bf16[4,64,128]{2,1,0:T(8,128)(2,1)S(1)}, bf16[4,64,128]{2,1,0:T(8,128)(2,1)S(1)}, u32[]{:S(2)}, u32[]{:S(2)}) collective-permute-start(bf16[4,64,128]{2,1,0:T(8,128)(2,1)S(1)} %get-tuple-element.76), channel_id=1, source_target_pairs={{0,64},{4,68},{8,72},{12,76},{16,80},{20,84},{24,88},{28,92},{32,9... | collective-permute-start | bytes 196616 | tf_op jit(solution)/shard_map/ppermute | solution.py:214
  73.1 22.5 %collective-permute-start.10 = (bf16[4,64,128]{2,1,0:T(8,128)(2,1)S(1)}, bf16[4,64,128]{2,1,0:T(8,128)(2,1)S(1)}, u32[]{:S(2)}, u32[]{:S(2)}) collective-permute-start(bf16[4,64,128]{2,1,0:T(8,128)(2,1)S(1)} %get-tuple-element.73), channel_id=1, source_target_pairs={{0,120},{4,124},{8,0},{12,4},{16,8},{20,12},{24,16},{28,20},{32,24... | collective-permute-start | bytes 196616 | tf_op jit(solution)/shard_map/ppermute | solution.py:214
  74.9 20.7 %collective-permute-start.11 = (bf16[4,64,128]{2,1,0:T(8,128)(2,1)S(1)}, bf16[4,64,128]{2,1,0:T(8,128)(2,1)S(1)}, u32[]{:S(2)}, u32[]{:S(2)}) collective-permute-start(bf16[4,64,128]{2,1,0:T(8,128)(2,1)S(1)} %get-tuple-element.72), channel_id=1, source_target_pairs={{0,64},{4,68},{8,72},{12,76},{16,80},{20,84},{24,88},{28,92},{32,9... | collective-permute-start | bytes 196616 | tf_op jit(solution)/shard_map/ppermute | solution.py:214
  75.3 20.4 %collective-permute-start.8 = (bf16[4,64,128]{2,1,0:T(8,128)(2,1)S(1)}, bf16[4,64,128]{2,1,0:T(8,128)(2,1)S(1)}, u32[]{:S(2)}, u32[]{:S(2)}) collective-permute-start(bf16[4,64,128]{2,1,0:T(8,128)(2,1)S(1)} %get-tuple-element.75), channel_id=1, source_target_pairs={{0,124},{4,0},{8,4},{12,8},{16,12},{20,16},{24,20},{28,24},{32,28}... | collective-permute-start | bytes 196616 | tf_op jit(solution)/shard_map/ppermute | solution.py:214
  77.5 18.2 %collective-permute-start.9 = (bf16[4,64,128]{2,1,0:T(8,128)(2,1)S(1)}, bf16[4,64,128]{2,1,0:T(8,128)(2,1)S(1)}, u32[]{:S(2)}, u32[]{:S(2)}) collective-permute-start(bf16[4,64,128]{2,1,0:T(8,128)(2,1)S(1)} %get-tuple-element.74), channel_id=1, source_target_pairs={{0,4},{4,8},{8,12},{12,16},{16,20},{20,24},{24,28},{28,32},{32,36}... | collective-permute-start | bytes 196616 | tf_op jit(solution)/shard_map/ppermute | solution.py:214
  102.7 25.4 %collective-permute-start.12 = (bf16[4,64,128]{2,1,0:T(8,128)(2,1)S(1)}, bf16[4,64,128]{2,1,0:T(8,128)(2,1)S(1)}, u32[]{:S(2)}, u32[]{:S(2)}) collective-permute-start(bf16[4,64,128]{2,1,0:T(8,128)(2,1)S(1)} %get-tuple-element.71), channel_id=1, source_target_pairs={{0,124},{4,0},{8,4},{12,8},{16,12},{20,16},{24,20},{28,24},{32,28}... | collective-permute-start | bytes 196616 | tf_op jit(solution)/shard_map/ppermute | solution.py:214
  108.1 20.0 %collective-permute-start.13 = (bf16[4,64,128]{2,1,0:T(8,128)(2,1)S(1)}, bf16[4,64,128]{2,1,0:T(8,128)(2,1)S(1)}, u32[]{:S(2)}, u32[]{:S(2)}) collective-permute-start(bf16[4,64,128]{2,1,0:T(8,128)(2,1)S(1)} %get-tuple-element.70), channel_id=1, source_target_pairs={{0,4},{4,8},{8,12},{12,16},{16,20},{20,24},{24,28},{28,32},{32,36}... | collective-permute-start | bytes 196616 | tf_op jit(solution)/shard_map/ppermute | solution.py:214
  108.1 20.0 %collective-permute-start.14 = (bf16[4,64,128]{2,1,0:T(8,128)(2,1)S(1)}, bf16[4,64,128]{2,1,0:T(8,128)(2,1)S(1)}, u32[]{:S(2)}, u32[]{:S(2)}) collective-permute-start(bf16[4,64,128]{2,1,0:T(8,128)(2,1)S(1)} %get-tuple-element.69), channel_id=1, source_target_pairs={{0,120},{4,124},{8,0},{12,4},{16,8},{20,12},{24,16},{28,20},{32,24... | collective-permute-start | bytes 196616 | tf_op jit(solution)/shard_map/ppermute | solution.py:214
  110.2 18.0 %collective-permute-start.15 = (bf16[4,64,128]{2,1,0:T(8,128)(2,1)S(1)}, bf16[4,64,128]{2,1,0:T(8,128)(2,1)S(1)}, u32[]{:S(2)}, u32[]{:S(2)}) collective-permute-start(bf16[4,64,128]{2,1,0:T(8,128)(2,1)S(1)} %get-tuple-element.68), channel_id=1, source_target_pairs={{0,64},{4,68},{8,72},{12,76},{16,80},{20,84},{24,88},{28,92},{32,9... | collective-permute-start | bytes 196616 | tf_op jit(solution)/shard_map/ppermute | solution.py:214
  135.8 6.5 %collective-permute-start.17 = (bf16[64,1024]{1,0:T(8,128)(2,1)S(1)}, bf16[64,1024]{1,0:T(8,128)(2,1)S(1)}, u32[]{:S(2)}, u32[]{:S(2)}) collective-permute-start(bf16[64,1024]{1,0:T(8,128)(2,1)S(1)} %get-tuple-element.62), channel_id=1, source_target_pairs={{0,2},{1,3},{2,0},{3,1},{4,6},{5,7},{6,4},{7,5},{8,10},{9,11},{10,... | collective-permute-start | bytes 393224 | tf_op jit(solution)/shard_map/ppermute | solution.py:214
  138.4 7.2 %collective-permute-start.18 = (bf16[64,1024]{1,0:T(8,128)(2,1)S(1)}, bf16[64,1024]{1,0:T(8,128)(2,1)S(1)}, u32[]{:S(2)}, u32[]{:S(2)}) collective-permute-start(bf16[64,1024]{1,0:T(8,128)(2,1)S(1)} %get-tuple-element.61), channel_id=1, source_target_pairs={{0,3},{1,0},{2,1},{3,2},{4,7},{5,4},{6,5},{7,6},{8,11},{9,8},{10,9... | collective-permute-start | bytes 393224 | tf_op jit(solution)/shard_map/ppermute | solution.py:214
  149.1 6.2 %collective-permute-start.20 = (f32[64,256]{1,0:T(8,128)S(1)}, f32[64,256]{1,0:T(8,128)S(1)}, u32[]{:S(2)}, u32[]{:S(2)}) collective-permute-start(f32[64,256]{1,0:T(8,128)S(1)} %get-tuple-element.67), channel_id=1, source_target_pairs={{0,2},{1,3},{2,0},{3,1},{4,6},{5,7},{6,4},{7,5},{8,10},{9,11},{10,... | collective-permute-start | bytes 196616 | tf_op jit(solution)/shard_map/ppermute | solution.py:214
  150.3 6.7 %collective-permute-start.21 = (f32[64,256]{1,0:T(8,128)S(1)}, f32[64,256]{1,0:T(8,128)S(1)}, u32[]{:S(2)}, u32[]{:S(2)}) collective-permute-start(f32[64,256]{1,0:T(8,128)S(1)} %get-tuple-element.66), channel_id=1, source_target_pairs={{0,3},{1,0},{2,1},{3,2},{4,7},{5,4},{6,5},{7,6},{8,11},{9,8},{10,9... | collective-permute-start | bytes 196616 | tf_op jit(solution)/shard_map/ppermute | solution.py:214
  157.0 8.0 %collective-permute-start.22 = (f32[64,256]{1,0:T(8,128)S(1)}, f32[64,256]{1,0:T(8,128)S(1)}, u32[]{:S(2)}, u32[]{:S(2)}) collective-permute-start(f32[64,256]{1,0:T(8,128)S(1)} %fusion.29), channel_id=1, source_target_pairs={{0,4},{4,0},{8,12},{12,8},{16,20},{20,16},{24,28},{28,24},{32,36},... | collective-permute-start | bytes 196616 | tf_op jit(solution)/shard_map/ppermute | solution.py:219
  157.2 11.3 %collective-permute-start.23 = (f32[64,256]{1,0:T(8,128)S(1)}, f32[64,256]{1,0:T(8,128)S(1)}, u32[]{:S(2)}, u32[]{:S(2)}) collective-permute-start(f32[64,256]{1,0:T(8,128)S(1)} %fusion.29), channel_id=1, source_target_pairs={{0,8},{4,12},{8,0},{12,4},{16,24},{20,28},{24,16},{28,20},{32,40},... | collective-permute-start | bytes 196616 | tf_op jit(solution)/shard_map/ppermute | solution.py:219
  158.6 9.9 %collective-permute-start.24 = (f32[64,256]{1,0:T(8,128)S(1)}, f32[64,256]{1,0:T(8,128)S(1)}, u32[]{:S(2)}, u32[]{:S(2)}) collective-permute-start(f32[64,256]{1,0:T(8,128)S(1)} %fusion.29), channel_id=1, source_target_pairs={{0,12},{4,8},{8,4},{12,0},{16,28},{20,24},{24,20},{28,16},{32,44},... | collective-permute-start | bytes 196616 | tf_op jit(solution)/shard_map/ppermute | solution.py:219
  158.9 11.8 %collective-permute-start.25 = (f32[64,256]{1,0:T(8,128)S(1)}, f32[64,256]{1,0:T(8,128)S(1)}, u32[]{:S(2)}, u32[]{:S(2)}) collective-permute-start(f32[64,256]{1,0:T(8,128)S(1)} %fusion.29), channel_id=1, source_target_pairs={{0,16},{4,20},{8,24},{12,28},{16,0},{20,4},{24,8},{28,12},{32,48},... | collective-permute-start | bytes 196616 | tf_op jit(solution)/shard_map/ppermute | solution.py:219
  165.0 8.0 %collective-permute-start.27 = (f32[64,256]{1,0:T(8,128)S(1)}, f32[64,256]{1,0:T(8,128)S(1)}, u32[]{:S(2)}, u32[]{:S(2)}) collective-permute-start(f32[64,256]{1,0:T(8,128)S(1)} %fusion.29), channel_id=1, source_target_pairs={{0,24},{4,28},{8,16},{12,20},{16,8},{20,12},{24,0},{28,4},{32,56},... | collective-permute-start | bytes 196616 | tf_op jit(solution)/shard_map/ppermute | solution.py:219
  175.6 6.1 %collective-permute-start.30 = (f32[64,256]{1,0:T(8,128)S(1)}, f32[64,256]{1,0:T(8,128)S(1)}, u32[]{:S(2)}, u32[]{:S(2)}) collective-permute-start(f32[64,256]{1,0:T(8,128)S(1)} %add_add_fusion.1), channel_id=1, source_target_pairs={{0,64},{4,68},{8,72},{12,76},{16,80},{20,84},{24,88},{28,92},{32,9... | collective-permute-start | bytes 196616 | tf_op jit(solution)/shard_map/ppermute | solution.py:219
  183.5 6.6 %collective-permute-start.32 = (f32[64,256]{1,0:T(8,128)S(1)}, f32[64,256]{1,0:T(8,128)S(1)}, u32[]{:S(2)}, u32[]{:S(2)}) collective-permute-start(f32[64,256]{1,0:T(8,128)S(1)} %add_add_fusion), channel_id=1, source_target_pairs={{0,1},{1,2},{2,3},{3,0},{4,5},{5,6},{6,7},{7,4},{8,9},{9,10},{10,1... | collective-permute-start | bytes 196616 | tf_op jit(solution)/shard_map/ppermute | solution.py:214
  184.6 6.6 %collective-permute-start.33 = (f32[64,256]{1,0:T(8,128)S(1)}, f32[64,256]{1,0:T(8,128)S(1)}, u32[]{:S(2)}, u32[]{:S(2)}) collective-permute-start(f32[64,256]{1,0:T(8,128)S(1)} %add_add_fusion), channel_id=1, source_target_pairs={{0,2},{1,3},{2,0},{3,1},{4,6},{5,7},{6,4},{7,5},{8,10},{9,11},{10,... | collective-permute-start | bytes 196616 | tf_op jit(solution)/shard_map/ppermute | solution.py:214
  186.2 14.7 %collective-permute-start.34 = (f32[64,256]{1,0:T(8,128)S(1)}, f32[64,256]{1,0:T(8,128)S(1)}, u32[]{:S(2)}, u32[]{:S(2)}) collective-permute-start(f32[64,256]{1,0:T(8,128)S(1)} %add_add_fusion), channel_id=1, source_target_pairs={{0,3},{1,0},{2,1},{3,2},{4,7},{5,4},{6,5},{7,6},{8,11},{9,8},{10,9... | collective-permute-start | bytes 196616 | tf_op jit(solution)/shard_map/ppermute | solution.py:214
  186.5 78.8 %collective-permute-start.35 = (bf16[64,4096]{1,0:T(8,128)(2,1)S(1)}, bf16[64,4096]{1,0:T(8,128)(2,1)S(1)}, u32[]{:S(2)}, u32[]{:S(2)}) collective-permute-start(bf16[64,4096]{1,0:T(8,128)(2,1)S(1)} %copy-done.17), channel_id=1, source_target_pairs={{0,1},{1,2},{2,3},{3,0},{4,5},{5,6},{6,7},{7,4},{8,9},{9,10},{10,1... | collective-permute-start | bytes 1572872 | tf_op jit(solution)/shard_map/ppermute | solution.py:214
  189.4 75.9 %collective-permute-start.36 = (bf16[64,4096]{1,0:T(8,128)(2,1)S(1)}, bf16[64,4096]{1,0:T(8,128)(2,1)S(1)}, u32[]{:S(2)}, u32[]{:S(2)}) collective-permute-start(bf16[64,4096]{1,0:T(8,128)(2,1)S(1)} %copy-done.17), channel_id=1, source_target_pairs={{0,2},{1,3},{2,0},{3,1},{4,6},{5,7},{6,4},{7,5},{8,10},{9,11},{10,... | collective-permute-start | bytes 1572872 | tf_op jit(solution)/shard_map/ppermute | solution.py:214
  190.1 75.2 %collective-permute-start.37 = (bf16[64,4096]{1,0:T(8,128)(2,1)S(1)}, bf16[64,4096]{1,0:T(8,128)(2,1)S(1)}, u32[]{:S(2)}, u32[]{:S(2)}) collective-permute-start(bf16[64,4096]{1,0:T(8,128)(2,1)S(1)} %copy-done.17), channel_id=1, source_target_pairs={{0,3},{1,0},{2,1},{3,2},{4,7},{5,4},{6,5},{7,6},{8,11},{9,8},{10,9... | collective-permute-start | bytes 1572872 | tf_op jit(solution)/shard_map/ppermute | solution.py:214
  (25 other events, 107.4 us)

commit v2 on v1

v2 whole, which is shorter than its diff:
```python
import functools
import math

import jax
import jax.numpy as jnp
from jax import lax
from jax.experimental import pallas as pl
from jax.experimental.pallas import tpu as pltpu
from jax.sharding import PartitionSpec as P

HALO = 4
FILTER = 4
UNROLL = 4
CHUNK = 8
PANEL = 16

filter_scale = 0.4


def offsets(row_count):
    return (1, -1, 2, row_count // 2)


def ranks_of(hits):
    return jnp.cumsum(hits.astype(jnp.int32), axis=-1) - 1


def plan(cols, row_index, row_count, local_blocks):
    slot_count = cols.shape[1]
    slots = local_blocks * slot_count
    by_device = cols.reshape(row_count, slots)
    deltas = jnp.array(offsets(row_count), jnp.int32)
    local_ids = jnp.arange(local_blocks, dtype=jnp.int32)
    own = lax.dynamic_index_in_dim(by_device, row_index, 0, keepdims=False)
    askers = (row_index - deltas) % row_count
    asked = jnp.take(by_device, askers, axis=0) - row_index * local_blocks
    asked_hits = jnp.any(asked[:, :, None] == local_ids, axis=1)
    asked_ranks = ranks_of(asked_hits)
    wanted = jnp.arange(HALO, dtype=jnp.int32)
    pick = asked_hits[:, None, :] & (asked_ranks[:, None, :] == wanted[None, :, None])
    send = jnp.sum(jnp.where(pick, local_ids, 0), axis=-1).reshape(-1)
    sources = (row_index + deltas) % row_count
    named_ids = (sources[:, None] * local_blocks + local_ids).reshape(-1)
    matches = own[:, None] == named_ids
    named_hits = jnp.any(matches, axis=0).reshape(len(deltas), local_blocks)
    base = HALO * jnp.arange(len(deltas), dtype=jnp.int32)
    places = (ranks_of(named_hits) + base[:, None]).reshape(-1)
    slot_place = jnp.sum(jnp.where(matches, places, 0), axis=-1)
    within = own - row_index * local_blocks
    is_local = (within >= 0) & (within < local_blocks)
    position = jnp.where(is_local, within, local_blocks)
    order = ranks_of(~is_local)
    slot_ids = jnp.arange(slots, dtype=jnp.int32)
    hit = (~is_local)[:, None] & (order[:, None] == slot_ids)
    code = slot_ids * 32 + slot_place
    pad_code = HALO * len(deltas)
    listed = jnp.sum(jnp.where(hit, code[:, None] - pad_code, 0), axis=0) + pad_code
    count = (order[-1:] + 1).astype(jnp.int32)
    return position, jnp.concatenate([count, send, listed])


def local_kernel(scale, first, pos, blocks, x, onsite, *refs):
    prev, y, held = (None, *refs) if first else refs
    slot_count, local_blocks, size, _ = blocks.shape
    for j in range(local_blocks):
        held[j] = x[:, j * size : (j + 1) * size]
    held[local_blocks] = jnp.zeros(held.shape[1:], held.dtype)

    @pl.loop(0, local_blocks // UNROLL)
    def _(group):
        for u in range(UNROLL):
            row = group * UNROLL + u
            total = None
            for s in range(0, slot_count, 2):
                at = row * slot_count + s
                taken = jnp.concatenate([held[pos[at]], held[pos[at + 1]]], axis=1)
                block = jnp.concatenate([blocks[s, row], blocks[s + 1, row]], axis=0)
                product = jnp.dot(taken, block, preferred_element_type=jnp.float32)
                total = product if total is None else total + product
            span = pl.ds(pl.multiple_of(row * size, size), size)
            value = scale * (total + onsite[:, span] * held[row].astype(jnp.float32))
            if prev is not None:
                value = value - prev[:, span].astype(jnp.float32)
            y[:, span] = value


def remote_kernel(scale, last, info, *refs):
    halos, (y_in, blocks, y, x), rest = refs[:4], refs[4:8], refs[8:]
    sends, zero = rest[:-1], rest[-1]
    slot_count, local_blocks, size, _ = blocks.shape
    per = halos[0].shape[0]
    count = info[0]
    list_at = 1 + 4 * per
    for q in range(4):
        zero[q * per : (q + 1) * per] = halos[q][...]
    zero[4 * per] = jnp.zeros(zero.shape[1:], zero.dtype)
    y[...] = y_in[...]

    @pl.loop(0, (count + CHUNK - 1) // CHUNK)
    def _(c):
        for k in range(CHUNK):
            code = info[list_at + c * CHUNK + k]
            entry = code // 32
            place = lax.rem(code, 32)
            row = entry // slot_count
            slot = entry - row * slot_count
            product = jnp.dot(zero[place], blocks[slot, row], preferred_element_type=jnp.float32)
            span = pl.ds(pl.multiple_of(row * size, size), size)
            y[:, span] = y[:, span] + scale * product

    x[...] = y[...].astype(jnp.bfloat16)
    if not last:
        for q in range(4):
            for k in range(per):
                j = info[1 + q * per + k]
                sends[q][k] = x[:, pl.ds(pl.multiple_of(j * size, size), size)]
    else:
        own = info[list_at + slot_count * local_blocks]
        piece = x.shape[1] // 4
        for k in range(4):
            at = lax.rem(own + k, 4) * piece
            sends[k][...] = x[:, pl.ds(pl.multiple_of(at, piece), piece)]


vmem = pl.BlockSpec(memory_space=pltpu.VMEM)
smem = pl.BlockSpec(memory_space=pltpu.SMEM)
grant = pltpu.CompilerParams(vmem_limit_bytes=16 << 20)


def local_part(scale, pos, blocks, x, onsite, prev):
    _, local_blocks, size, _ = blocks.shape
    args = [pos, blocks, x, onsite] + ([] if prev is None else [prev])
    return pl.pallas_call(
        functools.partial(local_kernel, scale, prev is None),
        out_shape=jax.ShapeDtypeStruct(x.shape, jnp.float32),
        in_specs=[smem] + [vmem] * (len(args) - 1),
        out_specs=vmem,
        scratch_shapes=[pltpu.VMEM((local_blocks + 1, x.shape[0], size), jnp.bfloat16)],
        compiler_params=grant,
        name="local_part",
    )(*args)


def remote_part(scale, last, info, halos, y, blocks):
    size = blocks.shape[2]
    width, local_rows = y.shape
    per = halos[0].shape[0]
    send = (width, local_rows // 4) if last else (per, width, size)
    return pl.pallas_call(
        functools.partial(remote_kernel, scale, last),
        out_shape=(
            jax.ShapeDtypeStruct(y.shape, jnp.float32),
            jax.ShapeDtypeStruct(y.shape, jnp.bfloat16),
        )
        + (jax.ShapeDtypeStruct(send, jnp.bfloat16),) * 4,
        in_specs=[smem] + [vmem] * 6,
        out_specs=(vmem,) * 6,
        scratch_shapes=[pltpu.VMEM((4 * per + 1, width, size), jnp.bfloat16)],
        compiler_params=grant,
        name="remote_part",
    )(info, *halos, y, blocks)


def gram_kernel(*refs):
    pieces, strips = refs[:4], refs[4:]
    stack = jnp.concatenate([p[...] for p in pieces], axis=0)
    gram = lax.dot_general(
        stack, stack, (((1,), (1,)), ((), ())), preferred_element_type=jnp.float32
    )
    width = pieces[0].shape[0]
    for k in range(4):
        at = (-k) % 4 * width
        rows = gram[at : at + width]
        order = [(j - k) % 4 * width for j in range(4)]
        strips[k][...] = jnp.concatenate([rows[:, o : o + width] for o in order], axis=1)


def gram_strips(pieces):
    width = pieces[0].shape[0]
    return pl.pallas_call(
        gram_kernel,
        out_shape=(jax.ShapeDtypeStruct((width, 4 * width), jnp.float32),) * 4,
        in_specs=[vmem] * 4,
        out_specs=(vmem,) * 4,
        compiler_params=grant,
        name="gram_strips",
    )(*pieces)


def three_parts(value):
    high = value.astype(jnp.bfloat16)
    rest = value - high.astype(jnp.float32)
    middle = rest.astype(jnp.bfloat16)
    low = (rest - middle.astype(jnp.float32)).astype(jnp.bfloat16)
    return high, middle, low


def solve_kernel(root, own_ref, *refs):
    strips, finals, (basis, factor, work, inverse) = refs[:4], refs[4:8], refs[8:]
    own = own_ref[0]
    width, n = strips[0].shape
    f32 = jnp.float32
    for k in range(4):
        at = pl.multiple_of(lax.rem(own + 4 - k, 4) * width, width)
        work[pl.ds(at, width), :] = strips[k][...]
    row_ids = lax.broadcasted_iota(jnp.int32, (PANEL, 128), 0)
    lane_ids = lax.broadcasted_iota(jnp.int32, (PANEL, 128), 1)
    for r0 in range(0, n, PANEL):
        r1 = r0 + PANEL
        at, tile = r0 % 128, r0 // 128
        rows = work[r0:r1, :]
        pivots = [
            jnp.broadcast_to(rows[:, r0 + k : r0 + k + 1], (PANEL, 128)) for k in range(PANEL)
        ]
        parts = [rows[:, t : t + 128] for t in range(0, n, 128)]
        parts.append(jnp.where(lane_ids - at == row_ids, 1.0, 0.0).astype(f32))
        diagonal = jnp.ones((PANEL, 128), f32)
        for j in range(PANEL):
            pivot = pivots[j][j : j + 1, :]
            diagonal = jnp.where(row_ids == j, pivot, diagonal)
            factors = jnp.where(row_ids > j, pivots[j] * (1.0 / pivot), 0.0)
            for k in range(j + 1, PANEL):
                pivots[k] = pivots[k] - factors * pivots[k][j : j + 1, :]
            parts = [q - factors * q[j : j + 1, :] for q in parts]
        roots = lax.rsqrt(diagonal)
        parts = [q * roots for q in parts]
        in_panel = (lane_ids >= at) & (lane_ids < at + PANEL)
        joined = []
        for t in range(n // 128):
            cols = lane_ids + 128 * t
            span = slice(128 * t, 128 * t + 128)
            factor[r0:r1, span] = jnp.where(cols >= row_ids + r0, parts[t] * (1.0 / root), 0.0)
            both = jnp.where(in_panel, parts[-1], parts[t]) if t == tile else parts[t]
            joined.append(both)
            inverse[r0:r1, span] = jnp.where(cols < r1, both, 0.0)
        if r1 < n:
            h, m, l = three_parts(jnp.concatenate(joined, axis=1))
            left = jnp.concatenate([h, h, m, m, h, l], axis=0)
            right = jnp.concatenate([h, m, h, m, l, h], axis=0)
            low = r1 // 128 * 128
            update = lax.dot_general(
                left[:, low:], right, (((0,), (0,)), ((), ())), preferred_element_type=f32
            )
            cols = lax.broadcasted_iota(jnp.int32, (n - r1, n), 1)
            kept = jnp.where((cols >= r0) & (cols < r1), 0.0, work[r1:, :])
            work[r1:, :] = kept - update[r1 - low :, :]
    mine = root * inverse[pl.ds(pl.multiple_of(own * width, width), width), :]
    blocks = [mine[:, b * width : (b + 1) * width] for b in range(4)]
    ordered = []
    for k in range(4):
        source = lax.rem(own + 4 - k, 4)
        block = blocks[0]
        for b in range(1, 4):
            block = jnp.where(source == b, blocks[b], block)
        ordered.append(block)
    ordered = jnp.concatenate(ordered, axis=1)
    left = jnp.concatenate(three_parts(ordered), axis=0)
    wide = 512
    for c in range(0, basis.shape[1], wide):
        right = jnp.concatenate([f[:, c : c + wide] for f in finals], axis=0)
        product = jnp.dot(left, right, preferred_element_type=f32)
        basis[:, c : c + wide] = (
            product[:width] + product[width : 2 * width] + product[2 * width :]
        )


def solve(root, own, strips, finals):
    n = strips[0].shape[1]
    return pl.pallas_call(
        functools.partial(solve_kernel, root),
        out_shape=(
            jax.ShapeDtypeStruct(finals[0].shape, jnp.float32),
            jax.ShapeDtypeStruct((n, n), jnp.float32),
        ),
        in_specs=[smem] + [vmem] * 8,
        out_specs=(vmem,) * 2,
        scratch_shapes=[pltpu.VMEM((n, n), jnp.float32)] * 2,
        compiler_params=grant,
        name="solve",
    )(own, *strips, *finals)


def shift(value, axis, by):
    n = lax.axis_size(axis)
    return lax.ppermute(value, axis, [(i, (i + by) % n) for i in range(n)])


def swap(value, axis, mask):
    n = lax.axis_size(axis)
    return lax.ppermute(value, axis, [(i, i ^ mask) for i in range(n)])


def xor_sum(value, axis, masks):
    terms = [value] + [swap(value, axis, m) for m in masks]
    while len(terms) > 1:
        terms = [terms[i] + terms[i + 1] for i in range(0, len(terms), 2)]
    return terms[0]


def body(subspace, onsite, blocks, cols):
    row_count = lax.axis_size("row")
    row_index = lax.axis_index("row")
    col_index = lax.axis_index("col").astype(jnp.int32)
    width, local_rows = subspace.shape
    slot_count, local_blocks, size, _ = blocks.shape
    pos, info = plan(cols, row_index, row_count, local_blocks)
    info = jnp.concatenate([info, col_index[None]])
    onsite = onsite[None, :]
    shaped = subspace.reshape(width, local_blocks, size)
    chosen = jnp.take(shaped, info[1 : 1 + 4 * HALO], axis=1)
    send = chosen.transpose(1, 0, 2).reshape(4, HALO, width, size)
    previous, before, x = None, subspace, subspace
    for step in range(FILTER):
        scale = filter_scale if step == 0 else 2.0 * filter_scale
        last = step == FILTER - 1
        halos = [shift(send[q], "row", -d) for q, d in enumerate(offsets(row_count))]
        partial = local_part(scale, pos, blocks, x, onsite, previous)
        y, x, *send = remote_part(scale, last, info, halos, partial, blocks)
        previous, before = before, y
    final = x
    pieces = [send[0]] + [shift(send[k], "col", k) for k in (1, 2, 3)]
    strips = gram_strips(pieces)
    finals = [final] + [shift(final, "col", k) for k in (1, 2, 3)]
    strip = strips[0]
    for k in (1, 2, 3):
        strip = strip + shift(strips[k], "col", k)
    low = row_count // 4
    strip = xor_sum(strip, "row", list(range(1, low)))
    strip = xor_sum(strip, "row", [low * m for m in (1, 2, 3)])
    blocks_of = [strip[:, j * width : (j + 1) * width] for j in range(4)]
    ordered = []
    for b in range(4):
        j = (col_index - b) % 4
        ordered.append(
            jnp.where(
                j < 2,
                jnp.where(j == 0, blocks_of[0], blocks_of[1]),
                jnp.where(j == 2, blocks_of[2], blocks_of[3]),
            )
        )
    strip = jnp.concatenate(ordered, axis=1)
    strips = [strip] + [shift(strip, "col", k) for k in (1, 2, 3)]
    root = math.sqrt(row_count * local_rows)
    return solve(root, col_index[None], strips, finals)


def solution(mesh):
    in_specs = (P("col", "row"), P("row"), P(None, "row", None, None), P())
    out_specs = (P("col", "row"), P())
    return jax.shard_map(body, mesh=mesh, in_specs=in_specs, out_specs=out_specs, check_vma=False)
```

time: 270 us -> 157 us (0.58)
  the two profiles are of different devices: /device:TPU:30 before, /device:TPU:0 now
where the time goes in v2:
time: 157 us
  starting transfers between devices  61.4 us (39%)
  Pallas kernels  45.4 us (29%)
  waiting for transfers between devices  33.1 us (21%)
  local copies, waits for them, and re-layouts  12 us (8%)
  other arithmetic  3.46 us (2%)
  between operations  1.67 us (1%)
    ppermute x28, starting transfers between devices, shift(): return lax.ppermute(value, axis, [(i, (i + by) % n) for i in range(n)])  47.8 us
    ppermute x28, waiting for transfers between devices, shift(): return lax.ppermute(value, axis, [(i, (i + by) % n) for i in range(n)])  28.8 us
    pallas_call x4, Pallas kernels, local_part(): pl.pallas_call(functools.partial(local_kernel, scale, prev is None), out_...  23.3 us
    ppermute x10, starting transfers between devices, swap(): return lax.ppermute(value, axis, [(i, i ^ mask) for i in range(n)])  13.6 us
    pallas_call x4, Pallas kernels, remote_part(): pl.pallas_call(functools.partial(remote_kernel, scale, last), out_shape=(...  12.6 us
    unnamed x11, local copies, waits for them, and re-layouts  9.2 us
    pallas_call x1, Pallas kernels, solve(): pl.pallas_call(functools.partial(solve_kernel, root), out_shape=(jax.Shap...  9.03 us
    ppermute x10, waiting for transfers between devices, swap(): return lax.ppermute(value, axis, [(i, i ^ mask) for i in range(n)])  4.33 us
  transfers between devices with their start and end apart: 38, of which 15 were waited for; matrix products, arithmetic and copies ran while one was open for 2% of the time, Pallas kernels for 15%

profile of v2, /device:TPU:0, one launch (start us, length us, event | category | flops | bytes accessed | tf_op | source)
XLA Modules:
  0.0 157.0 jit_solution(8902822058817904283)
XLA Ops:
  5.1 5.8 %collective-permute-start = (bf16[4,64,128]{2,1,0:T(8,128)(2,1)S(1)}, bf16[4,64,128]{2,1,0:T(8,128)(2,1)S(1)}, u32[]{:S(2)}, u32[]{:S(2)}) collective-permute-start(bf16[4,64,128]{2,1,0:T(8,128)(2,1)S(1)} %get-tuple-element.61), channel_id=1, source_target_pairs={{0,124},{4,0},{8,4},{12,8},{16,12},{20,16},{24,20},{28,24},{32,28}... | collective-permute-start | bytes 196616 | tf_op jit(solution)/shard_map/ppermute | solution.py:285
  16.2 7.0 %copy-done = bf16[20,32,128,128]{3,2,1,0:T(8,128)(2,1)S(1)} copy-done((bf16[20,32,128,128]{3,2,1,0:T(8,128)(2,1)S(1)}, bf16[20,32,128,128]{3,2,1,0:T(8,128)(2,1)}, u32[]{:S(2)}) %copy-start) | copy-done | bytes 20971544
  23.1 5.8 %local_part.4.refs_4_ = f32[64,4096]{1,0:T(8,128)S(1)} custom-call(s32[640]{0:T(1024)S(1)} %subtract_select_fusion.pos, bf16[20,32,128,128]{3,2,1,0:T(8,128)(2,1)S(1)} %copy-done, bf16[64,4096]{1,0:T(8,128)(2,1)S(1)} %copy-done.2, f32[1,4096]{1,0:T(1,128)S(1)} %bitcast.12), custom_call_target="tpu_custom_call" | custom-call | tf_op jit(solution)/shard_map/local_part/pallas_call | solution.py:133
  30.1 2.7 %remote_part.4 = (f32[64,4096]{1,0:T(8,128)S(1)}, bf16[64,4096]{1,0:T(8,128)(2,1)S(1)}, bf16[4,64,128]{2,1,0:T(8,128)(2,1)S(1)}, bf16[4,64,128]{2,1,0:T(8,128)(2...) custom-call(s32[658]{0:T(1024)S(1)} %pad_add_fusion.info, ...), custom_call_target="tpu_custom_call" | custom-call | tf_op jit(solution)/shard_map/remote_part/pallas_call | solution.py:149
  32.8 4.0 %collective-permute-start.4 = (bf16[4,64,128]{2,1,0:T(8,128)(2,1)S(1)}, bf16[4,64,128]{2,1,0:T(8,128)(2,1)S(1)}, u32[]{:S(2)}, u32[]{:S(2)}) collective-permute-start(bf16[4,64,128]{2,1,0:T(8,128)(2,1)S(1)} %get-tuple-element.28), channel_id=1, source_target_pairs={{0,124},{4,0},{8,4},{12,8},{16,12},{20,16},{24,20},{28,24},{32,28}... | collective-permute-start | bytes 196616 | tf_op jit(solution)/shard_map/ppermute | solution.py:285
  37.3 3.0 %collective-permute-start.7 = (bf16[4,64,128]{2,1,0:T(8,128)(2,1)S(1)}, bf16[4,64,128]{2,1,0:T(8,128)(2,1)S(1)}, u32[]{:S(2)}, u32[]{:S(2)}) collective-permute-start(bf16[4,64,128]{2,1,0:T(8,128)(2,1)S(1)} %get-tuple-element.31), channel_id=1, source_target_pairs={{0,64},{4,68},{8,72},{12,76},{16,80},{20,84},{24,88},{28,92},{32,9... | collective-permute-start | bytes 196616 | tf_op jit(solution)/shard_map/ppermute | solution.py:285
  40.3 5.8 %local_part.5.refs_4_ = f32[64,4096]{1,0:T(8,128)S(1)} custom-call(s32[640]{0:T(1024)S(1)} %subtract_select_fusion.pos, bf16[20,32,128,128]{3,2,1,0:T(8,128)(2,1)S(1)} %copy-done.1, bf16[64,4096]{1,0:T(8,128)(2,1)S(1)} %get-tuple-element.32.x, f32[1,4096]{1,0:T(1,128)S(1)} %bitcast.13, bf16[64,4096]{1,0:T(8,128)(2,1)S(1)} %copy-done.2), custom_call_target="tpu_custom_call" | custom-call | tf_op jit(solution)/shard_map/local_part/pallas_call | solution.py:133
  46.1 2.7 %remote_part.5 = (f32[64,4096]{1,0:T(8,128)S(1)}, bf16[64,4096]{1,0:T(8,128)(2,1)S(1)}, bf16[4,64,128]{2,1,0:T(8,128)(2,1)S(1)}, bf16[4,64,128]{2,1,0:T(8,128)(2...) custom-call(s32[658]{0:T(1024)S(1)} %pad_add_fusion.info, ...), custom_call_target="tpu_custom_call" | custom-call | tf_op jit(solution)/shard_map/remote_part/pallas_call | solution.py:149
  50.8 3.8 %collective-permute-start.8 = (bf16[4,64,128]{2,1,0:T(8,128)(2,1)S(1)}, bf16[4,64,128]{2,1,0:T(8,128)(2,1)S(1)}, u32[]{:S(2)}, u32[]{:S(2)}) collective-permute-start(bf16[4,64,128]{2,1,0:T(8,128)(2,1)S(1)} %get-tuple-element.33), channel_id=1, source_target_pairs={{0,124},{4,0},{8,4},{12,8},{16,12},{20,16},{24,20},{28,24},{32,28}... | collective-permute-start | bytes 196616 | tf_op jit(solution)/shard_map/ppermute | solution.py:285
  54.6 5.9 %local_part.6.refs_4_ = f32[64,4096]{1,0:T(8,128)S(1)} custom-call(s32[640]{0:T(1024)S(1)} %subtract_select_fusion.pos, bf16[20,32,128,128]{3,2,1,0:T(8,128)(2,1)S(1)} %copy-done.1, bf16[64,4096]{1,0:T(8,128)(2,1)S(1)} %get-tuple-element.37.x, f32[1,4096]{1,0:T(1,128)S(1)} %bitcast.14, f32[64,4096]{1,0:T(8,128)S(1)} %get-tuple-element.38.refs_0_), custom_call_target="tpu_custom_call" | custom-call | tf_op jit(solution)/shard_map/local_part/pallas_call | solution.py:133
  61.6 3.6 %remote_part.6 = (f32[64,4096]{1,0:T(8,128)}, bf16[64,4096]{1,0:T(8,128)(2,1)S(1)}, bf16[4,64,128]{2,1,0:T(8,128)(2,1)S(1)}, bf16[4,64,128]{2,1,0:T(8,128)(2,1)S...) custom-call(s32[658]{0:T(1024)S(1)} %pad_add_fusion.info, ...), custom_call_target="tpu_custom_call" | custom-call | tf_op jit(solution)/shard_map/remote_part/pallas_call | solution.py:149
  65.2 4.7 %collective-permute-start.12 = (bf16[4,64,128]{2,1,0:T(8,128)(2,1)S(1)}, bf16[4,64,128]{2,1,0:T(8,128)(2,1)S(1)}, u32[]{:S(2)}, u32[]{:S(2)}) collective-permute-start(bf16[4,64,128]{2,1,0:T(8,128)(2,1)S(1)} %get-tuple-element.39), channel_id=1, source_target_pairs={{0,124},{4,0},{8,4},{12,8},{16,12},{20,16},{24,20},{28,24},{32,28}... | collective-permute-start | bytes 196616 | tf_op jit(solution)/shard_map/ppermute | solution.py:285
  70.7 5.9 %local_part.7.refs_4_ = f32[64,4096]{1,0:T(8,128)S(1)} custom-call(s32[640]{0:T(1024)S(1)} %subtract_select_fusion.pos, bf16[20,32,128,128]{3,2,1,0:T(8,128)(2,1)S(1)} %copy-done.1, bf16[64,4096]{1,0:T(8,128)(2,1)S(1)} %get-tuple-element.43.x, f32[1,4096]{1,0:T(1,128)S(1)} %bitcast.15, f32[64,4096]{1,0:T(8,128)S(1)} %get-tuple-element.44.refs_0_), custom_call_target="tpu_custom_call" | custom-call | tf_op jit(solution)/shard_map/local_part/pallas_call | solution.py:133
  76.9 3.6 %remote_part.7 = (f32[64,4096]{1,0:T(8,128)}, bf16[64,4096]{1,0:T(8,128)(2,1)S(1)}, bf16[64,1024]{1,0:T(8,128)(2,1)S(1)}, bf16[64,1024]{1,0:T(8,128)(2,1)S(1)}, ...) custom-call(s32[658]{0:T(1024)S(1)} %pad_add_fusion.info, ...), custom_call_target="tpu_custom_call" | custom-call | tf_op jit(solution)/shard_map/remote_part/pallas_call | solution.py:149
  80.5 1.6 collective-permute-start.16
  82.1 2.9 %collective-permute-start.17 = (bf16[64,1024]{1,0:T(8,128)(2,1)S(1)}, bf16[64,1024]{1,0:T(8,128)(2,1)S(1)}, u32[]{:S(2)}, u32[]{:S(2)}) collective-permute-start(bf16[64,1024]{1,0:T(8,128)(2,1)S(1)} %get-tuple-element.47), channel_id=1, source_target_pairs={{0,2},{1,3},{2,0},{3,1},{4,6},{5,7},{6,4},{7,5},{8,10},{9,11},{10,... | collective-permute-start | bytes 393224 | tf_op jit(solution)/shard_map/ppermute | solution.py:285
  86.7 2.7 %collective-permute-done.17.refs_2_ = bf16[64,1024]{1,0:T(8,128)(2,1)S(1)} collective-permute-done((bf16[64,1024]{1,0:T(8,128)(2,1)S(1)}, bf16[64,1024]{1,0:T(8,128)(2,1)S(1)}, u32[]{:S(2)}, u32[]{:S(2)}) %collective-permute-start.17) | collective-permute-done | bytes 131104 | tf_op jit(solution)/shard_map/ppermute | solution.py:285
  91.4 3.3 %collective-permute-start.20 = (f32[64,256]{1,0:T(8,128)S(1)}, f32[64,256]{1,0:T(8,128)S(1)}, u32[]{:S(2)}, u32[]{:S(2)}) collective-permute-start(f32[64,256]{1,0:T(8,128)S(1)} %get-tuple-element.51), channel_id=1, source_target_pairs={{0,2},{1,3},{2,0},{3,1},{4,6},{5,7},{6,4},{7,5},{8,10},{9,11},{10,... | collective-permute-start | bytes 196616 | tf_op jit(solution)/shard_map/ppermute | solution.py:285
  96.3 1.4 collective-permute-done.20
  100.0 1.5 collective-permute-start.23
  101.5 1.8 %collective-permute-start.25 = (f32[64,256]{1,0:T(8,128)S(1)}, f32[64,256]{1,0:T(8,128)S(1)}, u32[]{:S(2)}, u32[]{:S(2)}) collective-permute-start(f32[64,256]{1,0:T(8,128)S(1)} %add_add_fusion.2), channel_id=1, source_target_pairs={{0,16},{4,20},{8,24},{12,28},{16,0},{20,4},{24,8},{28,12},{32,48},... | collective-permute-start | bytes 196616 | tf_op jit(solution)/shard_map/ppermute | solution.py:290
  103.3 1.7 %collective-permute-start.26 = (f32[64,256]{1,0:T(8,128)S(1)}, f32[64,256]{1,0:T(8,128)S(1)}, u32[]{:S(2)}, u32[]{:S(2)}) collective-permute-start(f32[64,256]{1,0:T(8,128)S(1)} %add_add_fusion.2), channel_id=1, source_target_pairs={{0,20},{4,16},{8,28},{12,24},{16,4},{20,0},{24,12},{28,8},{32,52},... | collective-permute-start | bytes 196616 | tf_op jit(solution)/shard_map/ppermute | solution.py:290
  105.9 1.8 %collective-permute-start.28 = (f32[64,256]{1,0:T(8,128)S(1)}, f32[64,256]{1,0:T(8,128)S(1)}, u32[]{:S(2)}, u32[]{:S(2)}) collective-permute-start(f32[64,256]{1,0:T(8,128)S(1)} %add_add_fusion.2), channel_id=1, source_target_pairs={{0,28},{4,24},{8,20},{12,16},{16,12},{20,8},{24,4},{28,0},{32,60},... | collective-permute-start | bytes 196616 | tf_op jit(solution)/shard_map/ppermute | solution.py:290
  108.9 2.1 %collective-permute-done.27 = f32[64,256]{1,0:T(8,128)S(1)} collective-permute-done((f32[64,256]{1,0:T(8,128)S(1)}, f32[64,256]{1,0:T(8,128)S(1)}, u32[]{:S(2)}, u32[]{:S(2)}) %collective-permute-start.27) | collective-permute-done | bytes 65568 | tf_op jit(solution)/shard_map/ppermute | solution.py:290
  111.6 1.5 collective-permute-start.29
  113.1 3.1 %collective-permute-start.30 = (f32[64,256]{1,0:T(8,128)S(1)}, f32[64,256]{1,0:T(8,128)S(1)}, u32[]{:S(2)}, u32[]{:S(2)}) collective-permute-start(f32[64,256]{1,0:T(8,128)S(1)} %add_add_fusion.1), channel_id=1, source_target_pairs={{0,64},{4,68},{8,72},{12,76},{16,80},{20,84},{24,88},{28,92},{32,9... | collective-permute-start | bytes 196616 | tf_op jit(solution)/shard_map/ppermute | solution.py:290
  117.6 3.1 %collective-permute-start.36 = (bf16[64,4096]{1,0:T(8,128)(2,1)S(1)}, bf16[64,4096]{1,0:T(8,128)(2,1)S(1)}, u32[]{:S(2)}, u32[]{:S(2)}) collective-permute-start(bf16[64,4096]{1,0:T(8,128)(2,1)S(1)} %get-tuple-element.53.refs_4_), channel_id=1, source_target_pairs={{0,2},{1,3},{2,0},{3,1},{4,6},{5,7},{6,4},{7,5},{8,10},{9,11},{10,... | collective-permute-start | bytes 1572872 | tf_op jit(solution)/shard_map/ppermute | solution.py:285
  123.2 2.7 %collective-permute-start.33 = (f32[64,256]{1,0:T(8,128)S(1)}, f32[64,256]{1,0:T(8,128)S(1)}, u32[]{:S(2)}, u32[]{:S(2)}) collective-permute-start(f32[64,256]{1,0:T(8,128)S(1)} %pad_maximum_fusion.refs_0_), channel_id=1, source_target_pairs={{0,2},{1,3},{2,0},{3,1},{4,6},{5,7},{6,4},{7,5},{8,10},{9,11},{10,... | collective-permute-start | bytes 196616 | tf_op jit(solution)/shard_map/ppermute | solution.py:285
  125.9 17.7 %collective-permute-done.32.refs_1_ = f32[64,256]{1,0:T(8,128)S(1)} collective-permute-done((f32[64,256]{1,0:T(8,128)S(1)}, f32[64,256]{1,0:T(8,128)S(1)}, u32[]{:S(2)}, u32[]{:S(2)}) %collective-permute-start.32) | collective-permute-done | bytes 65568 | tf_op jit(solution)/shard_map/ppermute | solution.py:285
  143.6 2.4 %collective-permute-start.34 = (f32[64,256]{1,0:T(8,128)S(1)}, f32[64,256]{1,0:T(8,128)S(1)}, u32[]{:S(2)}, u32[]{:S(2)}) collective-permute-start(f32[64,256]{1,0:T(8,128)S(1)} %pad_maximum_fusion.refs_0_), channel_id=1, source_target_pairs={{0,3},{1,0},{2,1},{3,2},{4,7},{5,4},{6,5},{7,6},{8,11},{9,8},{10,9... | collective-permute-start | bytes 196616 | tf_op jit(solution)/shard_map/ppermute | solution.py:285
  146.2 1.8 %collective-permute-done.34.refs_3_ = f32[64,256]{1,0:T(8,128)S(1)} collective-permute-done((f32[64,256]{1,0:T(8,128)S(1)}, f32[64,256]{1,0:T(8,128)S(1)}, u32[]{:S(2)}, u32[]{:S(2)}) %collective-permute-start.34) | collective-permute-done | bytes 65568 | tf_op jit(solution)/shard_map/ppermute | solution.py:285
  147.9 9.0 %solve.1 = (f32[64,4096]{1,0:T(8,128)}, f32[256,256]{1,0:T(8,128)}) custom-call(s32[1]{0:T(128)} %bitcast.own_ref, f32[64,256]{1,0:T(8,128)S(1)} %pad_maximum_fusion.refs_0_, f32[64,256]{1,0:T(8,128)S(1)} %collective-permute-done.32.refs_1_, f32[64,256]{1,0:T(8,128)S(1)} %collective-permute-done.33.refs_2_, f32[64,256]{1,0:T(8,128)S(1)} %collective-permute-done.34.refs_3_, ...), custom_call_target="tpu_custom_call" | custom-call | tf_op jit(solution)/shard_map/solve/pallas_call | solution.py:269
  (114 shorter events, 29.1 us)
Async XLA Ops:
  5.1 23.9 %collective-permute-start = (bf16[4,64,128]{2,1,0:T(8,128)(2,1)S(1)}, bf16[4,64,128]{2,1,0:T(8,128)(2,1)S(1)}, u32[]{:S(2)}, u32[]{:S(2)}) collective-permute-start(bf16[4,64,128]{2,1,0:T(8,128)(2,1)S(1)} %get-tuple-element.61), channel_id=1, source_target_pairs={{0,124},{4,0},{8,4},{12,8},{16,12},{20,16},{24,20},{28,24},{32,28}... | collective-permute-start | bytes 196616 | tf_op jit(solution)/shard_map/ppermute | solution.py:285
  10.9 18.1 %collective-permute-start.1 = (bf16[4,64,128]{2,1,0:T(8,128)(2,1)S(1)}, bf16[4,64,128]{2,1,0:T(8,128)(2,1)S(1)}, u32[]{:S(2)}, u32[]{:S(2)}) collective-permute-start(bf16[4,64,128]{2,1,0:T(8,128)(2,1)S(1)} %get-tuple-element.60), channel_id=1, source_target_pairs={{0,4},{4,8},{8,12},{12,16},{16,20},{20,24},{24,28},{28,32},{32,36}... | collective-permute-start | bytes 196616 | tf_op jit(solution)/shard_map/ppermute | solution.py:285
  10.9 18.1 %collective-permute-start.2 = (bf16[4,64,128]{2,1,0:T(8,128)(2,1)S(1)}, bf16[4,64,128]{2,1,0:T(8,128)(2,1)S(1)}, u32[]{:S(2)}, u32[]{:S(2)}) collective-permute-start(bf16[4,64,128]{2,1,0:T(8,128)(2,1)S(1)} %get-tuple-element.59), channel_id=1, source_target_pairs={{0,120},{4,124},{8,0},{12,4},{16,8},{20,12},{24,16},{28,20},{32,24... | collective-permute-start | bytes 196616 | tf_op jit(solution)/shard_map/ppermute | solution.py:285
  12.0 17.0 %collective-permute-start.3 = (bf16[4,64,128]{2,1,0:T(8,128)(2,1)S(1)}, bf16[4,64,128]{2,1,0:T(8,128)(2,1)S(1)}, u32[]{:S(2)}, u32[]{:S(2)}) collective-permute-start(bf16[4,64,128]{2,1,0:T(8,128)(2,1)S(1)} %get-tuple-element.58), channel_id=1, source_target_pairs={{0,64},{4,68},{8,72},{12,76},{16,80},{20,84},{24,88},{28,92},{32,9... | collective-permute-start | bytes 196616 | tf_op jit(solution)/shard_map/ppermute | solution.py:285
  32.8 13.2 %collective-permute-start.4 = (bf16[4,64,128]{2,1,0:T(8,128)(2,1)S(1)}, bf16[4,64,128]{2,1,0:T(8,128)(2,1)S(1)}, u32[]{:S(2)}, u32[]{:S(2)}) collective-permute-start(bf16[4,64,128]{2,1,0:T(8,128)(2,1)S(1)} %get-tuple-element.28), channel_id=1, source_target_pairs={{0,124},{4,0},{8,4},{12,8},{16,12},{20,16},{24,20},{28,24},{32,28}... | collective-permute-start | bytes 196616 | tf_op jit(solution)/shard_map/ppermute | solution.py:285
  36.8 9.3 %collective-permute-start.5 = (bf16[4,64,128]{2,1,0:T(8,128)(2,1)S(1)}, bf16[4,64,128]{2,1,0:T(8,128)(2,1)S(1)}, u32[]{:S(2)}, u32[]{:S(2)}) collective-permute-start(bf16[4,64,128]{2,1,0:T(8,128)(2,1)S(1)} %get-tuple-element.29), channel_id=1, source_target_pairs={{0,4},{4,8},{8,12},{12,16},{16,20},{20,24},{24,28},{28,32},{32,36}... | collective-permute-start | bytes 196616 | tf_op jit(solution)/shard_map/ppermute | solution.py:285
  36.8 9.3 %collective-permute-start.6 = (bf16[4,64,128]{2,1,0:T(8,128)(2,1)S(1)}, bf16[4,64,128]{2,1,0:T(8,128)(2,1)S(1)}, u32[]{:S(2)}, u32[]{:S(2)}) collective-permute-start(bf16[4,64,128]{2,1,0:T(8,128)(2,1)S(1)} %get-tuple-element.30), channel_id=1, source_target_pairs={{0,120},{4,124},{8,0},{12,4},{16,8},{20,12},{24,16},{28,20},{32,24... | collective-permute-start | bytes 196616 | tf_op jit(solution)/shard_map/ppermute | solution.py:285
  37.3 8.8 %collective-permute-start.7 = (bf16[4,64,128]{2,1,0:T(8,128)(2,1)S(1)}, bf16[4,64,128]{2,1,0:T(8,128)(2,1)S(1)}, u32[]{:S(2)}, u32[]{:S(2)}) collective-permute-start(bf16[4,64,128]{2,1,0:T(8,128)(2,1)S(1)} %get-tuple-element.31), channel_id=1, source_target_pairs={{0,64},{4,68},{8,72},{12,76},{16,80},{20,84},{24,88},{28,92},{32,9... | collective-permute-start | bytes 196616 | tf_op jit(solution)/shard_map/ppermute | solution.py:285
  48.9 11.6 %collective-permute-start.10 = (bf16[4,64,128]{2,1,0:T(8,128)(2,1)S(1)}, bf16[4,64,128]{2,1,0:T(8,128)(2,1)S(1)}, u32[]{:S(2)}, u32[]{:S(2)}) collective-permute-start(bf16[4,64,128]{2,1,0:T(8,128)(2,1)S(1)} %get-tuple-element.35), channel_id=1, source_target_pairs={{0,120},{4,124},{8,0},{12,4},{16,8},{20,12},{24,16},{28,20},{32,24... | collective-permute-start | bytes 196616 | tf_op jit(solution)/shard_map/ppermute | solution.py:285
  49.7 10.8 %collective-permute-start.11 = (bf16[4,64,128]{2,1,0:T(8,128)(2,1)S(1)}, bf16[4,64,128]{2,1,0:T(8,128)(2,1)S(1)}, u32[]{:S(2)}, u32[]{:S(2)}) collective-permute-start(bf16[4,64,128]{2,1,0:T(8,128)(2,1)S(1)} %get-tuple-element.36), channel_id=1, source_target_pairs={{0,64},{4,68},{8,72},{12,76},{16,80},{20,84},{24,88},{28,92},{32,9... | collective-permute-start | bytes 196616 | tf_op jit(solution)/shard_map/ppermute | solution.py:285
  50.8 9.7 %collective-permute-start.8 = (bf16[4,64,128]{2,1,0:T(8,128)(2,1)S(1)}, bf16[4,64,128]{2,1,0:T(8,128)(2,1)S(1)}, u32[]{:S(2)}, u32[]{:S(2)}) collective-permute-start(bf16[4,64,128]{2,1,0:T(8,128)(2,1)S(1)} %get-tuple-element.33), channel_id=1, source_target_pairs={{0,124},{4,0},{8,4},{12,8},{16,12},{20,16},{24,20},{28,24},{32,28}... | collective-permute-start | bytes 196616 | tf_op jit(solution)/shard_map/ppermute | solution.py:285
  54.6 7.0 %collective-permute-start.9 = (bf16[4,64,128]{2,1,0:T(8,128)(2,1)S(1)}, bf16[4,64,128]{2,1,0:T(8,128)(2,1)S(1)}, u32[]{:S(2)}, u32[]{:S(2)}) collective-permute-start(bf16[4,64,128]{2,1,0:T(8,128)(2,1)S(1)} %get-tuple-element.34), channel_id=1, source_target_pairs={{0,4},{4,8},{8,12},{12,16},{16,20},{20,24},{24,28},{28,32},{32,36}... | collective-permute-start | bytes 196616 | tf_op jit(solution)/shard_map/ppermute | solution.py:285
  65.2 11.4 %collective-permute-start.12 = (bf16[4,64,128]{2,1,0:T(8,128)(2,1)S(1)}, bf16[4,64,128]{2,1,0:T(8,128)(2,1)S(1)}, u32[]{:S(2)}, u32[]{:S(2)}) collective-permute-start(bf16[4,64,128]{2,1,0:T(8,128)(2,1)S(1)} %get-tuple-element.39), channel_id=1, source_target_pairs={{0,124},{4,0},{8,4},{12,8},{16,12},{20,16},{24,20},{28,24},{32,28}... | collective-permute-start | bytes 196616 | tf_op jit(solution)/shard_map/ppermute | solution.py:285
  69.9 7.0 %collective-permute-start.13 = (bf16[4,64,128]{2,1,0:T(8,128)(2,1)S(1)}, bf16[4,64,128]{2,1,0:T(8,128)(2,1)S(1)}, u32[]{:S(2)}, u32[]{:S(2)}) collective-permute-start(bf16[4,64,128]{2,1,0:T(8,128)(2,1)S(1)} %get-tuple-element.40), channel_id=1, source_target_pairs={{0,4},{4,8},{8,12},{12,16},{16,20},{20,24},{24,28},{28,32},{32,36}... | collective-permute-start | bytes 196616 | tf_op jit(solution)/shard_map/ppermute | solution.py:285
  69.9 7.0 %collective-permute-start.14 = (bf16[4,64,128]{2,1,0:T(8,128)(2,1)S(1)}, bf16[4,64,128]{2,1,0:T(8,128)(2,1)S(1)}, u32[]{:S(2)}, u32[]{:S(2)}) collective-permute-start(bf16[4,64,128]{2,1,0:T(8,128)(2,1)S(1)} %get-tuple-element.41), channel_id=1, source_target_pairs={{0,120},{4,124},{8,0},{12,4},{16,8},{20,12},{24,16},{28,20},{32,24... | collective-permute-start | bytes 196616 | tf_op jit(solution)/shard_map/ppermute | solution.py:285
  70.3 6.6 %collective-permute-start.15 = (bf16[4,64,128]{2,1,0:T(8,128)(2,1)S(1)}, bf16[4,64,128]{2,1,0:T(8,128)(2,1)S(1)}, u32[]{:S(2)}, u32[]{:S(2)}) collective-permute-start(bf16[4,64,128]{2,1,0:T(8,128)(2,1)S(1)} %get-tuple-element.42), channel_id=1, source_target_pairs={{0,64},{4,68},{8,72},{12,76},{16,80},{20,84},{24,88},{28,92},{32,9... | collective-permute-start | bytes 196616 | tf_op jit(solution)/shard_map/ppermute | solution.py:285
  80.5 6.2 %collective-permute-start.16 = (bf16[64,1024]{1,0:T(8,128)(2,1)S(1)}, bf16[64,1024]{1,0:T(8,128)(2,1)S(1)}, u32[]{:S(2)}, u32[]{:S(2)}) collective-permute-start(bf16[64,1024]{1,0:T(8,128)(2,1)S(1)} %get-tuple-element.46), channel_id=1, source_target_pairs={{0,1},{1,2},{2,3},{3,0},{4,5},{5,6},{6,7},{7,4},{8,9},{9,10},{10,1... | collective-permute-start | bytes 393224 | tf_op jit(solution)/shard_map/ppermute | solution.py:285
  82.1 7.3 %collective-permute-start.17 = (bf16[64,1024]{1,0:T(8,128)(2,1)S(1)}, bf16[64,1024]{1,0:T(8,128)(2,1)S(1)}, u32[]{:S(2)}, u32[]{:S(2)}) collective-permute-start(bf16[64,1024]{1,0:T(8,128)(2,1)S(1)} %get-tuple-element.47), channel_id=1, source_target_pairs={{0,2},{1,3},{2,0},{3,1},{4,6},{5,7},{6,4},{7,5},{8,10},{9,11},{10,... | collective-permute-start | bytes 393224 | tf_op jit(solution)/shard_map/ppermute | solution.py:285
  91.4 6.3 %collective-permute-start.20 = (f32[64,256]{1,0:T(8,128)S(1)}, f32[64,256]{1,0:T(8,128)S(1)}, u32[]{:S(2)}, u32[]{:S(2)}) collective-permute-start(f32[64,256]{1,0:T(8,128)S(1)} %get-tuple-element.51), channel_id=1, source_target_pairs={{0,2},{1,3},{2,0},{3,1},{4,6},{5,7},{6,4},{7,5},{8,10},{9,11},{10,... | collective-permute-start | bytes 196616 | tf_op jit(solution)/shard_map/ppermute | solution.py:285
  99.1 5.9 %collective-permute-start.22 = (f32[64,256]{1,0:T(8,128)S(1)}, f32[64,256]{1,0:T(8,128)S(1)}, u32[]{:S(2)}, u32[]{:S(2)}) collective-permute-start(f32[64,256]{1,0:T(8,128)S(1)} %add_add_fusion.2), channel_id=1, source_target_pairs={{0,4},{4,0},{8,12},{12,8},{16,20},{20,16},{24,28},{28,24},{32,36},... | collective-permute-start | bytes 196616 | tf_op jit(solution)/shard_map/ppermute | solution.py:290
  100.0 6.0 %collective-permute-start.23 = (f32[64,256]{1,0:T(8,128)S(1)}, f32[64,256]{1,0:T(8,128)S(1)}, u32[]{:S(2)}, u32[]{:S(2)}) collective-permute-start(f32[64,256]{1,0:T(8,128)S(1)} %add_add_fusion.2), channel_id=1, source_target_pairs={{0,8},{4,12},{8,0},{12,4},{16,24},{20,28},{24,16},{28,20},{32,40},... | collective-permute-start | bytes 196616 | tf_op jit(solution)/shard_map/ppermute | solution.py:290
  101.4 6.3 %collective-permute-start.24 = (f32[64,256]{1,0:T(8,128)S(1)}, f32[64,256]{1,0:T(8,128)S(1)}, u32[]{:S(2)}, u32[]{:S(2)}) collective-permute-start(f32[64,256]{1,0:T(8,128)S(1)} %add_add_fusion.2), channel_id=1, source_target_pairs={{0,12},{4,8},{8,4},{12,0},{16,28},{20,24},{24,20},{28,16},{32,44},... | collective-permute-start | bytes 196616 | tf_op jit(solution)/shard_map/ppermute | solution.py:290
  101.5 6.2 %collective-permute-start.25 = (f32[64,256]{1,0:T(8,128)S(1)}, f32[64,256]{1,0:T(8,128)S(1)}, u32[]{:S(2)}, u32[]{:S(2)}) collective-permute-start(f32[64,256]{1,0:T(8,128)S(1)} %add_add_fusion.2), channel_id=1, source_target_pairs={{0,16},{4,20},{8,24},{12,28},{16,0},{20,4},{24,8},{28,12},{32,48},... | collective-permute-start | bytes 196616 | tf_op jit(solution)/shard_map/ppermute | solution.py:290
  103.3 5.7 %collective-permute-start.26 = (f32[64,256]{1,0:T(8,128)S(1)}, f32[64,256]{1,0:T(8,128)S(1)}, u32[]{:S(2)}, u32[]{:S(2)}) collective-permute-start(f32[64,256]{1,0:T(8,128)S(1)} %add_add_fusion.2), channel_id=1, source_target_pairs={{0,20},{4,16},{8,28},{12,24},{16,4},{20,0},{24,12},{28,8},{32,52},... | collective-permute-start | bytes 196616 | tf_op jit(solution)/shard_map/ppermute | solution.py:290
  105.0 6.0 %collective-permute-start.27 = (f32[64,256]{1,0:T(8,128)S(1)}, f32[64,256]{1,0:T(8,128)S(1)}, u32[]{:S(2)}, u32[]{:S(2)}) collective-permute-start(f32[64,256]{1,0:T(8,128)S(1)} %add_add_fusion.2), channel_id=1, source_target_pairs={{0,24},{4,28},{8,16},{12,20},{16,8},{20,12},{24,0},{28,4},{32,56},... | collective-permute-start | bytes 196616 | tf_op jit(solution)/shard_map/ppermute | solution.py:290
  111.6 9.1 %collective-permute-start.29 = (f32[64,256]{1,0:T(8,128)S(1)}, f32[64,256]{1,0:T(8,128)S(1)}, u32[]{:S(2)}, u32[]{:S(2)}) collective-permute-start(f32[64,256]{1,0:T(8,128)S(1)} %add_add_fusion.1), channel_id=1, source_target_pairs={{0,32},{4,36},{8,40},{12,44},{16,48},{20,52},{24,56},{28,60},{32,0... | collective-permute-start | bytes 196616 | tf_op jit(solution)/shard_map/ppermute | solution.py:290
  113.1 8.0 %collective-permute-start.30 = (f32[64,256]{1,0:T(8,128)S(1)}, f32[64,256]{1,0:T(8,128)S(1)}, u32[]{:S(2)}, u32[]{:S(2)}) collective-permute-start(f32[64,256]{1,0:T(8,128)S(1)} %add_add_fusion.1), channel_id=1, source_target_pairs={{0,64},{4,68},{8,72},{12,76},{16,80},{20,84},{24,88},{28,92},{32,9... | collective-permute-start | bytes 196616 | tf_op jit(solution)/shard_map/ppermute | solution.py:290
  116.5 31.4 %collective-permute-start.35 = (bf16[64,4096]{1,0:T(8,128)(2,1)S(1)}, bf16[64,4096]{1,0:T(8,128)(2,1)S(1)}, u32[]{:S(2)}, u32[]{:S(2)}) collective-permute-start(bf16[64,4096]{1,0:T(8,128)(2,1)S(1)} %get-tuple-element.53.refs_4_), channel_id=1, source_target_pairs={{0,1},{1,2},{2,3},{3,0},{4,5},{5,6},{6,7},{7,4},{8,9},{9,10},{10,1... | collective-permute-start | bytes 1572872 | tf_op jit(solution)/shard_map/ppermute | solution.py:285
  117.6 30.3 %collective-permute-start.36 = (bf16[64,4096]{1,0:T(8,128)(2,1)S(1)}, bf16[64,4096]{1,0:T(8,128)(2,1)S(1)}, u32[]{:S(2)}, u32[]{:S(2)}) collective-permute-start(bf16[64,4096]{1,0:T(8,128)(2,1)S(1)} %get-tuple-element.53.refs_4_), channel_id=1, source_target_pairs={{0,2},{1,3},{2,0},{3,1},{4,6},{5,7},{6,4},{7,5},{8,10},{9,11},{10,... | collective-permute-start | bytes 1572872 | tf_op jit(solution)/shard_map/ppermute | solution.py:285
  120.7 27.3 %collective-permute-start.37 = (bf16[64,4096]{1,0:T(8,128)(2,1)S(1)}, bf16[64,4096]{1,0:T(8,128)(2,1)S(1)}, u32[]{:S(2)}, u32[]{:S(2)}) collective-permute-start(bf16[64,4096]{1,0:T(8,128)(2,1)S(1)} %get-tuple-element.53.refs_4_), channel_id=1, source_target_pairs={{0,3},{1,0},{2,1},{3,2},{4,7},{5,4},{6,5},{7,6},{8,11},{9,8},{10,9... | collective-permute-start | bytes 1572872 | tf_op jit(solution)/shard_map/ppermute | solution.py:285
  121.9 21.7 %collective-permute-start.32 = (f32[64,256]{1,0:T(8,128)S(1)}, f32[64,256]{1,0:T(8,128)S(1)}, u32[]{:S(2)}, u32[]{:S(2)}) collective-permute-start(f32[64,256]{1,0:T(8,128)S(1)} %pad_maximum_fusion.refs_0_), channel_id=1, source_target_pairs={{0,1},{1,2},{2,3},{3,0},{4,5},{5,6},{6,7},{7,4},{8,9},{9,10},{10,1... | collective-permute-start | bytes 196616 | tf_op jit(solution)/shard_map/ppermute | solution.py:285
  123.2 22.9 %collective-permute-start.33 = (f32[64,256]{1,0:T(8,128)S(1)}, f32[64,256]{1,0:T(8,128)S(1)}, u32[]{:S(2)}, u32[]{:S(2)}) collective-permute-start(f32[64,256]{1,0:T(8,128)S(1)} %pad_maximum_fusion.refs_0_), channel_id=1, source_target_pairs={{0,2},{1,3},{2,0},{3,1},{4,6},{5,7},{6,4},{7,5},{8,10},{9,11},{10,... | collective-permute-start | bytes 196616 | tf_op jit(solution)/shard_map/ppermute | solution.py:285
  (11 other events, 73.5 us)

commit v3 on v2

--- a/solution.py
+++ b/solution.py
@@ -11,7 +11,7 @@
 HALO = 4
 FILTER = 4
 UNROLL = 4
-CHUNK = 8
+LATE = 4
 PANEL = 16
 
 filter_scale = 0.4
@@ -48,18 +48,38 @@
     slot_place = jnp.sum(jnp.where(matches, places, 0), axis=-1)
     within = own - row_index * local_blocks
     is_local = (within >= 0) & (within < local_blocks)
-    position = jnp.where(is_local, within, local_blocks)
-    order = ranks_of(~is_local)
-    slot_ids = jnp.arange(slots, dtype=jnp.int32)
-    hit = (~is_local)[:, None] & (order[:, None] == slot_ids)
-    code = slot_ids * 32 + slot_place
-    pad_code = HALO * len(deltas)
-    listed = jnp.sum(jnp.where(hit, code[:, None] - pad_code, 0), axis=0) + pad_code
-    count = (order[-1:] + 1).astype(jnp.int32)
-    return position, jnp.concatenate([count, send, listed])
-
-
-def local_kernel(scale, first, pos, blocks, x, onsite, *refs):
+    place = jnp.where(is_local, within, local_blocks + 1 + slot_place)
+    near = is_local.reshape(local_blocks, slot_count)
+    near_rank = ranks_of(near)
+    far_rank = near_rank[:, -1:] + 1 + ranks_of(~near)
+    rank = jnp.where(near, near_rank, far_rank)
+    slot_ids = jnp.arange(slot_count, dtype=jnp.int32)
+    code = slot_ids * 64 + place.reshape(local_blocks, slot_count)
+    sorts = rank[:, :, None] == slot_ids
+    table = jnp.sum(jnp.where(sorts, code[:, :, None], 0), axis=1)
+    extra = (slot_ids < slot_count - LATE) & (table % 64 > local_blocks)
+    extra_code = (local_ids[:, None] * 2048 + table).reshape(-1)
+    order = jnp.where(extra.reshape(-1), ranks_of(extra.reshape(-1)), -1)
+    hit = order[:, None] == jnp.arange(slots, dtype=jnp.int32)
+    listed = jnp.sum(jnp.where(hit, extra_code[:, None], 0), axis=0)
+    count = jnp.sum(extra.astype(jnp.int32)).reshape(1)
+    return table.reshape(-1), jnp.concatenate([send, count, listed])
+
+
+def slot_pairs(table, row, slots, held, blocks, limit):
+    slot_count = blocks.shape[0]
+    total = None
+    for t in range(slots.start, slots.stop, 2):
+        codes = [table[row * slot_count + t + k] for k in range(2)]
+        places = [jnp.minimum(code & 63, limit) for code in codes]
+        taken = jnp.concatenate([held[p] for p in places], axis=1)
+        block = jnp.concatenate([blocks[code >> 6, row] for code in codes], axis=0)
+        product = jnp.dot(taken, block, preferred_element_type=jnp.float32)
+        total = product if total is None else total + product
+    return total
+
+
+def local_kernel(scale, first, table, blocks, x, onsite, *refs):
     prev, y, held = (None, *refs) if first else refs
     slot_count, local_blocks, size, _ = blocks.shape
     for j in range(local_blocks):
@@ -70,13 +90,8 @@
     def _(group):
         for u in range(UNROLL):
             row = group * UNROLL + u
-            total = None
-            for s in range(0, slot_count, 2):
-                at = row * slot_count + s
-                taken = jnp.concatenate([held[pos[at]], held[pos[at + 1]]], axis=1)
-                block = jnp.concatenate([blocks[s, row], blocks[s + 1, row]], axis=0)
-                product = jnp.dot(taken, block, preferred_element_type=jnp.float32)
-                total = product if total is None else total + product
+            early = range(slot_count - LATE)
+            total = slot_pairs(table, row, early, held, blocks, local_blocks)
             span = pl.ds(pl.multiple_of(row * size, size), size)
             value = scale * (total + onsite[:, span] * held[row].astype(jnp.float32))
             if prev is not None:
@@ -84,42 +99,48 @@
             y[:, span] = value
 
 
-def remote_kernel(scale, last, info, *refs):
-    halos, (y_in, blocks, y, x), rest = refs[:4], refs[4:8], refs[8:]
-    sends, zero = rest[:-1], rest[-1]
+def remote_kernel(scale, last, info, table, *refs):
+    halos, (y_in, x_in, blocks, y, x), rest = refs[:4], refs[4:9], refs[9:]
+    sends, held = rest[:-1], rest[-1]
     slot_count, local_blocks, size, _ = blocks.shape
     per = halos[0].shape[0]
-    count = info[0]
-    list_at = 1 + 4 * per
+    count = info[4 * per]
+    for j in range(local_blocks):
+        held[j] = x_in[:, j * size : (j + 1) * size]
+    held[local_blocks] = jnp.zeros(held.shape[1:], held.dtype)
     for q in range(4):
-        zero[q * per : (q + 1) * per] = halos[q][...]
-    zero[4 * per] = jnp.zeros(zero.shape[1:], zero.dtype)
-    y[...] = y_in[...]
-
-    @pl.loop(0, (count + CHUNK - 1) // CHUNK)
-    def _(c):
-        for k in range(CHUNK):
-            code = info[list_at + c * CHUNK + k]
-            entry = code // 32
-            place = lax.rem(code, 32)
-            row = entry // slot_count
-            slot = entry - row * slot_count
-            product = jnp.dot(zero[place], blocks[slot, row], preferred_element_type=jnp.float32)
+        at = local_blocks + 1 + q * per
+        held[at : at + per] = halos[q][...]
+
+    @pl.loop(0, local_blocks // UNROLL)
+    def _(group):
+        for u in range(UNROLL):
+            row = group * UNROLL + u
+            late = range(slot_count - LATE, slot_count)
+            total = slot_pairs(table, row, late, held, blocks, held.shape[0] - 1)
             span = pl.ds(pl.multiple_of(row * size, size), size)
-            y[:, span] = y[:, span] + scale * product
-
-    x[...] = y[...].astype(jnp.bfloat16)
+            value = y_in[:, span] + scale * total
+            y[:, span] = value
+            x[:, span] = value.astype(jnp.bfloat16)
+
+    @pl.loop(0, count)
+    def _(k):
+        code = info[4 * per + 1 + k]
+        row = code >> 11
+        slot = (code >> 6) & 31
+        product = jnp.dot(held[code & 63], blocks[slot, row], preferred_element_type=jnp.float32)
+        span = pl.ds(pl.multiple_of(row * size, size), size)
+        y[:, span] = y[:, span] + scale * product
+
+    @pl.when(count > 0)
+    def _():
+        x[...] = y[...].astype(jnp.bfloat16)
+
     if not last:
         for q in range(4):
             for k in range(per):
-                j = info[1 + q * per + k]
+                j = info[q * per + k]
                 sends[q][k] = x[:, pl.ds(pl.multiple_of(j * size, size), size)]
-    else:
-        own = info[list_at + slot_count * local_blocks]
-        piece = x.shape[1] // 4
-        for k in range(4):
-            at = lax.rem(own + k, 4) * piece
-            sends[k][...] = x[:, pl.ds(pl.multiple_of(at, piece), piece)]
 
 
 vmem = pl.BlockSpec(memory_space=pltpu.VMEM)
@@ -141,50 +162,49 @@
     )(*args)
 
 
-def remote_part(scale, last, info, halos, y, blocks):
-    size = blocks.shape[2]
-    width, local_rows = y.shape
+def remote_part(scale, last, info, table, halos, y, x, blocks):
+    _, local_blocks, size, _ = blocks.shape
+    width = y.shape[0]
     per = halos[0].shape[0]
-    send = (width, local_rows // 4) if last else (per, width, size)
+    sends = () if last else (jax.ShapeDtypeStruct((per, width, size), jnp.bfloat16),) * 4
     return pl.pallas_call(
         functools.partial(remote_kernel, scale, last),
         out_shape=(
             jax.ShapeDtypeStruct(y.shape, jnp.float32),
             jax.ShapeDtypeStruct(y.shape, jnp.bfloat16),
         )
-        + (jax.ShapeDtypeStruct(send, jnp.bfloat16),) * 4,
-        in_specs=[smem] + [vmem] * 6,
-        out_specs=(vmem,) * 6,
-        scratch_shapes=[pltpu.VMEM((4 * per + 1, width, size), jnp.bfloat16)],
+        + sends,
+        in_specs=[smem] * 2 + [vmem] * 7,
+        out_specs=(vmem,) * (2 + len(sends)),
+        scratch_shapes=[pltpu.VMEM((local_blocks + 1 + 4 * per, width, size), jnp.bfloat16)],
         compiler_params=grant,
         name="remote_part",
-    )(info, *halos, y, blocks)
-
-
-def gram_kernel(*refs):
-    pieces, strips = refs[:4], refs[4:]
-    stack = jnp.concatenate([p[...] for p in pieces], axis=0)
-    gram = lax.dot_general(
-        stack, stack, (((1,), (1,)), ((), ())), preferred_element_type=jnp.float32
-    )
-    width = pieces[0].shape[0]
-    for k in range(4):
-        at = (-k) % 4 * width
-        rows = gram[at : at + width]
-        order = [(j - k) % 4 * width for j in range(4)]
-        strips[k][...] = jnp.concatenate([rows[:, o : o + width] for o in order], axis=1)
-
-
-def gram_strips(pieces):
-    width = pieces[0].shape[0]
+    )(info, table, *halos, y, x, blocks)
+
+
+def gram_kernel(own, one, *refs):
+    halves, strip = refs[:-1], refs[-1]
+    f32 = jnp.float32
+    nt = (((1,), (1,)), ((), ()))
+    width = own.shape[0]
+    other = jnp.concatenate([own[...], one[...]], axis=0)
+    strip[:width, :] = lax.dot_general(own[...], other, nt, preferred_element_type=f32)
+    two = jnp.concatenate([h[...] for h in halves], axis=1)
+    block = lax.dot_general(own[...], two, nt, preferred_element_type=f32)
+    half = width // 2
+    strip[width:, :] = jnp.concatenate([block[:half], block[half:]], axis=1)
+
+
+def gram_strip(own, one, halves):
+    width = own.shape[0]
     return pl.pallas_call(
         gram_kernel,
-        out_shape=(jax.ShapeDtypeStruct((width, 4 * width), jnp.float32),) * 4,
+        out_shape=jax.ShapeDtypeStruct((width + width // 2, 2 * width), jnp.float32),
         in_specs=[vmem] * 4,
-        out_specs=(vmem,) * 4,
+        out_specs=vmem,
         compiler_params=grant,
-        name="gram_strips",
-    )(*pieces)
+        name="gram_strip",
+    )(own, one, *halves)
 
 
 def three_parts(value):
@@ -196,13 +216,34 @@
 
 
 def solve_kernel(root, own_ref, *refs):
-    strips, finals, (basis, factor, work, inverse) = refs[:4], refs[4:8], refs[8:]
+    strips, finals, (basis, factor, work, inverse) = refs[:4], refs[4:9], refs[9:]
     own = own_ref[0]
-    width, n = strips[0].shape
+    n = work.shape[0]
+    width = n // 4
+    half = width // 2
     f32 = jnp.float32
     for k in range(4):
-        at = pl.multiple_of(lax.rem(own + 4 - k, 4) * width, width)
-        work[pl.ds(at, width), :] = strips[k][...]
+        row = lax.rem(own + 4 - k, 4)
+        tail = strips[k][width:, :]
+        blocks = [
+            strips[k][:width, :width],
+            strips[k][:width, width:],
+            jnp.concatenate([tail[:, :width], tail[:, width:]], axis=0),
+        ]
+        for part in range(4):
+
+            @pl.when(row == part)
+            def _(part=part, blocks=blocks):
+                at = slice(part * width, (part + 1) * width)
+                work[at, at] = blocks[0]
+                for j in (1, 2):
+                    col = (part - j) % 4
+                    to = slice(col * width, (col + 1) * width)
+                    if col > part:
+                        work[at, to] = blocks[j]
+                    elif j == 1:
+                        work[to, at] = blocks[j].T
+
     row_ids = lax.broadcasted_iota(jnp.int32, (PANEL, 128), 0)
     lane_ids = lax.broadcasted_iota(jnp.int32, (PANEL, 128), 1)
     for r0 in range(0, n, PANEL):
@@ -255,24 +296,25 @@
         ordered.append(block)
     ordered = jnp.concatenate(ordered, axis=1)
     left = jnp.concatenate(three_parts(ordered), axis=0)
-    wide = 512
-    for c in range(0, basis.shape[1], wide):
-        right = jnp.concatenate([f[:, c : c + wide] for f in finals], axis=0)
+    span = basis.shape[1] // 2
+    for c in range(2):
+        at = slice(c * span, (c + 1) * span)
+        right = jnp.concatenate(
+            [finals[0][:, at], finals[1][:, at], finals[3 + c][...], finals[2][:, at]], axis=0
+        )
         product = jnp.dot(left, right, preferred_element_type=f32)
-        basis[:, c : c + wide] = (
-            product[:width] + product[width : 2 * width] + product[2 * width :]
-        )
+        basis[:, at] = product[:width] + product[width : 2 * width] + product[2 * width :]
 
 
 def solve(root, own, strips, finals):
-    n = strips[0].shape[1]
+    n = 2 * strips[0].shape[1]
     return pl.pallas_call(
         functools.partial(solve_kernel, root),
         out_shape=(
             jax.ShapeDtypeStruct(finals[0].shape, jnp.float32),
             jax.ShapeDtypeStruct((n, n), jnp.float32),
         ),
-        in_specs=[smem] + [vmem] * 8,
+        in_specs=[smem] + [vmem] * 9,
         out_specs=(vmem,) * 2,
         scratch_shapes=[pltpu.VMEM((n, n), jnp.float32)] * 2,
         compiler_params=grant,
@@ -303,45 +345,32 @@
     col_index = lax.axis_index("col").astype(jnp.int32)
     width, local_rows = subspace.shape
     slot_count, local_blocks, size, _ = blocks.shape
-    pos, info = plan(cols, row_index, row_count, local_blocks)
-    info = jnp.concatenate([info, col_index[None]])
+    table, info = plan(cols, row_index, row_count, local_blocks)
     onsite = onsite[None, :]
     shaped = subspace.reshape(width, local_blocks, size)
-    chosen = jnp.take(shaped, info[1 : 1 + 4 * HALO], axis=1)
+    chosen = jnp.take(shaped, info[: 4 * HALO], axis=1)
     send = chosen.transpose(1, 0, 2).reshape(4, HALO, width, size)
     previous, before, x = None, subspace, subspace
     for step in range(FILTER):
         scale = filter_scale if step == 0 else 2.0 * filter_scale
         last = step == FILTER - 1
         halos = [shift(send[q], "row", -d) for q, d in enumerate(offsets(row_count))]
-        partial = local_part(scale, pos, blocks, x, onsite, previous)
-        y, x, *send = remote_part(scale, last, info, halos, partial, blocks)
+        partial = local_part(scale, table, blocks, x, onsite, previous)
+        y, x, *send = remote_part(scale, last, info, table, halos, partial, x, blocks)
         previous, before = before, y
     final = x
-    pieces = [send[0]] + [shift(send[k], "col", k) for k in (1, 2, 3)]
-    strips = gram_strips(pieces)
-    finals = [final] + [shift(final, "col", k) for k in (1, 2, 3)]
-    strip = strips[0]
-    for k in (1, 2, 3):
-        strip = strip + shift(strips[k], "col", k)
-    low = row_count // 4
-    strip = xor_sum(strip, "row", list(range(1, low)))
-    strip = xor_sum(strip, "row", [low * m for m in (1, 2, 3)])
-    blocks_of = [strip[:, j * width : (j + 1) * width] for j in range(4)]
-    ordered = []
-    for b in range(4):
-        j = (col_index - b) % 4
-        ordered.append(
-            jnp.where(
-                j < 2,
-                jnp.where(j == 0, blocks_of[0], blocks_of[1]),
-                jnp.where(j == 2, blocks_of[2], blocks_of[3]),
-            )
-        )
-    strip = jnp.concatenate(ordered, axis=1)
+    half = local_rows // 2
+    one = shift(final, "col", 1)
+    three = shift(final, "col", -1)
+    two = [shift(one[:, :half], "col", 1), shift(three[:, half:], "col", -1)]
+    strip = gram_strip(final, one, two)
+    x_bit = row_count // 4
+    strip = xor_sum(strip, "row", [1])
+    strip = xor_sum(strip, "row", [2, 4, 6])
+    strip = xor_sum(strip, "row", [x_bit, 2 * x_bit, 3 * x_bit])
     strips = [strip] + [shift(strip, "col", k) for k in (1, 2, 3)]
     root = math.sqrt(row_count * local_rows)
-    return solve(root, col_index[None], strips, finals)
+    return solve(root, col_index[None], strips, [final, one, three] + two)
 
 
 def solution(mesh):

time: 157 us -> 140 us (0.89)
  starting transfers between devices: 61.4 us -> 44 us
  Pallas kernels: 45.4 us -> 41.9 us
  waiting for transfers between devices: 33.1 us -> 36 us
    ppermute x28 -> x23, starting transfers between devices: 47.8 us -> 34.8 us  [shift(): return lax.ppermute(value, axis, [(i, (i + by) % n) for i in range(n)])]
    pallas_call x4, Pallas kernels: 23.3 us -> 18.6 us  [local_part(): pl.pallas_call(functools.partial(local_kernel, scale, prev is None), out_...]
    ppermute x10 -> x7, starting transfers between devices: 13.6 us -> 9.22 us  [swap(): return lax.ppermute(value, axis, [(i, i ^ mask) for i in range(n)])]
    ppermute x10 -> x7, waiting for transfers between devices: 4.33 us -> 7.59 us  [swap(): return lax.ppermute(value, axis, [(i, i ^ mask) for i in range(n)])]
    unnamed x11 -> x9, local copies, waits for them, and re-layouts: 9.2 us -> 8.08 us
    ppermute x28 -> x23, waiting for transfers between devices: 28.8 us -> 28.4 us  [shift(): return lax.ppermute(value, axis, [(i, (i + by) % n) for i in range(n)])]
  transfers between devices with their start and end apart: 38 -> 30, of which waited for: 15 -> 16; matrix products, arithmetic and copies ran while one was open for 2% -> 4% of each run, Pallas kernels for 15% -> 13%
where the time goes in v3:
time: 140 us; the launch traced here: 139 us
  starting transfers between devices  44 us (31%)
  Pallas kernels  41.9 us (30%)
  waiting for transfers between devices  36 us (26%)
  local copies, waits for them, and re-layouts  11.7 us (8%)
  other arithmetic  4.94 us (4%)
    ppermute x23, starting transfers between devices, shift(): return lax.ppermute(value, axis, [(i, (i + by) % n) for i in range(n)])  34.8 us
    ppermute x23, waiting for transfers between devices, shift(): return lax.ppermute(value, axis, [(i, (i + by) % n) for i in range(n)])  28.4 us
    pallas_call x4, Pallas kernels, local_part(): pl.pallas_call(functools.partial(local_kernel, scale, prev is None), out_...  18.6 us
    pallas_call x4, Pallas kernels, remote_part(): pl.pallas_call(functools.partial(remote_kernel, scale, last), out_shape=(...  12.7 us
    pallas_call x1, Pallas kernels, solve(): pl.pallas_call(functools.partial(solve_kernel, root), out_shape=(jax.Shap...  9.88 us
    ppermute x7, starting transfers between devices, swap(): return lax.ppermute(value, axis, [(i, i ^ mask) for i in range(n)])  9.22 us
    unnamed x9, local copies, waits for them, and re-layouts  8.08 us
    ppermute x7, waiting for transfers between devices, swap(): return lax.ppermute(value, axis, [(i, i ^ mask) for i in range(n)])  7.59 us
  transfers between devices with their start and end apart: 30, of which 16 were waited for; matrix products, arithmetic and copies ran while one was open for 4% of the time, Pallas kernels for 13%

profile of v3, /device:TPU:0, one launch (start us, length us, event | category | flops | bytes accessed | tf_op | source)
XLA Modules:
  0.0 139.5 jit_solution(6303252408243335289)
XLA Ops:
  1.4 1.1 copy.20
  5.1 3.2 %collective-permute-start.3 = (bf16[4,64,128]{2,1,0:T(8,128)(2,1)S(1)}, bf16[4,64,128]{2,1,0:T(8,128)(2,1)S(1)}, u32[]{:S(2)}, u32[]{:S(2)}) collective-permute-start(bf16[4,64,128]{2,1,0:T(8,128)(2,1)S(1)} %get-tuple-element.44), channel_id=1, source_target_pairs={{0,64},{4,68},{8,72},{12,76},{16,80},{20,84},{24,88},{28,92},{32,9... | collective-permute-start | bytes 196616 | tf_op jit(solution)/shard_map/ppermute | solution.py:327
  8.3 4.6 %collective-permute-start.2 = (bf16[4,64,128]{2,1,0:T(8,128)(2,1)S(1)}, bf16[4,64,128]{2,1,0:T(8,128)(2,1)S(1)}, u32[]{:S(2)}, u32[]{:S(2)}) collective-permute-start(bf16[4,64,128]{2,1,0:T(8,128)(2,1)S(1)} %get-tuple-element.45), channel_id=1, source_target_pairs={{0,120},{4,124},{8,0},{12,4},{16,8},{20,12},{24,16},{28,20},{32,24... | collective-permute-start | bytes 196616 | tf_op jit(solution)/shard_map/ppermute | solution.py:327
  12.9 5.1 %collective-permute-start = (bf16[4,64,128]{2,1,0:T(8,128)(2,1)S(1)}, bf16[4,64,128]{2,1,0:T(8,128)(2,1)S(1)}, u32[]{:S(2)}, u32[]{:S(2)}) collective-permute-start(bf16[4,64,128]{2,1,0:T(8,128)(2,1)S(1)} %get-tuple-element.47), channel_id=1, source_target_pairs={{0,124},{4,0},{8,4},{12,8},{16,12},{20,16},{24,20},{28,24},{32,28}... | collective-permute-start | bytes 196616 | tf_op jit(solution)/shard_map/ppermute | solution.py:327
  22.6 7.0 %copy-done = bf16[20,32,128,128]{3,2,1,0:T(8,128)(2,1)S(1)} copy-done((bf16[20,32,128,128]{3,2,1,0:T(8,128)(2,1)S(1)}, bf16[20,32,128,128]{3,2,1,0:T(8,128)(2,1)}, u32[]{:S(2)}) %copy-start) | copy-done | bytes 20971544
  29.6 4.6 %local_part.4.refs_4_ = f32[64,4096]{1,0:T(8,128)S(1)} custom-call(s32[640]{0:T(1024)S(1)} %reduce_sum.53.table, bf16[20,32,128,128]{3,2,1,0:T(8,128)(2,1)S(1)} %copy-done, bf16[64,4096]{1,0:T(8,128)(2,1)S(1)} %copy-done.1, f32[1,4096]{1,0:T(1,128)S(1)} %bitcast.14), custom_call_target="tpu_custom_call" | custom-call | tf_op jit(solution)/shard_map/local_part/pallas_call | solution.py:154
  34.9 2.7 %remote_part.4 = (f32[64,4096]{1,0:T(8,128)S(1)}, bf16[64,4096]{1,0:T(8,128)(2,1)S(1)}, bf16[4,64,128]{2,1,0:T(8,128)(2,1)S(1)}, bf16[4,64,128]{2,1,0:T(8,128)(2...) custom-call(s32[657]{0:T(1024)S(1)} %pad_add_fusion.info, s32[640]{0:T(1024)S(1)} %reduce_sum.53.table, ...), custom_call_target="tpu_custom_call" | custom-call | tf_op jit(solution)/shard_map/remote_part/pallas_call | solution.py:170
  38.6 4.7 %local_part.5.refs_4_ = f32[64,4096]{1,0:T(8,128)S(1)} custom-call(s32[640]{0:T(1024)S(1)} %reduce_sum.53.table, bf16[20,32,128,128]{3,2,1,0:T(8,128)(2,1)S(1)} %copy-done, bf16[64,4096]{1,0:T(8,128)(2,1)S(1)} %get-tuple-element.24.x.refs_5_, f32[1,4096]{1,0:T(1,128)S(1)} %bitcast.15, bf16[64,4096]{1,0:T(8,128)(2,1)S(1)} %copy-done.1), custom_call_target="tpu_custom_call" | custom-call | tf_op jit(solution)/shard_map/local_part/pallas_call | solution.py:154
  43.3 1.9 %collective-permute-done.5.refs_1_ = bf16[4,64,128]{2,1,0:T(8,128)(2,1)S(1)} collective-permute-done((bf16[4,64,128]{2,1,0:T(8,128)(2,1)S(1)}, bf16[4,64,128]{2,1,0:T(8,128)(2,1)S(1)}, u32[]{:S(2)}, u32[]{:S(2)}) %collective-permute-start.5) | collective-permute-done | bytes 65568 | tf_op jit(solution)/shard_map/ppermute | solution.py:327
  45.2 2.7 %remote_part.5 = (f32[64,4096]{1,0:T(8,128)S(1)}, bf16[64,4096]{1,0:T(8,128)(2,1)S(1)}, bf16[4,64,128]{2,1,0:T(8,128)(2,1)S(1)}, bf16[4,64,128]{2,1,0:T(8,128)(2...) custom-call(s32[657]{0:T(1024)S(1)} %pad_add_fusion.info, s32[640]{0:T(1024)S(1)} %reduce_sum.53.table, ...), custom_call_target="tpu_custom_call" | custom-call | tf_op jit(solution)/shard_map/remote_part/pallas_call | solution.py:170
  48.0 4.2 %collective-permute-start.8 = (bf16[4,64,128]{2,1,0:T(8,128)(2,1)S(1)}, bf16[4,64,128]{2,1,0:T(8,128)(2,1)S(1)}, u32[]{:S(2)}, u32[]{:S(2)}) collective-permute-start(bf16[4,64,128]{2,1,0:T(8,128)(2,1)S(1)} %get-tuple-element.25), channel_id=1, source_target_pairs={{0,124},{4,0},{8,4},{12,8},{16,12},{20,16},{24,20},{28,24},{32,28}... | collective-permute-start | bytes 196616 | tf_op jit(solution)/shard_map/ppermute | solution.py:327
  52.6 1.3 collective-permute-start.11
  53.9 4.7 %local_part.6.refs_4_ = f32[64,4096]{1,0:T(8,128)S(1)} custom-call(s32[640]{0:T(1024)S(1)} %reduce_sum.53.table, bf16[20,32,128,128]{3,2,1,0:T(8,128)(2,1)S(1)} %copy-done, bf16[64,4096]{1,0:T(8,128)(2,1)S(1)} %get-tuple-element.29.x.refs_5_, f32[1,4096]{1,0:T(1,128)S(1)} %bitcast.16, f32[64,4096]{1,0:T(8,128)S(1)} %get-tuple-element.30.refs_0_), custom_call_target="tpu_custom_call" | custom-call | tf_op jit(solution)/shard_map/local_part/pallas_call | solution.py:154
  59.1 3.7 %remote_part.6 = (f32[64,4096]{1,0:T(8,128)}, bf16[64,4096]{1,0:T(8,128)(2,1)S(1)}, bf16[4,64,128]{2,1,0:T(8,128)(2,1)S(1)}, bf16[4,64,128]{2,1,0:T(8,128)(2,1)S...) custom-call(s32[657]{0:T(1024)S(1)} %pad_add_fusion.info, s32[640]{0:T(1024)S(1)} %reduce_sum.53.table, ...), custom_call_target="tpu_custom_call" | custom-call | tf_op jit(solution)/shard_map/remote_part/pallas_call | solution.py:170
  62.8 4.5 %collective-permute-start.12 = (bf16[4,64,128]{2,1,0:T(8,128)(2,1)S(1)}, bf16[4,64,128]{2,1,0:T(8,128)(2,1)S(1)}, u32[]{:S(2)}, u32[]{:S(2)}) collective-permute-start(bf16[4,64,128]{2,1,0:T(8,128)(2,1)S(1)} %get-tuple-element.31), channel_id=1, source_target_pairs={{0,124},{4,0},{8,4},{12,8},{16,12},{20,16},{24,20},{28,24},{32,28}... | collective-permute-start | bytes 196616 | tf_op jit(solution)/shard_map/ppermute | solution.py:327
  67.7 1.2 collective-permute-start.15
  68.9 4.7 %local_part.7.refs_4_ = f32[64,4096]{1,0:T(8,128)S(1)} custom-call(s32[640]{0:T(1024)S(1)} %reduce_sum.53.table, bf16[20,32,128,128]{3,2,1,0:T(8,128)(2,1)S(1)} %copy-done, bf16[64,4096]{1,0:T(8,128)(2,1)S(1)} %get-tuple-element.35.x.refs_5_, f32[1,4096]{1,0:T(1,128)S(1)} %bitcast.17, f32[64,4096]{1,0:T(8,128)S(1)} %get-tuple-element.36.refs_0_), custom_call_target="tpu_custom_call" | custom-call | tf_op jit(solution)/shard_map/local_part/pallas_call | solution.py:154
  74.3 3.6 %remote_part.7 = (f32[64,4096]{1,0:T(8,128)}, bf16[64,4096]{1,0:T(8,128)(2,1)S(1)}) custom-call(s32[657]{0:T(1024)S(1)} %pad_add_fusion.info, s32[640]{0:T(1024)S(1)} %reduce_sum.53.table, bf16[4,64,128]{2,1,0:T(8,128)(2,1)S(1)} %collective-permute-done.12.refs_0_, bf16[4,64,128]{2,1,0:T(8,128)(2,1)S(1)} %collective-permute-done.13.refs_1_, ...), custom_call_target="tpu_custom_call" | custom-call | tf_op jit(solution)/shard_map/remote_part/pallas_call | solution.py:170
  77.9 3.0 %collective-permute-start.18 = (bf16[64,4096]{1,0:T(8,128)(2,1)S(1)}, bf16[64,4096]{1,0:T(8,128)(2,1)S(1)}, u32[]{:S(2)}, u32[]{:S(2)}) collective-permute-start(bf16[64,4096]{1,0:T(8,128)(2,1)S(1)} %get-tuple-element.37.own.refs_4_), channel_id=1, source_target_pairs={{0,3},{1,0},{2,1},{3,2},{4,7},{5,4},{6,5},{7,6},{8,11},{9,8},{10,9... | collective-permute-start | bytes 1572872 | tf_op jit(solution)/shard_map/ppermute | solution.py:327
  80.9 10.3 %collective-permute-done.18.refs_6_ = bf16[64,4096]{1,0:T(8,128)(2,1)S(1)} collective-permute-done((bf16[64,4096]{1,0:T(8,128)(2,1)S(1)}, bf16[64,4096]{1,0:T(8,128)(2,1)S(1)}, u32[]{:S(2)}, u32[]{:S(2)}) %collective-permute-start.18) | collective-permute-done | bytes 524320 | tf_op jit(solution)/shard_map/ppermute | solution.py:327
  91.3 3.8 %collective-permute-start.19 = (bf16[64,2048]{1,0:T(8,128)(2,1)S(1)}, bf16[64,2048]{1,0:T(8,128)(2,1)S(1)}, u32[]{:S(2)}, u32[]{:S(2)}) collective-permute-start(bf16[64,2048]{1,0:T(8,128)(2,1)S(1)} %slice.51), channel_id=1, source_target_pairs={{0,3},{1,0},{2,1},{3,2},{4,7},{5,4},{6,5},{7,6},{8,11},{9,8},{10,9... | collective-permute-start | bytes 786440 | tf_op jit(solution)/shard_map/ppermute | solution.py:327
  95.3 5.6 %collective-permute-done.19.refs_1_.refs_8_ = bf16[64,2048]{1,0:T(8,128)(2,1)S(1)} collective-permute-done((bf16[64,2048]{1,0:T(8,128)(2,1)S(1)}, bf16[64,2048]{1,0:T(8,128)(2,1)S(1)}, u32[]{:S(2)}, u32[]{:S(2)}) %collective-permute-start.19) | collective-permute-done | bytes 262176 | tf_op jit(solution)/shard_map/ppermute | solution.py:327
  100.9 4.3 %collective-permute-done.17.refs_0_.refs_7_ = bf16[64,2048]{1,0:T(8,128)(2,1)S(1)} collective-permute-done((bf16[64,2048]{1,0:T(8,128)(2,1)S(1)}, bf16[64,2048]{1,0:T(8,128)(2,1)S(1)}, u32[]{:S(2)}, u32[]{:S(2)}) %collective-permute-start.17) | collective-permute-done | bytes 262176 | tf_op jit(solution)/shard_map/ppermute | solution.py:327
  107.2 4.6 %collective-permute-start.22 = (f32[96,128]{1,0:T(8,128)S(1)}, f32[96,128]{1,0:T(8,128)S(1)}, u32[]{:S(2)}, u32[]{:S(2)}) collective-permute-start(f32[96,128]{1,0:T(8,128)S(1)} %add.220), channel_id=1, source_target_pairs={{0,16},{4,20},{8,24},{12,28},{16,0},{20,4},{24,8},{28,12},{32,48},... | collective-permute-start | bytes 147464 | tf_op jit(solution)/shard_map/ppermute | solution.py:332
  112.5 1.4 %collective-permute-done.22 = f32[96,128]{1,0:T(8,128)S(1)} collective-permute-done((f32[96,128]{1,0:T(8,128)S(1)}, f32[96,128]{1,0:T(8,128)S(1)}, u32[]{:S(2)}, u32[]{:S(2)}) %collective-permute-start.22) | collective-permute-done | bytes 49184 | tf_op jit(solution)/shard_map/ppermute | solution.py:332
  113.9 2.0 %collective-permute-done.21 = f32[96,128]{1,0:T(8,128)S(1)} collective-permute-done((f32[96,128]{1,0:T(8,128)S(1)}, f32[96,128]{1,0:T(8,128)S(1)}, u32[]{:S(2)}, u32[]{:S(2)}) %collective-permute-start.21) | collective-permute-done | bytes 49184 | tf_op jit(solution)/shard_map/ppermute | solution.py:332
  116.2 4.0 %collective-permute-start.24 = (f32[96,128]{1,0:T(8,128)S(1)}, f32[96,128]{1,0:T(8,128)S(1)}, u32[]{:S(2)}, u32[]{:S(2)}) collective-permute-start(f32[96,128]{1,0:T(8,128)S(1)} %add_add_fusion.1), channel_id=1, source_target_pairs={{0,32},{4,36},{8,40},{12,44},{16,48},{20,52},{24,56},{28,60},{32,0... | collective-permute-start | bytes 147464 | tf_op jit(solution)/shard_map/ppermute | solution.py:332
  120.2 1.7 %collective-permute-done.26 = f32[96,128]{1,0:T(8,128)S(1)} collective-permute-done((f32[96,128]{1,0:T(8,128)S(1)}, f32[96,128]{1,0:T(8,128)S(1)}, u32[]{:S(2)}, u32[]{:S(2)}) %collective-permute-start.26) | collective-permute-done | bytes 49184 | tf_op jit(solution)/shard_map/ppermute | solution.py:332
  122.8 1.1 collective-permute-start.28
  124.9 2.1 %collective-permute-done.29.refs_3_ = f32[96,128]{1,0:T(8,128)S(1)} collective-permute-done((f32[96,128]{1,0:T(8,128)S(1)}, f32[96,128]{1,0:T(8,128)S(1)}, u32[]{:S(2)}, u32[]{:S(2)}) %collective-permute-start.29) | collective-permute-done | bytes 49184 | tf_op jit(solution)/shard_map/ppermute | solution.py:327
  126.9 1.6 %collective-permute-done.28.refs_2_ = f32[96,128]{1,0:T(8,128)S(1)} collective-permute-done((f32[96,128]{1,0:T(8,128)S(1)}, f32[96,128]{1,0:T(8,128)S(1)}, u32[]{:S(2)}, u32[]{:S(2)}) %collective-permute-start.28) | collective-permute-done | bytes 49184 | tf_op jit(solution)/shard_map/ppermute | solution.py:327
  129.6 9.9 %solve.1 = (f32[64,4096]{1,0:T(8,128)}, f32[256,256]{1,0:T(8,128)}) custom-call(s32[1]{0:T(128)} %bitcast.own_ref, f32[96,128]{1,0:T(8,128)S(1)} %add_add_fusion.refs_0_, f32[96,128]{1,0:T(8,128)S(1)} %collective-permute-done.27.refs_1_, f32[96,128]{1,0:T(8,128)S(1)} %collective-permute-done.28.refs_2_, f32[96,128]{1,0:T(8,128)S(1)} %collective-permute-done.29.refs_3_, ...), custom_call_target="tpu_custom_call" | custom-call | tf_op jit(solution)/shard_map/solve/pallas_call | solution.py:311
  (120 shorter events, 17.7 us)
Async XLA Ops:
  2.5 15.7 %copy-start.3 = (s32[4]{0:T(128)S(1)}, s32[4]{0:T(128)}, u32[]{:S(2)}) copy-start(s32[4]{0:T(128)} %constant.118.clone) | copy-start | bytes 52
  4.2 18.4 %copy-start.2 = (f32[4096]{0:T(1024)S(1)}, f32[4096]{0:T(1024)}, u32[]{:S(2)}) copy-start(f32[4096]{0:T(1024)} %param.6) | copy-start | bytes 49156
  5.1 29.9 %collective-permute-start.3 = (bf16[4,64,128]{2,1,0:T(8,128)(2,1)S(1)}, bf16[4,64,128]{2,1,0:T(8,128)(2,1)S(1)}, u32[]{:S(2)}, u32[]{:S(2)}) collective-permute-start(bf16[4,64,128]{2,1,0:T(8,128)(2,1)S(1)} %get-tuple-element.44), channel_id=1, source_target_pairs={{0,64},{4,68},{8,72},{12,76},{16,80},{20,84},{24,88},{28,92},{32,9... | collective-permute-start | bytes 196616 | tf_op jit(solution)/shard_map/ppermute | solution.py:327
  8.3 26.7 %collective-permute-start.2 = (bf16[4,64,128]{2,1,0:T(8,128)(2,1)S(1)}, bf16[4,64,128]{2,1,0:T(8,128)(2,1)S(1)}, u32[]{:S(2)}, u32[]{:S(2)}) collective-permute-start(bf16[4,64,128]{2,1,0:T(8,128)(2,1)S(1)} %get-tuple-element.45), channel_id=1, source_target_pairs={{0,120},{4,124},{8,0},{12,4},{16,8},{20,12},{24,16},{28,20},{32,24... | collective-permute-start | bytes 196616 | tf_op jit(solution)/shard_map/ppermute | solution.py:327
  12.9 22.1 %collective-permute-start.1 = (bf16[4,64,128]{2,1,0:T(8,128)(2,1)S(1)}, bf16[4,64,128]{2,1,0:T(8,128)(2,1)S(1)}, u32[]{:S(2)}, u32[]{:S(2)}) collective-permute-start(bf16[4,64,128]{2,1,0:T(8,128)(2,1)S(1)} %get-tuple-element.46), channel_id=1, source_target_pairs={{0,4},{4,8},{8,12},{12,16},{16,20},{20,24},{24,28},{28,32},{32,36}... | collective-permute-start | bytes 196616 | tf_op jit(solution)/shard_map/ppermute | solution.py:327
  12.9 22.1 %collective-permute-start = (bf16[4,64,128]{2,1,0:T(8,128)(2,1)S(1)}, bf16[4,64,128]{2,1,0:T(8,128)(2,1)S(1)}, u32[]{:S(2)}, u32[]{:S(2)}) collective-permute-start(bf16[4,64,128]{2,1,0:T(8,128)(2,1)S(1)} %get-tuple-element.47), channel_id=1, source_target_pairs={{0,124},{4,0},{8,4},{12,8},{16,12},{20,16},{24,20},{28,24},{32,28}... | collective-permute-start | bytes 196616 | tf_op jit(solution)/shard_map/ppermute | solution.py:327
  37.7 5.6 %collective-permute-start.4 = (bf16[4,64,128]{2,1,0:T(8,128)(2,1)S(1)}, bf16[4,64,128]{2,1,0:T(8,128)(2,1)S(1)}, u32[]{:S(2)}, u32[]{:S(2)}) collective-permute-start(bf16[4,64,128]{2,1,0:T(8,128)(2,1)S(1)} %get-tuple-element.20), channel_id=1, source_target_pairs={{0,124},{4,0},{8,4},{12,8},{16,12},{20,16},{24,20},{28,24},{32,28}... | collective-permute-start | bytes 196616 | tf_op jit(solution)/shard_map/ppermute | solution.py:327
  37.8 7.5 %collective-permute-start.5 = (bf16[4,64,128]{2,1,0:T(8,128)(2,1)S(1)}, bf16[4,64,128]{2,1,0:T(8,128)(2,1)S(1)}, u32[]{:S(2)}, u32[]{:S(2)}) collective-permute-start(bf16[4,64,128]{2,1,0:T(8,128)(2,1)S(1)} %get-tuple-element.21), channel_id=1, source_target_pairs={{0,4},{4,8},{8,12},{12,16},{16,20},{20,24},{24,28},{28,32},{32,36}... | collective-permute-start | bytes 196616 | tf_op jit(solution)/shard_map/ppermute | solution.py:327
  38.2 7.0 %collective-permute-start.6 = (bf16[4,64,128]{2,1,0:T(8,128)(2,1)S(1)}, bf16[4,64,128]{2,1,0:T(8,128)(2,1)S(1)}, u32[]{:S(2)}, u32[]{:S(2)}) collective-permute-start(bf16[4,64,128]{2,1,0:T(8,128)(2,1)S(1)} %get-tuple-element.22), channel_id=1, source_target_pairs={{0,120},{4,124},{8,0},{12,4},{16,8},{20,12},{24,16},{28,20},{32,24... | collective-permute-start | bytes 196616 | tf_op jit(solution)/shard_map/ppermute | solution.py:327
  38.2 7.0 %collective-permute-start.7 = (bf16[4,64,128]{2,1,0:T(8,128)(2,1)S(1)}, bf16[4,64,128]{2,1,0:T(8,128)(2,1)S(1)}, u32[]{:S(2)}, u32[]{:S(2)}) collective-permute-start(bf16[4,64,128]{2,1,0:T(8,128)(2,1)S(1)} %get-tuple-element.23), channel_id=1, source_target_pairs={{0,64},{4,68},{8,72},{12,76},{16,80},{20,84},{24,88},{28,92},{32,9... | collective-permute-start | bytes 196616 | tf_op jit(solution)/shard_map/ppermute | solution.py:327
  48.0 10.6 %collective-permute-start.8 = (bf16[4,64,128]{2,1,0:T(8,128)(2,1)S(1)}, bf16[4,64,128]{2,1,0:T(8,128)(2,1)S(1)}, u32[]{:S(2)}, u32[]{:S(2)}) collective-permute-start(bf16[4,64,128]{2,1,0:T(8,128)(2,1)S(1)} %get-tuple-element.25), channel_id=1, source_target_pairs={{0,124},{4,0},{8,4},{12,8},{16,12},{20,16},{24,20},{28,24},{32,28}... | collective-permute-start | bytes 196616 | tf_op jit(solution)/shard_map/ppermute | solution.py:327
  52.1 7.0 %collective-permute-start.9 = (bf16[4,64,128]{2,1,0:T(8,128)(2,1)S(1)}, bf16[4,64,128]{2,1,0:T(8,128)(2,1)S(1)}, u32[]{:S(2)}, u32[]{:S(2)}) collective-permute-start(bf16[4,64,128]{2,1,0:T(8,128)(2,1)S(1)} %get-tuple-element.26), channel_id=1, source_target_pairs={{0,4},{4,8},{8,12},{12,16},{16,20},{20,24},{24,28},{28,32},{32,36}... | collective-permute-start | bytes 196616 | tf_op jit(solution)/shard_map/ppermute | solution.py:327
  52.1 7.0 %collective-permute-start.10 = (bf16[4,64,128]{2,1,0:T(8,128)(2,1)S(1)}, bf16[4,64,128]{2,1,0:T(8,128)(2,1)S(1)}, u32[]{:S(2)}, u32[]{:S(2)}) collective-permute-start(bf16[4,64,128]{2,1,0:T(8,128)(2,1)S(1)} %get-tuple-element.27), channel_id=1, source_target_pairs={{0,120},{4,124},{8,0},{12,4},{16,8},{20,12},{24,16},{28,20},{32,24... | collective-permute-start | bytes 196616 | tf_op jit(solution)/shard_map/ppermute | solution.py:327
  52.6 6.5 %collective-permute-start.11 = (bf16[4,64,128]{2,1,0:T(8,128)(2,1)S(1)}, bf16[4,64,128]{2,1,0:T(8,128)(2,1)S(1)}, u32[]{:S(2)}, u32[]{:S(2)}) collective-permute-start(bf16[4,64,128]{2,1,0:T(8,128)(2,1)S(1)} %get-tuple-element.28), channel_id=1, source_target_pairs={{0,64},{4,68},{8,72},{12,76},{16,80},{20,84},{24,88},{28,92},{32,9... | collective-permute-start | bytes 196616 | tf_op jit(solution)/shard_map/ppermute | solution.py:327
  62.8 10.8 %collective-permute-start.12 = (bf16[4,64,128]{2,1,0:T(8,128)(2,1)S(1)}, bf16[4,64,128]{2,1,0:T(8,128)(2,1)S(1)}, u32[]{:S(2)}, u32[]{:S(2)}) collective-permute-start(bf16[4,64,128]{2,1,0:T(8,128)(2,1)S(1)} %get-tuple-element.31), channel_id=1, source_target_pairs={{0,124},{4,0},{8,4},{12,8},{16,12},{20,16},{24,20},{28,24},{32,28}... | collective-permute-start | bytes 196616 | tf_op jit(solution)/shard_map/ppermute | solution.py:327
  67.3 7.0 %collective-permute-start.13 = (bf16[4,64,128]{2,1,0:T(8,128)(2,1)S(1)}, bf16[4,64,128]{2,1,0:T(8,128)(2,1)S(1)}, u32[]{:S(2)}, u32[]{:S(2)}) collective-permute-start(bf16[4,64,128]{2,1,0:T(8,128)(2,1)S(1)} %get-tuple-element.32), channel_id=1, source_target_pairs={{0,4},{4,8},{8,12},{12,16},{16,20},{20,24},{24,28},{28,32},{32,36}... | collective-permute-start | bytes 196616 | tf_op jit(solution)/shard_map/ppermute | solution.py:327
  67.3 7.0 %collective-permute-start.14 = (bf16[4,64,128]{2,1,0:T(8,128)(2,1)S(1)}, bf16[4,64,128]{2,1,0:T(8,128)(2,1)S(1)}, u32[]{:S(2)}, u32[]{:S(2)}) collective-permute-start(bf16[4,64,128]{2,1,0:T(8,128)(2,1)S(1)} %get-tuple-element.33), channel_id=1, source_target_pairs={{0,120},{4,124},{8,0},{12,4},{16,8},{20,12},{24,16},{28,20},{32,24... | collective-permute-start | bytes 196616 | tf_op jit(solution)/shard_map/ppermute | solution.py:327
  67.7 6.6 %collective-permute-start.15 = (bf16[4,64,128]{2,1,0:T(8,128)(2,1)S(1)}, bf16[4,64,128]{2,1,0:T(8,128)(2,1)S(1)}, u32[]{:S(2)}, u32[]{:S(2)}) collective-permute-start(bf16[4,64,128]{2,1,0:T(8,128)(2,1)S(1)} %get-tuple-element.34), channel_id=1, source_target_pairs={{0,64},{4,68},{8,72},{12,76},{16,80},{20,84},{24,88},{28,92},{32,9... | collective-permute-start | bytes 196616 | tf_op jit(solution)/shard_map/ppermute | solution.py:327
  77.9 13.4 %collective-permute-start.18 = (bf16[64,4096]{1,0:T(8,128)(2,1)S(1)}, bf16[64,4096]{1,0:T(8,128)(2,1)S(1)}, u32[]{:S(2)}, u32[]{:S(2)}) collective-permute-start(bf16[64,4096]{1,0:T(8,128)(2,1)S(1)} %get-tuple-element.37.own.refs_4_), channel_id=1, source_target_pairs={{0,3},{1,0},{2,1},{3,2},{4,7},{5,4},{6,5},{7,6},{8,11},{9,8},{10,9... | collective-permute-start | bytes 1572872 | tf_op jit(solution)/shard_map/ppermute | solution.py:327
  80.9 14.3 %collective-permute-start.16 = (bf16[64,4096]{1,0:T(8,128)(2,1)S(1)}, bf16[64,4096]{1,0:T(8,128)(2,1)S(1)}, u32[]{:S(2)}, u32[]{:S(2)}) collective-permute-start(bf16[64,4096]{1,0:T(8,128)(2,1)S(1)} %get-tuple-element.37.own.refs_4_), channel_id=1, source_target_pairs={{0,1},{1,2},{2,3},{3,0},{4,5},{5,6},{6,7},{7,4},{8,9},{9,10},{10,1... | collective-permute-start | bytes 1572872 | tf_op jit(solution)/shard_map/ppermute | solution.py:327
  91.3 9.6 %collective-permute-start.19 = (bf16[64,2048]{1,0:T(8,128)(2,1)S(1)}, bf16[64,2048]{1,0:T(8,128)(2,1)S(1)}, u32[]{:S(2)}, u32[]{:S(2)}) collective-permute-start(bf16[64,2048]{1,0:T(8,128)(2,1)S(1)} %slice.51), channel_id=1, source_target_pairs={{0,3},{1,0},{2,1},{3,2},{4,7},{5,4},{6,5},{7,6},{8,11},{9,8},{10,9... | collective-permute-start | bytes 786440 | tf_op jit(solution)/shard_map/ppermute | solution.py:327
  95.2 10.0 %collective-permute-start.17 = (bf16[64,2048]{1,0:T(8,128)(2,1)S(1)}, bf16[64,2048]{1,0:T(8,128)(2,1)S(1)}, u32[]{:S(2)}, u32[]{:S(2)}) collective-permute-start(bf16[64,2048]{1,0:T(8,128)(2,1)S(1)} %slice.50), channel_id=1, source_target_pairs={{0,1},{1,2},{2,3},{3,0},{4,5},{5,6},{6,7},{7,4},{8,9},{9,10},{10,1... | collective-permute-start | bytes 786440 | tf_op jit(solution)/shard_map/ppermute | solution.py:327
  105.9 1.3 collective-permute-start.20
  107.2 5.4 %collective-permute-start.23 = (f32[96,128]{1,0:T(8,128)S(1)}, f32[96,128]{1,0:T(8,128)S(1)}, u32[]{:S(2)}, u32[]{:S(2)}) collective-permute-start(f32[96,128]{1,0:T(8,128)S(1)} %add.220), channel_id=1, source_target_pairs={{0,24},{4,28},{8,16},{12,20},{16,8},{20,12},{24,0},{28,4},{32,56},... | collective-permute-start | bytes 147464 | tf_op jit(solution)/shard_map/ppermute | solution.py:332
  107.2 6.7 %collective-permute-start.22 = (f32[96,128]{1,0:T(8,128)S(1)}, f32[96,128]{1,0:T(8,128)S(1)}, u32[]{:S(2)}, u32[]{:S(2)}) collective-permute-start(f32[96,128]{1,0:T(8,128)S(1)} %add.220), channel_id=1, source_target_pairs={{0,16},{4,20},{8,24},{12,28},{16,0},{20,4},{24,8},{28,12},{32,48},... | collective-permute-start | bytes 147464 | tf_op jit(solution)/shard_map/ppermute | solution.py:332
  111.9 4.1 %collective-permute-start.21 = (f32[96,128]{1,0:T(8,128)S(1)}, f32[96,128]{1,0:T(8,128)S(1)}, u32[]{:S(2)}, u32[]{:S(2)}) collective-permute-start(f32[96,128]{1,0:T(8,128)S(1)} %add.220), channel_id=1, source_target_pairs={{0,8},{4,12},{8,0},{12,4},{16,24},{20,28},{24,16},{28,20},{32,40},... | collective-permute-start | bytes 147464 | tf_op jit(solution)/shard_map/ppermute | solution.py:332
  116.0 5.9 %collective-permute-start.26 = (f32[96,128]{1,0:T(8,128)S(1)}, f32[96,128]{1,0:T(8,128)S(1)}, u32[]{:S(2)}, u32[]{:S(2)}) collective-permute-start(f32[96,128]{1,0:T(8,128)S(1)} %add_add_fusion.1), channel_id=1, source_target_pairs={{0,96},{4,100},{8,104},{12,108},{16,112},{20,116},{24,120},{28,124... | collective-permute-start | bytes 147464 | tf_op jit(solution)/shard_map/ppermute | solution.py:332
  116.1 5.8 %collective-permute-start.25 = (f32[96,128]{1,0:T(8,128)S(1)}, f32[96,128]{1,0:T(8,128)S(1)}, u32[]{:S(2)}, u32[]{:S(2)}) collective-permute-start(f32[96,128]{1,0:T(8,128)S(1)} %add_add_fusion.1), channel_id=1, source_target_pairs={{0,64},{4,68},{8,72},{12,76},{16,80},{20,84},{24,88},{28,92},{32,9... | collective-permute-start | bytes 147464 | tf_op jit(solution)/shard_map/ppermute | solution.py:332
  116.2 6.6 %collective-permute-start.24 = (f32[96,128]{1,0:T(8,128)S(1)}, f32[96,128]{1,0:T(8,128)S(1)}, u32[]{:S(2)}, u32[]{:S(2)}) collective-permute-start(f32[96,128]{1,0:T(8,128)S(1)} %add_add_fusion.1), channel_id=1, source_target_pairs={{0,32},{4,36},{8,40},{12,44},{16,48},{20,52},{24,56},{28,60},{32,0... | collective-permute-start | bytes 147464 | tf_op jit(solution)/shard_map/ppermute | solution.py:332
  122.8 4.2 %collective-permute-start.29 = (f32[96,128]{1,0:T(8,128)S(1)}, f32[96,128]{1,0:T(8,128)S(1)}, u32[]{:S(2)}, u32[]{:S(2)}) collective-permute-start(f32[96,128]{1,0:T(8,128)S(1)} %add_add_fusion.refs_0_), channel_id=1, source_target_pairs={{0,3},{1,0},{2,1},{3,2},{4,7},{5,4},{6,5},{7,6},{8,11},{9,8},{10,9... | collective-permute-start | bytes 147464 | tf_op jit(solution)/shard_map/ppermute | solution.py:327
  122.8 5.7 %collective-permute-start.28 = (f32[96,128]{1,0:T(8,128)S(1)}, f32[96,128]{1,0:T(8,128)S(1)}, u32[]{:S(2)}, u32[]{:S(2)}) collective-permute-start(f32[96,128]{1,0:T(8,128)S(1)} %add_add_fusion.refs_0_), channel_id=1, source_target_pairs={{0,2},{1,3},{2,0},{3,1},{4,6},{5,7},{6,4},{7,5},{8,10},{9,11},{10,... | collective-permute-start | bytes 147464 | tf_op jit(solution)/shard_map/ppermute | solution.py:327
  124.0 5.6 %collective-permute-start.27 = (f32[96,128]{1,0:T(8,128)S(1)}, f32[96,128]{1,0:T(8,128)S(1)}, u32[]{:S(2)}, u32[]{:S(2)}) collective-permute-start(f32[96,128]{1,0:T(8,128)S(1)} %add_add_fusion.refs_0_), channel_id=1, source_target_pairs={{0,1},{1,2},{2,3},{3,0},{4,5},{5,6},{6,7},{7,4},{8,9},{9,10},{10,1... | collective-permute-start | bytes 147464 | tf_op jit(solution)/shard_map/ppermute | solution.py:327
  (2 other events, 10.5 us)

commit v4 on v3

v4 whole, which is shorter than its diff:
```python
import functools
import math

import jax
import jax.numpy as jnp
from jax import lax
from jax.experimental import pallas as pl
from jax.experimental.pallas import tpu as pltpu
from jax.sharding import PartitionSpec as P

HALO = 4
FILTER = 4
UNROLL = 4
LATE = 4
LOADS = 4
LANES = 128
PANEL = 16

filter_scale = 0.4


def offsets(row_count):
    return (1, -1, 2, row_count // 2)


def spread(values, s, rows):
    return jnp.broadcast_to(values[:, s : s + 1], (rows, LANES))


def ranks_of(named, local_blocks):
    hits = jnp.max(named, axis=0, keepdims=True)
    above = lax.broadcasted_iota(jnp.int32, (LANES, LANES), 0)
    here = lax.broadcasted_iota(jnp.int32, (LANES, LANES), 1)
    before = (above < here) & (above // local_blocks == here // local_blocks)
    ranks = jnp.dot(
        jnp.broadcast_to(hits, (16, LANES)).astype(jnp.bfloat16),
        jnp.where(before, 1.0, 0.0).astype(jnp.bfloat16),
        preferred_element_type=jnp.float32,
    )
    return hits, ranks[:1]


def send_kernel(row_count, at, cols, x, info, *sends):
    slot_count = cols.shape[1]
    size = sends[0].shape[2]
    local_blocks = x.shape[1] // size
    here = at[0]
    lane = lax.broadcasted_iota(jnp.int32, (local_blocks, LANES), 1)
    named = jnp.zeros((local_blocks, LANES), jnp.float32)
    for q, delta in enumerate(offsets(row_count)):
        asker = lax.rem(here + row_count - delta, row_count)
        start = pl.multiple_of(asker * local_blocks, local_blocks)
        values = cols[pl.ds(start, local_blocks), :] - (here * local_blocks - q * local_blocks)
        group = lane // local_blocks == q
        for s in range(slot_count):
            named = jnp.where(group & (spread(values, s, local_blocks) == lane), 1.0, named)
    hits, ranks = ranks_of(named, local_blocks)
    lane = lane[:1]
    for q in range(4):
        mine = (hits > 0) & (lane // local_blocks == q)
        for k in range(HALO):
            number = jnp.where(mine & (ranks == k), (lane % local_blocks).astype(jnp.float32), 0.0)
            j = jnp.sum(number).astype(jnp.int32)
            info[q * HALO + k] = j
            sends[q][k] = x[:, pl.ds(pl.multiple_of(j * size, size), size)]


def send_part(row_count, at, cols, x, size):
    send = jax.ShapeDtypeStruct((HALO, x.shape[0], size), jnp.bfloat16)
    return pl.pallas_call(
        functools.partial(send_kernel, row_count),
        out_shape=(jax.ShapeDtypeStruct((4 * HALO,), jnp.int32),) + (send,) * 4,
        in_specs=[smem] + [vmem] * 2,
        out_specs=(smem,) + (vmem,) * 4,
        compiler_params=grant,
        name="send_part",
    )(at, cols, x)


def build_table(row_count, here, values):
    rows, slot_count = values.shape
    lane = lax.broadcasted_iota(jnp.int32, (rows, LANES), 1)
    ids = jnp.zeros((rows, LANES), jnp.int32)
    for q, delta in enumerate(offsets(row_count)):
        source = lax.rem(here + row_count + delta, row_count)
        ids = jnp.where(lane // rows == q, (source - q) * rows + lane, ids)
    columns = [spread(values, s, rows) for s in range(slot_count)]
    named = jnp.zeros((rows, LANES), jnp.float32)
    near_total = jnp.zeros((rows, LANES), jnp.int32)
    nears = []
    for column in columns:
        named = jnp.where(column == ids, 1.0, named)
        within = column - here * rows
        nears.append((within >= 0) & (within < rows))
        near_total = near_total + nears[-1].astype(jnp.int32)
    _, ranks = ranks_of(named, rows)
    group = lane[:1] // rows
    places = ranks + (HALO * group + rows + 1).astype(jnp.float32)
    near_count = jnp.zeros((rows, LANES), jnp.int32)
    table = jnp.zeros((rows, LANES), jnp.int32)
    for s, (column, near) in enumerate(zip(columns, nears)):
        far = jnp.sum(jnp.where(column == ids, places, 0.0), axis=1, keepdims=True)
        place = jnp.where(near, column - here * rows, far.astype(jnp.int32))
        rank = jnp.where(near, near_count, near_total + s - near_count)
        near_count = near_count + near.astype(jnp.int32)
        table = jnp.where(lane == rank, s * 64 + place, table)
    extra = (lane < slot_count - LATE) & ((table & 63) > rows)
    count = jnp.sum(extra.astype(jnp.float32)).astype(jnp.int32)
    return jnp.where(lane == LANES // 2, count, table)


def slot_pairs(table, row, slots, held, blocks, limit):
    total = None
    for t in range(slots.start, slots.stop, 2):
        codes = [table[row, t + k] for k in range(2)]
        places = [jnp.minimum(code & 63, limit) for code in codes]
        taken = jnp.concatenate([held[p] for p in places], axis=1)
        block = jnp.concatenate([blocks[code >> 6, row] for code in codes], axis=0)
        product = jnp.dot(taken, block, preferred_element_type=jnp.float32)
        total = product if total is None else total + product
    return total


def local_rows_of(scale, table, groups, blocks, onsite, prev, y, held):
    slot_count, local_blocks, size, _ = blocks.shape

    @pl.loop(groups[0], groups[1])
    def _(group):
        for u in range(UNROLL):
            row = group * UNROLL + u
            early = range(slot_count - LATE)
            total = slot_pairs(table, row, early, held, blocks, local_blocks)
            span = pl.ds(pl.multiple_of(row * size, size), size)
            value = scale * (total + onsite[:, span] * held[row].astype(jnp.float32))
            if prev is not None:
                value = value - prev[:, span].astype(jnp.float32)
            y[:, span] = value


def hold(x, held, local_blocks):
    size = held.shape[2]
    for j in range(local_blocks):
        held[j] = x[:, j * size : (j + 1) * size]
    held[local_blocks] = jnp.zeros(held.shape[1:], held.dtype)


def local_kernel(scale, table, blocks, x, onsite, prev, y, held):
    local_blocks = blocks.shape[1]
    hold(x, held, local_blocks)
    groups = (0, local_blocks // UNROLL)
    local_rows_of(scale, table, groups, blocks, onsite, prev, y, held)


def first_kernel(scale, row_count, at, cols, far, x, onsite, y, table, blocks, held, near, sems):
    slot_count, local_blocks, _, _ = blocks.shape
    here = at[0]
    share = local_blocks // LOADS

    def rows(ref, g):
        return ref.at[:, pl.ds(g * share, share)]

    for g in range(LOADS):
        for s in range(slot_count):
            part = pl.ds(g * share, share)
            pltpu.make_async_copy(far.at[s, part], blocks.at[s, part], sems.at[g]).start()
    start = pl.multiple_of(here * local_blocks, local_blocks)
    table[...] = build_table(row_count, here, cols[pl.ds(start, local_blocks), :])
    copy = pltpu.make_async_copy(table, near, sems.at[LOADS])
    copy.start()
    hold(x, held, local_blocks)
    copy.wait()
    for g in range(LOADS):
        pltpu.make_async_copy(rows(far, g), rows(blocks, g), sems.at[g]).wait()
        groups = (g * share // UNROLL, (g + 1) * share // UNROLL)
        local_rows_of(scale, near, groups, blocks, onsite, None, y, held)


def remote_kernel(scale, keep, last, info, table, *refs):
    halos, (y_in, x_in, blocks, x), rest = refs[:4], refs[4:8], refs[8:]
    y, sends, held = (rest[0], rest[1:-1], rest[-1]) if keep else (rest[-1], rest[:-2], rest[-2])
    slot_count, local_blocks, size, _ = blocks.shape
    per = halos[0].shape[0]
    count = table[0, LANES // 2]
    hold(x_in, held, local_blocks)
    for q in range(4):
        at = local_blocks + 1 + q * per
        held[at : at + per] = halos[q][...]

    @pl.loop(0, local_blocks // UNROLL)
    def _(group):
        for u in range(UNROLL):
            row = group * UNROLL + u
            late = range(slot_count - LATE, slot_count)
            total = slot_pairs(table, row, late, held, blocks, held.shape[0] - 1)
            span = pl.ds(pl.multiple_of(row * size, size), size)
            value = y_in[:, span] + scale * total
            y[:, span] = value
            x[:, span] = value.astype(jnp.bfloat16)

    @pl.when(count > 0)
    def _():
        @pl.loop(0, local_blocks)
        def _(row):
            @pl.loop(0, slot_count - LATE)
            def _(t):
                code = table[row, t]

                @pl.when((code & 63) > local_blocks)
                def _():
                    product = jnp.dot(
                        held[code & 63], blocks[code >> 6, row], preferred_element_type=jnp.float32
                    )
                    span = pl.ds(pl.multiple_of(row * size, size), size)
                    y[:, span] = y[:, span] + scale * product

        x[...] = y[...].astype(jnp.bfloat16)

    if not last:
        for q in range(4):
            for k in range(per):
                j = info[q * per + k]
                sends[q][k] = x[:, pl.ds(pl.multiple_of(j * size, size), size)]


vmem = pl.BlockSpec(memory_space=pltpu.VMEM)
smem = pl.BlockSpec(memory_space=pltpu.SMEM)
grant = pltpu.CompilerParams(vmem_limit_bytes=16 << 20)


def local_part(scale, table, blocks, x, onsite, prev):
    _, local_blocks, size, _ = blocks.shape
    return pl.pallas_call(
        functools.partial(local_kernel, scale),
        out_shape=jax.ShapeDtypeStruct(x.shape, jnp.float32),
        in_specs=[smem] + [vmem] * 4,
        out_specs=vmem,
        scratch_shapes=[pltpu.VMEM((local_blocks + 1, x.shape[0], size), jnp.bfloat16)],
        compiler_params=grant,
        name="local_part",
    )(table, blocks, x, onsite, prev)


def first_part(scale, row_count, at, cols, blocks, x, onsite):
    _, local_blocks, size, _ = blocks.shape
    table = (local_blocks, LANES)
    return pl.pallas_call(
        functools.partial(first_kernel, scale, row_count),
        out_shape=(
            jax.ShapeDtypeStruct(x.shape, jnp.float32),
            jax.ShapeDtypeStruct(table, jnp.int32),
            jax.ShapeDtypeStruct(blocks.shape, blocks.dtype),
        ),
        in_specs=[smem, vmem, pl.BlockSpec(memory_space=pl.ANY), vmem, vmem],
        out_specs=(vmem,) * 3,
        scratch_shapes=[
            pltpu.VMEM((local_blocks + 1, x.shape[0], size), jnp.bfloat16),
            pltpu.SMEM(table, jnp.int32),
            pltpu.SemaphoreType.DMA((LOADS + 1,)),
        ],
        compiler_params=grant,
        name="first_part",
    )(at, cols, blocks, x, onsite)


def remote_part(scale, keep, last, info, table, halos, y, x, blocks):
    _, local_blocks, size, _ = blocks.shape
    width = y.shape[0]
    per = halos[0].shape[0]
    sends = () if last else (jax.ShapeDtypeStruct((per, width, size), jnp.bfloat16),) * 4
    kept = (jax.ShapeDtypeStruct(y.shape, jnp.float32),) if keep else ()
    scratch = [pltpu.VMEM((local_blocks + 1 + 4 * per, width, size), jnp.bfloat16)]
    if not keep:
        scratch.append(pltpu.VMEM(y.shape, jnp.float32))
    return pl.pallas_call(
        functools.partial(remote_kernel, scale, keep, last),
        out_shape=(jax.ShapeDtypeStruct(y.shape, jnp.bfloat16),) + kept + sends,
        in_specs=[smem] * 2 + [vmem] * 7,
        out_specs=(vmem,) * (1 + len(kept) + len(sends)),
        scratch_shapes=scratch,
        compiler_params=grant,
        name="remote_part",
    )(info, table, *halos, y, x, blocks)


def gram_kernel(own, one, three, strip):
    f32 = jnp.float32
    nt = (((1,), (1,)), ((), ()))
    width = own.shape[0]
    half = width // 2
    pair = jnp.concatenate([own[...], one[...]], axis=0)
    strip[:width, :] = lax.dot_general(own[...], pair, nt, preferred_element_type=f32)
    block = lax.dot_general(one[...], three[...], nt, preferred_element_type=f32)
    strip[width:, :] = jnp.concatenate([block[:half], block[half:]], axis=1)


def gram_strip(own, one, three):
    width = own.shape[0]
    return pl.pallas_call(
        gram_kernel,
        out_shape=jax.ShapeDtypeStruct((width + width // 2, 2 * width), jnp.float32),
        in_specs=[vmem] * 3,
        out_specs=vmem,
        compiler_params=grant,
        name="gram_strip",
    )(own, one, three)


def three_parts(value):
    high = value.astype(jnp.bfloat16)
    rest = value - high.astype(jnp.float32)
    middle = rest.astype(jnp.bfloat16)
    low = (rest - middle.astype(jnp.float32)).astype(jnp.bfloat16)
    return high, middle, low


def solve_kernel(root, own_ref, *refs):
    strips, finals, (basis, factor, work, inverse) = refs[:4], refs[4:9], refs[9:]
    own = own_ref[0]
    n = work.shape[0]
    width = n // 4
    f32 = jnp.float32
    for k in range(4):
        source = lax.rem(own + 4 - k, 4)
        for part in range(4):

            @pl.when(source == part)
            def _(part=part, strip=strips[k]):
                spans = [slice(p * width, (p + 1) * width) for p in range(4)]
                here, back, ahead = spans[part], spans[part - 1], spans[(part + 1) % 4]
                work[here, here] = strip[:width, :width]
                if part == 0:
                    work[here, back] = strip[:width, width:]
                else:
                    work[back, here] = strip[:width, width:].T
                if part in (1, 2):
                    tail = strip[width:, :]
                    work[back, ahead] = jnp.concatenate([tail[:, :width], tail[:, width:]], axis=0)

    row_ids = lax.broadcasted_iota(jnp.int32, (PANEL, 128), 0)
    lane_ids = lax.broadcasted_iota(jnp.int32, (PANEL, 128), 1)
    for r0 in range(0, n, PANEL):
        r1 = r0 + PANEL
        at, tile = r0 % 128, r0 // 128
        rows = work[r0:r1, :]
        pivots = [
            jnp.broadcast_to(rows[:, r0 + k : r0 + k + 1], (PANEL, 128)) for k in range(PANEL)
        ]
        parts = [rows[:, t : t + 128] for t in range(0, n, 128)]
        parts.append(jnp.where(lane_ids - at == row_ids, 1.0, 0.0).astype(f32))
        diagonal = jnp.ones((PANEL, 128), f32)
        for j in range(PANEL):
            pivot = pivots[j][j : j + 1, :]
            diagonal = jnp.where(row_ids == j, pivot, diagonal)
            factors = jnp.where(row_ids > j, pivots[j] * (1.0 / pivot), 0.0)
            for k in range(j + 1, PANEL):
                pivots[k] = pivots[k] - factors * pivots[k][j : j + 1, :]
            parts = [q - factors * q[j : j + 1, :] for q in parts]
        roots = lax.rsqrt(diagonal)
        parts = [q * roots for q in parts]
        in_panel = (lane_ids >= at) & (lane_ids < at + PANEL)
        joined = []
        for t in range(n // 128):
            cols = lane_ids + 128 * t
            span = slice(128 * t, 128 * t + 128)
            factor[r0:r1, span] = jnp.where(cols >= row_ids + r0, parts[t] * (1.0 / root), 0.0)
            both = jnp.where(in_panel, parts[-1], parts[t]) if t == tile else parts[t]
            joined.append(both)
            inverse[r0:r1, span] = jnp.where(cols < r1, both, 0.0)
        if r1 < n:
            h, m, l = three_parts(jnp.concatenate(joined, axis=1))
            left = jnp.concatenate([h, h, m, m, h, l], axis=0)
            right = jnp.concatenate([h, m, h, m, l, h], axis=0)
            low = r1 // 128 * 128
            update = lax.dot_general(
                left[:, low:], right, (((0,), (0,)), ((), ())), preferred_element_type=f32
            )
            cols = lax.broadcasted_iota(jnp.int32, (n - r1, n), 1)
            kept = jnp.where((cols >= r0) & (cols < r1), 0.0, work[r1:, :])
            work[r1:, :] = kept - update[r1 - low :, :]
    mine = root * inverse[pl.ds(pl.multiple_of(own * width, width), width), :]
    blocks = [mine[:, b * width : (b + 1) * width] for b in range(4)]
    ordered = []
    for k in range(4):
        source = lax.rem(own + 4 - k, 4)
        block = blocks[0]
        for b in range(1, 4):
            block = jnp.where(source == b, blocks[b], block)
        ordered.append(block)
    ordered = jnp.concatenate(ordered, axis=1)
    left = jnp.concatenate(three_parts(ordered), axis=0)
    span = basis.shape[1] // 2
    for c in range(2):
        at = slice(c * span, (c + 1) * span)
        right = jnp.concatenate(
            [finals[0][:, at], finals[1][:, at], finals[3 + c][...], finals[2][:, at]], axis=0
        )
        product = jnp.dot(left, right, preferred_element_type=f32)
        basis[:, at] = product[:width] + product[width : 2 * width] + product[2 * width :]


def solve(root, own, strips, finals):
    n = 2 * strips[0].shape[1]
    return pl.pallas_call(
        functools.partial(solve_kernel, root),
        out_shape=(
            jax.ShapeDtypeStruct(finals[0].shape, jnp.float32),
            jax.ShapeDtypeStruct((n, n), jnp.float32),
        ),
        in_specs=[smem] + [vmem] * 9,
        out_specs=(vmem,) * 2,
        scratch_shapes=[pltpu.VMEM((n, n), jnp.float32)] * 2,
        compiler_params=grant,
        name="solve",
    )(own, *strips, *finals)


def shift(value, axis, by):
    n = lax.axis_size(axis)
    return lax.ppermute(value, axis, [(i, (i + by) % n) for i in range(n)])


def swap(value, axis, mask):
    n = lax.axis_size(axis)
    return lax.ppermute(value, axis, [(i, i ^ mask) for i in range(n)])


def xor_sum(value, axis, masks):
    terms = [value] + [swap(value, axis, m) for m in masks]
    while len(terms) > 1:
        terms = [terms[i] + terms[i + 1] for i in range(0, len(terms), 2)]
    return terms[0]


def body(subspace, onsite, blocks, cols):
    row_count = lax.axis_size("row")
    row_index = lax.axis_index("row")
    col_index = lax.axis_index("col").astype(jnp.int32)
    width, local_rows = subspace.shape
    slot_count, local_blocks, size, _ = blocks.shape
    at = jnp.stack([row_index.astype(jnp.int32), col_index])
    onsite = onsite[None, :]
    info, *send = send_part(row_count, at, cols, subspace, size)
    previous, before, x = None, subspace, subspace
    for step in range(FILTER):
        scale = filter_scale if step == 0 else 2.0 * filter_scale
        last = step == FILTER - 1
        keep = step < FILTER - 2
        halos = [shift(send[q], "row", -d) for q, d in enumerate(offsets(row_count))]
        if step == 0:
            partial, table, held = first_part(scale, row_count, at, cols, blocks, x, onsite)
        else:
            partial = local_part(scale, table, held, x, onsite, previous)
        x, *send = remote_part(scale, keep, last, info, table, halos, partial, x, held)
        previous = before
        if keep:
            before, *send = send
    final = x
    half = local_rows // 2
    one = shift(final, "col", 1)
    three = shift(final, "col", -1)
    two = [shift(one[:, :half], "col", 1), shift(three[:, half:], "col", -1)]
    strip = gram_strip(final, one, three)
    x_bit = row_count // 4
    strip = xor_sum(strip, "row", [1])
    strip = xor_sum(strip, "row", [2, 4, 6])
    strip, *two = lax.optimization_barrier((strip, *two))
    strip = xor_sum(strip, "row", [x_bit, 2 * x_bit, 3 * x_bit])
    strips = [strip] + [shift(strip, "col", k) for k in (1, 2, 3)]
    root = math.sqrt(row_count * local_rows)
    return solve(root, at[1:], strips, [final, one, three] + two)


def solution(mesh):
    in_specs = (P("col", "row"), P("row"), P(None, "row", None, None), P())
    out_specs = (P("col", "row"), P())
    return jax.shard_map(body, mesh=mesh, in_specs=in_specs, out_specs=out_specs, check_vma=False)
```

time: 140 us -> 126 us (0.900)
  local copies, waits for them, and re-layouts: 11.7 us -> 2.96 us
  Pallas kernels: 41.9 us -> 47.5 us
  waiting for transfers between devices: 36 us -> 30.8 us
  other arithmetic: 4.94 us -> 0.11 us
    pallas_call x8 -> x9, Pallas kernels: 31.3 us -> 37.2 us  [the longest x3 15 us: local_part(): pl.pallas_call(functools.partial(local_kernel, scale), out_shape=jax.Shap...]
    unnamed x9, local copies, waits for them, and re-layouts: 8.08 us -> 2.93 us
    ppermute x23, waiting for transfers between devices: 28.4 us -> 25.5 us  [shift(): return lax.ppermute(value, axis, [(i, (i + by) % n) for i in range(n)])]
    ppermute x7, waiting for transfers between devices: 7.59 us -> 5.35 us  [swap(): return lax.ppermute(value, axis, [(i, i ^ mask) for i in range(n)])]
    reduce_sum x5 -> x0, other arithmetic: 1.44 us -> none  [the longest x1 0.71 us: plan(): count = jnp.sum(extra.astype(jnp.int32)).reshape(1)]
    ppermute x23, starting transfers between devices: 34.8 us -> 33.4 us  [shift(): return lax.ppermute(value, axis, [(i, (i + by) % n) for i in range(n)])]
  transfers between devices with their start and end apart: 30 -> 30, of which waited for: 16 -> 12; matrix products, arithmetic and copies ran while one was open for 4% -> 0% of each run, Pallas kernels for 13% -> 19%
where the time goes in v4:
time: 126 us
  Pallas kernels  47.5 us (38%)
  starting transfers between devices  43.8 us (35%)
  waiting for transfers between devices  30.8 us (24%)
  local copies, waits for them, and re-layouts  2.96 us (2%)
    ppermute x23, starting transfers between devices, shift(): return lax.ppermute(value, axis, [(i, (i + by) % n) for i in range(n)])  33.4 us
    ppermute x23, waiting for transfers between devices, shift(): return lax.ppermute(value, axis, [(i, (i + by) % n) for i in range(n)])  25.5 us
    pallas_call x3, Pallas kernels, local_part(): pl.pallas_call(functools.partial(local_kernel, scale), out_shape=jax.Shap...  15 us
    pallas_call x4, Pallas kernels, remote_part(): pl.pallas_call(functools.partial(remote_kernel, scale, keep, last), out_s...  11.6 us
    ppermute x7, starting transfers between devices, swap(): return lax.ppermute(value, axis, [(i, i ^ mask) for i in range(n)])  10.4 us
    pallas_call x1, Pallas kernels, solve(): pl.pallas_call(functools.partial(solve_kernel, root), out_shape=(jax.Shap...  9.63 us
    pallas_call x1, Pallas kernels, first_part(): pl.pallas_call(functools.partial(first_kernel, scale, row_count), out_sha...  8.65 us
    ppermute x7, waiting for transfers between devices, swap(): return lax.ppermute(value, axis, [(i, i ^ mask) for i in range(n)])  5.35 us
  transfers between devices with their start and end apart: 30, of which 12 were waited for; matrix products, arithmetic and copies ran while one was open for 0% of the time, Pallas kernels for 19%

profile of v4, /device:TPU:0, one launch (start us, length us, event | category | flops | bytes accessed | tf_op | source)
XLA Modules:
  0.0 126.1 jit_solution(16882529543561937198)
XLA Ops:
  2.9 2.0 %send_part.1 = (s32[16]{0:T(128)S(1)}, bf16[4,64,128]{2,1,0:T(8,128)(2,1)S(1)}, bf16[4,64,128]{2,1,0:T(8,128)(2,1)S(1)}, bf16[4,64,128]{2,1,0:T(8,128)(2,1)S(1)}, bf16[4,64,128]{2,1,0:T(8,128)(2,1)S(1)}) custom-call(s32[2]{0:T(128)S(1)} %pad_add_fusion.at, s32[1024,20]{1,0:T(8,128)S(1)} %copy.6.cols, bf16[64,4096]{1,0:T(8,128)(2,1)S(1)} %copy-done), custom_call_target="tpu_custom_call" | custom-call | tf_op jit(solution)/shard_map/send_part/pallas_call | solution.py:70
  4.9 5.8 %collective-permute-start = (bf16[4,64,128]{2,1,0:T(8,128)(2,1)S(1)}, bf16[4,64,128]{2,1,0:T(8,128)(2,1)S(1)}, u32[]{:S(2)}, u32[]{:S(2)}) collective-permute-start(bf16[4,64,128]{2,1,0:T(8,128)(2,1)S(1)} %get-tuple-element.32), channel_id=1, source_target_pairs={{0,124},{4,0},{8,4},{12,8},{16,12},{20,16},{24,20},{28,24},{32,28}... | collective-permute-start | bytes 196616 | tf_op jit(solution)/shard_map/ppermute | solution.py:419
  13.3 8.7 %first_part.1 = (f32[64,4096]{1,0:T(8,128)S(1)}, s32[32,128]{1,0:T(8,128)S(1)}, bf16[20,32,128,128]{3,2,1,0:T(8,128)(2,1)S(1)}) custom-call(s32[2]{0:T(128)S(1)} %pad_add_fusion.at, s32[1024,20]{1,0:T(8,128)S(1)} %copy.6.cols, bf16[20,32,128,128]{3,2,1,0:T(8,128)(2,1)} %far.1, bf16[64,4096]{1,0:T(8,128)(2,1)S(1)} %copy-done, f32[1,4096]{1,0:T(1,128)S(1)} %bitcast.3), custom_call_target="tpu_custom_call" | custom-call | tf_op jit(solution)/shard_map/first_part/pallas_call | solution.py:246
  22.0 2.9 %remote_part.4 = (bf16[64,4096]{1,0:T(8,128)(2,1)S(1)}, f32[64,4096]{1,0:T(8,128)S(1)}, bf16[4,64,128]{2,1,0:T(8,128)(2,1)S(1)}, bf16[4,64,128]{2,1,0:T(8,128)(2...) custom-call(s32[16]{0:T(128)S(1)} %get-tuple-element.30.info, ...), custom_call_target="tpu_custom_call" | custom-call | tf_op jit(solution)/shard_map/remote_part/pallas_call | solution.py:274
  25.0 3.3 %collective-permute-start.4 = (bf16[4,64,128]{2,1,0:T(8,128)(2,1)S(1)}, bf16[4,64,128]{2,1,0:T(8,128)(2,1)S(1)}, u32[]{:S(2)}, u32[]{:S(2)}) collective-permute-start(bf16[4,64,128]{2,1,0:T(8,128)(2,1)S(1)} %get-tuple-element.38), channel_id=1, source_target_pairs={{0,124},{4,0},{8,4},{12,8},{16,12},{20,16},{24,20},{28,24},{32,28}... | collective-permute-start | bytes 196616 | tf_op jit(solution)/shard_map/ppermute | solution.py:419
  28.7 3.0 %collective-permute-start.7 = (bf16[4,64,128]{2,1,0:T(8,128)(2,1)S(1)}, bf16[4,64,128]{2,1,0:T(8,128)(2,1)S(1)}, u32[]{:S(2)}, u32[]{:S(2)}) collective-permute-start(bf16[4,64,128]{2,1,0:T(8,128)(2,1)S(1)} %get-tuple-element.41), channel_id=1, source_target_pairs={{0,64},{4,68},{8,72},{12,76},{16,80},{20,84},{24,88},{28,92},{32,9... | collective-permute-start | bytes 196616 | tf_op jit(solution)/shard_map/ppermute | solution.py:419
  31.7 5.0 %local_part.3.refs_4_ = f32[64,4096]{1,0:T(8,128)S(1)} custom-call(s32[32,128]{1,0:T(8,128)S(1)} %get-tuple-element.31.table, bf16[20,32,128,128]{3,2,1,0:T(8,128)(2,1)S(1)} %get-tuple-element.37.refs_6_.blocks, bf16[64,4096]{1,0:T(8,128)(2,1)S(1)} %get-tuple-element.42.x.refs_5_, f32[1,4096]{1,0:T(1,128)S(1)} %bitcast.4, bf16[64,4096]{1,0:T(8,128)(2,1)S(1)} %copy-done.1), custom_call_target="tpu_custom_call" | custom-call | tf_op jit(solution)/shard_map/local_part/pallas_call | solution.py:232
  36.7 2.9 %remote_part.5 = (bf16[64,4096]{1,0:T(8,128)(2,1)S(1)}, f32[64,4096]{1,0:T(8,128)S(1)}, bf16[4,64,128]{2,1,0:T(8,128)(2,1)S(1)}, bf16[4,64,128]{2,1,0:T(8,128)(2...) custom-call(s32[16]{0:T(128)S(1)} %get-tuple-element.30.info, ...), custom_call_target="tpu_custom_call" | custom-call | tf_op jit(solution)/shard_map/remote_part/pallas_call | solution.py:274
  39.7 3.5 %collective-permute-start.8 = (bf16[4,64,128]{2,1,0:T(8,128)(2,1)S(1)}, bf16[4,64,128]{2,1,0:T(8,128)(2,1)S(1)}, u32[]{:S(2)}, u32[]{:S(2)}) collective-permute-start(bf16[4,64,128]{2,1,0:T(8,128)(2,1)S(1)} %get-tuple-element.43), channel_id=1, source_target_pairs={{0,124},{4,0},{8,4},{12,8},{16,12},{20,16},{24,20},{28,24},{32,28}... | collective-permute-start | bytes 196616 | tf_op jit(solution)/shard_map/ppermute | solution.py:419
  44.8 5.0 %local_part.4.refs_4_ = f32[64,4096]{1,0:T(8,128)S(1)} custom-call(s32[32,128]{1,0:T(8,128)S(1)} %get-tuple-element.31.table, bf16[20,32,128,128]{3,2,1,0:T(8,128)(2,1)S(1)} %get-tuple-element.37.refs_6_.blocks, bf16[64,4096]{1,0:T(8,128)(2,1)S(1)} %get-tuple-element.47.x.refs_5_, f32[1,4096]{1,0:T(1,128)S(1)} %bitcast.5, f32[64,4096]{1,0:T(8,128)S(1)} %get-tuple-element.48.prev), custom_call_target="tpu_custom_call" | custom-call | tf_op jit(solution)/shard_map/local_part/pallas_call | solution.py:232
  50.9 2.9 %remote_part.6 = (bf16[64,4096]{1,0:T(8,128)(2,1)S(1)}, bf16[4,64,128]{2,1,0:T(8,128)(2,1)S(1)}, bf16[4,64,128]{2,1,0:T(8,128)(2,1)S(1)}, bf16[4,64,128]{2,1,0:T(8,128)(2,1)S(1)}, bf16[4,64,128]{2,1,0:T(8,128)(2,1)S(1)}) custom-call(s32[16]{0:T(128)S(1)} %get-tuple-element.30.info, s32[32,128]{1,0:T(8,128)S(1)} %get-tuple-element.31.table, ...), custom_call_target="tpu_custom_call" | custom-call | tf_op jit(solution)/shard_map/remote_part/pallas_call | solution.py:274
  53.8 3.9 %collective-permute-start.12 = (bf16[4,64,128]{2,1,0:T(8,128)(2,1)S(1)}, bf16[4,64,128]{2,1,0:T(8,128)(2,1)S(1)}, u32[]{:S(2)}, u32[]{:S(2)}) collective-permute-start(bf16[4,64,128]{2,1,0:T(8,128)(2,1)S(1)} %get-tuple-element.49), channel_id=1, source_target_pairs={{0,124},{4,0},{8,4},{12,8},{16,12},{20,16},{24,20},{28,24},{32,28}... | collective-permute-start | bytes 196616 | tf_op jit(solution)/shard_map/ppermute | solution.py:419
  58.2 1.5 %collective-permute-start.15 = (bf16[4,64,128]{2,1,0:T(8,128)(2,1)S(1)}, bf16[4,64,128]{2,1,0:T(8,128)(2,1)S(1)}, u32[]{:S(2)}, u32[]{:S(2)}) collective-permute-start(bf16[4,64,128]{2,1,0:T(8,128)(2,1)S(1)} %get-tuple-element.52), channel_id=1, source_target_pairs={{0,64},{4,68},{8,72},{12,76},{16,80},{20,84},{24,88},{28,92},{32,9... | collective-permute-start | bytes 196616 | tf_op jit(solution)/shard_map/ppermute | solution.py:419
  59.7 5.0 %local_part.5.refs_4_ = f32[64,4096]{1,0:T(8,128)S(1)} custom-call(s32[32,128]{1,0:T(8,128)S(1)} %get-tuple-element.31.table, bf16[20,32,128,128]{3,2,1,0:T(8,128)(2,1)S(1)} %get-tuple-element.37.refs_6_.blocks, bf16[64,4096]{1,0:T(8,128)(2,1)S(1)} %get-tuple-element.53.x.refs_5_, f32[1,4096]{1,0:T(1,128)S(1)} %bitcast.6, f32[64,4096]{1,0:T(8,128)S(1)} %get-tuple-element.54.prev), custom_call_target="tpu_custom_call" | custom-call | tf_op jit(solution)/shard_map/local_part/pallas_call | solution.py:232
  64.7 2.8 %remote_part.7.own.refs_4_ = bf16[64,4096]{1,0:T(8,128)(2,1)S(1)} custom-call(s32[16]{0:T(128)S(1)} %get-tuple-element.30.info, s32[32,128]{1,0:T(8,128)S(1)} %get-tuple-element.31.table, bf16[4,64,128]{2,1,0:T(8,128)(2,1)S(1)} %collective-permute-done.12.refs_0_, bf16[4,64,128]{2,1,0:T(8,128)(2,1)S(1)} %collective-permute-done.13.refs_1_, ...), custom_call_target="tpu_custom_call" | custom-call | tf_op jit(solution)/shard_map/remote_part/pallas_call | solution.py:274
  67.6 3.1 %collective-permute-start.17 = (bf16[64,4096]{1,0:T(8,128)(2,1)S(1)}, bf16[64,4096]{1,0:T(8,128)(2,1)S(1)}, u32[]{:S(2)}, u32[]{:S(2)}) collective-permute-start(bf16[64,4096]{1,0:T(8,128)(2,1)S(1)} %remote_part.7.own.refs_4_), channel_id=1, source_target_pairs={{0,3},{1,0},{2,1},{3,2},{4,7},{5,4},{6,5},{7,6},{8,11},{9,8},{10,9... | collective-permute-start | bytes 1572872 | tf_op jit(solution)/shard_map/ppermute | solution.py:419
  70.7 10.1 %collective-permute-done.17.three.refs_6_ = bf16[64,4096]{1,0:T(8,128)(2,1)S(1)} collective-permute-done((bf16[64,4096]{1,0:T(8,128)(2,1)S(1)}, bf16[64,4096]{1,0:T(8,128)(2,1)S(1)}, u32[]{:S(2)}, u32[]{:S(2)}) %collective-permute-start.17) | collective-permute-done | bytes 524320 | tf_op jit(solution)/shard_map/ppermute | solution.py:419
  80.8 4.0 %collective-permute-done.16.one.refs_5_ = bf16[64,4096]{1,0:T(8,128)(2,1)S(1)} collective-permute-done((bf16[64,4096]{1,0:T(8,128)(2,1)S(1)}, bf16[64,4096]{1,0:T(8,128)(2,1)S(1)}, u32[]{:S(2)}, u32[]{:S(2)}) %collective-permute-start.16) | collective-permute-done | bytes 524320 | tf_op jit(solution)/shard_map/ppermute | solution.py:419
  85.4 1.8 %collective-permute-start.18 = (f32[96,128]{1,0:T(8,128)S(1)}, f32[96,128]{1,0:T(8,128)S(1)}, u32[]{:S(2)}, u32[]{:S(2)}) collective-permute-start(f32[96,128]{1,0:T(8,128)S(1)} %gram_strip.1), channel_id=1, source_target_pairs={{0,4},{4,0},{8,12},{12,8},{16,20},{20,16},{24,28},{28,24},{32,36},... | collective-permute-start | bytes 147464 | tf_op jit(solution)/shard_map/ppermute | solution.py:424
  88.1 4.5 %collective-permute-start.20 = (f32[96,128]{1,0:T(8,128)S(1)}, f32[96,128]{1,0:T(8,128)S(1)}, u32[]{:S(2)}, u32[]{:S(2)}) collective-permute-start(f32[96,128]{1,0:T(8,128)S(1)} %add.21), channel_id=1, source_target_pairs={{0,16},{4,20},{8,24},{12,28},{16,0},{20,4},{24,8},{28,12},{32,48},... | collective-permute-start | bytes 147464 | tf_op jit(solution)/shard_map/ppermute | solution.py:424
  92.8 2.1 %collective-permute-start.22 = (bf16[64,2048]{1,0:T(8,128)(2,1)S(1)}, bf16[64,2048]{1,0:T(8,128)(2,1)S(1)}, u32[]{:S(2)}, u32[]{:S(2)}) collective-permute-start(bf16[64,2048]{1,0:T(8,128)(2,1)S(1)} %slice.8), channel_id=1, source_target_pairs={{0,1},{1,2},{2,3},{3,0},{4,5},{5,6},{6,7},{7,4},{8,9},{9,10},{10,1... | collective-permute-start | bytes 786440 | tf_op jit(solution)/shard_map/ppermute | solution.py:419
  94.9 1.9 %collective-permute-done.19 = f32[96,128]{1,0:T(8,128)S(1)} collective-permute-done((f32[96,128]{1,0:T(8,128)S(1)}, f32[96,128]{1,0:T(8,128)S(1)}, u32[]{:S(2)}, u32[]{:S(2)}) %collective-permute-start.19) | collective-permute-done | bytes 49184 | tf_op jit(solution)/shard_map/ppermute | solution.py:424
  96.8 3.7 %collective-permute-done.23.refs_8_ = bf16[64,2048]{1,0:T(8,128)(2,1)S(1)} collective-permute-done((bf16[64,2048]{1,0:T(8,128)(2,1)S(1)}, bf16[64,2048]{1,0:T(8,128)(2,1)S(1)}, u32[]{:S(2)}, u32[]{:S(2)}) %collective-permute-start.23) | collective-permute-done | bytes 262176 | tf_op jit(solution)/shard_map/ppermute | solution.py:419
  100.5 1.3 %collective-permute-done.22.refs_7_ = bf16[64,2048]{1,0:T(8,128)(2,1)S(1)} collective-permute-done((bf16[64,2048]{1,0:T(8,128)(2,1)S(1)}, bf16[64,2048]{1,0:T(8,128)(2,1)S(1)}, u32[]{:S(2)}, u32[]{:S(2)}) %collective-permute-start.22) | collective-permute-done | bytes 262176 | tf_op jit(solution)/shard_map/ppermute | solution.py:419
  101.8 1.6 %collective-permute-start.25 = (f32[96,128]{1,0:T(8,128)S(1)}, f32[96,128]{1,0:T(8,128)S(1)}, u32[]{:S(2)}, u32[]{:S(2)}) collective-permute-start(f32[96,128]{1,0:T(8,128)S(1)} %add_add_fusion.1), channel_id=1, source_target_pairs={{0,64},{4,68},{8,72},{12,76},{16,80},{20,84},{24,88},{28,92},{32,9... | collective-permute-start | bytes 147464 | tf_op jit(solution)/shard_map/ppermute | solution.py:424
  103.4 2.5 %collective-permute-start.24 = (f32[96,128]{1,0:T(8,128)S(1)}, f32[96,128]{1,0:T(8,128)S(1)}, u32[]{:S(2)}, u32[]{:S(2)}) collective-permute-start(f32[96,128]{1,0:T(8,128)S(1)} %add_add_fusion.1), channel_id=1, source_target_pairs={{0,32},{4,36},{8,40},{12,44},{16,48},{20,52},{24,56},{28,60},{32,0... | collective-permute-start | bytes 147464 | tf_op jit(solution)/shard_map/ppermute | solution.py:424
  105.9 1.7 %collective-permute-done.26 = f32[96,128]{1,0:T(8,128)S(1)} collective-permute-done((f32[96,128]{1,0:T(8,128)S(1)}, f32[96,128]{1,0:T(8,128)S(1)}, u32[]{:S(2)}, u32[]{:S(2)}) %collective-permute-start.26) | collective-permute-done | bytes 49184 | tf_op jit(solution)/shard_map/ppermute | solution.py:424
  108.8 2.4 %collective-permute-start.28 = (f32[96,128]{1,0:T(8,128)S(1)}, f32[96,128]{1,0:T(8,128)S(1)}, u32[]{:S(2)}, u32[]{:S(2)}) collective-permute-start(f32[96,128]{1,0:T(8,128)S(1)} %add_add_fusion.refs_0_), channel_id=1, source_target_pairs={{0,2},{1,3},{2,0},{3,1},{4,6},{5,7},{6,4},{7,5},{8,10},{9,11},{10,... | collective-permute-start | bytes 147464 | tf_op jit(solution)/shard_map/ppermute | solution.py:419
  111.2 1.5 %collective-permute-done.29.refs_3_ = f32[96,128]{1,0:T(8,128)S(1)} collective-permute-done((f32[96,128]{1,0:T(8,128)S(1)}, f32[96,128]{1,0:T(8,128)S(1)}, u32[]{:S(2)}, u32[]{:S(2)}) %collective-permute-start.29) | collective-permute-done | bytes 49184 | tf_op jit(solution)/shard_map/ppermute | solution.py:419
  112.7 1.7 %collective-permute-done.28.refs_2_ = f32[96,128]{1,0:T(8,128)S(1)} collective-permute-done((f32[96,128]{1,0:T(8,128)S(1)}, f32[96,128]{1,0:T(8,128)S(1)}, u32[]{:S(2)}, u32[]{:S(2)}) %collective-permute-start.28) | collective-permute-done | bytes 49184 | tf_op jit(solution)/shard_map/ppermute | solution.py:419
  114.4 2.1 %collective-permute-done.27.refs_1_ = f32[96,128]{1,0:T(8,128)S(1)} collective-permute-done((f32[96,128]{1,0:T(8,128)S(1)}, f32[96,128]{1,0:T(8,128)S(1)}, u32[]{:S(2)}, u32[]{:S(2)}) %collective-permute-start.27) | collective-permute-done | bytes 49184 | tf_op jit(solution)/shard_map/ppermute | solution.py:419
  116.5 9.6 %solve.1 = (f32[64,4096]{1,0:T(8,128)}, f32[256,256]{1,0:T(8,128)}) custom-call(s32[1]{0:T(128)} %bitcast.own_ref, f32[96,128]{1,0:T(8,128)S(1)} %add_add_fusion.refs_0_, f32[96,128]{1,0:T(8,128)S(1)} %collective-permute-done.27.refs_1_, f32[96,128]{1,0:T(8,128)S(1)} %collective-permute-done.28.refs_2_, f32[96,128]{1,0:T(8,128)S(1)} %collective-permute-done.29.refs_3_, ...), custom_call_target="tpu_custom_call" | custom-call | tf_op jit(solution)/shard_map/solve/pallas_call | solution.py:403
  (54 shorter events, 11.4 us)
Async XLA Ops:
  0.6 21.4 %copy-start.1 = (bf16[64,4096]{1,0:T(8,128)(2,1)S(1)}, bf16[64,4096]{1,0:T(8,128)(2,1)}, u32[]{:S(2)}) copy-start(bf16[64,4096]{1,0:T(8,128)(2,1)} %prev.1) | copy-start | bytes 1572868
  4.9 17.1 %collective-permute-start = (bf16[4,64,128]{2,1,0:T(8,128)(2,1)S(1)}, bf16[4,64,128]{2,1,0:T(8,128)(2,1)S(1)}, u32[]{:S(2)}, u32[]{:S(2)}) collective-permute-start(bf16[4,64,128]{2,1,0:T(8,128)(2,1)S(1)} %get-tuple-element.32), channel_id=1, source_target_pairs={{0,124},{4,0},{8,4},{12,8},{16,12},{20,16},{24,20},{28,24},{32,28}... | collective-permute-start | bytes 196616 | tf_op jit(solution)/shard_map/ppermute | solution.py:419
  10.7 11.3 %collective-permute-start.1 = (bf16[4,64,128]{2,1,0:T(8,128)(2,1)S(1)}, bf16[4,64,128]{2,1,0:T(8,128)(2,1)S(1)}, u32[]{:S(2)}, u32[]{:S(2)}) collective-permute-start(bf16[4,64,128]{2,1,0:T(8,128)(2,1)S(1)} %get-tuple-element.33), channel_id=1, source_target_pairs={{0,4},{4,8},{8,12},{12,16},{16,20},{20,24},{24,28},{28,32},{32,36}... | collective-permute-start | bytes 196616 | tf_op jit(solution)/shard_map/ppermute | solution.py:419
  10.7 11.3 %collective-permute-start.2 = (bf16[4,64,128]{2,1,0:T(8,128)(2,1)S(1)}, bf16[4,64,128]{2,1,0:T(8,128)(2,1)S(1)}, u32[]{:S(2)}, u32[]{:S(2)}) collective-permute-start(bf16[4,64,128]{2,1,0:T(8,128)(2,1)S(1)} %get-tuple-element.34), channel_id=1, source_target_pairs={{0,120},{4,124},{8,0},{12,4},{16,8},{20,12},{24,16},{28,20},{32,24... | collective-permute-start | bytes 196616 | tf_op jit(solution)/shard_map/ppermute | solution.py:419
  11.8 10.2 %collective-permute-start.3 = (bf16[4,64,128]{2,1,0:T(8,128)(2,1)S(1)}, bf16[4,64,128]{2,1,0:T(8,128)(2,1)S(1)}, u32[]{:S(2)}, u32[]{:S(2)}) collective-permute-start(bf16[4,64,128]{2,1,0:T(8,128)(2,1)S(1)} %get-tuple-element.35), channel_id=1, source_target_pairs={{0,64},{4,68},{8,72},{12,76},{16,80},{20,84},{24,88},{28,92},{32,9... | collective-permute-start | bytes 196616 | tf_op jit(solution)/shard_map/ppermute | solution.py:419
  13.3 18.4 %copy-start.3 = (f32[4096]{0:T(1024)S(1)}, f32[4096]{0:T(1024)}, u32[]{:S(2)}) copy-start(f32[4096]{0:T(1024)} %param.5) | copy-start | bytes 49156
  25.0 11.7 %collective-permute-start.4 = (bf16[4,64,128]{2,1,0:T(8,128)(2,1)S(1)}, bf16[4,64,128]{2,1,0:T(8,128)(2,1)S(1)}, u32[]{:S(2)}, u32[]{:S(2)}) collective-permute-start(bf16[4,64,128]{2,1,0:T(8,128)(2,1)S(1)} %get-tuple-element.38), channel_id=1, source_target_pairs={{0,124},{4,0},{8,4},{12,8},{16,12},{20,16},{24,20},{28,24},{32,28}... | collective-permute-start | bytes 196616 | tf_op jit(solution)/shard_map/ppermute | solution.py:419
  28.2 8.5 %collective-permute-start.5 = (bf16[4,64,128]{2,1,0:T(8,128)(2,1)S(1)}, bf16[4,64,128]{2,1,0:T(8,128)(2,1)S(1)}, u32[]{:S(2)}, u32[]{:S(2)}) collective-permute-start(bf16[4,64,128]{2,1,0:T(8,128)(2,1)S(1)} %get-tuple-element.39), channel_id=1, source_target_pairs={{0,4},{4,8},{8,12},{12,16},{16,20},{20,24},{24,28},{28,32},{32,36}... | collective-permute-start | bytes 196616 | tf_op jit(solution)/shard_map/ppermute | solution.py:419
  28.4 8.3 %collective-permute-start.6 = (bf16[4,64,128]{2,1,0:T(8,128)(2,1)S(1)}, bf16[4,64,128]{2,1,0:T(8,128)(2,1)S(1)}, u32[]{:S(2)}, u32[]{:S(2)}) collective-permute-start(bf16[4,64,128]{2,1,0:T(8,128)(2,1)S(1)} %get-tuple-element.40), channel_id=1, source_target_pairs={{0,120},{4,124},{8,0},{12,4},{16,8},{20,12},{24,16},{28,20},{32,24... | collective-permute-start | bytes 196616 | tf_op jit(solution)/shard_map/ppermute | solution.py:419
  28.7 8.0 %collective-permute-start.7 = (bf16[4,64,128]{2,1,0:T(8,128)(2,1)S(1)}, bf16[4,64,128]{2,1,0:T(8,128)(2,1)S(1)}, u32[]{:S(2)}, u32[]{:S(2)}) collective-permute-start(bf16[4,64,128]{2,1,0:T(8,128)(2,1)S(1)} %get-tuple-element.41), channel_id=1, source_target_pairs={{0,64},{4,68},{8,72},{12,76},{16,80},{20,84},{24,88},{28,92},{32,9... | collective-permute-start | bytes 196616 | tf_op jit(solution)/shard_map/ppermute | solution.py:419
  39.7 10.1 %collective-permute-start.8 = (bf16[4,64,128]{2,1,0:T(8,128)(2,1)S(1)}, bf16[4,64,128]{2,1,0:T(8,128)(2,1)S(1)}, u32[]{:S(2)}, u32[]{:S(2)}) collective-permute-start(bf16[4,64,128]{2,1,0:T(8,128)(2,1)S(1)} %get-tuple-element.43), channel_id=1, source_target_pairs={{0,124},{4,0},{8,4},{12,8},{16,12},{20,16},{24,20},{28,24},{32,28}... | collective-permute-start | bytes 196616 | tf_op jit(solution)/shard_map/ppermute | solution.py:419
  43.2 7.7 %collective-permute-start.9 = (bf16[4,64,128]{2,1,0:T(8,128)(2,1)S(1)}, bf16[4,64,128]{2,1,0:T(8,128)(2,1)S(1)}, u32[]{:S(2)}, u32[]{:S(2)}) collective-permute-start(bf16[4,64,128]{2,1,0:T(8,128)(2,1)S(1)} %get-tuple-element.44), channel_id=1, source_target_pairs={{0,4},{4,8},{8,12},{12,16},{16,20},{20,24},{24,28},{28,32},{32,36}... | collective-permute-start | bytes 196616 | tf_op jit(solution)/shard_map/ppermute | solution.py:419
  43.2 7.7 %collective-permute-start.10 = (bf16[4,64,128]{2,1,0:T(8,128)(2,1)S(1)}, bf16[4,64,128]{2,1,0:T(8,128)(2,1)S(1)}, u32[]{:S(2)}, u32[]{:S(2)}) collective-permute-start(bf16[4,64,128]{2,1,0:T(8,128)(2,1)S(1)} %get-tuple-element.45), channel_id=1, source_target_pairs={{0,120},{4,124},{8,0},{12,4},{16,8},{20,12},{24,16},{28,20},{32,24... | collective-permute-start | bytes 196616 | tf_op jit(solution)/shard_map/ppermute | solution.py:419
  43.7 7.2 %collective-permute-start.11 = (bf16[4,64,128]{2,1,0:T(8,128)(2,1)S(1)}, bf16[4,64,128]{2,1,0:T(8,128)(2,1)S(1)}, u32[]{:S(2)}, u32[]{:S(2)}) collective-permute-start(bf16[4,64,128]{2,1,0:T(8,128)(2,1)S(1)} %get-tuple-element.46), channel_id=1, source_target_pairs={{0,64},{4,68},{8,72},{12,76},{16,80},{20,84},{24,88},{28,92},{32,9... | collective-permute-start | bytes 196616 | tf_op jit(solution)/shard_map/ppermute | solution.py:419
  53.8 10.9 %collective-permute-start.12 = (bf16[4,64,128]{2,1,0:T(8,128)(2,1)S(1)}, bf16[4,64,128]{2,1,0:T(8,128)(2,1)S(1)}, u32[]{:S(2)}, u32[]{:S(2)}) collective-permute-start(bf16[4,64,128]{2,1,0:T(8,128)(2,1)S(1)} %get-tuple-element.49), channel_id=1, source_target_pairs={{0,124},{4,0},{8,4},{12,8},{16,12},{20,16},{24,20},{28,24},{32,28}... | collective-permute-start | bytes 196616 | tf_op jit(solution)/shard_map/ppermute | solution.py:419
  57.7 7.0 %collective-permute-start.13 = (bf16[4,64,128]{2,1,0:T(8,128)(2,1)S(1)}, bf16[4,64,128]{2,1,0:T(8,128)(2,1)S(1)}, u32[]{:S(2)}, u32[]{:S(2)}) collective-permute-start(bf16[4,64,128]{2,1,0:T(8,128)(2,1)S(1)} %get-tuple-element.50), channel_id=1, source_target_pairs={{0,4},{4,8},{8,12},{12,16},{16,20},{20,24},{24,28},{28,32},{32,36}... | collective-permute-start | bytes 196616 | tf_op jit(solution)/shard_map/ppermute | solution.py:419
  57.7 7.0 %collective-permute-start.14 = (bf16[4,64,128]{2,1,0:T(8,128)(2,1)S(1)}, bf16[4,64,128]{2,1,0:T(8,128)(2,1)S(1)}, u32[]{:S(2)}, u32[]{:S(2)}) collective-permute-start(bf16[4,64,128]{2,1,0:T(8,128)(2,1)S(1)} %get-tuple-element.51), channel_id=1, source_target_pairs={{0,120},{4,124},{8,0},{12,4},{16,8},{20,12},{24,16},{28,20},{32,24... | collective-permute-start | bytes 196616 | tf_op jit(solution)/shard_map/ppermute | solution.py:419
  58.2 6.6 %collective-permute-start.15 = (bf16[4,64,128]{2,1,0:T(8,128)(2,1)S(1)}, bf16[4,64,128]{2,1,0:T(8,128)(2,1)S(1)}, u32[]{:S(2)}, u32[]{:S(2)}) collective-permute-start(bf16[4,64,128]{2,1,0:T(8,128)(2,1)S(1)} %get-tuple-element.52), channel_id=1, source_target_pairs={{0,64},{4,68},{8,72},{12,76},{16,80},{20,84},{24,88},{28,92},{32,9... | collective-permute-start | bytes 196616 | tf_op jit(solution)/shard_map/ppermute | solution.py:419
  67.6 13.2 %collective-permute-start.17 = (bf16[64,4096]{1,0:T(8,128)(2,1)S(1)}, bf16[64,4096]{1,0:T(8,128)(2,1)S(1)}, u32[]{:S(2)}, u32[]{:S(2)}) collective-permute-start(bf16[64,4096]{1,0:T(8,128)(2,1)S(1)} %remote_part.7.own.refs_4_), channel_id=1, source_target_pairs={{0,3},{1,0},{2,1},{3,2},{4,7},{5,4},{6,5},{7,6},{8,11},{9,8},{10,9... | collective-permute-start | bytes 1572872 | tf_op jit(solution)/shard_map/ppermute | solution.py:419
  70.7 14.0 %collective-permute-start.16 = (bf16[64,4096]{1,0:T(8,128)(2,1)S(1)}, bf16[64,4096]{1,0:T(8,128)(2,1)S(1)}, u32[]{:S(2)}, u32[]{:S(2)}) collective-permute-start(bf16[64,4096]{1,0:T(8,128)(2,1)S(1)} %remote_part.7.own.refs_4_), channel_id=1, source_target_pairs={{0,1},{1,2},{2,3},{3,0},{4,5},{5,6},{6,7},{7,4},{8,9},{9,10},{10,1... | collective-permute-start | bytes 1572872 | tf_op jit(solution)/shard_map/ppermute | solution.py:419
  85.4 2.7 %collective-permute-start.18 = (f32[96,128]{1,0:T(8,128)S(1)}, f32[96,128]{1,0:T(8,128)S(1)}, u32[]{:S(2)}, u32[]{:S(2)}) collective-permute-start(f32[96,128]{1,0:T(8,128)S(1)} %gram_strip.1), channel_id=1, source_target_pairs={{0,4},{4,0},{8,12},{12,8},{16,20},{20,16},{24,28},{28,24},{32,36},... | collective-permute-start | bytes 147464 | tf_op jit(solution)/shard_map/ppermute | solution.py:424
  88.1 6.8 %collective-permute-start.21 = (f32[96,128]{1,0:T(8,128)S(1)}, f32[96,128]{1,0:T(8,128)S(1)}, u32[]{:S(2)}, u32[]{:S(2)}) collective-permute-start(f32[96,128]{1,0:T(8,128)S(1)} %add.21), channel_id=1, source_target_pairs={{0,24},{4,28},{8,16},{12,20},{16,8},{20,12},{24,0},{28,4},{32,56},... | collective-permute-start | bytes 147464 | tf_op jit(solution)/shard_map/ppermute | solution.py:424
  88.1 6.7 %collective-permute-start.20 = (f32[96,128]{1,0:T(8,128)S(1)}, f32[96,128]{1,0:T(8,128)S(1)}, u32[]{:S(2)}, u32[]{:S(2)}) collective-permute-start(f32[96,128]{1,0:T(8,128)S(1)} %add.21), channel_id=1, source_target_pairs={{0,16},{4,20},{8,24},{12,28},{16,0},{20,4},{24,8},{28,12},{32,48},... | collective-permute-start | bytes 147464 | tf_op jit(solution)/shard_map/ppermute | solution.py:424
  92.7 4.1 %collective-permute-start.19 = (f32[96,128]{1,0:T(8,128)S(1)}, f32[96,128]{1,0:T(8,128)S(1)}, u32[]{:S(2)}, u32[]{:S(2)}) collective-permute-start(f32[96,128]{1,0:T(8,128)S(1)} %add.21), channel_id=1, source_target_pairs={{0,8},{4,12},{8,0},{12,4},{16,24},{20,28},{24,16},{28,20},{32,40},... | collective-permute-start | bytes 147464 | tf_op jit(solution)/shard_map/ppermute | solution.py:424
  92.7 7.8 %collective-permute-start.23 = (bf16[64,2048]{1,0:T(8,128)(2,1)S(1)}, bf16[64,2048]{1,0:T(8,128)(2,1)S(1)}, u32[]{:S(2)}, u32[]{:S(2)}) collective-permute-start(bf16[64,2048]{1,0:T(8,128)(2,1)S(1)} %slice.9), channel_id=1, source_target_pairs={{0,3},{1,0},{2,1},{3,2},{4,7},{5,4},{6,5},{7,6},{8,11},{9,8},{10,9... | collective-permute-start | bytes 786440 | tf_op jit(solution)/shard_map/ppermute | solution.py:419
  92.8 9.0 %collective-permute-start.22 = (bf16[64,2048]{1,0:T(8,128)(2,1)S(1)}, bf16[64,2048]{1,0:T(8,128)(2,1)S(1)}, u32[]{:S(2)}, u32[]{:S(2)}) collective-permute-start(bf16[64,2048]{1,0:T(8,128)(2,1)S(1)} %slice.8), channel_id=1, source_target_pairs={{0,1},{1,2},{2,3},{3,0},{4,5},{5,6},{6,7},{7,4},{8,9},{9,10},{10,1... | collective-permute-start | bytes 786440 | tf_op jit(solution)/shard_map/ppermute | solution.py:419
  101.8 5.8 %collective-permute-start.26 = (f32[96,128]{1,0:T(8,128)S(1)}, f32[96,128]{1,0:T(8,128)S(1)}, u32[]{:S(2)}, u32[]{:S(2)}) collective-permute-start(f32[96,128]{1,0:T(8,128)S(1)} %add_add_fusion.1), channel_id=1, source_target_pairs={{0,96},{4,100},{8,104},{12,108},{16,112},{20,116},{24,120},{28,124... | collective-permute-start | bytes 147464 | tf_op jit(solution)/shard_map/ppermute | solution.py:424
  101.8 5.8 %collective-permute-start.25 = (f32[96,128]{1,0:T(8,128)S(1)}, f32[96,128]{1,0:T(8,128)S(1)}, u32[]{:S(2)}, u32[]{:S(2)}) collective-permute-start(f32[96,128]{1,0:T(8,128)S(1)} %add_add_fusion.1), channel_id=1, source_target_pairs={{0,64},{4,68},{8,72},{12,76},{16,80},{20,84},{24,88},{28,92},{32,9... | collective-permute-start | bytes 147464 | tf_op jit(solution)/shard_map/ppermute | solution.py:424
  103.4 5.1 %collective-permute-start.24 = (f32[96,128]{1,0:T(8,128)S(1)}, f32[96,128]{1,0:T(8,128)S(1)}, u32[]{:S(2)}, u32[]{:S(2)}) collective-permute-start(f32[96,128]{1,0:T(8,128)S(1)} %add_add_fusion.1), channel_id=1, source_target_pairs={{0,32},{4,36},{8,40},{12,44},{16,48},{20,52},{24,56},{28,60},{32,0... | collective-permute-start | bytes 147464 | tf_op jit(solution)/shard_map/ppermute | solution.py:424
  108.5 4.2 %collective-permute-start.29 = (f32[96,128]{1,0:T(8,128)S(1)}, f32[96,128]{1,0:T(8,128)S(1)}, u32[]{:S(2)}, u32[]{:S(2)}) collective-permute-start(f32[96,128]{1,0:T(8,128)S(1)} %add_add_fusion.refs_0_), channel_id=1, source_target_pairs={{0,3},{1,0},{2,1},{3,2},{4,7},{5,4},{6,5},{7,6},{8,11},{9,8},{10,9... | collective-permute-start | bytes 147464 | tf_op jit(solution)/shard_map/ppermute | solution.py:419
  108.8 5.6 %collective-permute-start.28 = (f32[96,128]{1,0:T(8,128)S(1)}, f32[96,128]{1,0:T(8,128)S(1)}, u32[]{:S(2)}, u32[]{:S(2)}) collective-permute-start(f32[96,128]{1,0:T(8,128)S(1)} %add_add_fusion.refs_0_), channel_id=1, source_target_pairs={{0,2},{1,3},{2,0},{3,1},{4,6},{5,7},{6,4},{7,5},{8,10},{9,11},{10,... | collective-permute-start | bytes 147464 | tf_op jit(solution)/shard_map/ppermute | solution.py:419
  111.2 5.3 %collective-permute-start.27 = (f32[96,128]{1,0:T(8,128)S(1)}, f32[96,128]{1,0:T(8,128)S(1)}, u32[]{:S(2)}, u32[]{:S(2)}) collective-permute-start(f32[96,128]{1,0:T(8,128)S(1)} %add_add_fusion.refs_0_), channel_id=1, source_target_pairs={{0,1},{1,2},{2,3},{3,0},{4,5},{5,6},{6,7},{7,4},{8,9},{9,10},{10,1... | collective-permute-start | bytes 147464 | tf_op jit(solution)/shard_map/ppermute | solution.py:419
  (2 other events, 1.8 us)

commit v5 on v4

--- a/solution.py
+++ b/solution.py
@@ -10,10 +10,13 @@
 
 HALO = 4
 FILTER = 4
-UNROLL = 4
+UNROLL = 16
 LATE = 4
-LOADS = 4
+LOADS = 8
+EARLY = 1
 LANES = 128
+COUNT = 32
+SEND = 64
 PANEL = 16
 
 filter_scale = 0.4
@@ -40,22 +43,58 @@
     return hits, ranks[:1]
 
 
-def send_kernel(row_count, at, cols, x, info, *sends):
-    slot_count = cols.shape[1]
-    size = sends[0].shape[2]
-    local_blocks = x.shape[1] // size
+def load(far, blocks, sem, g):
+    slot_count, local_blocks, _, _ = blocks.shape
+    share = local_blocks // LOADS
+    for s in range(slot_count):
+        part = pl.ds(g * share, share)
+        pltpu.make_async_copy(far.at[s, part], blocks.at[s, part], sem).start()
+
+
+def loaded(blocks, sem, g):
+    share = blocks.shape[1] // LOADS
+    part = blocks.at[:, pl.ds(g * share, share)]
+    pltpu.make_async_copy(part, part, sem).wait()
+
+
+def send_kernel(row_count, at, far_cols, far_x, far_onsite, far, *refs):
+    info, own, x, onsite, blocks, *sends, cols, turned, sems = refs
+    slot_count = cols.shape[0]
+    _, local_blocks, size, _ = blocks.shape
     here = at[0]
+    copies = [
+        pltpu.make_async_copy(far_cols, cols, sems.at[0]),
+        pltpu.make_async_copy(far_x, x, sems.at[1]),
+        pltpu.make_async_copy(far_onsite, onsite, sems.at[2]),
+    ]
+    for copy in copies:
+        copy.start()
+    for g in range(EARLY):
+        load(far, blocks, sems.at[3 + g], g)
+    copies[0].wait()
+    per_tile = LANES // local_blocks
+
+    def rows_of(device):
+        start = pl.multiple_of(device // per_tile * LANES, LANES)
+        tile = cols[:, pl.ds(start, LANES)]
+        pad = jnp.zeros((-slot_count % 8, LANES), jnp.int32)
+        turned[:, : slot_count + pad.shape[0]] = jnp.concatenate([tile, pad], axis=0).T
+        start = pl.multiple_of(lax.rem(device, per_tile) * local_blocks, local_blocks)
+        return turned[pl.ds(start, local_blocks), :]
+
     lane = lax.broadcasted_iota(jnp.int32, (local_blocks, LANES), 1)
     named = jnp.zeros((local_blocks, LANES), jnp.float32)
     for q, delta in enumerate(offsets(row_count)):
         asker = lax.rem(here + row_count - delta, row_count)
-        start = pl.multiple_of(asker * local_blocks, local_blocks)
-        values = cols[pl.ds(start, local_blocks), :] - (here * local_blocks - q * local_blocks)
+        values = rows_of(asker) - (here - q) * local_blocks
         group = lane // local_blocks == q
         for s in range(slot_count):
             named = jnp.where(group & (spread(values, s, local_blocks) == lane), 1.0, named)
+    own[...] = rows_of(here)
     hits, ranks = ranks_of(named, local_blocks)
     lane = lane[:1]
+    for copy in copies[1:]:
+        copy.wait()
     for q in range(4):
         mine = (hits > 0) & (lane // local_blocks == q)
         for k in range(HALO):
@@ -63,22 +102,37 @@
             j = jnp.sum(number).astype(jnp.int32)
             info[q * HALO + k] = j
             sends[q][k] = x[:, pl.ds(pl.multiple_of(j * size, size), size)]
-
-
-def send_part(row_count, at, cols, x, size):
+    for g in range(EARLY):
+        loaded(blocks, sems.at[3 + g], g)
+
+
+def send_part(row_count, at, cols, x, onsite, blocks):
+    _, local_blocks, size, _ = blocks.shape
     send = jax.ShapeDtypeStruct((HALO, x.shape[0], size), jnp.bfloat16)
+    whole = [jax.ShapeDtypeStruct(v.shape, v.dtype) for v in (x, onsite, blocks)]
+    hbm = pl.BlockSpec(memory_space=pltpu.HBM)
     return pl.pallas_call(
         functools.partial(send_kernel, row_count),
-        out_shape=(jax.ShapeDtypeStruct((4 * HALO,), jnp.int32),) + (send,) * 4,
-        in_specs=[smem] + [vmem] * 2,
-        out_specs=(smem,) + (vmem,) * 4,
+        out_shape=(
+            jax.ShapeDtypeStruct((4 * HALO,), jnp.int32),
+            jax.ShapeDtypeStruct((local_blocks, LANES), jnp.int32),
+            *whole,
+        )
+        + (send,) * 4,
+        in_specs=[smem] + [hbm] * 4,
+        out_specs=(smem,) + (vmem,) * 8,
+        scratch_shapes=[
+            pltpu.VMEM(cols.shape, jnp.int32),
+            pltpu.VMEM((LANES, LANES), jnp.int32),
+            pltpu.SemaphoreType.DMA((3 + EARLY,)),
+        ],
         compiler_params=grant,
         name="send_part",
-    )(at, cols, x)
-
-
-def build_table(row_count, here, values):
-    rows, slot_count = values.shape
+    )(at, *[far_away(v) for v in (cols, x, onsite, blocks)])
+
+
+def build_table(row_count, here, slot_count, values, info):
+    rows = values.shape[0]
     lane = lax.broadcasted_iota(jnp.int32, (rows, LANES), 1)
     ids = jnp.zeros((rows, LANES), jnp.int32)
     for q, delta in enumerate(offsets(row_count)):
@@ -106,7 +160,10 @@
         table = jnp.where(lane == rank, s * 64 + place, table)
     extra = (lane < slot_count - LATE) & ((table & 63) > rows)
     count = jnp.sum(extra.astype(jnp.float32)).astype(jnp.int32)
-    return jnp.where(lane == LANES // 2, count, table)
+    table = jnp.where(lane == COUNT, count, table)
+    for k in range(4 * HALO):
+        table = jnp.where(lane == SEND + k, info[k], table)
+    return table
 
 
 def slot_pairs(table, row, slots, held, blocks, limit):
@@ -121,13 +178,13 @@
     return total
 
 
-def local_rows_of(scale, table, groups, blocks, onsite, prev, y, held):
+def local_rows_of(scale, table, groups, unroll, blocks, onsite, prev, y, held):
     slot_count, local_blocks, size, _ = blocks.shape
 
     @pl.loop(groups[0], groups[1])
     def _(group):
-        for u in range(UNROLL):
-            row = group * UNROLL + u
+        for u in range(unroll):
+            row = group * unroll + u
             early = range(slot_count - LATE)
             total = slot_pairs(table, row, early, held, blocks, local_blocks)
             span = pl.ds(pl.multiple_of(row * size, size), size)
@@ -148,39 +205,33 @@
     local_blocks = blocks.shape[1]
     hold(x, held, local_blocks)
     groups = (0, local_blocks // UNROLL)
-    local_rows_of(scale, table, groups, blocks, onsite, prev, y, held)
-
-
-def first_kernel(scale, row_count, at, cols, far, x, onsite, y, table, blocks, held, near, sems):
+    local_rows_of(scale, table, groups, UNROLL, blocks, onsite, prev, y, held)
+
+
+def first_kernel(scale, row_count, at, info, own, far, started, x, onsite, *refs):
+    y, table, blocks, held, near, sems = refs
     slot_count, local_blocks, _, _ = blocks.shape
-    here = at[0]
     share = local_blocks // LOADS
-
-    def rows(ref, g):
-        return ref.at[:, pl.ds(g * share, share)]
-
-    for g in range(LOADS):
-        for s in range(slot_count):
-            part = pl.ds(g * share, share)
-            pltpu.make_async_copy(far.at[s, part], blocks.at[s, part], sems.at[g]).start()
-    start = pl.multiple_of(here * local_blocks, local_blocks)
-    table[...] = build_table(row_count, here, cols[pl.ds(start, local_blocks), :])
+    for g in range(EARLY, LOADS):
+        load(far, blocks, sems.at[g], g)
+    table[...] = build_table(row_count, at[0], slot_count, own[...], info)
     copy = pltpu.make_async_copy(table, near, sems.at[LOADS])
     copy.start()
     hold(x, held, local_blocks)
     copy.wait()
     for g in range(LOADS):
-        pltpu.make_async_copy(rows(far, g), rows(blocks, g), sems.at[g]).wait()
-        groups = (g * share // UNROLL, (g + 1) * share // UNROLL)
-        local_rows_of(scale, near, groups, blocks, onsite, None, y, held)
-
-
-def remote_kernel(scale, keep, last, info, table, *refs):
+        if g >= EARLY:
+            loaded(blocks, sems.at[g], g)
+        groups = (g, g + 1)
+        local_rows_of(scale, near, groups, share, blocks, onsite, None, y, held)
+
+
+def remote_kernel(scale, keep, last, table, *refs):
     halos, (y_in, x_in, blocks, x), rest = refs[:4], refs[4:8], refs[8:]
     y, sends, held = (rest[0], rest[1:-1], rest[-1]) if keep else (rest[-1], rest[:-2], rest[-2])
     slot_count, local_blocks, size, _ = blocks.shape
     per = halos[0].shape[0]
-    count = table[0, LANES // 2]
+    count = table[0, COUNT]
     hold(x_in, held, local_blocks)
     for q in range(4):
         at = local_blocks + 1 + q * per
@@ -218,7 +269,7 @@
     if not last:
         for q in range(4):
             for k in range(per):
-                j = info[q * per + k]
+                j = table[0, SEND + q * per + k]
                 sends[q][k] = x[:, pl.ds(pl.multiple_of(j * size, size), size)]
 
 
@@ -240,29 +291,31 @@
     )(table, blocks, x, onsite, prev)
 
 
-def first_part(scale, row_count, at, cols, blocks, x, onsite):
-    _, local_blocks, size, _ = blocks.shape
+def first_part(scale, row_count, at, info, own, far, started, x, onsite):
+    _, local_blocks, size, _ = far.shape
     table = (local_blocks, LANES)
+    hbm = pl.BlockSpec(memory_space=pltpu.HBM)
     return pl.pallas_call(
         functools.partial(first_kernel, scale, row_count),
         out_shape=(
             jax.ShapeDtypeStruct(x.shape, jnp.float32),
             jax.ShapeDtypeStruct(table, jnp.int32),
-            jax.ShapeDtypeStruct(blocks.shape, blocks.dtype),
+            jax.ShapeDtypeStruct(far.shape, far.dtype),
         ),
-        in_specs=[smem, vmem, pl.BlockSpec(memory_space=pl.ANY), vmem, vmem],
+        in_specs=[smem, smem, vmem, hbm, vmem, vmem, vmem],
         out_specs=(vmem,) * 3,
         scratch_shapes=[
             pltpu.VMEM((local_blocks + 1, x.shape[0], size), jnp.bfloat16),
             pltpu.SMEM(table, jnp.int32),
             pltpu.SemaphoreType.DMA((LOADS + 1,)),
         ],
+        input_output_aliases={4: 2},
         compiler_params=grant,
         name="first_part",
-    )(at, cols, blocks, x, onsite)
-
-
-def remote_part(scale, keep, last, info, table, halos, y, x, blocks):
+    )(at, info, own, far, started, x, onsite)
+
+
+def remote_part(scale, keep, last, table, halos, y, x, blocks):
     _, local_blocks, size, _ = blocks.shape
     width = y.shape[0]
     per = halos[0].shape[0]
@@ -274,12 +327,12 @@
     return pl.pallas_call(
         functools.partial(remote_kernel, scale, keep, last),
         out_shape=(jax.ShapeDtypeStruct(y.shape, jnp.bfloat16),) + kept + sends,
-        in_specs=[smem] * 2 + [vmem] * 7,
+        in_specs=[smem] + [vmem] * 7,
         out_specs=(vmem,) * (1 + len(kept) + len(sends)),
         scratch_shapes=scratch,
         compiler_params=grant,
         name="remote_part",
-    )(info, table, *halos, y, x, blocks)
+    )(table, *halos, y, x, blocks)
 
 
 def gram_kernel(own, one, three, strip):
@@ -314,7 +367,7 @@
 
 
 def solve_kernel(root, own_ref, *refs):
-    strips, finals, (basis, factor, work, inverse) = refs[:4], refs[4:9], refs[9:]
+    strips, finals, (basis, factor, work, inverse) = refs[:4], refs[4:8], refs[8:]
     own = own_ref[0]
     n = work.shape[0]
     width = n // 4
@@ -388,14 +441,13 @@
         ordered.append(block)
     ordered = jnp.concatenate(ordered, axis=1)
     left = jnp.concatenate(three_parts(ordered), axis=0)
-    span = basis.shape[1] // 2
-    for c in range(2):
-        at = slice(c * span, (c + 1) * span)
-        right = jnp.concatenate(
-            [finals[0][:, at], finals[1][:, at], finals[3 + c][...], finals[2][:, at]], axis=0
+    wide = 512
+    for c in range(0, basis.shape[1], wide):
+        right = jnp.concatenate([f[:, c : c + wide] for f in finals], axis=0)
+        product = jnp.dot(left, right, preferred_element_type=f32)
+        basis[:, c : c + wide] = (
+            product[:width] + product[width : 2 * width] + product[2 * width :]
         )
-        product = jnp.dot(left, right, preferred_element_type=f32)
-        basis[:, at] = product[:width] + product[width : 2 * width] + product[2 * width :]
 
 
 def solve(root, own, strips, finals):
@@ -406,7 +458,7 @@
             jax.ShapeDtypeStruct(finals[0].shape, jnp.float32),
             jax.ShapeDtypeStruct((n, n), jnp.float32),
         ),
-        in_specs=[smem] + [vmem] * 9,
+        in_specs=[smem] + [vmem] * 8,
         out_specs=(vmem,) * 2,
         scratch_shapes=[pltpu.VMEM((n, n), jnp.float32)] * 2,
         compiler_params=grant,
@@ -429,6 +481,10 @@
     while len(terms) > 1:
         terms = [terms[i] + terms[i + 1] for i in range(0, len(terms), 2)]
     return terms[0]
+
+
+def far_away(value):
+    return pltpu.with_memory_space_constraint(value, pltpu.HBM)
 
 
 def body(subspace, onsite, blocks, cols):
@@ -439,35 +495,35 @@
     slot_count, local_blocks, size, _ = blocks.shape
     at = jnp.stack([row_index.astype(jnp.int32), col_index])
     onsite = onsite[None, :]
-    info, *send = send_part(row_count, at, cols, subspace, size)
-    previous, before, x = None, subspace, subspace
+    info, own, x, onsite, held, *send = send_part(row_count, at, cols.T, subspace, onsite, blocks)
+    previous, before = None, x
     for step in range(FILTER):
         scale = filter_scale if step == 0 else 2.0 * filter_scale
         last = step == FILTER - 1
         keep = step < FILTER - 2
         halos = [shift(send[q], "row", -d) for q, d in enumerate(offsets(row_count))]
         if step == 0:
-            partial, table, held = first_part(scale, row_count, at, cols, blocks, x, onsite)
+            partial, table, held = first_part(
+                scale, row_count, at, info, own, blocks, held, x, onsite
+            )
         else:
             partial = local_part(scale, table, held, x, onsite, previous)
-        x, *send = remote_part(scale, keep, last, info, table, halos, partial, x, held)
+        x, *send = remote_part(scale, keep, last, table, halos, partial, x, held)
         previous = before
         if keep:
             before, *send = send
     final = x
-    half = local_rows // 2
     one = shift(final, "col", 1)
     three = shift(final, "col", -1)
-    two = [shift(one[:, :half], "col", 1), shift(three[:, half:], "col", -1)]
+    two = shift(one, "col", 1)
     strip = gram_strip(final, one, three)
     x_bit = row_count // 4
     strip = xor_sum(strip, "row", [1])
     strip = xor_sum(strip, "row", [2, 4, 6])
-    strip, *two = lax.optimization_barrier((strip, *two))
     strip = xor_sum(strip, "row", [x_bit, 2 * x_bit, 3 * x_bit])
     strips = [strip] + [shift(strip, "col", k) for k in (1, 2, 3)]
     root = math.sqrt(row_count * local_rows)
-    return solve(root, at[1:], strips, [final, one, three] + two)
+    return solve(root, at[1:], strips, [final, one, two, three])
 
 
 def solution(mesh):

time: 126 us -> 112 us (0.89)
  Pallas kernels: 47.5 us -> 39.7 us
  starting transfers between devices: 43.8 us -> 39.9 us
  local copies, waits for them, and re-layouts: 2.96 us -> 0 us
    pallas_call x3, Pallas kernels: 15 us -> 10.9 us  [local_part(): pl.pallas_call(functools.partial(local_kernel, scale), out_shape=jax.Shap...]
    pallas_call x4, Pallas kernels: 11.6 us -> 7.64 us  [remote_part(): pl.pallas_call(functools.partial(remote_kernel, scale, keep, last), out_s...]
    ppermute x23 -> x22, starting transfers between devices: 33.4 us -> 30.2 us  [shift(): return lax.ppermute(value, axis, [(i, (i + by) % n) for i in range(n)])]
    unnamed x9 -> x0, local copies, waits for them, and re-layouts: 2.93 us -> none
    ppermute x23 -> x22, waiting for transfers between devices: 25.5 us -> 25 us  [shift(): return lax.ppermute(value, axis, [(i, (i + by) % n) for i in range(n)])]
  transfers between devices with their start and end apart: 30 -> 29, of which waited for: 12 -> 13; matrix products, arithmetic and copies ran while one was open for 0% -> 0% of each run, Pallas kernels for 19% -> 16%
where the time goes in v5:
time: 112 us
  starting transfers between devices  39.9 us (36%)
  Pallas kernels  39.7 us (35%)
  waiting for transfers between devices  31.3 us (28%)
    ppermute x22, starting transfers between devices, shift(): return lax.ppermute(value, axis, [(i, (i + by) % n) for i in range(n)])  30.2 us
    ppermute x22, waiting for transfers between devices, shift(): return lax.ppermute(value, axis, [(i, (i + by) % n) for i in range(n)])  25 us
    pallas_call x3, Pallas kernels, local_part(): pl.pallas_call(functools.partial(local_kernel, scale), out_shape=jax.Shap...  10.9 us
    pallas_call x1, Pallas kernels, solve(): pl.pallas_call(functools.partial(solve_kernel, root), out_shape=(jax.Shap...  9.89 us
    ppermute x7, starting transfers between devices, swap(): return lax.ppermute(value, axis, [(i, i ^ mask) for i in range(n)])  9.7 us
    pallas_call x4, Pallas kernels, remote_part(): pl.pallas_call(functools.partial(remote_kernel, scale, keep, last), out_s...  7.64 us
    pallas_call x1, Pallas kernels, first_part(): pl.pallas_call(functools.partial(first_kernel, scale, row_count), out_sha...  7.54 us
    ppermute x7, waiting for transfers between devices, swap(): return lax.ppermute(value, axis, [(i, i ^ mask) for i in range(n)])  6.3 us
  transfers between devices with their start and end apart: 29, of which 13 were waited for; matrix products, arithmetic and copies ran while one was open for 0% of the time, Pallas kernels for 16%

profile of v5, /device:TPU:0, one launch (start us, length us, event | category | flops | bytes accessed | tf_op | source)
XLA Modules:
  0.0 111.8 jit_solution(4806743346692783490)
XLA Ops:
  0.7 3.0 %send_part.1 = (s32[16]{0:T(128)S(1)}, s32[32,128]{1,0:T(8,128)S(1)}, bf16[64,4096]{1,0:T(8,128)(2,1)S(1)}, f32[1,4096]{1,0:T(1,128)S(1)}, bf16[20,32,128,128]{3...) custom-call(s32[2]{0:T(128)S(1)} %pad_add_fusion.at, ...), custom_call_target="tpu_custom_call" | custom-call | tf_op jit(solution)/shard_map/send_part/pallas_call | solution.py:114
  3.8 5.8 %collective-permute-start = (bf16[4,64,128]{2,1,0:T(8,128)(2,1)S(1)}, bf16[4,64,128]{2,1,0:T(8,128)(2,1)S(1)}, u32[]{:S(2)}, u32[]{:S(2)}) collective-permute-start(bf16[4,64,128]{2,1,0:T(8,128)(2,1)S(1)} %get-tuple-element.37), channel_id=1, source_target_pairs={{0,124},{4,0},{8,4},{12,8},{16,12},{20,16},{24,20},{28,24},{32,28}... | collective-permute-start | bytes 196616 | tf_op jit(solution)/shard_map/ppermute | solution.py:471
  9.6 1.1 collective-permute-start.2
  11.5 7.5 %first_part.1 = (f32[64,4096]{1,0:T(8,128)S(1)}, s32[32,128]{1,0:T(8,128)S(1)}, bf16[20,32,128,128]{3,2,1,0:T(8,128)(2,1)S(1)}) custom-call(s32[2]{0:T(128)S(1)} %pad_add_fusion.at, s32[16]{0:T(128)S(1)} %get-tuple-element.31.info, s32[32,128]{1,0:T(8,128)S(1)} %get-tuple-element.32.own, ...), custom_call_target="tpu_custom_call", output_to_operand_aliasing={{2}: (4, {})} | custom-call | tf_op jit(solution)/shard_map/first_part/pallas_call | solution.py:298
  19.0 1.9 %remote_part.4 = (bf16[64,4096]{1,0:T(8,128)(2,1)S(1)}, f32[64,4096]{1,0:T(8,128)S(1)}, bf16[4,64,128]{2,1,0:T(8,128)(2,1)S(1)}, bf16[4,64,128]{2,1,0:T(8,128)(2...) custom-call(s32[32,128]{1,0:T(8,128)S(1)} %get-tuple-element.36.table, ...), custom_call_target="tpu_custom_call" | custom-call | tf_op jit(solution)/shard_map/remote_part/pallas_call | solution.py:327
  21.0 3.3 %collective-permute-start.4 = (bf16[4,64,128]{2,1,0:T(8,128)(2,1)S(1)}, bf16[4,64,128]{2,1,0:T(8,128)(2,1)S(1)}, u32[]{:S(2)}, u32[]{:S(2)}) collective-permute-start(bf16[4,64,128]{2,1,0:T(8,128)(2,1)S(1)} %get-tuple-element.43), channel_id=1, source_target_pairs={{0,124},{4,0},{8,4},{12,8},{16,12},{20,16},{24,20},{28,24},{32,28}... | collective-permute-start | bytes 196616 | tf_op jit(solution)/shard_map/ppermute | solution.py:471
  24.7 3.0 %collective-permute-start.7 = (bf16[4,64,128]{2,1,0:T(8,128)(2,1)S(1)}, bf16[4,64,128]{2,1,0:T(8,128)(2,1)S(1)}, u32[]{:S(2)}, u32[]{:S(2)}) collective-permute-start(bf16[4,64,128]{2,1,0:T(8,128)(2,1)S(1)} %get-tuple-element.46), channel_id=1, source_target_pairs={{0,64},{4,68},{8,72},{12,76},{16,80},{20,84},{24,88},{28,92},{32,9... | collective-permute-start | bytes 196616 | tf_op jit(solution)/shard_map/ppermute | solution.py:471
  27.7 3.6 %local_part.3.refs_4_ = f32[64,4096]{1,0:T(8,128)S(1)} custom-call(s32[32,128]{1,0:T(8,128)S(1)} %get-tuple-element.36.table, bf16[20,32,128,128]{3,2,1,0:T(8,128)(2,1)S(1)} %get-tuple-element.42.refs_6_.blocks, bf16[64,4096]{1,0:T(8,128)(2,1)S(1)} %get-tuple-element.47.x.refs_5_, f32[1,4096]{1,0:T(1,128)S(1)} %get-tuple-element.35.onsite, ...), custom_call_target="tpu_custom_call" | custom-call | tf_op jit(solution)/shard_map/local_part/pallas_call | solution.py:283
  31.4 1.9 %remote_part.5 = (bf16[64,4096]{1,0:T(8,128)(2,1)S(1)}, f32[64,4096]{1,0:T(8,128)S(1)}, bf16[4,64,128]{2,1,0:T(8,128)(2,1)S(1)}, bf16[4,64,128]{2,1,0:T(8,128)(2...) custom-call(s32[32,128]{1,0:T(8,128)S(1)} %get-tuple-element.36.table, ...), custom_call_target="tpu_custom_call" | custom-call | tf_op jit(solution)/shard_map/remote_part/pallas_call | solution.py:327
  33.3 4.9 %collective-permute-start.8 = (bf16[4,64,128]{2,1,0:T(8,128)(2,1)S(1)}, bf16[4,64,128]{2,1,0:T(8,128)(2,1)S(1)}, u32[]{:S(2)}, u32[]{:S(2)}) collective-permute-start(bf16[4,64,128]{2,1,0:T(8,128)(2,1)S(1)} %get-tuple-element.48), channel_id=1, source_target_pairs={{0,124},{4,0},{8,4},{12,8},{16,12},{20,16},{24,20},{28,24},{32,28}... | collective-permute-start | bytes 196616 | tf_op jit(solution)/shard_map/ppermute | solution.py:471
  38.7 3.6 %local_part.4.refs_4_ = f32[64,4096]{1,0:T(8,128)S(1)} custom-call(s32[32,128]{1,0:T(8,128)S(1)} %get-tuple-element.36.table, bf16[20,32,128,128]{3,2,1,0:T(8,128)(2,1)S(1)} %get-tuple-element.42.refs_6_.blocks, bf16[64,4096]{1,0:T(8,128)(2,1)S(1)} %get-tuple-element.52.x.refs_5_, f32[1,4096]{1,0:T(1,128)S(1)} %get-tuple-element.35.onsite, ...), custom_call_target="tpu_custom_call" | custom-call | tf_op jit(solution)/shard_map/local_part/pallas_call | solution.py:283
  42.3 2.9 %collective-permute-done.9.refs_1_ = bf16[4,64,128]{2,1,0:T(8,128)(2,1)S(1)} collective-permute-done((bf16[4,64,128]{2,1,0:T(8,128)(2,1)S(1)}, bf16[4,64,128]{2,1,0:T(8,128)(2,1)S(1)}, u32[]{:S(2)}, u32[]{:S(2)}) %collective-permute-start.9) | collective-permute-done | bytes 65568 | tf_op jit(solution)/shard_map/ppermute | solution.py:471
  45.2 1.9 %remote_part.6 = (bf16[64,4096]{1,0:T(8,128)(2,1)S(1)}, bf16[4,64,128]{2,1,0:T(8,128)(2,1)S(1)}, bf16[4,64,128]{2,1,0:T(8,128)(2,1)S(1)}, bf16[4,64,128]{2,1,0:T(8,128)(2,1)S(1)}, bf16[4,64,128]{2,1,0:T(8,128)(2,1)S(1)}) custom-call(s32[32,128]{1,0:T(8,128)S(1)} %get-tuple-element.36.table, bf16[4,64,128]{2,1,0:T(8,128)(2,1)S(1)} %collective-permute-done.8.refs_0_, ...), custom_call_target="tpu_custom_call" | custom-call | tf_op jit(solution)/shard_map/remote_part/pallas_call | solution.py:327
  47.1 4.6 %collective-permute-start.12 = (bf16[4,64,128]{2,1,0:T(8,128)(2,1)S(1)}, bf16[4,64,128]{2,1,0:T(8,128)(2,1)S(1)}, u32[]{:S(2)}, u32[]{:S(2)}) collective-permute-start(bf16[4,64,128]{2,1,0:T(8,128)(2,1)S(1)} %get-tuple-element.54), channel_id=1, source_target_pairs={{0,124},{4,0},{8,4},{12,8},{16,12},{20,16},{24,20},{28,24},{32,28}... | collective-permute-start | bytes 196616 | tf_op jit(solution)/shard_map/ppermute | solution.py:471
  52.4 3.6 %local_part.5.refs_4_ = f32[64,4096]{1,0:T(8,128)S(1)} custom-call(s32[32,128]{1,0:T(8,128)S(1)} %get-tuple-element.36.table, bf16[20,32,128,128]{3,2,1,0:T(8,128)(2,1)S(1)} %get-tuple-element.42.refs_6_.blocks, bf16[64,4096]{1,0:T(8,128)(2,1)S(1)} %get-tuple-element.58.x.refs_5_, f32[1,4096]{1,0:T(1,128)S(1)} %get-tuple-element.35.onsite, ...), custom_call_target="tpu_custom_call" | custom-call | tf_op jit(solution)/shard_map/local_part/pallas_call | solution.py:283
  56.0 2.7 %collective-permute-done.13.refs_1_ = bf16[4,64,128]{2,1,0:T(8,128)(2,1)S(1)} collective-permute-done((bf16[4,64,128]{2,1,0:T(8,128)(2,1)S(1)}, bf16[4,64,128]{2,1,0:T(8,128)(2,1)S(1)}, u32[]{:S(2)}, u32[]{:S(2)}) %collective-permute-start.13) | collective-permute-done | bytes 65568 | tf_op jit(solution)/shard_map/ppermute | solution.py:471
  58.7 1.9 %remote_part.7.own.refs_4_ = bf16[64,4096]{1,0:T(8,128)(2,1)S(1)} custom-call(s32[32,128]{1,0:T(8,128)S(1)} %get-tuple-element.36.table, bf16[4,64,128]{2,1,0:T(8,128)(2,1)S(1)} %collective-permute-done.12.refs_0_, bf16[4,64,128]{2,1,0:T(8,128)(2,1)S(1)} %collective-permute-done.13.refs_1_, bf16[4,64,128]{2,1,0:T(8,128)(2,1)S(1)} %collective-permute-done.14.refs_2_, ...), custom_call_target="tpu_custom_call" | custom-call | tf_op jit(solution)/shard_map/remote_part/pallas_call | solution.py:327
  60.6 3.1 %collective-permute-start.17 = (bf16[64,4096]{1,0:T(8,128)(2,1)S(1)}, bf16[64,4096]{1,0:T(8,128)(2,1)S(1)}, u32[]{:S(2)}, u32[]{:S(2)}) collective-permute-start(bf16[64,4096]{1,0:T(8,128)(2,1)S(1)} %remote_part.7.own.refs_4_), channel_id=1, source_target_pairs={{0,3},{1,0},{2,1},{3,2},{4,7},{5,4},{6,5},{7,6},{8,11},{9,8},{10,9... | collective-permute-start | bytes 1572872 | tf_op jit(solution)/shard_map/ppermute | solution.py:471
  63.7 10.4 %collective-permute-done.17.three.refs_7_ = bf16[64,4096]{1,0:T(8,128)(2,1)S(1)} collective-permute-done((bf16[64,4096]{1,0:T(8,128)(2,1)S(1)}, bf16[64,4096]{1,0:T(8,128)(2,1)S(1)}, u32[]{:S(2)}, u32[]{:S(2)}) %collective-permute-start.17) | collective-permute-done | bytes 524320 | tf_op jit(solution)/shard_map/ppermute | solution.py:471
  74.1 4.0 %collective-permute-done.16.one.refs_5_ = bf16[64,4096]{1,0:T(8,128)(2,1)S(1)} collective-permute-done((bf16[64,4096]{1,0:T(8,128)(2,1)S(1)}, bf16[64,4096]{1,0:T(8,128)(2,1)S(1)}, u32[]{:S(2)}, u32[]{:S(2)}) %collective-permute-start.16) | collective-permute-done | bytes 524320 | tf_op jit(solution)/shard_map/ppermute | solution.py:471
  78.8 1.4 %collective-permute-start.18 = (f32[96,128]{1,0:T(8,128)S(1)}, f32[96,128]{1,0:T(8,128)S(1)}, u32[]{:S(2)}, u32[]{:S(2)}) collective-permute-start(f32[96,128]{1,0:T(8,128)S(1)} %gram_strip.1), channel_id=1, source_target_pairs={{0,4},{4,0},{8,12},{12,8},{16,20},{20,16},{24,28},{28,24},{32,36},... | collective-permute-start | bytes 147464 | tf_op jit(solution)/shard_map/ppermute | solution.py:476
  81.1 1.9 %collective-permute-start.20 = (f32[96,128]{1,0:T(8,128)S(1)}, f32[96,128]{1,0:T(8,128)S(1)}, u32[]{:S(2)}, u32[]{:S(2)}) collective-permute-start(f32[96,128]{1,0:T(8,128)S(1)} %add.21), channel_id=1, source_target_pairs={{0,16},{4,20},{8,24},{12,28},{16,0},{20,4},{24,8},{28,12},{32,48},... | collective-permute-start | bytes 147464 | tf_op jit(solution)/shard_map/ppermute | solution.py:476
  83.0 2.2 %collective-permute-start.19 = (f32[96,128]{1,0:T(8,128)S(1)}, f32[96,128]{1,0:T(8,128)S(1)}, u32[]{:S(2)}, u32[]{:S(2)}) collective-permute-start(f32[96,128]{1,0:T(8,128)S(1)} %add.21), channel_id=1, source_target_pairs={{0,8},{4,12},{8,0},{12,4},{16,24},{20,28},{24,16},{28,20},{32,40},... | collective-permute-start | bytes 147464 | tf_op jit(solution)/shard_map/ppermute | solution.py:476
  85.2 2.3 %collective-permute-done.21 = f32[96,128]{1,0:T(8,128)S(1)} collective-permute-done((f32[96,128]{1,0:T(8,128)S(1)}, f32[96,128]{1,0:T(8,128)S(1)}, u32[]{:S(2)}, u32[]{:S(2)}) %collective-permute-start.21) | collective-permute-done | bytes 49184 | tf_op jit(solution)/shard_map/ppermute | solution.py:476
  88.9 3.3 %collective-permute-start.22 = (f32[96,128]{1,0:T(8,128)S(1)}, f32[96,128]{1,0:T(8,128)S(1)}, u32[]{:S(2)}, u32[]{:S(2)}) collective-permute-start(f32[96,128]{1,0:T(8,128)S(1)} %add_add_fusion.1), channel_id=1, source_target_pairs={{0,32},{4,36},{8,40},{12,44},{16,48},{20,52},{24,56},{28,60},{32,0... | collective-permute-start | bytes 147464 | tf_op jit(solution)/shard_map/ppermute | solution.py:476
  92.2 1.2 %collective-permute-done.24 = f32[96,128]{1,0:T(8,128)S(1)} collective-permute-done((f32[96,128]{1,0:T(8,128)S(1)}, f32[96,128]{1,0:T(8,128)S(1)}, u32[]{:S(2)}, u32[]{:S(2)}) %collective-permute-start.24) | collective-permute-done | bytes 49184 | tf_op jit(solution)/shard_map/ppermute | solution.py:476
  93.4 1.1 collective-permute-done.23
  95.8 1.2 %collective-permute-start.25 = (f32[96,128]{1,0:T(8,128)S(1)}, f32[96,128]{1,0:T(8,128)S(1)}, u32[]{:S(2)}, u32[]{:S(2)}) collective-permute-start(f32[96,128]{1,0:T(8,128)S(1)} %add_add_fusion.refs_0_), channel_id=1, source_target_pairs={{0,1},{1,2},{2,3},{3,0},{4,5},{5,6},{6,7},{7,4},{8,9},{9,10},{10,1... | collective-permute-start | bytes 147464 | tf_op jit(solution)/shard_map/ppermute | solution.py:471
  96.9 2.1 %collective-permute-done.27.refs_3_ = f32[96,128]{1,0:T(8,128)S(1)} collective-permute-done((f32[96,128]{1,0:T(8,128)S(1)}, f32[96,128]{1,0:T(8,128)S(1)}, u32[]{:S(2)}, u32[]{:S(2)}) %collective-permute-start.27) | collective-permute-done | bytes 49184 | tf_op jit(solution)/shard_map/ppermute | solution.py:471
  99.0 2.0 %collective-permute-done.26.refs_2_ = f32[96,128]{1,0:T(8,128)S(1)} collective-permute-done((f32[96,128]{1,0:T(8,128)S(1)}, f32[96,128]{1,0:T(8,128)S(1)}, u32[]{:S(2)}, u32[]{:S(2)}) %collective-permute-start.26) | collective-permute-done | bytes 49184 | tf_op jit(solution)/shard_map/ppermute | solution.py:471
  101.0 0.9 collective-permute-done.25.refs_1_
  101.9 9.9 %solve.1 = (f32[64,4096]{1,0:T(8,128)}, f32[256,256]{1,0:T(8,128)}) custom-call(s32[1]{0:T(128)} %bitcast.own_ref, f32[96,128]{1,0:T(8,128)S(1)} %add_add_fusion.refs_0_, f32[96,128]{1,0:T(8,128)S(1)} %collective-permute-done.25.refs_1_, f32[96,128]{1,0:T(8,128)S(1)} %collective-permute-done.26.refs_2_, f32[96,128]{1,0:T(8,128)S(1)} %collective-permute-done.27.refs_3_, ...), custom_call_target="tpu_custom_call" | custom-call | tf_op jit(solution)/shard_map/solve/pallas_call | solution.py:455
  (41 shorter events, 6.9 us)
Async XLA Ops:
  3.8 15.2 %collective-permute-start = (bf16[4,64,128]{2,1,0:T(8,128)(2,1)S(1)}, bf16[4,64,128]{2,1,0:T(8,128)(2,1)S(1)}, u32[]{:S(2)}, u32[]{:S(2)}) collective-permute-start(bf16[4,64,128]{2,1,0:T(8,128)(2,1)S(1)} %get-tuple-element.37), channel_id=1, source_target_pairs={{0,124},{4,0},{8,4},{12,8},{16,12},{20,16},{24,20},{28,24},{32,28}... | collective-permute-start | bytes 196616 | tf_op jit(solution)/shard_map/ppermute | solution.py:471
  9.6 9.4 %collective-permute-start.1 = (bf16[4,64,128]{2,1,0:T(8,128)(2,1)S(1)}, bf16[4,64,128]{2,1,0:T(8,128)(2,1)S(1)}, u32[]{:S(2)}, u32[]{:S(2)}) collective-permute-start(bf16[4,64,128]{2,1,0:T(8,128)(2,1)S(1)} %get-tuple-element.38), channel_id=1, source_target_pairs={{0,4},{4,8},{8,12},{12,16},{16,20},{20,24},{24,28},{28,32},{32,36}... | collective-permute-start | bytes 196616 | tf_op jit(solution)/shard_map/ppermute | solution.py:471
  9.6 9.4 %collective-permute-start.2 = (bf16[4,64,128]{2,1,0:T(8,128)(2,1)S(1)}, bf16[4,64,128]{2,1,0:T(8,128)(2,1)S(1)}, u32[]{:S(2)}, u32[]{:S(2)}) collective-permute-start(bf16[4,64,128]{2,1,0:T(8,128)(2,1)S(1)} %get-tuple-element.39), channel_id=1, source_target_pairs={{0,120},{4,124},{8,0},{12,4},{16,8},{20,12},{24,16},{28,20},{32,24... | collective-permute-start | bytes 196616 | tf_op jit(solution)/shard_map/ppermute | solution.py:471
  10.7 8.4 %collective-permute-start.3 = (bf16[4,64,128]{2,1,0:T(8,128)(2,1)S(1)}, bf16[4,64,128]{2,1,0:T(8,128)(2,1)S(1)}, u32[]{:S(2)}, u32[]{:S(2)}) collective-permute-start(bf16[4,64,128]{2,1,0:T(8,128)(2,1)S(1)} %get-tuple-element.40), channel_id=1, source_target_pairs={{0,64},{4,68},{8,72},{12,76},{16,80},{20,84},{24,88},{28,92},{32,9... | collective-permute-start | bytes 196616 | tf_op jit(solution)/shard_map/ppermute | solution.py:471
  21.0 10.4 %collective-permute-start.4 = (bf16[4,64,128]{2,1,0:T(8,128)(2,1)S(1)}, bf16[4,64,128]{2,1,0:T(8,128)(2,1)S(1)}, u32[]{:S(2)}, u32[]{:S(2)}) collective-permute-start(bf16[4,64,128]{2,1,0:T(8,128)(2,1)S(1)} %get-tuple-element.43), channel_id=1, source_target_pairs={{0,124},{4,0},{8,4},{12,8},{16,12},{20,16},{24,20},{28,24},{32,28}... | collective-permute-start | bytes 196616 | tf_op jit(solution)/shard_map/ppermute | solution.py:471
  24.3 7.1 %collective-permute-start.5 = (bf16[4,64,128]{2,1,0:T(8,128)(2,1)S(1)}, bf16[4,64,128]{2,1,0:T(8,128)(2,1)S(1)}, u32[]{:S(2)}, u32[]{:S(2)}) collective-permute-start(bf16[4,64,128]{2,1,0:T(8,128)(2,1)S(1)} %get-tuple-element.44), channel_id=1, source_target_pairs={{0,4},{4,8},{8,12},{12,16},{16,20},{20,24},{24,28},{28,32},{32,36}... | collective-permute-start | bytes 196616 | tf_op jit(solution)/shard_map/ppermute | solution.py:471
  24.5 6.9 %collective-permute-start.6 = (bf16[4,64,128]{2,1,0:T(8,128)(2,1)S(1)}, bf16[4,64,128]{2,1,0:T(8,128)(2,1)S(1)}, u32[]{:S(2)}, u32[]{:S(2)}) collective-permute-start(bf16[4,64,128]{2,1,0:T(8,128)(2,1)S(1)} %get-tuple-element.45), channel_id=1, source_target_pairs={{0,120},{4,124},{8,0},{12,4},{16,8},{20,12},{24,16},{28,20},{32,24... | collective-permute-start | bytes 196616 | tf_op jit(solution)/shard_map/ppermute | solution.py:471
  24.7 6.6 %collective-permute-start.7 = (bf16[4,64,128]{2,1,0:T(8,128)(2,1)S(1)}, bf16[4,64,128]{2,1,0:T(8,128)(2,1)S(1)}, u32[]{:S(2)}, u32[]{:S(2)}) collective-permute-start(bf16[4,64,128]{2,1,0:T(8,128)(2,1)S(1)} %get-tuple-element.46), channel_id=1, source_target_pairs={{0,64},{4,68},{8,72},{12,76},{16,80},{20,84},{24,88},{28,92},{32,9... | collective-permute-start | bytes 196616 | tf_op jit(solution)/shard_map/ppermute | solution.py:471
  33.3 9.0 %collective-permute-start.8 = (bf16[4,64,128]{2,1,0:T(8,128)(2,1)S(1)}, bf16[4,64,128]{2,1,0:T(8,128)(2,1)S(1)}, u32[]{:S(2)}, u32[]{:S(2)}) collective-permute-start(bf16[4,64,128]{2,1,0:T(8,128)(2,1)S(1)} %get-tuple-element.48), channel_id=1, source_target_pairs={{0,124},{4,0},{8,4},{12,8},{16,12},{20,16},{24,20},{28,24},{32,28}... | collective-permute-start | bytes 196616 | tf_op jit(solution)/shard_map/ppermute | solution.py:471
  38.2 7.0 %collective-permute-start.9 = (bf16[4,64,128]{2,1,0:T(8,128)(2,1)S(1)}, bf16[4,64,128]{2,1,0:T(8,128)(2,1)S(1)}, u32[]{:S(2)}, u32[]{:S(2)}) collective-permute-start(bf16[4,64,128]{2,1,0:T(8,128)(2,1)S(1)} %get-tuple-element.49), channel_id=1, source_target_pairs={{0,4},{4,8},{8,12},{12,16},{16,20},{20,24},{24,28},{28,32},{32,36}... | collective-permute-start | bytes 196616 | tf_op jit(solution)/shard_map/ppermute | solution.py:471
  38.2 7.0 %collective-permute-start.10 = (bf16[4,64,128]{2,1,0:T(8,128)(2,1)S(1)}, bf16[4,64,128]{2,1,0:T(8,128)(2,1)S(1)}, u32[]{:S(2)}, u32[]{:S(2)}) collective-permute-start(bf16[4,64,128]{2,1,0:T(8,128)(2,1)S(1)} %get-tuple-element.50), channel_id=1, source_target_pairs={{0,120},{4,124},{8,0},{12,4},{16,8},{20,12},{24,16},{28,20},{32,24... | collective-permute-start | bytes 196616 | tf_op jit(solution)/shard_map/ppermute | solution.py:471
  38.7 6.5 %collective-permute-start.11 = (bf16[4,64,128]{2,1,0:T(8,128)(2,1)S(1)}, bf16[4,64,128]{2,1,0:T(8,128)(2,1)S(1)}, u32[]{:S(2)}, u32[]{:S(2)}) collective-permute-start(bf16[4,64,128]{2,1,0:T(8,128)(2,1)S(1)} %get-tuple-element.51), channel_id=1, source_target_pairs={{0,64},{4,68},{8,72},{12,76},{16,80},{20,84},{24,88},{28,92},{32,9... | collective-permute-start | bytes 196616 | tf_op jit(solution)/shard_map/ppermute | solution.py:471
  47.1 8.9 %collective-permute-start.12 = (bf16[4,64,128]{2,1,0:T(8,128)(2,1)S(1)}, bf16[4,64,128]{2,1,0:T(8,128)(2,1)S(1)}, u32[]{:S(2)}, u32[]{:S(2)}) collective-permute-start(bf16[4,64,128]{2,1,0:T(8,128)(2,1)S(1)} %get-tuple-element.54), channel_id=1, source_target_pairs={{0,124},{4,0},{8,4},{12,8},{16,12},{20,16},{24,20},{28,24},{32,28}... | collective-permute-start | bytes 196616 | tf_op jit(solution)/shard_map/ppermute | solution.py:471
  51.7 7.0 %collective-permute-start.13 = (bf16[4,64,128]{2,1,0:T(8,128)(2,1)S(1)}, bf16[4,64,128]{2,1,0:T(8,128)(2,1)S(1)}, u32[]{:S(2)}, u32[]{:S(2)}) collective-permute-start(bf16[4,64,128]{2,1,0:T(8,128)(2,1)S(1)} %get-tuple-element.55), channel_id=1, source_target_pairs={{0,4},{4,8},{8,12},{12,16},{16,20},{20,24},{24,28},{28,32},{32,36}... | collective-permute-start | bytes 196616 | tf_op jit(solution)/shard_map/ppermute | solution.py:471
  51.7 7.0 %collective-permute-start.14 = (bf16[4,64,128]{2,1,0:T(8,128)(2,1)S(1)}, bf16[4,64,128]{2,1,0:T(8,128)(2,1)S(1)}, u32[]{:S(2)}, u32[]{:S(2)}) collective-permute-start(bf16[4,64,128]{2,1,0:T(8,128)(2,1)S(1)} %get-tuple-element.56), channel_id=1, source_target_pairs={{0,120},{4,124},{8,0},{12,4},{16,8},{20,12},{24,16},{28,20},{32,24... | collective-permute-start | bytes 196616 | tf_op jit(solution)/shard_map/ppermute | solution.py:471
  52.2 6.5 %collective-permute-start.15 = (bf16[4,64,128]{2,1,0:T(8,128)(2,1)S(1)}, bf16[4,64,128]{2,1,0:T(8,128)(2,1)S(1)}, u32[]{:S(2)}, u32[]{:S(2)}) collective-permute-start(bf16[4,64,128]{2,1,0:T(8,128)(2,1)S(1)} %get-tuple-element.57), channel_id=1, source_target_pairs={{0,64},{4,68},{8,72},{12,76},{16,80},{20,84},{24,88},{28,92},{32,9... | collective-permute-start | bytes 196616 | tf_op jit(solution)/shard_map/ppermute | solution.py:471
  60.6 13.6 %collective-permute-start.17 = (bf16[64,4096]{1,0:T(8,128)(2,1)S(1)}, bf16[64,4096]{1,0:T(8,128)(2,1)S(1)}, u32[]{:S(2)}, u32[]{:S(2)}) collective-permute-start(bf16[64,4096]{1,0:T(8,128)(2,1)S(1)} %remote_part.7.own.refs_4_), channel_id=1, source_target_pairs={{0,3},{1,0},{2,1},{3,2},{4,7},{5,4},{6,5},{7,6},{8,11},{9,8},{10,9... | collective-permute-start | bytes 1572872 | tf_op jit(solution)/shard_map/ppermute | solution.py:471
  63.7 14.4 %collective-permute-start.16 = (bf16[64,4096]{1,0:T(8,128)(2,1)S(1)}, bf16[64,4096]{1,0:T(8,128)(2,1)S(1)}, u32[]{:S(2)}, u32[]{:S(2)}) collective-permute-start(bf16[64,4096]{1,0:T(8,128)(2,1)S(1)} %remote_part.7.own.refs_4_), channel_id=1, source_target_pairs={{0,1},{1,2},{2,3},{3,0},{4,5},{5,6},{6,7},{7,4},{8,9},{9,10},{10,1... | collective-permute-start | bytes 1572872 | tf_op jit(solution)/shard_map/ppermute | solution.py:471
  78.8 2.3 %collective-permute-start.18 = (f32[96,128]{1,0:T(8,128)S(1)}, f32[96,128]{1,0:T(8,128)S(1)}, u32[]{:S(2)}, u32[]{:S(2)}) collective-permute-start(f32[96,128]{1,0:T(8,128)S(1)} %gram_strip.1), channel_id=1, source_target_pairs={{0,4},{4,0},{8,12},{12,8},{16,20},{20,16},{24,28},{28,24},{32,36},... | collective-permute-start | bytes 147464 | tf_op jit(solution)/shard_map/ppermute | solution.py:476
  81.1 6.3 %collective-permute-start.21 = (f32[96,128]{1,0:T(8,128)S(1)}, f32[96,128]{1,0:T(8,128)S(1)}, u32[]{:S(2)}, u32[]{:S(2)}) collective-permute-start(f32[96,128]{1,0:T(8,128)S(1)} %add.21), channel_id=1, source_target_pairs={{0,24},{4,28},{8,16},{12,20},{16,8},{20,12},{24,0},{28,4},{32,56},... | collective-permute-start | bytes 147464 | tf_op jit(solution)/shard_map/ppermute | solution.py:476
  81.1 6.3 %collective-permute-start.20 = (f32[96,128]{1,0:T(8,128)S(1)}, f32[96,128]{1,0:T(8,128)S(1)}, u32[]{:S(2)}, u32[]{:S(2)}) collective-permute-start(f32[96,128]{1,0:T(8,128)S(1)} %add.21), channel_id=1, source_target_pairs={{0,16},{4,20},{8,24},{12,28},{16,0},{20,4},{24,8},{28,12},{32,48},... | collective-permute-start | bytes 147464 | tf_op jit(solution)/shard_map/ppermute | solution.py:476
  83.0 5.0 %collective-permute-start.19 = (f32[96,128]{1,0:T(8,128)S(1)}, f32[96,128]{1,0:T(8,128)S(1)}, u32[]{:S(2)}, u32[]{:S(2)}) collective-permute-start(f32[96,128]{1,0:T(8,128)S(1)} %add.21), channel_id=1, source_target_pairs={{0,8},{4,12},{8,0},{12,4},{16,24},{20,28},{24,16},{28,20},{32,40},... | collective-permute-start | bytes 147464 | tf_op jit(solution)/shard_map/ppermute | solution.py:476
  85.2 16.7 %collective-permute-start.28 = (bf16[64,4096]{1,0:T(8,128)(2,1)S(1)}, bf16[64,4096]{1,0:T(8,128)(2,1)S(1)}, u32[]{:S(2)}, u32[]{:S(2)}) collective-permute-start(bf16[64,4096]{1,0:T(8,128)(2,1)S(1)} %collective-permute-done.16.one.refs_5_), channel_id=1, source_target_pairs={{0,1},{1,2},{2,3},{3,0},{4,5},{5,6},{6,7},{7,4},{8,9},{9,10},{10,1... | collective-permute-start | bytes 1572872 | tf_op jit(solution)/shard_map/ppermute | solution.py:471
  88.0 5.4 %collective-permute-start.24 = (f32[96,128]{1,0:T(8,128)S(1)}, f32[96,128]{1,0:T(8,128)S(1)}, u32[]{:S(2)}, u32[]{:S(2)}) collective-permute-start(f32[96,128]{1,0:T(8,128)S(1)} %add_add_fusion.1), channel_id=1, source_target_pairs={{0,96},{4,100},{8,104},{12,108},{16,112},{20,116},{24,120},{28,124... | collective-permute-start | bytes 147464 | tf_op jit(solution)/shard_map/ppermute | solution.py:476
  88.9 5.6 %collective-permute-start.23 = (f32[96,128]{1,0:T(8,128)S(1)}, f32[96,128]{1,0:T(8,128)S(1)}, u32[]{:S(2)}, u32[]{:S(2)}) collective-permute-start(f32[96,128]{1,0:T(8,128)S(1)} %add_add_fusion.1), channel_id=1, source_target_pairs={{0,64},{4,68},{8,72},{12,76},{16,80},{20,84},{24,88},{28,92},{32,9... | collective-permute-start | bytes 147464 | tf_op jit(solution)/shard_map/ppermute | solution.py:476
  88.9 5.9 %collective-permute-start.22 = (f32[96,128]{1,0:T(8,128)S(1)}, f32[96,128]{1,0:T(8,128)S(1)}, u32[]{:S(2)}, u32[]{:S(2)}) collective-permute-start(f32[96,128]{1,0:T(8,128)S(1)} %add_add_fusion.1), channel_id=1, source_target_pairs={{0,32},{4,36},{8,40},{12,44},{16,48},{20,52},{24,56},{28,60},{32,0... | collective-permute-start | bytes 147464 | tf_op jit(solution)/shard_map/ppermute | solution.py:476
  94.8 4.2 %collective-permute-start.27 = (f32[96,128]{1,0:T(8,128)S(1)}, f32[96,128]{1,0:T(8,128)S(1)}, u32[]{:S(2)}, u32[]{:S(2)}) collective-permute-start(f32[96,128]{1,0:T(8,128)S(1)} %add_add_fusion.refs_0_), channel_id=1, source_target_pairs={{0,3},{1,0},{2,1},{3,2},{4,7},{5,4},{6,5},{7,6},{8,11},{9,8},{10,9... | collective-permute-start | bytes 147464 | tf_op jit(solution)/shard_map/ppermute | solution.py:471
  95.3 5.7 %collective-permute-start.26 = (f32[96,128]{1,0:T(8,128)S(1)}, f32[96,128]{1,0:T(8,128)S(1)}, u32[]{:S(2)}, u32[]{:S(2)}) collective-permute-start(f32[96,128]{1,0:T(8,128)S(1)} %add_add_fusion.refs_0_), channel_id=1, source_target_pairs={{0,2},{1,3},{2,0},{3,1},{4,6},{5,7},{6,4},{7,5},{8,10},{9,11},{10,... | collective-permute-start | bytes 147464 | tf_op jit(solution)/shard_map/ppermute | solution.py:471
  95.8 6.2 %collective-permute-start.25 = (f32[96,128]{1,0:T(8,128)S(1)}, f32[96,128]{1,0:T(8,128)S(1)}, u32[]{:S(2)}, u32[]{:S(2)}) collective-permute-start(f32[96,128]{1,0:T(8,128)S(1)} %add_add_fusion.refs_0_), channel_id=1, source_target_pairs={{0,1},{1,2},{2,3},{3,0},{4,5},{5,6},{6,7},{7,4},{8,9},{9,10},{10,1... | collective-permute-start | bytes 147464 | tf_op jit(solution)/shard_map/ppermute | solution.py:471

commit v6 on v5

--- a/solution.py
+++ b/solution.py
@@ -22,8 +22,32 @@
 filter_scale = 0.4
 
 
-def offsets(row_count):
-    return (1, -1, 2, row_count // 2)
+def beside(here, row_count):
+    odd = lax.rem(here, 2)
+    return [here + 1 - 2 * odd, lax.rem(here + row_count - 1 + 2 * odd, row_count)]
+
+
+def sources_of(here, row_count):
+    ahead = [lax.rem(here + by, row_count) for by in (2, row_count // 2)]
+    return beside(here, row_count) + ahead
+
+
+def askers_of(here, row_count):
+    behind = [lax.rem(here + row_count - by, row_count) for by in (2, row_count // 2)]
+    return beside(here, row_count) + behind
+
+
+def exchange(sends, row_count):
+    devices = range(row_count)
+    targets = [
+        [i ^ 1 for i in devices],
+        [(i + 1 if i % 2 else i - 1) % row_count for i in devices],
+        [(i - 2) % row_count for i in devices],
+        [(i - row_count // 2) % row_count for i in devices],
+    ]
+    return [
+        lax.ppermute(send, "row", list(zip(devices, to))) for send, to in zip(sends, targets)
+    ]
 
 
 def spread(values, s, rows):
@@ -84,8 +108,7 @@
 
     lane = lax.broadcasted_iota(jnp.int32, (local_blocks, LANES), 1)
     named = jnp.zeros((local_blocks, LANES), jnp.float32)
-    for q, delta in enumerate(offsets(row_count)):
-        asker = lax.rem(here + row_count - delta, row_count)
+    for q, asker in enumerate(askers_of(here, row_count)):
         values = rows_of(asker) - (here - q) * local_blocks
         group = lane // local_blocks == q
         for s in range(slot_count):
@@ -135,8 +158,7 @@
     rows = values.shape[0]
     lane = lax.broadcasted_iota(jnp.int32, (rows, LANES), 1)
     ids = jnp.zeros((rows, LANES), jnp.int32)
-    for q, delta in enumerate(offsets(row_count)):
-        source = lax.rem(here + row_count + delta, row_count)
+    for q, source in enumerate(sources_of(here, row_count)):
         ids = jnp.where(lane // rows == q, (source - q) * rows + lane, ids)
     columns = [spread(values, s, rows) for s in range(slot_count)]
     named = jnp.zeros((rows, LANES), jnp.float32)
@@ -501,7 +523,7 @@
         scale = filter_scale if step == 0 else 2.0 * filter_scale
         last = step == FILTER - 1
         keep = step < FILTER - 2
-        halos = [shift(send[q], "row", -d) for q, d in enumerate(offsets(row_count))]
+        halos = exchange(send, row_count)
         if step == 0:
             partial, table, held = first_part(
                 scale, row_count, at, info, own, blocks, held, x, onsite

time: 112 us -> 108 us (0.964)
  starting transfers between devices: 39.9 us -> 34.7 us
  waiting for transfers between devices: 31.3 us -> 33 us
    ppermute x22 -> x6, starting transfers between devices: 30.2 us -> 5.19 us  [shift(): return lax.ppermute(value, axis, [(i, (i + by) % n) for i in range(n)])]
    ppermute x0 -> x16, starting transfers between devices: none -> 21 us  [exchange(): lax.ppermute(send, 'row', list(zip(devices, to)))]
    ppermute x0 -> x16, waiting for transfers between devices: none -> 4.47 us  [exchange(): lax.ppermute(send, 'row', list(zip(devices, to)))]
    ppermute x22 -> x6, waiting for transfers between devices: 25 us -> 20.7 us  [shift(): return lax.ppermute(value, axis, [(i, (i + by) % n) for i in range(n)])]
    ppermute x7, waiting for transfers between devices: 6.3 us -> 7.88 us  [swap(): return lax.ppermute(value, axis, [(i, i ^ mask) for i in range(n)])]
    ppermute x7, starting transfers between devices: 9.7 us -> 8.47 us  [swap(): return lax.ppermute(value, axis, [(i, i ^ mask) for i in range(n)])]
  transfers between devices with their start and end apart: 29 -> 29, of which waited for: 13 -> 17; matrix products, arithmetic and copies ran while one was open for 0% -> 0% of each run, Pallas kernels for 16% -> 17%
where the time goes in v6:
time: 108 us
  Pallas kernels  39.7 us (37%)
  starting transfers between devices  34.7 us (32%)
  waiting for transfers between devices  33 us (31%)
    ppermute x16, starting transfers between devices, exchange(): lax.ppermute(send, 'row', list(zip(devices, to)))  21 us
    ppermute x6, waiting for transfers between devices, shift(): return lax.ppermute(value, axis, [(i, (i + by) % n) for i in range(n)])  20.7 us
    pallas_call x3, Pallas kernels, local_part(): pl.pallas_call(functools.partial(local_kernel, scale), out_shape=jax.Shap...  10.9 us
    pallas_call x1, Pallas kernels, solve(): pl.pallas_call(functools.partial(solve_kernel, root), out_shape=(jax.Shap...  9.88 us
    ppermute x7, starting transfers between devices, swap(): return lax.ppermute(value, axis, [(i, i ^ mask) for i in range(n)])  8.47 us
    ppermute x7, waiting for transfers between devices, swap(): return lax.ppermute(value, axis, [(i, i ^ mask) for i in range(n)])  7.88 us
    pallas_call x4, Pallas kernels, remote_part(): pl.pallas_call(functools.partial(remote_kernel, scale, keep, last), out_s...  7.61 us
    pallas_call x1, Pallas kernels, first_part(): pl.pallas_call(functools.partial(first_kernel, scale, row_count), out_sha...  7.54 us
  transfers between devices with their start and end apart: 29, of which 17 were waited for; matrix products, arithmetic and copies ran while one was open for 0% of the time, Pallas kernels for 17%

profile of v6, /device:TPU:0, one launch (start us, length us, event | category | flops | bytes accessed | tf_op | source)
XLA Modules:
  0.0 108.3 jit_solution(112211602216362222)
XLA Ops:
  0.7 3.0 %send_part.1 = (s32[16]{0:T(128)S(1)}, s32[32,128]{1,0:T(8,128)S(1)}, bf16[64,4096]{1,0:T(8,128)(2,1)S(1)}, f32[1,4096]{1,0:T(1,128)S(1)}, bf16[20,32,128,128]{3...) custom-call(s32[2]{0:T(128)S(1)} %pad_add_fusion.at, ...), custom_call_target="tpu_custom_call" | custom-call | tf_op jit(solution)/shard_map/send_part/pallas_call | solution.py:137
  3.9 6.4 %collective-permute-start.1 = (bf16[4,64,128]{2,1,0:T(8,128)(2,1)S(1)}, bf16[4,64,128]{2,1,0:T(8,128)(2,1)S(1)}, u32[]{:S(2)}, u32[]{:S(2)}) collective-permute-start(bf16[4,64,128]{2,1,0:T(8,128)(2,1)S(1)} %get-tuple-element.38), channel_id=1, source_target_pairs={{0,124},{4,8},{8,4},{12,16},{16,12},{20,24},{24,20},{28,32},{32,28... | collective-permute-start | bytes 196616 | tf_op jit(solution)/shard_map/ppermute | solution.py:49
  11.5 7.5 %first_part.1 = (f32[64,4096]{1,0:T(8,128)S(1)}, s32[32,128]{1,0:T(8,128)S(1)}, bf16[20,32,128,128]{3,2,1,0:T(8,128)(2,1)S(1)}) custom-call(s32[2]{0:T(128)S(1)} %pad_add_fusion.at, s32[16]{0:T(128)S(1)} %get-tuple-element.31.info, s32[32,128]{1,0:T(8,128)S(1)} %get-tuple-element.32.own, ...), custom_call_target="tpu_custom_call", output_to_operand_aliasing={{2}: (4, {})} | custom-call | tf_op jit(solution)/shard_map/first_part/pallas_call | solution.py:320
  19.1 1.9 %remote_part.4 = (bf16[64,4096]{1,0:T(8,128)(2,1)S(1)}, f32[64,4096]{1,0:T(8,128)S(1)}, bf16[4,64,128]{2,1,0:T(8,128)(2,1)S(1)}, bf16[4,64,128]{2,1,0:T(8,128)(2...) custom-call(s32[32,128]{1,0:T(8,128)S(1)} %get-tuple-element.36.table, ...), custom_call_target="tpu_custom_call" | custom-call | tf_op jit(solution)/shard_map/remote_part/pallas_call | solution.py:349
  21.1 1.4 %collective-permute-start.5 = (bf16[4,64,128]{2,1,0:T(8,128)(2,1)S(1)}, bf16[4,64,128]{2,1,0:T(8,128)(2,1)S(1)}, u32[]{:S(2)}, u32[]{:S(2)}) collective-permute-start(bf16[4,64,128]{2,1,0:T(8,128)(2,1)S(1)} %get-tuple-element.44), channel_id=1, source_target_pairs={{0,124},{4,8},{8,4},{12,16},{16,12},{20,24},{24,20},{28,32},{32,28... | collective-permute-start | bytes 196616 | tf_op jit(solution)/shard_map/ppermute | solution.py:49
  22.9 1.5 %collective-permute-start.7 = (bf16[4,64,128]{2,1,0:T(8,128)(2,1)S(1)}, bf16[4,64,128]{2,1,0:T(8,128)(2,1)S(1)}, u32[]{:S(2)}, u32[]{:S(2)}) collective-permute-start(bf16[4,64,128]{2,1,0:T(8,128)(2,1)S(1)} %get-tuple-element.46), channel_id=1, source_target_pairs={{0,64},{4,68},{8,72},{12,76},{16,80},{20,84},{24,88},{28,92},{32,9... | collective-permute-start | bytes 196616 | tf_op jit(solution)/shard_map/ppermute | solution.py:49
  24.5 3.6 %local_part.3.refs_4_ = f32[64,4096]{1,0:T(8,128)S(1)} custom-call(s32[32,128]{1,0:T(8,128)S(1)} %get-tuple-element.36.table, bf16[20,32,128,128]{3,2,1,0:T(8,128)(2,1)S(1)} %get-tuple-element.42.refs_6_.blocks, bf16[64,4096]{1,0:T(8,128)(2,1)S(1)} %get-tuple-element.47.x.refs_5_, f32[1,4096]{1,0:T(1,128)S(1)} %get-tuple-element.35.onsite, ...), custom_call_target="tpu_custom_call" | custom-call | tf_op jit(solution)/shard_map/local_part/pallas_call | solution.py:305
  28.7 1.9 %remote_part.5 = (bf16[64,4096]{1,0:T(8,128)(2,1)S(1)}, f32[64,4096]{1,0:T(8,128)S(1)}, bf16[4,64,128]{2,1,0:T(8,128)(2,1)S(1)}, bf16[4,64,128]{2,1,0:T(8,128)(2...) custom-call(s32[32,128]{1,0:T(8,128)S(1)} %get-tuple-element.36.table, ...), custom_call_target="tpu_custom_call" | custom-call | tf_op jit(solution)/shard_map/remote_part/pallas_call | solution.py:349
  30.6 2.6 %collective-permute-start.8 = (bf16[4,64,128]{2,1,0:T(8,128)(2,1)S(1)}, bf16[4,64,128]{2,1,0:T(8,128)(2,1)S(1)}, u32[]{:S(2)}, u32[]{:S(2)}) collective-permute-start(bf16[4,64,128]{2,1,0:T(8,128)(2,1)S(1)} %get-tuple-element.48), channel_id=1, source_target_pairs={{0,4},{4,0},{8,12},{12,8},{16,20},{20,16},{24,28},{28,24},{32,36},... | collective-permute-start | bytes 196616 | tf_op jit(solution)/shard_map/ppermute | solution.py:49
  33.3 2.2 %collective-permute-start.9 = (bf16[4,64,128]{2,1,0:T(8,128)(2,1)S(1)}, bf16[4,64,128]{2,1,0:T(8,128)(2,1)S(1)}, u32[]{:S(2)}, u32[]{:S(2)}) collective-permute-start(bf16[4,64,128]{2,1,0:T(8,128)(2,1)S(1)} %get-tuple-element.49), channel_id=1, source_target_pairs={{0,124},{4,8},{8,4},{12,16},{16,12},{20,24},{24,20},{28,32},{32,28... | collective-permute-start | bytes 196616 | tf_op jit(solution)/shard_map/ppermute | solution.py:49
  36.2 3.6 %local_part.4.refs_4_ = f32[64,4096]{1,0:T(8,128)S(1)} custom-call(s32[32,128]{1,0:T(8,128)S(1)} %get-tuple-element.36.table, bf16[20,32,128,128]{3,2,1,0:T(8,128)(2,1)S(1)} %get-tuple-element.42.refs_6_.blocks, bf16[64,4096]{1,0:T(8,128)(2,1)S(1)} %get-tuple-element.52.x.refs_5_, f32[1,4096]{1,0:T(1,128)S(1)} %get-tuple-element.35.onsite, ...), custom_call_target="tpu_custom_call" | custom-call | tf_op jit(solution)/shard_map/local_part/pallas_call | solution.py:305
  39.8 1.7 %collective-permute-done.9.refs_1_ = bf16[4,64,128]{2,1,0:T(8,128)(2,1)S(1)} collective-permute-done((bf16[4,64,128]{2,1,0:T(8,128)(2,1)S(1)}, bf16[4,64,128]{2,1,0:T(8,128)(2,1)S(1)}, u32[]{:S(2)}, u32[]{:S(2)}) %collective-permute-start.9) | collective-permute-done | bytes 65568 | tf_op jit(solution)/shard_map/ppermute | solution.py:49
  41.6 1.9 %remote_part.6 = (bf16[64,4096]{1,0:T(8,128)(2,1)S(1)}, bf16[4,64,128]{2,1,0:T(8,128)(2,1)S(1)}, bf16[4,64,128]{2,1,0:T(8,128)(2,1)S(1)}, bf16[4,64,128]{2,1,0:T(8,128)(2,1)S(1)}, bf16[4,64,128]{2,1,0:T(8,128)(2,1)S(1)}) custom-call(s32[32,128]{1,0:T(8,128)S(1)} %get-tuple-element.36.table, bf16[4,64,128]{2,1,0:T(8,128)(2,1)S(1)} %collective-permute-done.8.refs_0_, ...), custom_call_target="tpu_custom_call" | custom-call | tf_op jit(solution)/shard_map/remote_part/pallas_call | solution.py:349
  43.5 1.6 %collective-permute-start.12 = (bf16[4,64,128]{2,1,0:T(8,128)(2,1)S(1)}, bf16[4,64,128]{2,1,0:T(8,128)(2,1)S(1)}, u32[]{:S(2)}, u32[]{:S(2)}) collective-permute-start(bf16[4,64,128]{2,1,0:T(8,128)(2,1)S(1)} %get-tuple-element.54), channel_id=1, source_target_pairs={{0,4},{4,0},{8,12},{12,8},{16,20},{20,16},{24,28},{28,24},{32,36},... | collective-permute-start | bytes 196616 | tf_op jit(solution)/shard_map/ppermute | solution.py:49
  45.1 2.4 %collective-permute-start.13 = (bf16[4,64,128]{2,1,0:T(8,128)(2,1)S(1)}, bf16[4,64,128]{2,1,0:T(8,128)(2,1)S(1)}, u32[]{:S(2)}, u32[]{:S(2)}) collective-permute-start(bf16[4,64,128]{2,1,0:T(8,128)(2,1)S(1)} %get-tuple-element.55), channel_id=1, source_target_pairs={{0,124},{4,8},{8,4},{12,16},{16,12},{20,24},{24,20},{28,32},{32,28... | collective-permute-start | bytes 196616 | tf_op jit(solution)/shard_map/ppermute | solution.py:49
  47.8 3.6 %local_part.5.refs_4_ = f32[64,4096]{1,0:T(8,128)S(1)} custom-call(s32[32,128]{1,0:T(8,128)S(1)} %get-tuple-element.36.table, bf16[20,32,128,128]{3,2,1,0:T(8,128)(2,1)S(1)} %get-tuple-element.42.refs_6_.blocks, bf16[64,4096]{1,0:T(8,128)(2,1)S(1)} %get-tuple-element.58.x.refs_5_, f32[1,4096]{1,0:T(1,128)S(1)} %get-tuple-element.35.onsite, ...), custom_call_target="tpu_custom_call" | custom-call | tf_op jit(solution)/shard_map/local_part/pallas_call | solution.py:305
  52.1 1.5 %collective-permute-done.15.refs_3_ = bf16[4,64,128]{2,1,0:T(8,128)(2,1)S(1)} collective-permute-done((bf16[4,64,128]{2,1,0:T(8,128)(2,1)S(1)}, bf16[4,64,128]{2,1,0:T(8,128)(2,1)S(1)}, u32[]{:S(2)}, u32[]{:S(2)}) %collective-permute-start.15) | collective-permute-done | bytes 65568 | tf_op jit(solution)/shard_map/ppermute | solution.py:49
  53.6 1.8 %remote_part.7.own.refs_4_ = bf16[64,4096]{1,0:T(8,128)(2,1)S(1)} custom-call(s32[32,128]{1,0:T(8,128)S(1)} %get-tuple-element.36.table, bf16[4,64,128]{2,1,0:T(8,128)(2,1)S(1)} %collective-permute-done.12.refs_0_, bf16[4,64,128]{2,1,0:T(8,128)(2,1)S(1)} %collective-permute-done.13.refs_1_, bf16[4,64,128]{2,1,0:T(8,128)(2,1)S(1)} %collective-permute-done.14.refs_2_, ...), custom_call_target="tpu_custom_call" | custom-call | tf_op jit(solution)/shard_map/remote_part/pallas_call | solution.py:349
  55.5 3.1 %collective-permute-start.17 = (bf16[64,4096]{1,0:T(8,128)(2,1)S(1)}, bf16[64,4096]{1,0:T(8,128)(2,1)S(1)}, u32[]{:S(2)}, u32[]{:S(2)}) collective-permute-start(bf16[64,4096]{1,0:T(8,128)(2,1)S(1)} %remote_part.7.own.refs_4_), channel_id=1, source_target_pairs={{0,3},{1,0},{2,1},{3,2},{4,7},{5,4},{6,5},{7,6},{8,11},{9,8},{10,9... | collective-permute-start | bytes 1572872 | tf_op jit(solution)/shard_map/ppermute | solution.py:493
  58.6 12.1 %collective-permute-done.17.three.refs_7_ = bf16[64,4096]{1,0:T(8,128)(2,1)S(1)} collective-permute-done((bf16[64,4096]{1,0:T(8,128)(2,1)S(1)}, bf16[64,4096]{1,0:T(8,128)(2,1)S(1)}, u32[]{:S(2)}, u32[]{:S(2)}) %collective-permute-start.17) | collective-permute-done | bytes 524320 | tf_op jit(solution)/shard_map/ppermute | solution.py:493
  70.6 3.9 %collective-permute-done.16.one.refs_5_ = bf16[64,4096]{1,0:T(8,128)(2,1)S(1)} collective-permute-done((bf16[64,4096]{1,0:T(8,128)(2,1)S(1)}, bf16[64,4096]{1,0:T(8,128)(2,1)S(1)}, u32[]{:S(2)}, u32[]{:S(2)}) %collective-permute-start.16) | collective-permute-done | bytes 524320 | tf_op jit(solution)/shard_map/ppermute | solution.py:493
  75.3 1.1 %collective-permute-done.18 = f32[96,128]{1,0:T(8,128)S(1)} collective-permute-done((f32[96,128]{1,0:T(8,128)S(1)}, f32[96,128]{1,0:T(8,128)S(1)}, u32[]{:S(2)}, u32[]{:S(2)}) %collective-permute-start.18) | collective-permute-done | bytes 49184 | tf_op jit(solution)/shard_map/ppermute | solution.py:498
  76.6 4.0 %collective-permute-start.19 = (f32[96,128]{1,0:T(8,128)S(1)}, f32[96,128]{1,0:T(8,128)S(1)}, u32[]{:S(2)}, u32[]{:S(2)}) collective-permute-start(f32[96,128]{1,0:T(8,128)S(1)} %add.21), channel_id=1, source_target_pairs={{0,8},{4,12},{8,0},{12,4},{16,24},{20,28},{24,16},{28,20},{32,40},... | collective-permute-start | bytes 147464 | tf_op jit(solution)/shard_map/ppermute | solution.py:498
  80.6 1.8 %collective-permute-done.21 = f32[96,128]{1,0:T(8,128)S(1)} collective-permute-done((f32[96,128]{1,0:T(8,128)S(1)}, f32[96,128]{1,0:T(8,128)S(1)}, u32[]{:S(2)}, u32[]{:S(2)}) %collective-permute-start.21) | collective-permute-done | bytes 49184 | tf_op jit(solution)/shard_map/ppermute | solution.py:498
  83.2 2.8 %collective-permute-start.24 = (f32[96,128]{1,0:T(8,128)S(1)}, f32[96,128]{1,0:T(8,128)S(1)}, u32[]{:S(2)}, u32[]{:S(2)}) collective-permute-start(f32[96,128]{1,0:T(8,128)S(1)} %add_add_fusion.1), channel_id=1, source_target_pairs={{0,96},{4,100},{8,104},{12,108},{16,112},{20,116},{24,120},{28,124... | collective-permute-start | bytes 147464 | tf_op jit(solution)/shard_map/ppermute | solution.py:498
  86.0 1.4 %collective-permute-start.22 = (f32[96,128]{1,0:T(8,128)S(1)}, f32[96,128]{1,0:T(8,128)S(1)}, u32[]{:S(2)}, u32[]{:S(2)}) collective-permute-start(f32[96,128]{1,0:T(8,128)S(1)} %add_add_fusion.1), channel_id=1, source_target_pairs={{0,32},{4,36},{8,40},{12,44},{16,48},{20,52},{24,56},{28,60},{32,0... | collective-permute-start | bytes 147464 | tf_op jit(solution)/shard_map/ppermute | solution.py:498
  87.4 1.7 %collective-permute-done.24 = f32[96,128]{1,0:T(8,128)S(1)} collective-permute-done((f32[96,128]{1,0:T(8,128)S(1)}, f32[96,128]{1,0:T(8,128)S(1)}, u32[]{:S(2)}, u32[]{:S(2)}) %collective-permute-start.24) | collective-permute-done | bytes 49184 | tf_op jit(solution)/shard_map/ppermute | solution.py:498
  89.1 2.4 %collective-permute-done.23 = f32[96,128]{1,0:T(8,128)S(1)} collective-permute-done((f32[96,128]{1,0:T(8,128)S(1)}, f32[96,128]{1,0:T(8,128)S(1)}, u32[]{:S(2)}, u32[]{:S(2)}) %collective-permute-start.23) | collective-permute-done | bytes 49184 | tf_op jit(solution)/shard_map/ppermute | solution.py:498
  92.8 0.9 collective-permute-start.25
  93.7 2.1 %collective-permute-done.27.refs_3_ = f32[96,128]{1,0:T(8,128)S(1)} collective-permute-done((f32[96,128]{1,0:T(8,128)S(1)}, f32[96,128]{1,0:T(8,128)S(1)}, u32[]{:S(2)}, u32[]{:S(2)}) %collective-permute-start.27) | collective-permute-done | bytes 49184 | tf_op jit(solution)/shard_map/ppermute | solution.py:493
  95.7 1.8 %collective-permute-done.26.refs_2_ = f32[96,128]{1,0:T(8,128)S(1)} collective-permute-done((f32[96,128]{1,0:T(8,128)S(1)}, f32[96,128]{1,0:T(8,128)S(1)}, u32[]{:S(2)}, u32[]{:S(2)}) %collective-permute-start.26) | collective-permute-done | bytes 49184 | tf_op jit(solution)/shard_map/ppermute | solution.py:493
  98.4 9.9 %solve.1 = (f32[64,4096]{1,0:T(8,128)}, f32[256,256]{1,0:T(8,128)}) custom-call(s32[1]{0:T(128)} %bitcast.own_ref, f32[96,128]{1,0:T(8,128)S(1)} %add_add_fusion.refs_0_, f32[96,128]{1,0:T(8,128)S(1)} %collective-permute-done.25.refs_1_, f32[96,128]{1,0:T(8,128)S(1)} %collective-permute-done.26.refs_2_, f32[96,128]{1,0:T(8,128)S(1)} %collective-permute-done.27.refs_3_, ...), custom_call_target="tpu_custom_call" | custom-call | tf_op jit(solution)/shard_map/solve/pallas_call | solution.py:477
  (41 shorter events, 8.1 us)
Async XLA Ops:
  3.8 15.3 %collective-permute-start = (bf16[4,64,128]{2,1,0:T(8,128)(2,1)S(1)}, bf16[4,64,128]{2,1,0:T(8,128)(2,1)S(1)}, u32[]{:S(2)}, u32[]{:S(2)}) collective-permute-start(bf16[4,64,128]{2,1,0:T(8,128)(2,1)S(1)} %get-tuple-element.37), channel_id=1, source_target_pairs={{0,4},{4,0},{8,12},{12,8},{16,20},{20,16},{24,28},{28,24},{32,36},... | collective-permute-start | bytes 196616 | tf_op jit(solution)/shard_map/ppermute | solution.py:49
  3.9 15.2 %collective-permute-start.1 = (bf16[4,64,128]{2,1,0:T(8,128)(2,1)S(1)}, bf16[4,64,128]{2,1,0:T(8,128)(2,1)S(1)}, u32[]{:S(2)}, u32[]{:S(2)}) collective-permute-start(bf16[4,64,128]{2,1,0:T(8,128)(2,1)S(1)} %get-tuple-element.38), channel_id=1, source_target_pairs={{0,124},{4,8},{8,4},{12,16},{16,12},{20,24},{24,20},{28,32},{32,28... | collective-permute-start | bytes 196616 | tf_op jit(solution)/shard_map/ppermute | solution.py:49
  10.3 8.8 %collective-permute-start.2 = (bf16[4,64,128]{2,1,0:T(8,128)(2,1)S(1)}, bf16[4,64,128]{2,1,0:T(8,128)(2,1)S(1)}, u32[]{:S(2)}, u32[]{:S(2)}) collective-permute-start(bf16[4,64,128]{2,1,0:T(8,128)(2,1)S(1)} %get-tuple-element.39), channel_id=1, source_target_pairs={{0,120},{4,124},{8,0},{12,4},{16,8},{20,12},{24,16},{28,20},{32,24... | collective-permute-start | bytes 196616 | tf_op jit(solution)/shard_map/ppermute | solution.py:49
  10.7 8.4 %collective-permute-start.3 = (bf16[4,64,128]{2,1,0:T(8,128)(2,1)S(1)}, bf16[4,64,128]{2,1,0:T(8,128)(2,1)S(1)}, u32[]{:S(2)}, u32[]{:S(2)}) collective-permute-start(bf16[4,64,128]{2,1,0:T(8,128)(2,1)S(1)} %get-tuple-element.40), channel_id=1, source_target_pairs={{0,64},{4,68},{8,72},{12,76},{16,80},{20,84},{24,88},{28,92},{32,9... | collective-permute-start | bytes 196616 | tf_op jit(solution)/shard_map/ppermute | solution.py:49
  21.0 7.1 %collective-permute-start.4 = (bf16[4,64,128]{2,1,0:T(8,128)(2,1)S(1)}, bf16[4,64,128]{2,1,0:T(8,128)(2,1)S(1)}, u32[]{:S(2)}, u32[]{:S(2)}) collective-permute-start(bf16[4,64,128]{2,1,0:T(8,128)(2,1)S(1)} %get-tuple-element.43), channel_id=1, source_target_pairs={{0,4},{4,0},{8,12},{12,8},{16,20},{20,16},{24,28},{28,24},{32,36},... | collective-permute-start | bytes 196616 | tf_op jit(solution)/shard_map/ppermute | solution.py:49
  21.1 7.1 %collective-permute-start.5 = (bf16[4,64,128]{2,1,0:T(8,128)(2,1)S(1)}, bf16[4,64,128]{2,1,0:T(8,128)(2,1)S(1)}, u32[]{:S(2)}, u32[]{:S(2)}) collective-permute-start(bf16[4,64,128]{2,1,0:T(8,128)(2,1)S(1)} %get-tuple-element.44), channel_id=1, source_target_pairs={{0,124},{4,8},{8,4},{12,16},{16,12},{20,24},{24,20},{28,32},{32,28... | collective-permute-start | bytes 196616 | tf_op jit(solution)/shard_map/ppermute | solution.py:49
  22.5 5.6 %collective-permute-start.6 = (bf16[4,64,128]{2,1,0:T(8,128)(2,1)S(1)}, bf16[4,64,128]{2,1,0:T(8,128)(2,1)S(1)}, u32[]{:S(2)}, u32[]{:S(2)}) collective-permute-start(bf16[4,64,128]{2,1,0:T(8,128)(2,1)S(1)} %get-tuple-element.45), channel_id=1, source_target_pairs={{0,120},{4,124},{8,0},{12,4},{16,8},{20,12},{24,16},{28,20},{32,24... | collective-permute-start | bytes 196616 | tf_op jit(solution)/shard_map/ppermute | solution.py:49
  22.9 5.8 %collective-permute-start.7 = (bf16[4,64,128]{2,1,0:T(8,128)(2,1)S(1)}, bf16[4,64,128]{2,1,0:T(8,128)(2,1)S(1)}, u32[]{:S(2)}, u32[]{:S(2)}) collective-permute-start(bf16[4,64,128]{2,1,0:T(8,128)(2,1)S(1)} %get-tuple-element.46), channel_id=1, source_target_pairs={{0,64},{4,68},{8,72},{12,76},{16,80},{20,84},{24,88},{28,92},{32,9... | collective-permute-start | bytes 196616 | tf_op jit(solution)/shard_map/ppermute | solution.py:49
  30.6 9.2 %collective-permute-start.8 = (bf16[4,64,128]{2,1,0:T(8,128)(2,1)S(1)}, bf16[4,64,128]{2,1,0:T(8,128)(2,1)S(1)}, u32[]{:S(2)}, u32[]{:S(2)}) collective-permute-start(bf16[4,64,128]{2,1,0:T(8,128)(2,1)S(1)} %get-tuple-element.48), channel_id=1, source_target_pairs={{0,4},{4,0},{8,12},{12,8},{16,20},{20,16},{24,28},{28,24},{32,36},... | collective-permute-start | bytes 196616 | tf_op jit(solution)/shard_map/ppermute | solution.py:49
  33.3 8.2 %collective-permute-start.9 = (bf16[4,64,128]{2,1,0:T(8,128)(2,1)S(1)}, bf16[4,64,128]{2,1,0:T(8,128)(2,1)S(1)}, u32[]{:S(2)}, u32[]{:S(2)}) collective-permute-start(bf16[4,64,128]{2,1,0:T(8,128)(2,1)S(1)} %get-tuple-element.49), channel_id=1, source_target_pairs={{0,124},{4,8},{8,4},{12,16},{16,12},{20,24},{24,20},{28,32},{32,28... | collective-permute-start | bytes 196616 | tf_op jit(solution)/shard_map/ppermute | solution.py:49
  35.5 6.0 %collective-permute-start.10 = (bf16[4,64,128]{2,1,0:T(8,128)(2,1)S(1)}, bf16[4,64,128]{2,1,0:T(8,128)(2,1)S(1)}, u32[]{:S(2)}, u32[]{:S(2)}) collective-permute-start(bf16[4,64,128]{2,1,0:T(8,128)(2,1)S(1)} %get-tuple-element.50), channel_id=1, source_target_pairs={{0,120},{4,124},{8,0},{12,4},{16,8},{20,12},{24,16},{28,20},{32,24... | collective-permute-start | bytes 196616 | tf_op jit(solution)/shard_map/ppermute | solution.py:49
  35.8 5.8 %collective-permute-start.11 = (bf16[4,64,128]{2,1,0:T(8,128)(2,1)S(1)}, bf16[4,64,128]{2,1,0:T(8,128)(2,1)S(1)}, u32[]{:S(2)}, u32[]{:S(2)}) collective-permute-start(bf16[4,64,128]{2,1,0:T(8,128)(2,1)S(1)} %get-tuple-element.51), channel_id=1, source_target_pairs={{0,64},{4,68},{8,72},{12,76},{16,80},{20,84},{24,88},{28,92},{32,9... | collective-permute-start | bytes 196616 | tf_op jit(solution)/shard_map/ppermute | solution.py:49
  43.5 8.0 %collective-permute-start.12 = (bf16[4,64,128]{2,1,0:T(8,128)(2,1)S(1)}, bf16[4,64,128]{2,1,0:T(8,128)(2,1)S(1)}, u32[]{:S(2)}, u32[]{:S(2)}) collective-permute-start(bf16[4,64,128]{2,1,0:T(8,128)(2,1)S(1)} %get-tuple-element.54), channel_id=1, source_target_pairs={{0,4},{4,0},{8,12},{12,8},{16,20},{20,16},{24,28},{28,24},{32,36},... | collective-permute-start | bytes 196616 | tf_op jit(solution)/shard_map/ppermute | solution.py:49
  45.1 7.0 %collective-permute-start.13 = (bf16[4,64,128]{2,1,0:T(8,128)(2,1)S(1)}, bf16[4,64,128]{2,1,0:T(8,128)(2,1)S(1)}, u32[]{:S(2)}, u32[]{:S(2)}) collective-permute-start(bf16[4,64,128]{2,1,0:T(8,128)(2,1)S(1)} %get-tuple-element.55), channel_id=1, source_target_pairs={{0,124},{4,8},{8,4},{12,16},{16,12},{20,24},{24,20},{28,32},{32,28... | collective-permute-start | bytes 196616 | tf_op jit(solution)/shard_map/ppermute | solution.py:49
  47.5 4.6 %collective-permute-start.14 = (bf16[4,64,128]{2,1,0:T(8,128)(2,1)S(1)}, bf16[4,64,128]{2,1,0:T(8,128)(2,1)S(1)}, u32[]{:S(2)}, u32[]{:S(2)}) collective-permute-start(bf16[4,64,128]{2,1,0:T(8,128)(2,1)S(1)} %get-tuple-element.56), channel_id=1, source_target_pairs={{0,120},{4,124},{8,0},{12,4},{16,8},{20,12},{24,16},{28,20},{32,24... | collective-permute-start | bytes 196616 | tf_op jit(solution)/shard_map/ppermute | solution.py:49
  47.8 5.8 %collective-permute-start.15 = (bf16[4,64,128]{2,1,0:T(8,128)(2,1)S(1)}, bf16[4,64,128]{2,1,0:T(8,128)(2,1)S(1)}, u32[]{:S(2)}, u32[]{:S(2)}) collective-permute-start(bf16[4,64,128]{2,1,0:T(8,128)(2,1)S(1)} %get-tuple-element.57), channel_id=1, source_target_pairs={{0,64},{4,68},{8,72},{12,76},{16,80},{20,84},{24,88},{28,92},{32,9... | collective-permute-start | bytes 196616 | tf_op jit(solution)/shard_map/ppermute | solution.py:49
  55.5 15.1 %collective-permute-start.17 = (bf16[64,4096]{1,0:T(8,128)(2,1)S(1)}, bf16[64,4096]{1,0:T(8,128)(2,1)S(1)}, u32[]{:S(2)}, u32[]{:S(2)}) collective-permute-start(bf16[64,4096]{1,0:T(8,128)(2,1)S(1)} %remote_part.7.own.refs_4_), channel_id=1, source_target_pairs={{0,3},{1,0},{2,1},{3,2},{4,7},{5,4},{6,5},{7,6},{8,11},{9,8},{10,9... | collective-permute-start | bytes 1572872 | tf_op jit(solution)/shard_map/ppermute | solution.py:493
  58.5 15.9 %collective-permute-start.16 = (bf16[64,4096]{1,0:T(8,128)(2,1)S(1)}, bf16[64,4096]{1,0:T(8,128)(2,1)S(1)}, u32[]{:S(2)}, u32[]{:S(2)}) collective-permute-start(bf16[64,4096]{1,0:T(8,128)(2,1)S(1)} %remote_part.7.own.refs_4_), channel_id=1, source_target_pairs={{0,1},{1,2},{2,3},{3,0},{4,5},{5,6},{6,7},{7,4},{8,9},{9,10},{10,1... | collective-permute-start | bytes 1572872 | tf_op jit(solution)/shard_map/ppermute | solution.py:493
  75.2 1.3 %collective-permute-start.18 = (f32[96,128]{1,0:T(8,128)S(1)}, f32[96,128]{1,0:T(8,128)S(1)}, u32[]{:S(2)}, u32[]{:S(2)}) collective-permute-start(f32[96,128]{1,0:T(8,128)S(1)} %gram_strip.1), channel_id=1, source_target_pairs={{0,4},{4,0},{8,12},{12,8},{16,20},{20,16},{24,28},{28,24},{32,36},... | collective-permute-start | bytes 147464 | tf_op jit(solution)/shard_map/ppermute | solution.py:498
  76.4 5.9 %collective-permute-start.21 = (f32[96,128]{1,0:T(8,128)S(1)}, f32[96,128]{1,0:T(8,128)S(1)}, u32[]{:S(2)}, u32[]{:S(2)}) collective-permute-start(f32[96,128]{1,0:T(8,128)S(1)} %add.21), channel_id=1, source_target_pairs={{0,24},{4,28},{8,16},{12,20},{16,8},{20,12},{24,0},{28,4},{32,56},... | collective-permute-start | bytes 147464 | tf_op jit(solution)/shard_map/ppermute | solution.py:498
  76.5 6.2 %collective-permute-start.20 = (f32[96,128]{1,0:T(8,128)S(1)}, f32[96,128]{1,0:T(8,128)S(1)}, u32[]{:S(2)}, u32[]{:S(2)}) collective-permute-start(f32[96,128]{1,0:T(8,128)S(1)} %add.21), channel_id=1, source_target_pairs={{0,16},{4,20},{8,24},{12,28},{16,0},{20,4},{24,8},{28,12},{32,48},... | collective-permute-start | bytes 147464 | tf_op jit(solution)/shard_map/ppermute | solution.py:498
  76.6 6.6 %collective-permute-start.19 = (f32[96,128]{1,0:T(8,128)S(1)}, f32[96,128]{1,0:T(8,128)S(1)}, u32[]{:S(2)}, u32[]{:S(2)}) collective-permute-start(f32[96,128]{1,0:T(8,128)S(1)} %add.21), channel_id=1, source_target_pairs={{0,8},{4,12},{8,0},{12,4},{16,24},{20,28},{24,16},{28,20},{32,40},... | collective-permute-start | bytes 147464 | tf_op jit(solution)/shard_map/ppermute | solution.py:498
  80.6 17.8 %collective-permute-start.28 = (bf16[64,4096]{1,0:T(8,128)(2,1)S(1)}, bf16[64,4096]{1,0:T(8,128)(2,1)S(1)}, u32[]{:S(2)}, u32[]{:S(2)}) collective-permute-start(bf16[64,4096]{1,0:T(8,128)(2,1)S(1)} %collective-permute-done.16.one.refs_5_), channel_id=1, source_target_pairs={{0,1},{1,2},{2,3},{3,0},{4,5},{5,6},{6,7},{7,4},{8,9},{9,10},{10,1... | collective-permute-start | bytes 1572872 | tf_op jit(solution)/shard_map/ppermute | solution.py:493
  83.2 5.9 %collective-permute-start.24 = (f32[96,128]{1,0:T(8,128)S(1)}, f32[96,128]{1,0:T(8,128)S(1)}, u32[]{:S(2)}, u32[]{:S(2)}) collective-permute-start(f32[96,128]{1,0:T(8,128)S(1)} %add_add_fusion.1), channel_id=1, source_target_pairs={{0,96},{4,100},{8,104},{12,108},{16,112},{20,116},{24,120},{28,124... | collective-permute-start | bytes 147464 | tf_op jit(solution)/shard_map/ppermute | solution.py:498
  86.0 5.6 %collective-permute-start.23 = (f32[96,128]{1,0:T(8,128)S(1)}, f32[96,128]{1,0:T(8,128)S(1)}, u32[]{:S(2)}, u32[]{:S(2)}) collective-permute-start(f32[96,128]{1,0:T(8,128)S(1)} %add_add_fusion.1), channel_id=1, source_target_pairs={{0,64},{4,68},{8,72},{12,76},{16,80},{20,84},{24,88},{28,92},{32,9... | collective-permute-start | bytes 147464 | tf_op jit(solution)/shard_map/ppermute | solution.py:498
  86.0 5.6 %collective-permute-start.22 = (f32[96,128]{1,0:T(8,128)S(1)}, f32[96,128]{1,0:T(8,128)S(1)}, u32[]{:S(2)}, u32[]{:S(2)}) collective-permute-start(f32[96,128]{1,0:T(8,128)S(1)} %add_add_fusion.1), channel_id=1, source_target_pairs={{0,32},{4,36},{8,40},{12,44},{16,48},{20,52},{24,56},{28,60},{32,0... | collective-permute-start | bytes 147464 | tf_op jit(solution)/shard_map/ppermute | solution.py:498
  91.6 4.2 %collective-permute-start.27 = (f32[96,128]{1,0:T(8,128)S(1)}, f32[96,128]{1,0:T(8,128)S(1)}, u32[]{:S(2)}, u32[]{:S(2)}) collective-permute-start(f32[96,128]{1,0:T(8,128)S(1)} %add_add_fusion.refs_0_), channel_id=1, source_target_pairs={{0,3},{1,0},{2,1},{3,2},{4,7},{5,4},{6,5},{7,6},{8,11},{9,8},{10,9... | collective-permute-start | bytes 147464 | tf_op jit(solution)/shard_map/ppermute | solution.py:493
  91.9 5.6 %collective-permute-start.26 = (f32[96,128]{1,0:T(8,128)S(1)}, f32[96,128]{1,0:T(8,128)S(1)}, u32[]{:S(2)}, u32[]{:S(2)}) collective-permute-start(f32[96,128]{1,0:T(8,128)S(1)} %add_add_fusion.refs_0_), channel_id=1, source_target_pairs={{0,2},{1,3},{2,0},{3,1},{4,6},{5,7},{6,4},{7,5},{8,10},{9,11},{10,... | collective-permute-start | bytes 147464 | tf_op jit(solution)/shard_map/ppermute | solution.py:493
  92.8 5.6 %collective-permute-start.25 = (f32[96,128]{1,0:T(8,128)S(1)}, f32[96,128]{1,0:T(8,128)S(1)}, u32[]{:S(2)}, u32[]{:S(2)}) collective-permute-start(f32[96,128]{1,0:T(8,128)S(1)} %add_add_fusion.refs_0_), channel_id=1, source_target_pairs={{0,1},{1,2},{2,3},{3,0},{4,5},{5,6},{6,7},{7,4},{8,9},{9,10},{10,1... | collective-permute-start | bytes 147464 | tf_op jit(solution)/shard_map/ppermute | solution.py:493

commit v7 on v6

--- a/solution.py
+++ b/solution.py
@@ -18,6 +18,7 @@
 COUNT = 32
 SEND = 64
 PANEL = 16
+PIECES = 4
 
 filter_scale = 0.4
 
@@ -115,14 +116,17 @@
             named = jnp.where(group & (spread(values, s, local_blocks) == lane), 1.0, named)
     own[...] = rows_of(here)
     hits, ranks = ranks_of(named, local_blocks)
-    lane = lane[:1]
+    entry = lax.broadcasted_iota(jnp.int32, (4 * HALO, LANES), 0)
+    lane = lax.broadcasted_iota(jnp.int32, (4 * HALO, LANES), 1)
+    chosen = (hits > 0) & (lane // local_blocks == entry // HALO)
+    chosen = chosen & (ranks.astype(jnp.int32) == entry % HALO)
+    numbers = jnp.where(chosen, (lane % local_blocks).astype(jnp.float32), 0.0)
+    numbers = jnp.sum(numbers, axis=1, keepdims=True).astype(jnp.int32)
     for copy in copies[1:]:
         copy.wait()
     for q in range(4):
-        mine = (hits > 0) & (lane // local_blocks == q)
         for k in range(HALO):
-            number = jnp.where(mine & (ranks == k), (lane % local_blocks).astype(jnp.float32), 0.0)
-            j = jnp.sum(number).astype(jnp.int32)
+            j = numbers[q * HALO + k, 0]
             info[q * HALO + k] = j
             sends[q][k] = x[:, pl.ds(pl.multiple_of(j * size, size), size)]
     for g in range(EARLY):
@@ -389,7 +393,8 @@
 
 
 def solve_kernel(root, own_ref, *refs):
-    strips, finals, (basis, factor, work, inverse) = refs[:4], refs[4:8], refs[8:]
+    strips, finals, rest = refs[:4], refs[4:8], refs[8:]
+    far_basis, far_factor, basis, factor, work, inverse, sems = rest
     own = own_ref[0]
     n = work.shape[0]
     width = n // 4
@@ -413,10 +418,10 @@
 
     row_ids = lax.broadcasted_iota(jnp.int32, (PANEL, 128), 0)
     lane_ids = lax.broadcasted_iota(jnp.int32, (PANEL, 128), 1)
+    rows = work[:PANEL, :]
     for r0 in range(0, n, PANEL):
         r1 = r0 + PANEL
         at, tile = r0 % 128, r0 // 128
-        rows = work[r0:r1, :]
         pivots = [
             jnp.broadcast_to(rows[:, r0 + k : r0 + k + 1], (PANEL, 128)) for k in range(PANEL)
         ]
@@ -446,12 +451,19 @@
             left = jnp.concatenate([h, h, m, m, h, l], axis=0)
             right = jnp.concatenate([h, m, h, m, l, h], axis=0)
             low = r1 // 128 * 128
-            update = lax.dot_general(
-                left[:, low:], right, (((0,), (0,)), ((), ())), preferred_element_type=f32
-            )
-            cols = lax.broadcasted_iota(jnp.int32, (n - r1, n), 1)
-            kept = jnp.where((cols >= r0) & (cols < r1), 0.0, work[r1:, :])
-            work[r1:, :] = kept - update[r1 - low :, :]
+            turned = left[:, low:].T
+            for top, end in ((r1, r1 + PANEL), (r1 + PANEL, n)):
+                if top < end:
+                    span = slice(top - low, end - low)
+                    update = jnp.dot(turned[span], right, preferred_element_type=f32)
+                    cols = lax.broadcasted_iota(jnp.int32, (end - top, n), 1)
+                    kept = jnp.where((cols >= r0) & (cols < r1), 0.0, work[top:end, :])
+                    if top == r1:
+                        rows = kept - update
+                    else:
+                        work[top:end, :] = kept - update
+    copies = [pltpu.make_async_copy(factor, far_factor, sems.at[0])]
+    copies[0].start()
     mine = root * inverse[pl.ds(pl.multiple_of(own * width, width), width), :]
     blocks = [mine[:, b * width : (b + 1) * width] for b in range(4)]
     ordered = []
@@ -463,17 +475,25 @@
         ordered.append(block)
     ordered = jnp.concatenate(ordered, axis=1)
     left = jnp.concatenate(three_parts(ordered), axis=0)
-    wide = 512
-    for c in range(0, basis.shape[1], wide):
-        right = jnp.concatenate([f[:, c : c + wide] for f in finals], axis=0)
+    wide = basis.shape[1] // PIECES
+    for piece in range(PIECES):
+        at = slice(piece * wide, (piece + 1) * wide)
+        right = jnp.concatenate([f[:, at] for f in finals], axis=0)
         product = jnp.dot(left, right, preferred_element_type=f32)
-        basis[:, c : c + wide] = (
-            product[:width] + product[width : 2 * width] + product[2 * width :]
+        basis[:, at] = product[:width] + product[width : 2 * width] + product[2 * width :]
+        span = pl.ds(piece * wide, wide)
+        copy = pltpu.make_async_copy(
+            basis.at[:, span], far_basis.at[:, span], sems.at[1 + piece]
         )
+        copy.start()
+        copies.append(copy)
+    for copy in copies:
+        copy.wait()
 
 
 def solve(root, own, strips, finals):
     n = 2 * strips[0].shape[1]
+    hbm = pl.BlockSpec(memory_space=pltpu.HBM)
     return pl.pallas_call(
         functools.partial(solve_kernel, root),
         out_shape=(
@@ -481,8 +501,14 @@
             jax.ShapeDtypeStruct((n, n), jnp.float32),
         ),
         in_specs=[smem] + [vmem] * 8,
-        out_specs=(vmem,) * 2,
-        scratch_shapes=[pltpu.VMEM((n, n), jnp.float32)] * 2,
+        out_specs=(hbm,) * 2,
+        scratch_shapes=[
+            pltpu.VMEM(finals[0].shape, jnp.float32),
+            pltpu.VMEM((n, n), jnp.float32),
+            pltpu.VMEM((n, n), jnp.float32),
+            pltpu.VMEM((n, n), jnp.float32),
+            pltpu.SemaphoreType.DMA((1 + PIECES,)),
+        ],
         compiler_params=grant,
         name="solve",
     )(own, *strips, *finals)

time: 108 us -> 108 us (level)
  no operation moved by 1% of the time
where the time goes in v7:
time: 108 us
  Pallas kernels  39.3 us (36%)
  starting transfers between devices  34.7 us (32%)
  waiting for transfers between devices  33 us (31%)
    ppermute x16, starting transfers between devices, exchange(): lax.ppermute(send, 'row', list(zip(devices, to)))  21 us
    ppermute x6, waiting for transfers between devices, shift(): return lax.ppermute(value, axis, [(i, (i + by) % n) for i in range(n)])  20.7 us
    pallas_call x3, Pallas kernels, local_part(): pl.pallas_call(functools.partial(local_kernel, scale), out_shape=jax.Shap...  10.9 us
    pallas_call x1, Pallas kernels, solve(): pl.pallas_call(functools.partial(solve_kernel, root), out_shape=(jax.Shap...  9.51 us
    ppermute x7, starting transfers between devices, swap(): return lax.ppermute(value, axis, [(i, i ^ mask) for i in range(n)])  8.47 us
    ppermute x7, waiting for transfers between devices, swap(): return lax.ppermute(value, axis, [(i, i ^ mask) for i in range(n)])  7.88 us
    pallas_call x4, Pallas kernels, remote_part(): pl.pallas_call(functools.partial(remote_kernel, scale, keep, last), out_s...  7.61 us
    pallas_call x1, Pallas kernels, first_part(): pl.pallas_call(functools.partial(first_kernel, scale, row_count), out_sha...  7.54 us
  transfers between devices with their start and end apart: 29, of which 17 were waited for; matrix products, arithmetic and copies ran while one was open for 0% of the time, Pallas kernels for 17%

profile of v7, /device:TPU:0, one launch (start us, length us, event | category | flops | bytes accessed | tf_op | source)
XLA Modules:
  0.0 108.1 jit_solution(4479421166711583400)
XLA Ops:
  0.7 3.0 %send_part.1 = (s32[16]{0:T(128)S(1)}, s32[32,128]{1,0:T(8,128)S(1)}, bf16[64,4096]{1,0:T(8,128)(2,1)S(1)}, f32[1,4096]{1,0:T(1,128)S(1)}, bf16[20,32,128,128]{3...) custom-call(s32[2]{0:T(128)S(1)} %pad_add_fusion.at, ...), custom_call_target="tpu_custom_call" | custom-call | tf_op jit(solution)/shard_map/send_part/pallas_call | solution.py:141
  3.9 6.4 %collective-permute-start.1 = (bf16[4,64,128]{2,1,0:T(8,128)(2,1)S(1)}, bf16[4,64,128]{2,1,0:T(8,128)(2,1)S(1)}, u32[]{:S(2)}, u32[]{:S(2)}) collective-permute-start(bf16[4,64,128]{2,1,0:T(8,128)(2,1)S(1)} %get-tuple-element.38), channel_id=1, source_target_pairs={{0,124},{4,8},{8,4},{12,16},{16,12},{20,24},{24,20},{28,32},{32,28... | collective-permute-start | bytes 196616 | tf_op jit(solution)/shard_map/ppermute | solution.py:50
  11.5 7.5 %first_part.1 = (f32[64,4096]{1,0:T(8,128)S(1)}, s32[32,128]{1,0:T(8,128)S(1)}, bf16[20,32,128,128]{3,2,1,0:T(8,128)(2,1)S(1)}) custom-call(s32[2]{0:T(128)S(1)} %pad_add_fusion.at, s32[16]{0:T(128)S(1)} %get-tuple-element.31.info, s32[32,128]{1,0:T(8,128)S(1)} %get-tuple-element.32.own, ...), custom_call_target="tpu_custom_call", output_to_operand_aliasing={{2}: (4, {})} | custom-call | tf_op jit(solution)/shard_map/first_part/pallas_call | solution.py:324
  19.1 1.9 %remote_part.4 = (bf16[64,4096]{1,0:T(8,128)(2,1)S(1)}, f32[64,4096]{1,0:T(8,128)S(1)}, bf16[4,64,128]{2,1,0:T(8,128)(2,1)S(1)}, bf16[4,64,128]{2,1,0:T(8,128)(2...) custom-call(s32[32,128]{1,0:T(8,128)S(1)} %get-tuple-element.36.table, ...), custom_call_target="tpu_custom_call" | custom-call | tf_op jit(solution)/shard_map/remote_part/pallas_call | solution.py:353
  21.1 1.4 %collective-permute-start.5 = (bf16[4,64,128]{2,1,0:T(8,128)(2,1)S(1)}, bf16[4,64,128]{2,1,0:T(8,128)(2,1)S(1)}, u32[]{:S(2)}, u32[]{:S(2)}) collective-permute-start(bf16[4,64,128]{2,1,0:T(8,128)(2,1)S(1)} %get-tuple-element.44), channel_id=1, source_target_pairs={{0,124},{4,8},{8,4},{12,16},{16,12},{20,24},{24,20},{28,32},{32,28... | collective-permute-start | bytes 196616 | tf_op jit(solution)/shard_map/ppermute | solution.py:50
  22.9 1.5 %collective-permute-start.7 = (bf16[4,64,128]{2,1,0:T(8,128)(2,1)S(1)}, bf16[4,64,128]{2,1,0:T(8,128)(2,1)S(1)}, u32[]{:S(2)}, u32[]{:S(2)}) collective-permute-start(bf16[4,64,128]{2,1,0:T(8,128)(2,1)S(1)} %get-tuple-element.46), channel_id=1, source_target_pairs={{0,64},{4,68},{8,72},{12,76},{16,80},{20,84},{24,88},{28,92},{32,9... | collective-permute-start | bytes 196616 | tf_op jit(solution)/shard_map/ppermute | solution.py:50
  24.5 3.6 %local_part.3.refs_4_ = f32[64,4096]{1,0:T(8,128)S(1)} custom-call(s32[32,128]{1,0:T(8,128)S(1)} %get-tuple-element.36.table, bf16[20,32,128,128]{3,2,1,0:T(8,128)(2,1)S(1)} %get-tuple-element.42.refs_6_.blocks, bf16[64,4096]{1,0:T(8,128)(2,1)S(1)} %get-tuple-element.47.x.refs_5_, f32[1,4096]{1,0:T(1,128)S(1)} %get-tuple-element.35.onsite, ...), custom_call_target="tpu_custom_call" | custom-call | tf_op jit(solution)/shard_map/local_part/pallas_call | solution.py:309
  28.7 1.9 %remote_part.5 = (bf16[64,4096]{1,0:T(8,128)(2,1)S(1)}, f32[64,4096]{1,0:T(8,128)S(1)}, bf16[4,64,128]{2,1,0:T(8,128)(2,1)S(1)}, bf16[4,64,128]{2,1,0:T(8,128)(2...) custom-call(s32[32,128]{1,0:T(8,128)S(1)} %get-tuple-element.36.table, ...), custom_call_target="tpu_custom_call" | custom-call | tf_op jit(solution)/shard_map/remote_part/pallas_call | solution.py:353
  30.6 2.6 %collective-permute-start.8 = (bf16[4,64,128]{2,1,0:T(8,128)(2,1)S(1)}, bf16[4,64,128]{2,1,0:T(8,128)(2,1)S(1)}, u32[]{:S(2)}, u32[]{:S(2)}) collective-permute-start(bf16[4,64,128]{2,1,0:T(8,128)(2,1)S(1)} %get-tuple-element.48), channel_id=1, source_target_pairs={{0,4},{4,0},{8,12},{12,8},{16,20},{20,16},{24,28},{28,24},{32,36},... | collective-permute-start | bytes 196616 | tf_op jit(solution)/shard_map/ppermute | solution.py:50
  33.3 2.2 %collective-permute-start.9 = (bf16[4,64,128]{2,1,0:T(8,128)(2,1)S(1)}, bf16[4,64,128]{2,1,0:T(8,128)(2,1)S(1)}, u32[]{:S(2)}, u32[]{:S(2)}) collective-permute-start(bf16[4,64,128]{2,1,0:T(8,128)(2,1)S(1)} %get-tuple-element.49), channel_id=1, source_target_pairs={{0,124},{4,8},{8,4},{12,16},{16,12},{20,24},{24,20},{28,32},{32,28... | collective-permute-start | bytes 196616 | tf_op jit(solution)/shard_map/ppermute | solution.py:50
  36.2 3.6 %local_part.4.refs_4_ = f32[64,4096]{1,0:T(8,128)S(1)} custom-call(s32[32,128]{1,0:T(8,128)S(1)} %get-tuple-element.36.table, bf16[20,32,128,128]{3,2,1,0:T(8,128)(2,1)S(1)} %get-tuple-element.42.refs_6_.blocks, bf16[64,4096]{1,0:T(8,128)(2,1)S(1)} %get-tuple-element.52.x.refs_5_, f32[1,4096]{1,0:T(1,128)S(1)} %get-tuple-element.35.onsite, ...), custom_call_target="tpu_custom_call" | custom-call | tf_op jit(solution)/shard_map/local_part/pallas_call | solution.py:309
  39.8 1.7 %collective-permute-done.9.refs_1_ = bf16[4,64,128]{2,1,0:T(8,128)(2,1)S(1)} collective-permute-done((bf16[4,64,128]{2,1,0:T(8,128)(2,1)S(1)}, bf16[4,64,128]{2,1,0:T(8,128)(2,1)S(1)}, u32[]{:S(2)}, u32[]{:S(2)}) %collective-permute-start.9) | collective-permute-done | bytes 65568 | tf_op jit(solution)/shard_map/ppermute | solution.py:50
  41.6 1.9 %remote_part.6 = (bf16[64,4096]{1,0:T(8,128)(2,1)S(1)}, bf16[4,64,128]{2,1,0:T(8,128)(2,1)S(1)}, bf16[4,64,128]{2,1,0:T(8,128)(2,1)S(1)}, bf16[4,64,128]{2,1,0:T(8,128)(2,1)S(1)}, bf16[4,64,128]{2,1,0:T(8,128)(2,1)S(1)}) custom-call(s32[32,128]{1,0:T(8,128)S(1)} %get-tuple-element.36.table, bf16[4,64,128]{2,1,0:T(8,128)(2,1)S(1)} %collective-permute-done.8.refs_0_, ...), custom_call_target="tpu_custom_call" | custom-call | tf_op jit(solution)/shard_map/remote_part/pallas_call | solution.py:353
  43.5 1.6 %collective-permute-start.12 = (bf16[4,64,128]{2,1,0:T(8,128)(2,1)S(1)}, bf16[4,64,128]{2,1,0:T(8,128)(2,1)S(1)}, u32[]{:S(2)}, u32[]{:S(2)}) collective-permute-start(bf16[4,64,128]{2,1,0:T(8,128)(2,1)S(1)} %get-tuple-element.54), channel_id=1, source_target_pairs={{0,4},{4,0},{8,12},{12,8},{16,20},{20,16},{24,28},{28,24},{32,36},... | collective-permute-start | bytes 196616 | tf_op jit(solution)/shard_map/ppermute | solution.py:50
  45.1 2.4 %collective-permute-start.13 = (bf16[4,64,128]{2,1,0:T(8,128)(2,1)S(1)}, bf16[4,64,128]{2,1,0:T(8,128)(2,1)S(1)}, u32[]{:S(2)}, u32[]{:S(2)}) collective-permute-start(bf16[4,64,128]{2,1,0:T(8,128)(2,1)S(1)} %get-tuple-element.55), channel_id=1, source_target_pairs={{0,124},{4,8},{8,4},{12,16},{16,12},{20,24},{24,20},{28,32},{32,28... | collective-permute-start | bytes 196616 | tf_op jit(solution)/shard_map/ppermute | solution.py:50
  47.8 3.6 %local_part.5.refs_4_ = f32[64,4096]{1,0:T(8,128)S(1)} custom-call(s32[32,128]{1,0:T(8,128)S(1)} %get-tuple-element.36.table, bf16[20,32,128,128]{3,2,1,0:T(8,128)(2,1)S(1)} %get-tuple-element.42.refs_6_.blocks, bf16[64,4096]{1,0:T(8,128)(2,1)S(1)} %get-tuple-element.58.x.refs_5_, f32[1,4096]{1,0:T(1,128)S(1)} %get-tuple-element.35.onsite, ...), custom_call_target="tpu_custom_call" | custom-call | tf_op jit(solution)/shard_map/local_part/pallas_call | solution.py:309
  52.1 1.5 %collective-permute-done.15.refs_3_ = bf16[4,64,128]{2,1,0:T(8,128)(2,1)S(1)} collective-permute-done((bf16[4,64,128]{2,1,0:T(8,128)(2,1)S(1)}, bf16[4,64,128]{2,1,0:T(8,128)(2,1)S(1)}, u32[]{:S(2)}, u32[]{:S(2)}) %collective-permute-start.15) | collective-permute-done | bytes 65568 | tf_op jit(solution)/shard_map/ppermute | solution.py:50
  53.6 1.8 %remote_part.7.own.refs_4_ = bf16[64,4096]{1,0:T(8,128)(2,1)S(1)} custom-call(s32[32,128]{1,0:T(8,128)S(1)} %get-tuple-element.36.table, bf16[4,64,128]{2,1,0:T(8,128)(2,1)S(1)} %collective-permute-done.12.refs_0_, bf16[4,64,128]{2,1,0:T(8,128)(2,1)S(1)} %collective-permute-done.13.refs_1_, bf16[4,64,128]{2,1,0:T(8,128)(2,1)S(1)} %collective-permute-done.14.refs_2_, ...), custom_call_target="tpu_custom_call" | custom-call | tf_op jit(solution)/shard_map/remote_part/pallas_call | solution.py:353
  55.5 3.1 %collective-permute-start.17 = (bf16[64,4096]{1,0:T(8,128)(2,1)S(1)}, bf16[64,4096]{1,0:T(8,128)(2,1)S(1)}, u32[]{:S(2)}, u32[]{:S(2)}) collective-permute-start(bf16[64,4096]{1,0:T(8,128)(2,1)S(1)} %remote_part.7.own.refs_4_), channel_id=1, source_target_pairs={{0,3},{1,0},{2,1},{3,2},{4,7},{5,4},{6,5},{7,6},{8,11},{9,8},{10,9... | collective-permute-start | bytes 1572872 | tf_op jit(solution)/shard_map/ppermute | solution.py:519
  58.6 12.1 %collective-permute-done.17.three.refs_7_ = bf16[64,4096]{1,0:T(8,128)(2,1)S(1)} collective-permute-done((bf16[64,4096]{1,0:T(8,128)(2,1)S(1)}, bf16[64,4096]{1,0:T(8,128)(2,1)S(1)}, u32[]{:S(2)}, u32[]{:S(2)}) %collective-permute-start.17) | collective-permute-done | bytes 524320 | tf_op jit(solution)/shard_map/ppermute | solution.py:519
  70.6 3.9 %collective-permute-done.16.one.refs_5_ = bf16[64,4096]{1,0:T(8,128)(2,1)S(1)} collective-permute-done((bf16[64,4096]{1,0:T(8,128)(2,1)S(1)}, bf16[64,4096]{1,0:T(8,128)(2,1)S(1)}, u32[]{:S(2)}, u32[]{:S(2)}) %collective-permute-start.16) | collective-permute-done | bytes 524320 | tf_op jit(solution)/shard_map/ppermute | solution.py:519
  75.3 1.1 %collective-permute-done.18 = f32[96,128]{1,0:T(8,128)S(1)} collective-permute-done((f32[96,128]{1,0:T(8,128)S(1)}, f32[96,128]{1,0:T(8,128)S(1)}, u32[]{:S(2)}, u32[]{:S(2)}) %collective-permute-start.18) | collective-permute-done | bytes 49184 | tf_op jit(solution)/shard_map/ppermute | solution.py:524
  76.6 4.0 %collective-permute-start.19 = (f32[96,128]{1,0:T(8,128)S(1)}, f32[96,128]{1,0:T(8,128)S(1)}, u32[]{:S(2)}, u32[]{:S(2)}) collective-permute-start(f32[96,128]{1,0:T(8,128)S(1)} %add.21), channel_id=1, source_target_pairs={{0,8},{4,12},{8,0},{12,4},{16,24},{20,28},{24,16},{28,20},{32,40},... | collective-permute-start | bytes 147464 | tf_op jit(solution)/shard_map/ppermute | solution.py:524
  80.6 1.8 %collective-permute-done.21 = f32[96,128]{1,0:T(8,128)S(1)} collective-permute-done((f32[96,128]{1,0:T(8,128)S(1)}, f32[96,128]{1,0:T(8,128)S(1)}, u32[]{:S(2)}, u32[]{:S(2)}) %collective-permute-start.21) | collective-permute-done | bytes 49184 | tf_op jit(solution)/shard_map/ppermute | solution.py:524
  83.2 2.8 %collective-permute-start.24 = (f32[96,128]{1,0:T(8,128)S(1)}, f32[96,128]{1,0:T(8,128)S(1)}, u32[]{:S(2)}, u32[]{:S(2)}) collective-permute-start(f32[96,128]{1,0:T(8,128)S(1)} %add_add_fusion.1), channel_id=1, source_target_pairs={{0,96},{4,100},{8,104},{12,108},{16,112},{20,116},{24,120},{28,124... | collective-permute-start | bytes 147464 | tf_op jit(solution)/shard_map/ppermute | solution.py:524
  86.0 1.4 %collective-permute-start.22 = (f32[96,128]{1,0:T(8,128)S(1)}, f32[96,128]{1,0:T(8,128)S(1)}, u32[]{:S(2)}, u32[]{:S(2)}) collective-permute-start(f32[96,128]{1,0:T(8,128)S(1)} %add_add_fusion.1), channel_id=1, source_target_pairs={{0,32},{4,36},{8,40},{12,44},{16,48},{20,52},{24,56},{28,60},{32,0... | collective-permute-start | bytes 147464 | tf_op jit(solution)/shard_map/ppermute | solution.py:524
  87.4 1.7 %collective-permute-done.24 = f32[96,128]{1,0:T(8,128)S(1)} collective-permute-done((f32[96,128]{1,0:T(8,128)S(1)}, f32[96,128]{1,0:T(8,128)S(1)}, u32[]{:S(2)}, u32[]{:S(2)}) %collective-permute-start.24) | collective-permute-done | bytes 49184 | tf_op jit(solution)/shard_map/ppermute | solution.py:524
  89.1 2.4 %collective-permute-done.23 = f32[96,128]{1,0:T(8,128)S(1)} collective-permute-done((f32[96,128]{1,0:T(8,128)S(1)}, f32[96,128]{1,0:T(8,128)S(1)}, u32[]{:S(2)}, u32[]{:S(2)}) %collective-permute-start.23) | collective-permute-done | bytes 49184 | tf_op jit(solution)/shard_map/ppermute | solution.py:524
  92.8 0.9 collective-permute-start.25
  93.7 2.1 %collective-permute-done.27.refs_3_ = f32[96,128]{1,0:T(8,128)S(1)} collective-permute-done((f32[96,128]{1,0:T(8,128)S(1)}, f32[96,128]{1,0:T(8,128)S(1)}, u32[]{:S(2)}, u32[]{:S(2)}) %collective-permute-start.27) | collective-permute-done | bytes 49184 | tf_op jit(solution)/shard_map/ppermute | solution.py:519
  95.7 1.8 %collective-permute-done.26.refs_2_ = f32[96,128]{1,0:T(8,128)S(1)} collective-permute-done((f32[96,128]{1,0:T(8,128)S(1)}, f32[96,128]{1,0:T(8,128)S(1)}, u32[]{:S(2)}, u32[]{:S(2)}) %collective-permute-start.26) | collective-permute-done | bytes 49184 | tf_op jit(solution)/shard_map/ppermute | solution.py:519
  98.4 9.5 %solve.1 = (f32[64,4096]{1,0:T(8,128)}, f32[256,256]{1,0:T(8,128)}) custom-call(s32[1]{0:T(128)} %bitcast.own_ref, f32[96,128]{1,0:T(8,128)S(1)} %add_add_fusion.refs_0_, f32[96,128]{1,0:T(8,128)S(1)} %collective-permute-done.25.refs_1_, f32[96,128]{1,0:T(8,128)S(1)} %collective-permute-done.26.refs_2_, f32[96,128]{1,0:T(8,128)S(1)} %collective-permute-done.27.refs_3_, ...), custom_call_target="tpu_custom_call" | custom-call | tf_op jit(solution)/shard_map/solve/pallas_call | solution.py:497
  (41 shorter events, 8.1 us)
Async XLA Ops:
  3.8 15.3 %collective-permute-start = (bf16[4,64,128]{2,1,0:T(8,128)(2,1)S(1)}, bf16[4,64,128]{2,1,0:T(8,128)(2,1)S(1)}, u32[]{:S(2)}, u32[]{:S(2)}) collective-permute-start(bf16[4,64,128]{2,1,0:T(8,128)(2,1)S(1)} %get-tuple-element.37), channel_id=1, source_target_pairs={{0,4},{4,0},{8,12},{12,8},{16,20},{20,16},{24,28},{28,24},{32,36},... | collective-permute-start | bytes 196616 | tf_op jit(solution)/shard_map/ppermute | solution.py:50
  3.9 15.2 %collective-permute-start.1 = (bf16[4,64,128]{2,1,0:T(8,128)(2,1)S(1)}, bf16[4,64,128]{2,1,0:T(8,128)(2,1)S(1)}, u32[]{:S(2)}, u32[]{:S(2)}) collective-permute-start(bf16[4,64,128]{2,1,0:T(8,128)(2,1)S(1)} %get-tuple-element.38), channel_id=1, source_target_pairs={{0,124},{4,8},{8,4},{12,16},{16,12},{20,24},{24,20},{28,32},{32,28... | collective-permute-start | bytes 196616 | tf_op jit(solution)/shard_map/ppermute | solution.py:50
  10.3 8.8 %collective-permute-start.2 = (bf16[4,64,128]{2,1,0:T(8,128)(2,1)S(1)}, bf16[4,64,128]{2,1,0:T(8,128)(2,1)S(1)}, u32[]{:S(2)}, u32[]{:S(2)}) collective-permute-start(bf16[4,64,128]{2,1,0:T(8,128)(2,1)S(1)} %get-tuple-element.39), channel_id=1, source_target_pairs={{0,120},{4,124},{8,0},{12,4},{16,8},{20,12},{24,16},{28,20},{32,24... | collective-permute-start | bytes 196616 | tf_op jit(solution)/shard_map/ppermute | solution.py:50
  10.7 8.4 %collective-permute-start.3 = (bf16[4,64,128]{2,1,0:T(8,128)(2,1)S(1)}, bf16[4,64,128]{2,1,0:T(8,128)(2,1)S(1)}, u32[]{:S(2)}, u32[]{:S(2)}) collective-permute-start(bf16[4,64,128]{2,1,0:T(8,128)(2,1)S(1)} %get-tuple-element.40), channel_id=1, source_target_pairs={{0,64},{4,68},{8,72},{12,76},{16,80},{20,84},{24,88},{28,92},{32,9... | collective-permute-start | bytes 196616 | tf_op jit(solution)/shard_map/ppermute | solution.py:50
  21.0 7.1 %collective-permute-start.4 = (bf16[4,64,128]{2,1,0:T(8,128)(2,1)S(1)}, bf16[4,64,128]{2,1,0:T(8,128)(2,1)S(1)}, u32[]{:S(2)}, u32[]{:S(2)}) collective-permute-start(bf16[4,64,128]{2,1,0:T(8,128)(2,1)S(1)} %get-tuple-element.43), channel_id=1, source_target_pairs={{0,4},{4,0},{8,12},{12,8},{16,20},{20,16},{24,28},{28,24},{32,36},... | collective-permute-start | bytes 196616 | tf_op jit(solution)/shard_map/ppermute | solution.py:50
  21.1 7.1 %collective-permute-start.5 = (bf16[4,64,128]{2,1,0:T(8,128)(2,1)S(1)}, bf16[4,64,128]{2,1,0:T(8,128)(2,1)S(1)}, u32[]{:S(2)}, u32[]{:S(2)}) collective-permute-start(bf16[4,64,128]{2,1,0:T(8,128)(2,1)S(1)} %get-tuple-element.44), channel_id=1, source_target_pairs={{0,124},{4,8},{8,4},{12,16},{16,12},{20,24},{24,20},{28,32},{32,28... | collective-permute-start | bytes 196616 | tf_op jit(solution)/shard_map/ppermute | solution.py:50
  22.5 5.6 %collective-permute-start.6 = (bf16[4,64,128]{2,1,0:T(8,128)(2,1)S(1)}, bf16[4,64,128]{2,1,0:T(8,128)(2,1)S(1)}, u32[]{:S(2)}, u32[]{:S(2)}) collective-permute-start(bf16[4,64,128]{2,1,0:T(8,128)(2,1)S(1)} %get-tuple-element.45), channel_id=1, source_target_pairs={{0,120},{4,124},{8,0},{12,4},{16,8},{20,12},{24,16},{28,20},{32,24... | collective-permute-start | bytes 196616 | tf_op jit(solution)/shard_map/ppermute | solution.py:50
  22.9 5.8 %collective-permute-start.7 = (bf16[4,64,128]{2,1,0:T(8,128)(2,1)S(1)}, bf16[4,64,128]{2,1,0:T(8,128)(2,1)S(1)}, u32[]{:S(2)}, u32[]{:S(2)}) collective-permute-start(bf16[4,64,128]{2,1,0:T(8,128)(2,1)S(1)} %get-tuple-element.46), channel_id=1, source_target_pairs={{0,64},{4,68},{8,72},{12,76},{16,80},{20,84},{24,88},{28,92},{32,9... | collective-permute-start | bytes 196616 | tf_op jit(solution)/shard_map/ppermute | solution.py:50
  30.6 9.2 %collective-permute-start.8 = (bf16[4,64,128]{2,1,0:T(8,128)(2,1)S(1)}, bf16[4,64,128]{2,1,0:T(8,128)(2,1)S(1)}, u32[]{:S(2)}, u32[]{:S(2)}) collective-permute-start(bf16[4,64,128]{2,1,0:T(8,128)(2,1)S(1)} %get-tuple-element.48), channel_id=1, source_target_pairs={{0,4},{4,0},{8,12},{12,8},{16,20},{20,16},{24,28},{28,24},{32,36},... | collective-permute-start | bytes 196616 | tf_op jit(solution)/shard_map/ppermute | solution.py:50
  33.3 8.2 %collective-permute-start.9 = (bf16[4,64,128]{2,1,0:T(8,128)(2,1)S(1)}, bf16[4,64,128]{2,1,0:T(8,128)(2,1)S(1)}, u32[]{:S(2)}, u32[]{:S(2)}) collective-permute-start(bf16[4,64,128]{2,1,0:T(8,128)(2,1)S(1)} %get-tuple-element.49), channel_id=1, source_target_pairs={{0,124},{4,8},{8,4},{12,16},{16,12},{20,24},{24,20},{28,32},{32,28... | collective-permute-start | bytes 196616 | tf_op jit(solution)/shard_map/ppermute | solution.py:50
  35.5 6.0 %collective-permute-start.10 = (bf16[4,64,128]{2,1,0:T(8,128)(2,1)S(1)}, bf16[4,64,128]{2,1,0:T(8,128)(2,1)S(1)}, u32[]{:S(2)}, u32[]{:S(2)}) collective-permute-start(bf16[4,64,128]{2,1,0:T(8,128)(2,1)S(1)} %get-tuple-element.50), channel_id=1, source_target_pairs={{0,120},{4,124},{8,0},{12,4},{16,8},{20,12},{24,16},{28,20},{32,24... | collective-permute-start | bytes 196616 | tf_op jit(solution)/shard_map/ppermute | solution.py:50
  35.8 5.8 %collective-permute-start.11 = (bf16[4,64,128]{2,1,0:T(8,128)(2,1)S(1)}, bf16[4,64,128]{2,1,0:T(8,128)(2,1)S(1)}, u32[]{:S(2)}, u32[]{:S(2)}) collective-permute-start(bf16[4,64,128]{2,1,0:T(8,128)(2,1)S(1)} %get-tuple-element.51), channel_id=1, source_target_pairs={{0,64},{4,68},{8,72},{12,76},{16,80},{20,84},{24,88},{28,92},{32,9... | collective-permute-start | bytes 196616 | tf_op jit(solution)/shard_map/ppermute | solution.py:50
  43.5 8.0 %collective-permute-start.12 = (bf16[4,64,128]{2,1,0:T(8,128)(2,1)S(1)}, bf16[4,64,128]{2,1,0:T(8,128)(2,1)S(1)}, u32[]{:S(2)}, u32[]{:S(2)}) collective-permute-start(bf16[4,64,128]{2,1,0:T(8,128)(2,1)S(1)} %get-tuple-element.54), channel_id=1, source_target_pairs={{0,4},{4,0},{8,12},{12,8},{16,20},{20,16},{24,28},{28,24},{32,36},... | collective-permute-start | bytes 196616 | tf_op jit(solution)/shard_map/ppermute | solution.py:50
  45.1 7.0 %collective-permute-start.13 = (bf16[4,64,128]{2,1,0:T(8,128)(2,1)S(1)}, bf16[4,64,128]{2,1,0:T(8,128)(2,1)S(1)}, u32[]{:S(2)}, u32[]{:S(2)}) collective-permute-start(bf16[4,64,128]{2,1,0:T(8,128)(2,1)S(1)} %get-tuple-element.55), channel_id=1, source_target_pairs={{0,124},{4,8},{8,4},{12,16},{16,12},{20,24},{24,20},{28,32},{32,28... | collective-permute-start | bytes 196616 | tf_op jit(solution)/shard_map/ppermute | solution.py:50
  47.5 4.6 %collective-permute-start.14 = (bf16[4,64,128]{2,1,0:T(8,128)(2,1)S(1)}, bf16[4,64,128]{2,1,0:T(8,128)(2,1)S(1)}, u32[]{:S(2)}, u32[]{:S(2)}) collective-permute-start(bf16[4,64,128]{2,1,0:T(8,128)(2,1)S(1)} %get-tuple-element.56), channel_id=1, source_target_pairs={{0,120},{4,124},{8,0},{12,4},{16,8},{20,12},{24,16},{28,20},{32,24... | collective-permute-start | bytes 196616 | tf_op jit(solution)/shard_map/ppermute | solution.py:50
  47.8 5.8 %collective-permute-start.15 = (bf16[4,64,128]{2,1,0:T(8,128)(2,1)S(1)}, bf16[4,64,128]{2,1,0:T(8,128)(2,1)S(1)}, u32[]{:S(2)}, u32[]{:S(2)}) collective-permute-start(bf16[4,64,128]{2,1,0:T(8,128)(2,1)S(1)} %get-tuple-element.57), channel_id=1, source_target_pairs={{0,64},{4,68},{8,72},{12,76},{16,80},{20,84},{24,88},{28,92},{32,9... | collective-permute-start | bytes 196616 | tf_op jit(solution)/shard_map/ppermute | solution.py:50
  55.5 15.1 %collective-permute-start.17 = (bf16[64,4096]{1,0:T(8,128)(2,1)S(1)}, bf16[64,4096]{1,0:T(8,128)(2,1)S(1)}, u32[]{:S(2)}, u32[]{:S(2)}) collective-permute-start(bf16[64,4096]{1,0:T(8,128)(2,1)S(1)} %remote_part.7.own.refs_4_), channel_id=1, source_target_pairs={{0,3},{1,0},{2,1},{3,2},{4,7},{5,4},{6,5},{7,6},{8,11},{9,8},{10,9... | collective-permute-start | bytes 1572872 | tf_op jit(solution)/shard_map/ppermute | solution.py:519
  58.5 15.9 %collective-permute-start.16 = (bf16[64,4096]{1,0:T(8,128)(2,1)S(1)}, bf16[64,4096]{1,0:T(8,128)(2,1)S(1)}, u32[]{:S(2)}, u32[]{:S(2)}) collective-permute-start(bf16[64,4096]{1,0:T(8,128)(2,1)S(1)} %remote_part.7.own.refs_4_), channel_id=1, source_target_pairs={{0,1},{1,2},{2,3},{3,0},{4,5},{5,6},{6,7},{7,4},{8,9},{9,10},{10,1... | collective-permute-start | bytes 1572872 | tf_op jit(solution)/shard_map/ppermute | solution.py:519
  75.2 1.3 %collective-permute-start.18 = (f32[96,128]{1,0:T(8,128)S(1)}, f32[96,128]{1,0:T(8,128)S(1)}, u32[]{:S(2)}, u32[]{:S(2)}) collective-permute-start(f32[96,128]{1,0:T(8,128)S(1)} %gram_strip.1), channel_id=1, source_target_pairs={{0,4},{4,0},{8,12},{12,8},{16,20},{20,16},{24,28},{28,24},{32,36},... | collective-permute-start | bytes 147464 | tf_op jit(solution)/shard_map/ppermute | solution.py:524
  76.4 5.9 %collective-permute-start.21 = (f32[96,128]{1,0:T(8,128)S(1)}, f32[96,128]{1,0:T(8,128)S(1)}, u32[]{:S(2)}, u32[]{:S(2)}) collective-permute-start(f32[96,128]{1,0:T(8,128)S(1)} %add.21), channel_id=1, source_target_pairs={{0,24},{4,28},{8,16},{12,20},{16,8},{20,12},{24,0},{28,4},{32,56},... | collective-permute-start | bytes 147464 | tf_op jit(solution)/shard_map/ppermute | solution.py:524
  76.5 6.2 %collective-permute-start.20 = (f32[96,128]{1,0:T(8,128)S(1)}, f32[96,128]{1,0:T(8,128)S(1)}, u32[]{:S(2)}, u32[]{:S(2)}) collective-permute-start(f32[96,128]{1,0:T(8,128)S(1)} %add.21), channel_id=1, source_target_pairs={{0,16},{4,20},{8,24},{12,28},{16,0},{20,4},{24,8},{28,12},{32,48},... | collective-permute-start | bytes 147464 | tf_op jit(solution)/shard_map/ppermute | solution.py:524
  76.6 6.6 %collective-permute-start.19 = (f32[96,128]{1,0:T(8,128)S(1)}, f32[96,128]{1,0:T(8,128)S(1)}, u32[]{:S(2)}, u32[]{:S(2)}) collective-permute-start(f32[96,128]{1,0:T(8,128)S(1)} %add.21), channel_id=1, source_target_pairs={{0,8},{4,12},{8,0},{12,4},{16,24},{20,28},{24,16},{28,20},{32,40},... | collective-permute-start | bytes 147464 | tf_op jit(solution)/shard_map/ppermute | solution.py:524
  80.6 17.8 %collective-permute-start.28 = (bf16[64,4096]{1,0:T(8,128)(2,1)S(1)}, bf16[64,4096]{1,0:T(8,128)(2,1)S(1)}, u32[]{:S(2)}, u32[]{:S(2)}) collective-permute-start(bf16[64,4096]{1,0:T(8,128)(2,1)S(1)} %collective-permute-done.16.one.refs_5_), channel_id=1, source_target_pairs={{0,1},{1,2},{2,3},{3,0},{4,5},{5,6},{6,7},{7,4},{8,9},{9,10},{10,1... | collective-permute-start | bytes 1572872 | tf_op jit(solution)/shard_map/ppermute | solution.py:519
  83.2 5.9 %collective-permute-start.24 = (f32[96,128]{1,0:T(8,128)S(1)}, f32[96,128]{1,0:T(8,128)S(1)}, u32[]{:S(2)}, u32[]{:S(2)}) collective-permute-start(f32[96,128]{1,0:T(8,128)S(1)} %add_add_fusion.1), channel_id=1, source_target_pairs={{0,96},{4,100},{8,104},{12,108},{16,112},{20,116},{24,120},{28,124... | collective-permute-start | bytes 147464 | tf_op jit(solution)/shard_map/ppermute | solution.py:524
  86.0 5.6 %collective-permute-start.23 = (f32[96,128]{1,0:T(8,128)S(1)}, f32[96,128]{1,0:T(8,128)S(1)}, u32[]{:S(2)}, u32[]{:S(2)}) collective-permute-start(f32[96,128]{1,0:T(8,128)S(1)} %add_add_fusion.1), channel_id=1, source_target_pairs={{0,64},{4,68},{8,72},{12,76},{16,80},{20,84},{24,88},{28,92},{32,9... | collective-permute-start | bytes 147464 | tf_op jit(solution)/shard_map/ppermute | solution.py:524
  86.0 5.6 %collective-permute-start.22 = (f32[96,128]{1,0:T(8,128)S(1)}, f32[96,128]{1,0:T(8,128)S(1)}, u32[]{:S(2)}, u32[]{:S(2)}) collective-permute-start(f32[96,128]{1,0:T(8,128)S(1)} %add_add_fusion.1), channel_id=1, source_target_pairs={{0,32},{4,36},{8,40},{12,44},{16,48},{20,52},{24,56},{28,60},{32,0... | collective-permute-start | bytes 147464 | tf_op jit(solution)/shard_map/ppermute | solution.py:524
  91.6 4.2 %collective-permute-start.27 = (f32[96,128]{1,0:T(8,128)S(1)}, f32[96,128]{1,0:T(8,128)S(1)}, u32[]{:S(2)}, u32[]{:S(2)}) collective-permute-start(f32[96,128]{1,0:T(8,128)S(1)} %add_add_fusion.refs_0_), channel_id=1, source_target_pairs={{0,3},{1,0},{2,1},{3,2},{4,7},{5,4},{6,5},{7,6},{8,11},{9,8},{10,9... | collective-permute-start | bytes 147464 | tf_op jit(solution)/shard_map/ppermute | solution.py:519
  91.9 5.6 %collective-permute-start.26 = (f32[96,128]{1,0:T(8,128)S(1)}, f32[96,128]{1,0:T(8,128)S(1)}, u32[]{:S(2)}, u32[]{:S(2)}) collective-permute-start(f32[96,128]{1,0:T(8,128)S(1)} %add_add_fusion.refs_0_), channel_id=1, source_target_pairs={{0,2},{1,3},{2,0},{3,1},{4,6},{5,7},{6,4},{7,5},{8,10},{9,11},{10,... | collective-permute-start | bytes 147464 | tf_op jit(solution)/shard_map/ppermute | solution.py:519
  92.8 5.6 %collective-permute-start.25 = (f32[96,128]{1,0:T(8,128)S(1)}, f32[96,128]{1,0:T(8,128)S(1)}, u32[]{:S(2)}, u32[]{:S(2)}) collective-permute-start(f32[96,128]{1,0:T(8,128)S(1)} %add_add_fusion.refs_0_), channel_id=1, source_target_pairs={{0,1},{1,2},{2,3},{3,0},{4,5},{5,6},{6,7},{7,4},{8,9},{9,10},{10,1... | collective-permute-start | bytes 147464 | tf_op jit(solution)/shard_map/ppermute | solution.py:519

commit v8 on v7

--- a/solution.py
+++ b/solution.py
@@ -82,11 +82,11 @@
     pltpu.make_async_copy(part, part, sem).wait()
 
 
-def send_kernel(row_count, at, far_cols, far_x, far_onsite, far, *refs):
+def send_kernel(row_count, far_cols, far_x, far_onsite, far, *refs):
     info, own, x, onsite, blocks, *sends, cols, turned, sems = refs
     slot_count = cols.shape[0]
     _, local_blocks, size, _ = blocks.shape
-    here = at[0]
+    here = lax.axis_index("row")
     copies = [
         pltpu.make_async_copy(far_cols, cols, sems.at[0]),
         pltpu.make_async_copy(far_x, x, sems.at[1]),
@@ -133,7 +133,7 @@
         loaded(blocks, sems.at[3 + g], g)
 
 
-def send_part(row_count, at, cols, x, onsite, blocks):
+def send_part(row_count, cols, x, onsite, blocks):
     _, local_blocks, size, _ = blocks.shape
     send = jax.ShapeDtypeStruct((HALO, x.shape[0], size), jnp.bfloat16)
     whole = [jax.ShapeDtypeStruct(v.shape, v.dtype) for v in (x, onsite, blocks)]
@@ -146,7 +146,7 @@
             *whole,
         )
         + (send,) * 4,
-        in_specs=[smem] + [hbm] * 4,
+        in_specs=[hbm] * 4,
         out_specs=(smem,) + (vmem,) * 8,
         scratch_shapes=[
             pltpu.VMEM(cols.shape, jnp.int32),
@@ -155,7 +155,7 @@
         ],
         compiler_params=grant,
         name="send_part",
-    )(at, *[far_away(v) for v in (cols, x, onsite, blocks)])
+    )(*[far_away(v) for v in (cols, x, onsite, blocks)])
 
 
 def build_table(row_count, here, slot_count, values, info):
@@ -234,13 +234,13 @@
     local_rows_of(scale, table, groups, UNROLL, blocks, onsite, prev, y, held)
 
 
-def first_kernel(scale, row_count, at, info, own, far, started, x, onsite, *refs):
+def first_kernel(scale, row_count, info, own, far, started, x, onsite, *refs):
     y, table, blocks, held, near, sems = refs
     slot_count, local_blocks, _, _ = blocks.shape
     share = local_blocks // LOADS
     for g in range(EARLY, LOADS):
         load(far, blocks, sems.at[g], g)
-    table[...] = build_table(row_count, at[0], slot_count, own[...], info)
+    table[...] = build_table(row_count, lax.axis_index("row"), slot_count, own[...], info)
     copy = pltpu.make_async_copy(table, near, sems.at[LOADS])
     copy.start()
     hold(x, held, local_blocks)
@@ -317,7 +317,7 @@
     )(table, blocks, x, onsite, prev)
 
 
-def first_part(scale, row_count, at, info, own, far, started, x, onsite):
+def first_part(scale, row_count, info, own, far, started, x, onsite):
     _, local_blocks, size, _ = far.shape
     table = (local_blocks, LANES)
     hbm = pl.BlockSpec(memory_space=pltpu.HBM)
@@ -328,17 +328,17 @@
             jax.ShapeDtypeStruct(table, jnp.int32),
             jax.ShapeDtypeStruct(far.shape, far.dtype),
         ),
-        in_specs=[smem, smem, vmem, hbm, vmem, vmem, vmem],
+        in_specs=[smem, vmem, hbm, vmem, vmem, vmem],
         out_specs=(vmem,) * 3,
         scratch_shapes=[
             pltpu.VMEM((local_blocks + 1, x.shape[0], size), jnp.bfloat16),
             pltpu.SMEM(table, jnp.int32),
             pltpu.SemaphoreType.DMA((LOADS + 1,)),
         ],
-        input_output_aliases={4: 2},
+        input_output_aliases={3: 2},
         compiler_params=grant,
         name="first_part",
-    )(at, info, own, far, started, x, onsite)
+    )(info, own, far, started, x, onsite)
 
 
 def remote_part(scale, keep, last, table, halos, y, x, blocks):
@@ -392,10 +392,10 @@
     return high, middle, low
 
 
-def solve_kernel(root, own_ref, *refs):
+def solve_kernel(root, *refs):
     strips, finals, rest = refs[:4], refs[4:8], refs[8:]
     far_basis, far_factor, basis, factor, work, inverse, sems = rest
-    own = own_ref[0]
+    own = lax.axis_index("col")
     n = work.shape[0]
     width = n // 4
     f32 = jnp.float32
@@ -491,7 +491,7 @@
         copy.wait()
 
 
-def solve(root, own, strips, finals):
+def solve(root, strips, finals):
     n = 2 * strips[0].shape[1]
     hbm = pl.BlockSpec(memory_space=pltpu.HBM)
     return pl.pallas_call(
@@ -500,7 +500,7 @@
             jax.ShapeDtypeStruct(finals[0].shape, jnp.float32),
             jax.ShapeDtypeStruct((n, n), jnp.float32),
         ),
-        in_specs=[smem] + [vmem] * 8,
+        in_specs=[vmem] * 8,
         out_specs=(hbm,) * 2,
         scratch_shapes=[
             pltpu.VMEM(finals[0].shape, jnp.float32),
@@ -511,7 +511,7 @@
         ],
         compiler_params=grant,
         name="solve",
-    )(own, *strips, *finals)
+    )(*strips, *finals)
 
 
 def shift(value, axis, by):
@@ -537,13 +537,10 @@
 
 def body(subspace, onsite, blocks, cols):
     row_count = lax.axis_size("row")
-    row_index = lax.axis_index("row")
-    col_index = lax.axis_index("col").astype(jnp.int32)
     width, local_rows = subspace.shape
     slot_count, local_blocks, size, _ = blocks.shape
-    at = jnp.stack([row_index.astype(jnp.int32), col_index])
     onsite = onsite[None, :]
-    info, own, x, onsite, held, *send = send_part(row_count, at, cols.T, subspace, onsite, blocks)
+    info, own, x, onsite, held, *send = send_part(row_count, cols.T, subspace, onsite, blocks)
     previous, before = None, x
     for step in range(FILTER):
         scale = filter_scale if step == 0 else 2.0 * filter_scale
@@ -552,7 +549,7 @@
         halos = exchange(send, row_count)
         if step == 0:
             partial, table, held = first_part(
-                scale, row_count, at, info, own, blocks, held, x, onsite
+                scale, row_count, info, own, blocks, held, x, onsite
             )
         else:
             partial = local_part(scale, table, held, x, onsite, previous)
@@ -571,7 +568,7 @@
     strip = xor_sum(strip, "row", [x_bit, 2 * x_bit, 3 * x_bit])
     strips = [strip] + [shift(strip, "col", k) for k in (1, 2, 3)]
     root = math.sqrt(row_count * local_rows)
-    return solve(root, at[1:], strips, [final, one, two, three])
+    return solve(root, strips, [final, one, two, three])
 
 
 def solution(mesh):

time: 108 us -> 108 us (level)
  no operation moved by 1% of the time
where the time goes in v8:
time: 108 us; the launch traced here: 107 us
  Pallas kernels  38.7 us (36%)
  starting transfers between devices  34.7 us (32%)
  waiting for transfers between devices  33.1 us (31%)
    ppermute x16, starting transfers between devices, exchange(): lax.ppermute(send, 'row', list(zip(devices, to)))  21 us
    ppermute x6, waiting for transfers between devices, shift(): return lax.ppermute(value, axis, [(i, (i + by) % n) for i in range(n)])  20.7 us
    pallas_call x3, Pallas kernels, local_part(): pl.pallas_call(functools.partial(local_kernel, scale), out_shape=jax.Shap...  10.9 us
    pallas_call x1, Pallas kernels, solve(): pl.pallas_call(functools.partial(solve_kernel, root), out_shape=(jax.Shap...  9.47 us
    ppermute x7, starting transfers between devices, swap(): return lax.ppermute(value, axis, [(i, i ^ mask) for i in range(n)])  8.47 us
    ppermute x7, waiting for transfers between devices, swap(): return lax.ppermute(value, axis, [(i, i ^ mask) for i in range(n)])  7.9 us
    pallas_call x4, Pallas kernels, remote_part(): pl.pallas_call(functools.partial(remote_kernel, scale, keep, last), out_s...  7.62 us
    pallas_call x1, Pallas kernels, first_part(): pl.pallas_call(functools.partial(first_kernel, scale, row_count), out_sha...  7.54 us
  transfers between devices with their start and end apart: 29, of which 17 were waited for; matrix products, arithmetic and copies ran while one was open for 0% of the time, Pallas kernels for 17%

profile of v8, /device:TPU:0, one launch (start us, length us, event | category | flops | bytes accessed | tf_op | source)
XLA Modules:
  0.0 107.5 jit_solution(262504211875851485)
XLA Ops:
  0.6 2.5 %send_part.1 = (s32[16]{0:T(128)S(1)}, s32[32,128]{1,0:T(8,128)S(1)}, bf16[64,4096]{1,0:T(8,128)(2,1)S(1)}, f32[1,4096]{1,0:T(1,128)S(1)}, bf16[20,32,128,128]{3...) custom-call(s32[20,1024]{1,0:T(8,128)} %bitcast.2, ...), custom_call_target="tpu_custom_call" | custom-call | tf_op jit(solution)/shard_map/send_part/pallas_call | solution.py:141
  3.2 6.4 %collective-permute-start.1 = (bf16[4,64,128]{2,1,0:T(8,128)(2,1)S(1)}, bf16[4,64,128]{2,1,0:T(8,128)(2,1)S(1)}, u32[]{:S(2)}, u32[]{:S(2)}) collective-permute-start(bf16[4,64,128]{2,1,0:T(8,128)(2,1)S(1)} %get-tuple-element.38), channel_id=1, source_target_pairs={{0,124},{4,8},{8,4},{12,16},{16,12},{20,24},{24,20},{28,32},{32,28... | collective-permute-start | bytes 196616 | tf_op jit(solution)/shard_map/ppermute | solution.py:50
  10.9 7.5 %first_part.1 = (f32[64,4096]{1,0:T(8,128)S(1)}, s32[32,128]{1,0:T(8,128)S(1)}, bf16[20,32,128,128]{3,2,1,0:T(8,128)(2,1)S(1)}) custom-call(s32[16]{0:T(128)S(1)} %get-tuple-element.31.info, s32[32,128]{1,0:T(8,128)S(1)} %get-tuple-element.32.own, bf16[20,32,128,128]{3,2,1,0:T(8,128)(2,1)} %far.3, ...), custom_call_target="tpu_custom_call", output_to_operand_aliasing={{2}: (3, {})} | custom-call | tf_op jit(solution)/shard_map/first_part/pallas_call | solution.py:324
  18.4 1.9 %remote_part.4 = (bf16[64,4096]{1,0:T(8,128)(2,1)S(1)}, f32[64,4096]{1,0:T(8,128)S(1)}, bf16[4,64,128]{2,1,0:T(8,128)(2,1)S(1)}, bf16[4,64,128]{2,1,0:T(8,128)(2...) custom-call(s32[32,128]{1,0:T(8,128)S(1)} %get-tuple-element.36.table, ...), custom_call_target="tpu_custom_call" | custom-call | tf_op jit(solution)/shard_map/remote_part/pallas_call | solution.py:353
  20.5 1.5 %collective-permute-start.5 = (bf16[4,64,128]{2,1,0:T(8,128)(2,1)S(1)}, bf16[4,64,128]{2,1,0:T(8,128)(2,1)S(1)}, u32[]{:S(2)}, u32[]{:S(2)}) collective-permute-start(bf16[4,64,128]{2,1,0:T(8,128)(2,1)S(1)} %get-tuple-element.44), channel_id=1, source_target_pairs={{0,124},{4,8},{8,4},{12,16},{16,12},{20,24},{24,20},{28,32},{32,28... | collective-permute-start | bytes 196616 | tf_op jit(solution)/shard_map/ppermute | solution.py:50
  22.3 1.5 %collective-permute-start.7 = (bf16[4,64,128]{2,1,0:T(8,128)(2,1)S(1)}, bf16[4,64,128]{2,1,0:T(8,128)(2,1)S(1)}, u32[]{:S(2)}, u32[]{:S(2)}) collective-permute-start(bf16[4,64,128]{2,1,0:T(8,128)(2,1)S(1)} %get-tuple-element.46), channel_id=1, source_target_pairs={{0,64},{4,68},{8,72},{12,76},{16,80},{20,84},{24,88},{28,92},{32,9... | collective-permute-start | bytes 196616 | tf_op jit(solution)/shard_map/ppermute | solution.py:50
  23.8 3.6 %local_part.3.refs_4_ = f32[64,4096]{1,0:T(8,128)S(1)} custom-call(s32[32,128]{1,0:T(8,128)S(1)} %get-tuple-element.36.table, bf16[20,32,128,128]{3,2,1,0:T(8,128)(2,1)S(1)} %get-tuple-element.42.refs_6_.blocks, bf16[64,4096]{1,0:T(8,128)(2,1)S(1)} %get-tuple-element.47.x.refs_5_, f32[1,4096]{1,0:T(1,128)S(1)} %get-tuple-element.35.onsite, ...), custom_call_target="tpu_custom_call" | custom-call | tf_op jit(solution)/shard_map/local_part/pallas_call | solution.py:309
  28.1 1.9 %remote_part.5 = (bf16[64,4096]{1,0:T(8,128)(2,1)S(1)}, f32[64,4096]{1,0:T(8,128)S(1)}, bf16[4,64,128]{2,1,0:T(8,128)(2,1)S(1)}, bf16[4,64,128]{2,1,0:T(8,128)(2...) custom-call(s32[32,128]{1,0:T(8,128)S(1)} %get-tuple-element.36.table, ...), custom_call_target="tpu_custom_call" | custom-call | tf_op jit(solution)/shard_map/remote_part/pallas_call | solution.py:353
  30.1 2.6 %collective-permute-start.8 = (bf16[4,64,128]{2,1,0:T(8,128)(2,1)S(1)}, bf16[4,64,128]{2,1,0:T(8,128)(2,1)S(1)}, u32[]{:S(2)}, u32[]{:S(2)}) collective-permute-start(bf16[4,64,128]{2,1,0:T(8,128)(2,1)S(1)} %get-tuple-element.48), channel_id=1, source_target_pairs={{0,4},{4,0},{8,12},{12,8},{16,20},{20,16},{24,28},{28,24},{32,36},... | collective-permute-start | bytes 196616 | tf_op jit(solution)/shard_map/ppermute | solution.py:50
  32.7 2.2 %collective-permute-start.9 = (bf16[4,64,128]{2,1,0:T(8,128)(2,1)S(1)}, bf16[4,64,128]{2,1,0:T(8,128)(2,1)S(1)}, u32[]{:S(2)}, u32[]{:S(2)}) collective-permute-start(bf16[4,64,128]{2,1,0:T(8,128)(2,1)S(1)} %get-tuple-element.49), channel_id=1, source_target_pairs={{0,124},{4,8},{8,4},{12,16},{16,12},{20,24},{24,20},{28,32},{32,28... | collective-permute-start | bytes 196616 | tf_op jit(solution)/shard_map/ppermute | solution.py:50
  35.5 3.6 %local_part.4.refs_4_ = f32[64,4096]{1,0:T(8,128)S(1)} custom-call(s32[32,128]{1,0:T(8,128)S(1)} %get-tuple-element.36.table, bf16[20,32,128,128]{3,2,1,0:T(8,128)(2,1)S(1)} %get-tuple-element.42.refs_6_.blocks, bf16[64,4096]{1,0:T(8,128)(2,1)S(1)} %get-tuple-element.52.x.refs_5_, f32[1,4096]{1,0:T(1,128)S(1)} %get-tuple-element.35.onsite, ...), custom_call_target="tpu_custom_call" | custom-call | tf_op jit(solution)/shard_map/local_part/pallas_call | solution.py:309
  39.2 1.7 %collective-permute-done.9.refs_1_ = bf16[4,64,128]{2,1,0:T(8,128)(2,1)S(1)} collective-permute-done((bf16[4,64,128]{2,1,0:T(8,128)(2,1)S(1)}, bf16[4,64,128]{2,1,0:T(8,128)(2,1)S(1)}, u32[]{:S(2)}, u32[]{:S(2)}) %collective-permute-start.9) | collective-permute-done | bytes 65568 | tf_op jit(solution)/shard_map/ppermute | solution.py:50
  41.0 1.9 %remote_part.6 = (bf16[64,4096]{1,0:T(8,128)(2,1)S(1)}, bf16[4,64,128]{2,1,0:T(8,128)(2,1)S(1)}, bf16[4,64,128]{2,1,0:T(8,128)(2,1)S(1)}, bf16[4,64,128]{2,1,0:T(8,128)(2,1)S(1)}, bf16[4,64,128]{2,1,0:T(8,128)(2,1)S(1)}) custom-call(s32[32,128]{1,0:T(8,128)S(1)} %get-tuple-element.36.table, bf16[4,64,128]{2,1,0:T(8,128)(2,1)S(1)} %collective-permute-done.8.refs_0_, ...), custom_call_target="tpu_custom_call" | custom-call | tf_op jit(solution)/shard_map/remote_part/pallas_call | solution.py:353
  42.9 1.6 %collective-permute-start.12 = (bf16[4,64,128]{2,1,0:T(8,128)(2,1)S(1)}, bf16[4,64,128]{2,1,0:T(8,128)(2,1)S(1)}, u32[]{:S(2)}, u32[]{:S(2)}) collective-permute-start(bf16[4,64,128]{2,1,0:T(8,128)(2,1)S(1)} %get-tuple-element.54), channel_id=1, source_target_pairs={{0,4},{4,0},{8,12},{12,8},{16,20},{20,16},{24,28},{28,24},{32,36},... | collective-permute-start | bytes 196616 | tf_op jit(solution)/shard_map/ppermute | solution.py:50
  44.5 2.4 %collective-permute-start.13 = (bf16[4,64,128]{2,1,0:T(8,128)(2,1)S(1)}, bf16[4,64,128]{2,1,0:T(8,128)(2,1)S(1)}, u32[]{:S(2)}, u32[]{:S(2)}) collective-permute-start(bf16[4,64,128]{2,1,0:T(8,128)(2,1)S(1)} %get-tuple-element.55), channel_id=1, source_target_pairs={{0,124},{4,8},{8,4},{12,16},{16,12},{20,24},{24,20},{28,32},{32,28... | collective-permute-start | bytes 196616 | tf_op jit(solution)/shard_map/ppermute | solution.py:50
  47.2 3.6 %local_part.5.refs_4_ = f32[64,4096]{1,0:T(8,128)S(1)} custom-call(s32[32,128]{1,0:T(8,128)S(1)} %get-tuple-element.36.table, bf16[20,32,128,128]{3,2,1,0:T(8,128)(2,1)S(1)} %get-tuple-element.42.refs_6_.blocks, bf16[64,4096]{1,0:T(8,128)(2,1)S(1)} %get-tuple-element.58.x.refs_5_, f32[1,4096]{1,0:T(1,128)S(1)} %get-tuple-element.35.onsite, ...), custom_call_target="tpu_custom_call" | custom-call | tf_op jit(solution)/shard_map/local_part/pallas_call | solution.py:309
  51.5 1.5 %collective-permute-done.15.refs_3_ = bf16[4,64,128]{2,1,0:T(8,128)(2,1)S(1)} collective-permute-done((bf16[4,64,128]{2,1,0:T(8,128)(2,1)S(1)}, bf16[4,64,128]{2,1,0:T(8,128)(2,1)S(1)}, u32[]{:S(2)}, u32[]{:S(2)}) %collective-permute-start.15) | collective-permute-done | bytes 65568 | tf_op jit(solution)/shard_map/ppermute | solution.py:50
  53.0 1.8 %remote_part.7.own.refs_4_ = bf16[64,4096]{1,0:T(8,128)(2,1)S(1)} custom-call(s32[32,128]{1,0:T(8,128)S(1)} %get-tuple-element.36.table, bf16[4,64,128]{2,1,0:T(8,128)(2,1)S(1)} %collective-permute-done.12.refs_0_, bf16[4,64,128]{2,1,0:T(8,128)(2,1)S(1)} %collective-permute-done.13.refs_1_, bf16[4,64,128]{2,1,0:T(8,128)(2,1)S(1)} %collective-permute-done.14.refs_2_, ...), custom_call_target="tpu_custom_call" | custom-call | tf_op jit(solution)/shard_map/remote_part/pallas_call | solution.py:353
  54.8 3.1 %collective-permute-start.17 = (bf16[64,4096]{1,0:T(8,128)(2,1)S(1)}, bf16[64,4096]{1,0:T(8,128)(2,1)S(1)}, u32[]{:S(2)}, u32[]{:S(2)}) collective-permute-start(bf16[64,4096]{1,0:T(8,128)(2,1)S(1)} %remote_part.7.own.refs_4_), channel_id=1, source_target_pairs={{0,3},{1,0},{2,1},{3,2},{4,7},{5,4},{6,5},{7,6},{8,11},{9,8},{10,9... | collective-permute-start | bytes 1572872 | tf_op jit(solution)/shard_map/ppermute | solution.py:519
  57.9 12.0 %collective-permute-done.17.three.refs_7_ = bf16[64,4096]{1,0:T(8,128)(2,1)S(1)} collective-permute-done((bf16[64,4096]{1,0:T(8,128)(2,1)S(1)}, bf16[64,4096]{1,0:T(8,128)(2,1)S(1)}, u32[]{:S(2)}, u32[]{:S(2)}) %collective-permute-start.17) | collective-permute-done | bytes 524320 | tf_op jit(solution)/shard_map/ppermute | solution.py:519
  69.9 4.0 %collective-permute-done.16.one.refs_5_ = bf16[64,4096]{1,0:T(8,128)(2,1)S(1)} collective-permute-done((bf16[64,4096]{1,0:T(8,128)(2,1)S(1)}, bf16[64,4096]{1,0:T(8,128)(2,1)S(1)}, u32[]{:S(2)}, u32[]{:S(2)}) %collective-permute-start.16) | collective-permute-done | bytes 524320 | tf_op jit(solution)/shard_map/ppermute | solution.py:519
  74.7 1.1 %collective-permute-done.18 = f32[96,128]{1,0:T(8,128)S(1)} collective-permute-done((f32[96,128]{1,0:T(8,128)S(1)}, f32[96,128]{1,0:T(8,128)S(1)}, u32[]{:S(2)}, u32[]{:S(2)}) %collective-permute-start.18) | collective-permute-done | bytes 49184 | tf_op jit(solution)/shard_map/ppermute | solution.py:524
  76.0 4.0 %collective-permute-start.19 = (f32[96,128]{1,0:T(8,128)S(1)}, f32[96,128]{1,0:T(8,128)S(1)}, u32[]{:S(2)}, u32[]{:S(2)}) collective-permute-start(f32[96,128]{1,0:T(8,128)S(1)} %add.21), channel_id=1, source_target_pairs={{0,8},{4,12},{8,0},{12,4},{16,24},{20,28},{24,16},{28,20},{32,40},... | collective-permute-start | bytes 147464 | tf_op jit(solution)/shard_map/ppermute | solution.py:524
  80.0 1.8 %collective-permute-done.21 = f32[96,128]{1,0:T(8,128)S(1)} collective-permute-done((f32[96,128]{1,0:T(8,128)S(1)}, f32[96,128]{1,0:T(8,128)S(1)}, u32[]{:S(2)}, u32[]{:S(2)}) %collective-permute-start.21) | collective-permute-done | bytes 49184 | tf_op jit(solution)/shard_map/ppermute | solution.py:524
  82.6 2.8 %collective-permute-start.24 = (f32[96,128]{1,0:T(8,128)S(1)}, f32[96,128]{1,0:T(8,128)S(1)}, u32[]{:S(2)}, u32[]{:S(2)}) collective-permute-start(f32[96,128]{1,0:T(8,128)S(1)} %add_add_fusion.1), channel_id=1, source_target_pairs={{0,96},{4,100},{8,104},{12,108},{16,112},{20,116},{24,120},{28,124... | collective-permute-start | bytes 147464 | tf_op jit(solution)/shard_map/ppermute | solution.py:524
  85.4 1.4 %collective-permute-start.22 = (f32[96,128]{1,0:T(8,128)S(1)}, f32[96,128]{1,0:T(8,128)S(1)}, u32[]{:S(2)}, u32[]{:S(2)}) collective-permute-start(f32[96,128]{1,0:T(8,128)S(1)} %add_add_fusion.1), channel_id=1, source_target_pairs={{0,32},{4,36},{8,40},{12,44},{16,48},{20,52},{24,56},{28,60},{32,0... | collective-permute-start | bytes 147464 | tf_op jit(solution)/shard_map/ppermute | solution.py:524
  86.8 1.7 %collective-permute-done.24 = f32[96,128]{1,0:T(8,128)S(1)} collective-permute-done((f32[96,128]{1,0:T(8,128)S(1)}, f32[96,128]{1,0:T(8,128)S(1)}, u32[]{:S(2)}, u32[]{:S(2)}) %collective-permute-start.24) | collective-permute-done | bytes 49184 | tf_op jit(solution)/shard_map/ppermute | solution.py:524
  88.5 2.5 %collective-permute-done.23 = f32[96,128]{1,0:T(8,128)S(1)} collective-permute-done((f32[96,128]{1,0:T(8,128)S(1)}, f32[96,128]{1,0:T(8,128)S(1)}, u32[]{:S(2)}, u32[]{:S(2)}) %collective-permute-start.23) | collective-permute-done | bytes 49184 | tf_op jit(solution)/shard_map/ppermute | solution.py:524
  92.2 0.9 collective-permute-start.25
  93.1 2.1 %collective-permute-done.27.refs_3_ = f32[96,128]{1,0:T(8,128)S(1)} collective-permute-done((f32[96,128]{1,0:T(8,128)S(1)}, f32[96,128]{1,0:T(8,128)S(1)}, u32[]{:S(2)}, u32[]{:S(2)}) %collective-permute-start.27) | collective-permute-done | bytes 49184 | tf_op jit(solution)/shard_map/ppermute | solution.py:519
  95.2 1.8 %collective-permute-done.26.refs_2_ = f32[96,128]{1,0:T(8,128)S(1)} collective-permute-done((f32[96,128]{1,0:T(8,128)S(1)}, f32[96,128]{1,0:T(8,128)S(1)}, u32[]{:S(2)}, u32[]{:S(2)}) %collective-permute-start.26) | collective-permute-done | bytes 49184 | tf_op jit(solution)/shard_map/ppermute | solution.py:519
  97.8 9.5 %solve.1 = (f32[64,4096]{1,0:T(8,128)}, f32[256,256]{1,0:T(8,128)}) custom-call(f32[96,128]{1,0:T(8,128)S(1)} %add_add_fusion.refs_0_, f32[96,128]{1,0:T(8,128)S(1)} %collective-permute-done.25.refs_1_, f32[96,128]{1,0:T(8,128)S(1)} %collective-permute-done.26.refs_2_, f32[96,128]{1,0:T(8,128)S(1)} %collective-permute-done.27.refs_3_, ...), custom_call_target="tpu_custom_call" | custom-call | tf_op jit(solution)/shard_map/solve/pallas_call | solution.py:497
  (40 shorter events, 8.0 us)
Async XLA Ops:
  3.1 15.3 %collective-permute-start = (bf16[4,64,128]{2,1,0:T(8,128)(2,1)S(1)}, bf16[4,64,128]{2,1,0:T(8,128)(2,1)S(1)}, u32[]{:S(2)}, u32[]{:S(2)}) collective-permute-start(bf16[4,64,128]{2,1,0:T(8,128)(2,1)S(1)} %get-tuple-element.37), channel_id=1, source_target_pairs={{0,4},{4,0},{8,12},{12,8},{16,20},{20,16},{24,28},{28,24},{32,36},... | collective-permute-start | bytes 196616 | tf_op jit(solution)/shard_map/ppermute | solution.py:50
  3.2 15.2 %collective-permute-start.1 = (bf16[4,64,128]{2,1,0:T(8,128)(2,1)S(1)}, bf16[4,64,128]{2,1,0:T(8,128)(2,1)S(1)}, u32[]{:S(2)}, u32[]{:S(2)}) collective-permute-start(bf16[4,64,128]{2,1,0:T(8,128)(2,1)S(1)} %get-tuple-element.38), channel_id=1, source_target_pairs={{0,124},{4,8},{8,4},{12,16},{16,12},{20,24},{24,20},{28,32},{32,28... | collective-permute-start | bytes 196616 | tf_op jit(solution)/shard_map/ppermute | solution.py:50
  9.7 8.8 %collective-permute-start.2 = (bf16[4,64,128]{2,1,0:T(8,128)(2,1)S(1)}, bf16[4,64,128]{2,1,0:T(8,128)(2,1)S(1)}, u32[]{:S(2)}, u32[]{:S(2)}) collective-permute-start(bf16[4,64,128]{2,1,0:T(8,128)(2,1)S(1)} %get-tuple-element.39), channel_id=1, source_target_pairs={{0,120},{4,124},{8,0},{12,4},{16,8},{20,12},{24,16},{28,20},{32,24... | collective-permute-start | bytes 196616 | tf_op jit(solution)/shard_map/ppermute | solution.py:50
  10.1 8.4 %collective-permute-start.3 = (bf16[4,64,128]{2,1,0:T(8,128)(2,1)S(1)}, bf16[4,64,128]{2,1,0:T(8,128)(2,1)S(1)}, u32[]{:S(2)}, u32[]{:S(2)}) collective-permute-start(bf16[4,64,128]{2,1,0:T(8,128)(2,1)S(1)} %get-tuple-element.40), channel_id=1, source_target_pairs={{0,64},{4,68},{8,72},{12,76},{16,80},{20,84},{24,88},{28,92},{32,9... | collective-permute-start | bytes 196616 | tf_op jit(solution)/shard_map/ppermute | solution.py:50
  20.4 7.1 %collective-permute-start.4 = (bf16[4,64,128]{2,1,0:T(8,128)(2,1)S(1)}, bf16[4,64,128]{2,1,0:T(8,128)(2,1)S(1)}, u32[]{:S(2)}, u32[]{:S(2)}) collective-permute-start(bf16[4,64,128]{2,1,0:T(8,128)(2,1)S(1)} %get-tuple-element.43), channel_id=1, source_target_pairs={{0,4},{4,0},{8,12},{12,8},{16,20},{20,16},{24,28},{28,24},{32,36},... | collective-permute-start | bytes 196616 | tf_op jit(solution)/shard_map/ppermute | solution.py:50
  20.5 7.1 %collective-permute-start.5 = (bf16[4,64,128]{2,1,0:T(8,128)(2,1)S(1)}, bf16[4,64,128]{2,1,0:T(8,128)(2,1)S(1)}, u32[]{:S(2)}, u32[]{:S(2)}) collective-permute-start(bf16[4,64,128]{2,1,0:T(8,128)(2,1)S(1)} %get-tuple-element.44), channel_id=1, source_target_pairs={{0,124},{4,8},{8,4},{12,16},{16,12},{20,24},{24,20},{28,32},{32,28... | collective-permute-start | bytes 196616 | tf_op jit(solution)/shard_map/ppermute | solution.py:50
  21.9 5.6 %collective-permute-start.6 = (bf16[4,64,128]{2,1,0:T(8,128)(2,1)S(1)}, bf16[4,64,128]{2,1,0:T(8,128)(2,1)S(1)}, u32[]{:S(2)}, u32[]{:S(2)}) collective-permute-start(bf16[4,64,128]{2,1,0:T(8,128)(2,1)S(1)} %get-tuple-element.45), channel_id=1, source_target_pairs={{0,120},{4,124},{8,0},{12,4},{16,8},{20,12},{24,16},{28,20},{32,24... | collective-permute-start | bytes 196616 | tf_op jit(solution)/shard_map/ppermute | solution.py:50
  22.3 5.8 %collective-permute-start.7 = (bf16[4,64,128]{2,1,0:T(8,128)(2,1)S(1)}, bf16[4,64,128]{2,1,0:T(8,128)(2,1)S(1)}, u32[]{:S(2)}, u32[]{:S(2)}) collective-permute-start(bf16[4,64,128]{2,1,0:T(8,128)(2,1)S(1)} %get-tuple-element.46), channel_id=1, source_target_pairs={{0,64},{4,68},{8,72},{12,76},{16,80},{20,84},{24,88},{28,92},{32,9... | collective-permute-start | bytes 196616 | tf_op jit(solution)/shard_map/ppermute | solution.py:50
  30.1 9.1 %collective-permute-start.8 = (bf16[4,64,128]{2,1,0:T(8,128)(2,1)S(1)}, bf16[4,64,128]{2,1,0:T(8,128)(2,1)S(1)}, u32[]{:S(2)}, u32[]{:S(2)}) collective-permute-start(bf16[4,64,128]{2,1,0:T(8,128)(2,1)S(1)} %get-tuple-element.48), channel_id=1, source_target_pairs={{0,4},{4,0},{8,12},{12,8},{16,20},{20,16},{24,28},{28,24},{32,36},... | collective-permute-start | bytes 196616 | tf_op jit(solution)/shard_map/ppermute | solution.py:50
  32.7 8.2 %collective-permute-start.9 = (bf16[4,64,128]{2,1,0:T(8,128)(2,1)S(1)}, bf16[4,64,128]{2,1,0:T(8,128)(2,1)S(1)}, u32[]{:S(2)}, u32[]{:S(2)}) collective-permute-start(bf16[4,64,128]{2,1,0:T(8,128)(2,1)S(1)} %get-tuple-element.49), channel_id=1, source_target_pairs={{0,124},{4,8},{8,4},{12,16},{16,12},{20,24},{24,20},{28,32},{32,28... | collective-permute-start | bytes 196616 | tf_op jit(solution)/shard_map/ppermute | solution.py:50
  34.9 6.0 %collective-permute-start.10 = (bf16[4,64,128]{2,1,0:T(8,128)(2,1)S(1)}, bf16[4,64,128]{2,1,0:T(8,128)(2,1)S(1)}, u32[]{:S(2)}, u32[]{:S(2)}) collective-permute-start(bf16[4,64,128]{2,1,0:T(8,128)(2,1)S(1)} %get-tuple-element.50), channel_id=1, source_target_pairs={{0,120},{4,124},{8,0},{12,4},{16,8},{20,12},{24,16},{28,20},{32,24... | collective-permute-start | bytes 196616 | tf_op jit(solution)/shard_map/ppermute | solution.py:50
  35.2 5.8 %collective-permute-start.11 = (bf16[4,64,128]{2,1,0:T(8,128)(2,1)S(1)}, bf16[4,64,128]{2,1,0:T(8,128)(2,1)S(1)}, u32[]{:S(2)}, u32[]{:S(2)}) collective-permute-start(bf16[4,64,128]{2,1,0:T(8,128)(2,1)S(1)} %get-tuple-element.51), channel_id=1, source_target_pairs={{0,64},{4,68},{8,72},{12,76},{16,80},{20,84},{24,88},{28,92},{32,9... | collective-permute-start | bytes 196616 | tf_op jit(solution)/shard_map/ppermute | solution.py:50
  42.9 8.0 %collective-permute-start.12 = (bf16[4,64,128]{2,1,0:T(8,128)(2,1)S(1)}, bf16[4,64,128]{2,1,0:T(8,128)(2,1)S(1)}, u32[]{:S(2)}, u32[]{:S(2)}) collective-permute-start(bf16[4,64,128]{2,1,0:T(8,128)(2,1)S(1)} %get-tuple-element.54), channel_id=1, source_target_pairs={{0,4},{4,0},{8,12},{12,8},{16,20},{20,16},{24,28},{28,24},{32,36},... | collective-permute-start | bytes 196616 | tf_op jit(solution)/shard_map/ppermute | solution.py:50
  44.5 7.0 %collective-permute-start.13 = (bf16[4,64,128]{2,1,0:T(8,128)(2,1)S(1)}, bf16[4,64,128]{2,1,0:T(8,128)(2,1)S(1)}, u32[]{:S(2)}, u32[]{:S(2)}) collective-permute-start(bf16[4,64,128]{2,1,0:T(8,128)(2,1)S(1)} %get-tuple-element.55), channel_id=1, source_target_pairs={{0,124},{4,8},{8,4},{12,16},{16,12},{20,24},{24,20},{28,32},{32,28... | collective-permute-start | bytes 196616 | tf_op jit(solution)/shard_map/ppermute | solution.py:50
  46.9 4.6 %collective-permute-start.14 = (bf16[4,64,128]{2,1,0:T(8,128)(2,1)S(1)}, bf16[4,64,128]{2,1,0:T(8,128)(2,1)S(1)}, u32[]{:S(2)}, u32[]{:S(2)}) collective-permute-start(bf16[4,64,128]{2,1,0:T(8,128)(2,1)S(1)} %get-tuple-element.56), channel_id=1, source_target_pairs={{0,120},{4,124},{8,0},{12,4},{16,8},{20,12},{24,16},{28,20},{32,24... | collective-permute-start | bytes 196616 | tf_op jit(solution)/shard_map/ppermute | solution.py:50
  47.2 5.8 %collective-permute-start.15 = (bf16[4,64,128]{2,1,0:T(8,128)(2,1)S(1)}, bf16[4,64,128]{2,1,0:T(8,128)(2,1)S(1)}, u32[]{:S(2)}, u32[]{:S(2)}) collective-permute-start(bf16[4,64,128]{2,1,0:T(8,128)(2,1)S(1)} %get-tuple-element.57), channel_id=1, source_target_pairs={{0,64},{4,68},{8,72},{12,76},{16,80},{20,84},{24,88},{28,92},{32,9... | collective-permute-start | bytes 196616 | tf_op jit(solution)/shard_map/ppermute | solution.py:50
  54.8 15.1 %collective-permute-start.17 = (bf16[64,4096]{1,0:T(8,128)(2,1)S(1)}, bf16[64,4096]{1,0:T(8,128)(2,1)S(1)}, u32[]{:S(2)}, u32[]{:S(2)}) collective-permute-start(bf16[64,4096]{1,0:T(8,128)(2,1)S(1)} %remote_part.7.own.refs_4_), channel_id=1, source_target_pairs={{0,3},{1,0},{2,1},{3,2},{4,7},{5,4},{6,5},{7,6},{8,11},{9,8},{10,9... | collective-permute-start | bytes 1572872 | tf_op jit(solution)/shard_map/ppermute | solution.py:519
  57.9 16.0 %collective-permute-start.16 = (bf16[64,4096]{1,0:T(8,128)(2,1)S(1)}, bf16[64,4096]{1,0:T(8,128)(2,1)S(1)}, u32[]{:S(2)}, u32[]{:S(2)}) collective-permute-start(bf16[64,4096]{1,0:T(8,128)(2,1)S(1)} %remote_part.7.own.refs_4_), channel_id=1, source_target_pairs={{0,1},{1,2},{2,3},{3,0},{4,5},{5,6},{6,7},{7,4},{8,9},{9,10},{10,1... | collective-permute-start | bytes 1572872 | tf_op jit(solution)/shard_map/ppermute | solution.py:519
  74.6 1.3 %collective-permute-start.18 = (f32[96,128]{1,0:T(8,128)S(1)}, f32[96,128]{1,0:T(8,128)S(1)}, u32[]{:S(2)}, u32[]{:S(2)}) collective-permute-start(f32[96,128]{1,0:T(8,128)S(1)} %gram_strip.1), channel_id=1, source_target_pairs={{0,4},{4,0},{8,12},{12,8},{16,20},{20,16},{24,28},{28,24},{32,36},... | collective-permute-start | bytes 147464 | tf_op jit(solution)/shard_map/ppermute | solution.py:524
  75.8 5.9 %collective-permute-start.21 = (f32[96,128]{1,0:T(8,128)S(1)}, f32[96,128]{1,0:T(8,128)S(1)}, u32[]{:S(2)}, u32[]{:S(2)}) collective-permute-start(f32[96,128]{1,0:T(8,128)S(1)} %add.21), channel_id=1, source_target_pairs={{0,24},{4,28},{8,16},{12,20},{16,8},{20,12},{24,0},{28,4},{32,56},... | collective-permute-start | bytes 147464 | tf_op jit(solution)/shard_map/ppermute | solution.py:524
  75.9 6.2 %collective-permute-start.20 = (f32[96,128]{1,0:T(8,128)S(1)}, f32[96,128]{1,0:T(8,128)S(1)}, u32[]{:S(2)}, u32[]{:S(2)}) collective-permute-start(f32[96,128]{1,0:T(8,128)S(1)} %add.21), channel_id=1, source_target_pairs={{0,16},{4,20},{8,24},{12,28},{16,0},{20,4},{24,8},{28,12},{32,48},... | collective-permute-start | bytes 147464 | tf_op jit(solution)/shard_map/ppermute | solution.py:524
  76.0 6.6 %collective-permute-start.19 = (f32[96,128]{1,0:T(8,128)S(1)}, f32[96,128]{1,0:T(8,128)S(1)}, u32[]{:S(2)}, u32[]{:S(2)}) collective-permute-start(f32[96,128]{1,0:T(8,128)S(1)} %add.21), channel_id=1, source_target_pairs={{0,8},{4,12},{8,0},{12,4},{16,24},{20,28},{24,16},{28,20},{32,40},... | collective-permute-start | bytes 147464 | tf_op jit(solution)/shard_map/ppermute | solution.py:524
  80.0 17.8 %collective-permute-start.28 = (bf16[64,4096]{1,0:T(8,128)(2,1)S(1)}, bf16[64,4096]{1,0:T(8,128)(2,1)S(1)}, u32[]{:S(2)}, u32[]{:S(2)}) collective-permute-start(bf16[64,4096]{1,0:T(8,128)(2,1)S(1)} %collective-permute-done.16.one.refs_5_), channel_id=1, source_target_pairs={{0,1},{1,2},{2,3},{3,0},{4,5},{5,6},{6,7},{7,4},{8,9},{9,10},{10,1... | collective-permute-start | bytes 1572872 | tf_op jit(solution)/shard_map/ppermute | solution.py:519
  82.6 5.9 %collective-permute-start.24 = (f32[96,128]{1,0:T(8,128)S(1)}, f32[96,128]{1,0:T(8,128)S(1)}, u32[]{:S(2)}, u32[]{:S(2)}) collective-permute-start(f32[96,128]{1,0:T(8,128)S(1)} %add_add_fusion.1), channel_id=1, source_target_pairs={{0,96},{4,100},{8,104},{12,108},{16,112},{20,116},{24,120},{28,124... | collective-permute-start | bytes 147464 | tf_op jit(solution)/shard_map/ppermute | solution.py:524
  85.4 5.6 %collective-permute-start.23 = (f32[96,128]{1,0:T(8,128)S(1)}, f32[96,128]{1,0:T(8,128)S(1)}, u32[]{:S(2)}, u32[]{:S(2)}) collective-permute-start(f32[96,128]{1,0:T(8,128)S(1)} %add_add_fusion.1), channel_id=1, source_target_pairs={{0,64},{4,68},{8,72},{12,76},{16,80},{20,84},{24,88},{28,92},{32,9... | collective-permute-start | bytes 147464 | tf_op jit(solution)/shard_map/ppermute | solution.py:524
  85.4 5.6 %collective-permute-start.22 = (f32[96,128]{1,0:T(8,128)S(1)}, f32[96,128]{1,0:T(8,128)S(1)}, u32[]{:S(2)}, u32[]{:S(2)}) collective-permute-start(f32[96,128]{1,0:T(8,128)S(1)} %add_add_fusion.1), channel_id=1, source_target_pairs={{0,32},{4,36},{8,40},{12,44},{16,48},{20,52},{24,56},{28,60},{32,0... | collective-permute-start | bytes 147464 | tf_op jit(solution)/shard_map/ppermute | solution.py:524
  91.0 4.2 %collective-permute-start.27 = (f32[96,128]{1,0:T(8,128)S(1)}, f32[96,128]{1,0:T(8,128)S(1)}, u32[]{:S(2)}, u32[]{:S(2)}) collective-permute-start(f32[96,128]{1,0:T(8,128)S(1)} %add_add_fusion.refs_0_), channel_id=1, source_target_pairs={{0,3},{1,0},{2,1},{3,2},{4,7},{5,4},{6,5},{7,6},{8,11},{9,8},{10,9... | collective-permute-start | bytes 147464 | tf_op jit(solution)/shard_map/ppermute | solution.py:519
  91.4 5.6 %collective-permute-start.26 = (f32[96,128]{1,0:T(8,128)S(1)}, f32[96,128]{1,0:T(8,128)S(1)}, u32[]{:S(2)}, u32[]{:S(2)}) collective-permute-start(f32[96,128]{1,0:T(8,128)S(1)} %add_add_fusion.refs_0_), channel_id=1, source_target_pairs={{0,2},{1,3},{2,0},{3,1},{4,6},{5,7},{6,4},{7,5},{8,10},{9,11},{10,... | collective-permute-start | bytes 147464 | tf_op jit(solution)/shard_map/ppermute | solution.py:519
  92.2 5.6 %collective-permute-start.25 = (f32[96,128]{1,0:T(8,128)S(1)}, f32[96,128]{1,0:T(8,128)S(1)}, u32[]{:S(2)}, u32[]{:S(2)}) collective-permute-start(f32[96,128]{1,0:T(8,128)S(1)} %add_add_fusion.refs_0_), channel_id=1, source_target_pairs={{0,1},{1,2},{2,3},{3,0},{4,5},{5,6},{6,7},{7,4},{8,9},{9,10},{10,1... | collective-permute-start | bytes 147464 | tf_op jit(solution)/shard_map/ppermute | solution.py:519
